TPU v7x, 128 devices: a whole 4x4x4 slice. The times are simulated.
128 devices in a mesh: xi: 4 (over x_hi, core), eta: 4 (over y), zeta: 8 (over z, x_lo).
Axes of the slice: x: 4 (x_hi: 2, x_lo: 2; x = x_hi * 2 + x_lo), y: 4, z: 4, core: 2. Of those that a mesh axis runs over, the one named last changes fastest.
Arguments:
- conserved_solution: float32 [5, 64, 64, 1024], P(None, 'xi', 'eta', 'zeta'), may hold values from -1.2 to 6, as said below
- metrics: float32 [3, 3, 64, 64, 1024], P(None, None, 'xi', 'eta', 'zeta'), may hold values from -0.4 to 1.4, as said below
- jacobian: float32 [64, 64, 1024], P('xi', 'eta', 'zeta'), may hold values from 0.7 to 1.4
Outputs:
- filtered: float32 [5, 64, 64, 1024], P(None, 'xi', 'eta', 'zeta')
Inputs may be any that keep to these rules, and one draw needn't show every extreme that they name: conserved_solution[0] (density) lies between 0.5 and 2, and the pressure 0.4 (conserved_solution[4] - (conserved_solution[1]^2 + conserved_solution[2]^2 + conserved_solution[3]^2) / (2 conserved_solution[0])) lies between 0.5 and 1.5. The entries metrics[k, k] lie between 0.7 and 1.4, the others between -0.4 and 0.4.
All inputs are finite; a program needn't handle non-finite values.
Results may differ from a plain program's by a relative error of at most 0.00005.
Values sent between devices are 32-bit elements; how exact they have to be, the bound alone decides.
A program may use at most 64 MiB of HBM per device.

v0:
```python
import jax
import jax.numpy as jnp
import numpy as np
from jax import lax
from jax.sharding import PartitionSpec as P

WIDTH = 5


viscosity = 0.15
conduction = 0.15 * 1.4 / (0.4 * 0.72)
step_duration = 0.08
line_forms = ("", "al,flyz->fayz", "al,fxlz->fxaz", "al,fxyl->fxya")


def with_halo(value, sides, width):
    for axis, dim in sides:
        count, length = (lax.axis_size(axis), value.shape[dim])
        up = [(i, (i + 1) % count) for i in range(count)]
        down = [(j, i) for i, j in up]
        last = lax.slice_in_dim(value, length - width, length, axis=dim)
        initial = lax.slice_in_dim(value, 0, width, axis=dim)
        before = lax.ppermute(last, axis, up)
        after = lax.ppermute(initial, axis, down)
        value = jnp.concatenate([before, value, after], axis=dim)
    return value


def banded_solve(system, source):
    extent = system.shape[0]
    lower = np.zeros(extent)
    upper = np.zeros(extent)
    middle = np.array([float(system[index, index]) for index in range(extent)])
    for index in range(1, extent):
        lower[index] = system[index, index - 1]
        upper[index - 1] = system[index - 1, index]
    rights = np.array(source)
    for index in range(1, extent):
        factor = lower[index] / middle[index - 1]
        middle[index] = middle[index] - factor * upper[index - 1]
        rights[index] = rights[index] - factor * rights[index - 1]
    answer = np.zeros(rights.shape)
    answer[extent - 1] = rights[extent - 1] / middle[extent - 1]
    for index in range(extent - 2, -1, -1):
        answer[index] = (rights[index] - upper[index] * answer[index + 1]) / middle[index]
    return answer


def derivative_table(length):
    extent = length + 2 * WIDTH
    system = np.eye(extent)
    source = np.zeros((extent, extent))
    for position in range(2, extent - 2):
        system[position, position - 1] = 1.0 / 3.0
        system[position, position + 1] = 1.0 / 3.0
        source[position, position + 1] = 7.0 / 9.0
        source[position, position - 1] = -7.0 / 9.0
        source[position, position + 2] = 1.0 / 36.0
        source[position, position - 2] = -1.0 / 36.0
    source[1, 2] = 0.5
    source[1, 0] = -0.5
    source[extent - 2, extent - 1] = 0.5
    source[extent - 2, extent - 3] = -0.5
    source[0, 1] = 1.0
    source[0, 0] = -1.0
    source[extent - 1, extent - 1] = 1.0
    source[extent - 1, extent - 2] = -1.0
    return banded_solve(system, source)[WIDTH : WIDTH + length]


def filter_table(length):
    strength = 0.4
    coeffs = [
        (193.0 + 126.0 * strength) / 256.0,
        (105.0 + 302.0 * strength) / 256.0,
        15.0 * (2.0 * strength - 1.0) / 64.0,
        45.0 * (1.0 - 2.0 * strength) / 512.0,
        5.0 * (2.0 * strength - 1.0) / 256.0,
        (1.0 - 2.0 * strength) / 512.0,
    ]
    extent = length + 2 * WIDTH
    system = np.eye(extent)
    source = np.eye(extent)
    for position in range(5, extent - 5):
        system[position, position - 1] = strength
        system[position, position + 1] = strength
        source[position, position] = coeffs[0]
        for offset in range(1, 6):
            source[position, position + offset] = coeffs[offset] / 2.0
            source[position, position - offset] = coeffs[offset] / 2.0
    return banded_solve(system, source)[WIDTH : WIDTH + length]


def sweep_lines(padded, matrix, dim):
    return jnp.einsum(line_forms[dim], matrix, padded, precision=lax.Precision.HIGHEST)


def faces_xi(values):
    return with_halo(values, (("xi", 1),), WIDTH)


def faces_eta(values):
    return with_halo(values, (("eta", 2),), WIDTH)


def faces_zeta(values):
    return with_halo(values, (("zeta", 3),), WIDTH)


def basic_quantities(conserved_solution):
    density = conserved_solution[0]
    fluid_speed_vector = conserved_solution[1:4] / density
    thermodynamic_stress_scalar = 0.4 * (
        conserved_solution[4] - 0.5 * jnp.sum(conserved_solution[1:4] * fluid_speed_vector, axis=0)
    )
    return (fluid_speed_vector, thermodynamic_stress_scalar, thermodynamic_stress_scalar / density)


def fluxes(
    conserved_solution, fluid_speed_vector, thermodynamic_stress_scalar, slopes, metrics, jacobian
):
    physical = [
        [
            jacobian
            * (
                metrics[0, column] * slopes[0][member]
                + metrics[1, column] * slopes[1][member]
                + metrics[2, column] * slopes[2][member]
            )
            for column in range(3)
        ]
        for member in range(4)
    ]
    spread = physical[0][0] + physical[1][1] + physical[2][2]
    totals = []
    for column in range(3):
        stress = [
            viscosity * (physical[member][column] + physical[column][member]) for member in range(3)
        ]
        stress[column] = stress[column] - 2.0 / 3.0 * viscosity * spread
        subdomain_parts = [conserved_solution[1 + column]]
        for member in range(3):
            carried = conserved_solution[1 + member] * fluid_speed_vector[column] - stress[member]
            if member == column:
                carried = carried + thermodynamic_stress_scalar
            subdomain_parts.append(carried)
        worked = (
            fluid_speed_vector[0] * stress[0]
            + fluid_speed_vector[1] * stress[1]
            + fluid_speed_vector[2] * stress[2]
        )
        subdomain_parts.append(
            (conserved_solution[4] + thermodynamic_stress_scalar) * fluid_speed_vector[column]
            - worked
            - conduction * physical[3][column]
        )
        totals.append(jnp.stack(subdomain_parts))
    return [
        metrics[direction, 0] * totals[0]
        + metrics[direction, 1] * totals[1]
        + metrics[direction, 2] * totals[2]
        for direction in range(3)
    ]


def local(conserved_solution, metrics, jacobian):
    lengths = conserved_solution.shape[1:]
    derive = [jnp.asarray(derivative_table(length), dtype=jnp.float32) for length in lengths]
    smooth = [jnp.asarray(filter_table(length), dtype=jnp.float32) for length in lengths]
    fluid_speed_vector, thermodynamic_stress_scalar, thermal_level = basic_quantities(
        conserved_solution
    )
    basic_quantity = jnp.concatenate([fluid_speed_vector, thermal_level[None]], axis=0)
    slopes = [
        sweep_lines(faces_xi(basic_quantity), derive[0], 1),
        sweep_lines(faces_eta(basic_quantity), derive[1], 2),
        sweep_lines(faces_zeta(basic_quantity), derive[2], 3),
    ]
    contra = fluxes(
        conserved_solution,
        fluid_speed_vector,
        thermodynamic_stress_scalar,
        slopes,
        metrics,
        jacobian,
    )
    divergence = sweep_lines(faces_xi(contra[0]), derive[0], 1)
    divergence = divergence + sweep_lines(faces_eta(contra[1]), derive[1], 2)
    divergence = divergence + sweep_lines(faces_zeta(contra[2]), derive[2], 3)
    sectioned = conserved_solution - step_duration * jacobian * divergence
    result = sweep_lines(faces_xi(sectioned), smooth[0], 1)
    result = sweep_lines(faces_eta(result), smooth[1], 2)
    result = sweep_lines(faces_zeta(result), smooth[2], 3)
    return result


def solution(mesh):
    in_specs = (
        P(None, "xi", "eta", "zeta"),
        P(None, None, "xi", "eta", "zeta"),
        P("xi", "eta", "zeta"),
    )
    out_specs = P(None, "xi", "eta", "zeta")
    return jax.shard_map(local, mesh=mesh, in_specs=in_specs, out_specs=out_specs, check_vma=False)
```

profile of v0, /device:TPU:1, one launch (start us, length us, event | category | flops | bytes accessed | tf_op | source)
XLA Modules:
  0.0 106.3 jit_solution(16992903408677247195)
XLA Ops:
  0.0 1.3 %copy.88 = f32[5,16,16,128]{3,1,2,0:T(8,128)S(1)} copy(f32[5,16,16,128]{3,2,1,0:T(8,128)} %param.9) | data formatting | bytes 1310720 | tf_op args[0]
  1.5 4.2 %collective-permute-start = (f32[4,5,16,128]{3,1,2,0:T(8,128)S(1)}, f32[4,5,16,128]{3,1,2,0:T(8,128)S(1)}, u32[]{:S(2)}, u32[]{:S(2)}) collective-permute-start(f32[4,5,16,128]{3,1,2,0:T(8,128)S(1)} %get-tuple-element.50), channel_id=1, source_target_pairs={{0,32},{32,64},{64,96},{96,0},{1,33},{33,65},{65,97},{97,1},{2,34}... | collective-permute-start | bytes 491528 | tf_op jit(solution)/shard_map/ppermute | solution.py:23
  5.7 1.4 %collective-permute-start.2 = (f32[4,16,5,128]{3,1,2,0:T(8,128)S(1)}, f32[4,16,5,128]{3,1,2,0:T(8,128)S(1)}, u32[]{:S(2)}, u32[]{:S(2)}) collective-permute-start(f32[4,16,5,128]{3,1,2,0:T(8,128)S(1)} %get-tuple-element.52), channel_id=1, source_target_pairs={{0,8},{8,16},{16,24},{24,0},{1,9},{9,17},{17,25},{25,1},{2,10},{10... | collective-permute-start | bytes 491528 | tf_op jit(solution)/shard_map/ppermute | solution.py:23
  7.3 0.4 collective-permute-start.4
  7.7 3.6 %collective-permute-start.5 = (f32[4,16,16,5]{3,1,2,0:T(8,128)S(1)}, f32[4,16,16,5]{3,1,2,0:T(8,128)S(1)}, u32[]{:S(2)}, u32[]{:S(2)}) collective-permute-start(f32[4,16,16,5]{3,1,2,0:T(8,128)S(1)} %get-tuple-element.55), channel_id=1, source_target_pairs={{1,0},{2,1},{3,2},{4,3},{5,4},{6,5},{7,6},{0,7},{9,8},{10,9},{11,1... | collective-permute-start | bytes 61448 | tf_op jit(solution)/shard_map/ppermute | solution.py:24
  11.7 0.5 copy-done
  12.3 13.5 %collective-permute-done.4 = f32[4,16,16,5]{3,1,2,0:T(8,128)S(1)} collective-permute-done((f32[4,16,16,5]{3,1,2,0:T(8,128)S(1)}, f32[4,16,16,5]{3,1,2,0:T(8,128)S(1)}, u32[]{:S(2)}, u32[]{:S(2)}) %collective-permute-start.4) | collective-permute-done | bytes 20512 | tf_op jit(solution)/shard_map/ppermute | solution.py:23
  25.8 2.7 %collective-permute-start.3 = (f32[4,16,5,128]{3,1,2,0:T(8,128)S(1)}, f32[4,16,5,128]{3,1,2,0:T(8,128)S(1)}, u32[]{:S(2)}, u32[]{:S(2)}) collective-permute-start(f32[4,16,5,128]{3,1,2,0:T(8,128)S(1)} %get-tuple-element.53), channel_id=1, source_target_pairs={{8,0},{16,8},{24,16},{0,24},{9,1},{17,9},{25,17},{1,25},{10,2},{18... | collective-permute-start | bytes 491528 | tf_op jit(solution)/shard_map/ppermute | solution.py:24
  28.5 5.4 %collective-permute-done.5 = f32[4,16,16,5]{3,1,2,0:T(8,128)S(1)} collective-permute-done((f32[4,16,16,5]{3,1,2,0:T(8,128)S(1)}, f32[4,16,16,5]{3,1,2,0:T(8,128)S(1)}, u32[]{:S(2)}, u32[]{:S(2)}) %collective-permute-start.5) | collective-permute-done | bytes 20512 | tf_op jit(solution)/shard_map/ppermute | solution.py:24
  33.9 1.1 %fusion.56 = f32[4,16,16,128]{3,1,2,0:T(8,128)S(1)} fusion(f32[128,138,1,1]{0,1,3,2:T(8,128)S(1)} %copy-done.3, f32[4,16,16,5]{3,1,2,0:T(8,128)S(1)} %collective-permute-done.5, f32[1,16,16,128]{3,1,2,0:T(8,128)S(1)} %get-tuple-element.48, f32[3,16,16,128]{3,1,2,0:T(8,128)S(1)} %get-tuple-element.18, f32[4,16,16,5]{3,1,2,0:T(8,128)S(1)} %collective-permute-done.4), kind=kOutput, calls=%fused_computation.50 | convolution fusion | flops 217479168 | bytes 1160192 | tf_op jit(solution)/shard_map/al,fxyl->fxya/dot_general | solution.py:95
  35.2 0.6 copy-done.4
  35.8 1.0 fusion.64
  37.0 0.9 convolution_bitcast_fusion
  37.9 0.5 bitcast_dynamic-update-slice_fusion.11
  38.4 0.3 bitcast_dynamic-update-slice_fusion.10
  40.4 0.4 multiply_add_fusion.1
  40.8 0.8 fusion.97
  41.6 1.3 %collective-permute-start.8 = (f32[5,16,5,128]{3,1,2,0:T(8,128)}, f32[5,16,5,128]{3,1,2,0:T(8,128)}, u32[]{:S(2)}, u32[]{:S(2)}) collective-permute-start(f32[5,16,5,128]{3,1,2,0:T(8,128)} %get-tuple-element.39), channel_id=1, source_target_pairs={{0,8},{8,16},{16,24},{24,0},{1,9},{9,17},{17,25},{25,1},{2,10},{10... | collective-permute-start | bytes 614408 | tf_op jit(solution)/shard_map/ppermute | solution.py:23
  42.9 1.4 %collective-permute-start.9 = (f32[5,16,5,128]{3,1,2,0:T(8,128)}, f32[5,16,5,128]{3,1,2,0:T(8,128)}, u32[]{:S(2)}, u32[]{:S(2)}) collective-permute-start(f32[5,16,5,128]{3,1,2,0:T(8,128)} %get-tuple-element.40), channel_id=1, source_target_pairs={{8,0},{16,8},{24,16},{0,24},{9,1},{17,9},{25,17},{1,25},{10,2},{18... | collective-permute-start | bytes 614408 | tf_op jit(solution)/shard_map/ppermute | solution.py:24
  44.5 1.3 %copy.82 = f32[5,16,16,5]{2,1,3,0:T(8,128)} copy(f32[5,16,16,5]{3,1,2,0:T(8,128)S(1)} %get-tuple-element.43) | data formatting | bytes 51200 | tf_op jit(solution)/shard_map/slice | solution.py:21
  45.8 3.2 %collective-permute-start.10 = (f32[5,16,16,5]{2,1,3,0:T(8,128)}, f32[5,16,16,5]{2,1,3,0:T(8,128)S(1)}, u32[]{:S(2)}, u32[]{:S(2)}) collective-permute-start(f32[5,16,16,5]{2,1,3,0:T(8,128)} %copy.82), channel_id=1, source_target_pairs={{0,1},{1,2},{2,3},{3,4},{4,5},{5,6},{6,7},{7,0},{8,9},{9,10},{10,1... | collective-permute-start | bytes 76808 | tf_op jit(solution)/shard_map/ppermute | solution.py:23
  48.9 0.6 copy.83
  49.5 1.0 collective-permute-start.11
  50.6 0.9 fusion.98
  51.5 4.1 %collective-permute-start.6 = (f32[5,5,16,128]{3,1,2,0:T(8,128)}, f32[5,5,16,128]{3,1,2,0:T(8,128)}, u32[]{:S(2)}, u32[]{:S(2)}) collective-permute-start(f32[5,5,16,128]{3,1,2,0:T(8,128)} %get-tuple-element.41), channel_id=1, source_target_pairs={{0,32},{32,64},{64,96},{96,0},{1,33},{33,65},{65,97},{97,1},{2,34}... | collective-permute-start | bytes 614408 | tf_op jit(solution)/shard_map/ppermute | solution.py:23
  55.6 2.8 %collective-permute-start.7 = (f32[5,5,16,128]{3,1,2,0:T(8,128)}, f32[5,5,16,128]{3,1,2,0:T(8,128)}, u32[]{:S(2)}, u32[]{:S(2)}) collective-permute-start(f32[5,5,16,128]{3,1,2,0:T(8,128)} %get-tuple-element.42), channel_id=1, source_target_pairs={{32,0},{64,32},{96,64},{0,96},{33,1},{65,33},{97,65},{1,97},{34,2}... | collective-permute-start | bytes 614408 | tf_op jit(solution)/shard_map/ppermute | solution.py:24
  58.3 0.6 copy.84
  58.9 1.5 %copy.85 = f32[5,16,16,5]{3,1,2,0:T(8,128)S(1)} copy(f32[5,16,16,5]{2,1,3,0:T(8,128)} %collective-permute-done.11) | data formatting | bytes 51200 | tf_op jit(solution)/shard_map/ppermute | solution.py:24
  60.4 1.4 %fusion.6 = f32[5,16,16,128]{3,1,2,0:T(8,128)S(1)} fusion(f32[128,138,1,1]{0,1,3,2:T(8,128)S(1)} %copy-done.3, f32[5,16,16,5]{3,1,2,0:T(8,128)S(1)} %copy.85, f32[5,16,16,128]{3,1,2,0:T(8,128)S(1)} %get-tuple-element.20, f32[5,16,16,5]{3,1,2,0:T(8,128)S(1)} %copy.84), kind=kOutput, calls=%fused_computation.6 | convolution fusion | flops 271672320 | bytes 1432576 | tf_op jit(solution)/shard_map/al,fxyl->fxya/dot_general | solution.py:95
  61.8 1.1 %pad_maximum_fusion = f32[5,16,26,128]{3,1,2,0:T(8,128)S(1)} fusion(f32[5,16,5,128]{3,1,2,0:T(8,128)} %collective-permute-done.9, f32[5,16,16,128]{3,1,2,0:T(8,128)S(1)} %get-tuple-element.19, f32[5,16,5,128]{3,1,2,0:T(8,128)} %collective-permute-done.8), kind=kLoop, calls=%fused_computation.41 | loop fusion | flops 532480 | bytes 2129920 | tf_op jit(solution)/shard_map/concatenate | solution.py:25
  62.9 1.2 %fusion.26 = f32[5,16,128,16]{2,3,1,0:T(8,128)S(1)} fusion(f32[16,26,1,1]{1,0,3,2:T(8,128)S(1)} %copy-done.4, f32[5,16,26,128]{3,1,2,0:T(8,128)S(1)} %pad_maximum_fusion), kind=kOutput, calls=%fused_computation.26 | convolution fusion | flops 51118080 | bytes 1721984 | tf_op jit(solution)/shard_map/al,fxlz->fxaz/dot_general | solution.py:95
  64.1 1.4 %collective-permute-done.7 = f32[5,5,16,128]{3,1,2,0:T(8,128)} collective-permute-done((f32[5,5,16,128]{3,1,2,0:T(8,128)}, f32[5,5,16,128]{3,1,2,0:T(8,128)}, u32[]{:S(2)}, u32[]{:S(2)}) %collective-permute-start.7) | collective-permute-done | bytes 204832 | tf_op jit(solution)/shard_map/ppermute | solution.py:24
  65.5 2.6 %fusion.46 = f32[5,16,16,128]{3,1,2,0:T(8,128)S(1)} fusion(f32[5,16,16,128]{3,1,2,0:T(8,128)S(1)} %fusion.6, f32[16,26,1,1]{1,0,3,2:T(8,128)S(1)} %copy-done.4, f32[5,5,16,128]{3,1,2,0:T(8,128)} %collective-permute-done.7, f32[5,16,16,128]{3,1,2,0:T(8,128)S(1)} %get-tuple-element.21, f32[5,5,16,128]{3,1,2,0:T(8,128)} %collective-permute-done.6, ...), kind=kOutput, calls=%fused_computation.34 | convolution fusion | flops 52305920 | bytes 3819136 | tf_op jit(solution)/shard_map/al,flyz->fayz/dot_general | solution.py:95
  68.2 2.0 %collective-permute-start.12 = (f32[5,5,16,128]{3,1,2,0:T(8,128)S(1)}, f32[5,5,16,128]{3,1,2,0:T(8,128)S(1)}, u32[]{:S(2)}, u32[]{:S(2)}) collective-permute-start(f32[5,5,16,128]{3,1,2,0:T(8,128)S(1)} %get-tuple-element.37), channel_id=1, source_target_pairs={{0,32},{32,64},{64,96},{96,0},{1,33},{33,65},{65,97},{97,1},{2,34}... | collective-permute-start | bytes 614408 | tf_op jit(solution)/shard_map/ppermute | solution.py:23
  70.2 4.0 %collective-permute-done.12 = f32[5,5,16,128]{3,1,2,0:T(8,128)S(1)} collective-permute-done((f32[5,5,16,128]{3,1,2,0:T(8,128)S(1)}, f32[5,5,16,128]{3,1,2,0:T(8,128)S(1)}, u32[]{:S(2)}, u32[]{:S(2)}) %collective-permute-start.12) | collective-permute-done | bytes 204832 | tf_op jit(solution)/shard_map/ppermute | solution.py:23
  74.2 6.8 %collective-permute-done.13 = f32[5,5,16,128]{3,1,2,0:T(8,128)S(1)} collective-permute-done((f32[5,5,16,128]{3,1,2,0:T(8,128)S(1)}, f32[5,5,16,128]{3,1,2,0:T(8,128)S(1)}, u32[]{:S(2)}, u32[]{:S(2)}) %collective-permute-start.13) | collective-permute-done | bytes 204832 | tf_op jit(solution)/shard_map/ppermute | solution.py:24
  81.0 1.1 %fusion.31 = f32[5,16,16,128]{3,1,2,0:T(8,128)S(1)} fusion(f32[16,26,1,1]{1,0,3,2:T(8,128)S(1)} %copy-done.6, f32[5,5,16,128]{3,1,2,0:T(8,128)S(1)} %collective-permute-done.13, f32[5,16,16,128]{3,1,2,0:T(8,128)S(1)} %fusion.46, f32[5,5,16,128]{3,1,2,0:T(8,128)S(1)} %collective-permute-done.12), kind=kOutput, calls=%fused_computation.29 | convolution fusion | flops 51650560 | bytes 1721984 | tf_op jit(solution)/shard_map/al,flyz->fayz/dot_general | solution.py:95
  82.3 2.6 %collective-permute-start.15 = (f32[5,16,5,128]{3,1,2,0:T(8,128)S(1)}, f32[5,16,5,128]{3,1,2,0:T(8,128)S(1)}, u32[]{:S(2)}, u32[]{:S(2)}) collective-permute-start(f32[5,16,5,128]{3,1,2,0:T(8,128)S(1)} %get-tuple-element.36), channel_id=1, source_target_pairs={{8,0},{16,8},{24,16},{0,24},{9,1},{17,9},{25,17},{1,25},{10,2},{18... | collective-permute-start | bytes 614408 | tf_op jit(solution)/shard_map/ppermute | solution.py:24
  84.9 5.3 %collective-permute-done.14 = f32[5,16,5,128]{3,1,2,0:T(8,128)S(1)} collective-permute-done((f32[5,16,5,128]{3,1,2,0:T(8,128)S(1)}, f32[5,16,5,128]{3,1,2,0:T(8,128)S(1)}, u32[]{:S(2)}, u32[]{:S(2)}) %collective-permute-start.14) | collective-permute-done | bytes 204832 | tf_op jit(solution)/shard_map/ppermute | solution.py:23
  90.2 1.2 %fusion.28 = f32[5,16,16,128]{3,2,1,0:T(8,128)S(1)} fusion(f32[16,26,1,1]{1,0,3,2:T(8,128)S(1)} %copy-done.6, f32[5,16,26,128]{3,1,2,0:T(8,128)S(1)} %pad_maximum_fusion.1), kind=kOutput, calls=%fused_computation.28 | convolution fusion | flops 51118080 | bytes 1721984 | tf_op jit(solution)/shard_map/al,fxlz->fxaz/dot_general | solution.py:95
  91.7 0.6 copy.90
  92.4 0.6 copy.91
  93.0 3.6 %collective-permute-start.17 = (f32[5,16,16,5]{2,1,3,0:T(8,128)S(1)}, f32[5,16,16,5]{2,1,3,0:T(8,128)S(1)}, u32[]{:S(2)}, u32[]{:S(2)}) collective-permute-start(f32[5,16,16,5]{2,1,3,0:T(8,128)S(1)} %copy.91), channel_id=1, source_target_pairs={{1,0},{2,1},{3,2},{4,3},{5,4},{6,5},{7,6},{0,7},{9,8},{10,9},{11,1... | collective-permute-start | bytes 76808 | tf_op jit(solution)/shard_map/ppermute | solution.py:24
  96.6 3.7 %collective-permute-done.16 = f32[5,16,16,5]{2,1,3,0:T(8,128)S(1)} collective-permute-done((f32[5,16,16,5]{2,1,3,0:T(8,128)S(1)}, f32[5,16,16,5]{2,1,3,0:T(8,128)S(1)}, u32[]{:S(2)}, u32[]{:S(2)}) %collective-permute-start.16) | collective-permute-done | bytes 25632 | tf_op jit(solution)/shard_map/ppermute | solution.py:23
  100.3 0.5 copy.92
  100.8 2.7 %collective-permute-done.17 = f32[5,16,16,5]{2,1,3,0:T(8,128)S(1)} collective-permute-done((f32[5,16,16,5]{2,1,3,0:T(8,128)S(1)}, f32[5,16,16,5]{2,1,3,0:T(8,128)S(1)}, u32[]{:S(2)}, u32[]{:S(2)}) %collective-permute-start.17) | collective-permute-done | bytes 25632 | tf_op jit(solution)/shard_map/ppermute | solution.py:24
  103.5 0.5 copy.93
  104.1 2.2 %fusion.18 = f32[5,16,16,128]{3,2,1,0:T(8,128)} fusion(f32[128,138,1,1]{0,1,3,2:T(8,128)S(1)} %copy-done.5, f32[5,16,16,5]{3,2,1,0:T(8,128)S(1)} %copy.93, f32[5,16,16,128]{3,2,1,0:T(8,128)S(1)} %fusion.28, f32[5,16,16,5]{3,2,1,0:T(8,128)S(1)} %copy.92), kind=kOutput, calls=%fused_computation.18 | convolution fusion | flops 271672320 | bytes 1432576 | tf_op jit(solution)/shard_map/al,fxyl->fxya/dot_general | solution.py:95
  (56 shorter events, 3.7 us)
Async XLA Ops:
  1.5 35.5 %collective-permute-start = (f32[4,5,16,128]{3,1,2,0:T(8,128)S(1)}, f32[4,5,16,128]{3,1,2,0:T(8,128)S(1)}, u32[]{:S(2)}, u32[]{:S(2)}) collective-permute-start(f32[4,5,16,128]{3,1,2,0:T(8,128)S(1)} %get-tuple-element.50), channel_id=1, source_target_pairs={{0,32},{32,64},{64,96},{96,0},{1,33},{33,65},{65,97},{97,1},{2,34}... | collective-permute-start | bytes 491528 | tf_op jit(solution)/shard_map/ppermute | solution.py:23
  5.7 5.5 %copy-start.2 = (f32[3,3,16,16,128]{4,3,2,1,0:T(8,128)S(1)}, f32[3,3,16,16,128]{4,3,2,1,0:T(8,128)}, u32[]{:S(2)}) copy-start(f32[3,3,16,16,128]{4,3,2,1,0:T(8,128)} %param.10) | copy-start | bytes 3538948
  5.7 31.3 %collective-permute-start.1 = (f32[4,5,16,128]{3,1,2,0:T(8,128)S(1)}, f32[4,5,16,128]{3,1,2,0:T(8,128)S(1)}, u32[]{:S(2)}, u32[]{:S(2)}) collective-permute-start(f32[4,5,16,128]{3,1,2,0:T(8,128)S(1)} %get-tuple-element.51), channel_id=1, source_target_pairs={{32,0},{64,32},{96,64},{0,96},{33,1},{65,33},{97,65},{1,97},{34,2}... | collective-permute-start | bytes 491528 | tf_op jit(solution)/shard_map/ppermute | solution.py:24
  5.7 29.4 %collective-permute-start.2 = (f32[4,16,5,128]{3,1,2,0:T(8,128)S(1)}, f32[4,16,5,128]{3,1,2,0:T(8,128)S(1)}, u32[]{:S(2)}, u32[]{:S(2)}) collective-permute-start(f32[4,16,5,128]{3,1,2,0:T(8,128)S(1)} %get-tuple-element.52), channel_id=1, source_target_pairs={{0,8},{8,16},{16,24},{24,0},{1,9},{9,17},{17,25},{25,1},{2,10},{10... | collective-permute-start | bytes 491528 | tf_op jit(solution)/shard_map/ppermute | solution.py:23
  7.3 18.5 %collective-permute-start.4 = (f32[4,16,16,5]{3,1,2,0:T(8,128)S(1)}, f32[4,16,16,5]{3,1,2,0:T(8,128)S(1)}, u32[]{:S(2)}, u32[]{:S(2)}) collective-permute-start(f32[4,16,16,5]{3,1,2,0:T(8,128)S(1)} %get-tuple-element.54), channel_id=1, source_target_pairs={{0,1},{1,2},{2,3},{3,4},{4,5},{5,6},{6,7},{7,0},{8,9},{9,10},{10,1... | collective-permute-start | bytes 61448 | tf_op jit(solution)/shard_map/ppermute | solution.py:23
  7.7 26.3 %collective-permute-start.5 = (f32[4,16,16,5]{3,1,2,0:T(8,128)S(1)}, f32[4,16,16,5]{3,1,2,0:T(8,128)S(1)}, u32[]{:S(2)}, u32[]{:S(2)}) collective-permute-start(f32[4,16,16,5]{3,1,2,0:T(8,128)S(1)} %get-tuple-element.55), channel_id=1, source_target_pairs={{1,0},{2,1},{3,2},{4,3},{5,4},{6,5},{7,6},{0,7},{9,8},{10,9},{11,1... | collective-permute-start | bytes 61448 | tf_op jit(solution)/shard_map/ppermute | solution.py:24
  11.3 0.9 copy-start
  11.4 22.5 %copy-start.3 = (f32[128,138,1,1]{0,1,3,2:T(8,128)S(1)}, f32[128,138,1,1]{0,1,3,2:T(8,128)}, u32[]{:S(2)}) copy-start(f32[128,138,1,1]{0,1,3,2:T(8,128)} %constant.27) | copy-start | bytes 211972
  25.8 9.3 %collective-permute-start.3 = (f32[4,16,5,128]{3,1,2,0:T(8,128)S(1)}, f32[4,16,5,128]{3,1,2,0:T(8,128)S(1)}, u32[]{:S(2)}, u32[]{:S(2)}) collective-permute-start(f32[4,16,5,128]{3,1,2,0:T(8,128)S(1)} %get-tuple-element.53), channel_id=1, source_target_pairs={{8,0},{16,8},{24,16},{0,24},{9,1},{17,9},{25,17},{1,25},{10,2},{18... | collective-permute-start | bytes 491528 | tf_op jit(solution)/shard_map/ppermute | solution.py:24
  35.1 0.7 copy-start.4
  41.6 20.2 %collective-permute-start.8 = (f32[5,16,5,128]{3,1,2,0:T(8,128)}, f32[5,16,5,128]{3,1,2,0:T(8,128)}, u32[]{:S(2)}, u32[]{:S(2)}) collective-permute-start(f32[5,16,5,128]{3,1,2,0:T(8,128)} %get-tuple-element.39), channel_id=1, source_target_pairs={{0,8},{8,16},{16,24},{24,0},{1,9},{9,17},{17,25},{25,1},{2,10},{10... | collective-permute-start | bytes 614408 | tf_op jit(solution)/shard_map/ppermute | solution.py:23
  42.9 18.9 %collective-permute-start.9 = (f32[5,16,5,128]{3,1,2,0:T(8,128)}, f32[5,16,5,128]{3,1,2,0:T(8,128)}, u32[]{:S(2)}, u32[]{:S(2)}) collective-permute-start(f32[5,16,5,128]{3,1,2,0:T(8,128)} %get-tuple-element.40), channel_id=1, source_target_pairs={{8,0},{16,8},{24,16},{0,24},{9,1},{17,9},{25,17},{1,25},{10,2},{18... | collective-permute-start | bytes 614408 | tf_op jit(solution)/shard_map/ppermute | solution.py:24
  45.8 9.8 %collective-permute-start.10 = (f32[5,16,16,5]{2,1,3,0:T(8,128)}, f32[5,16,16,5]{2,1,3,0:T(8,128)S(1)}, u32[]{:S(2)}, u32[]{:S(2)}) collective-permute-start(f32[5,16,16,5]{2,1,3,0:T(8,128)} %copy.82), channel_id=1, source_target_pairs={{0,1},{1,2},{2,3},{3,4},{4,5},{5,6},{6,7},{7,0},{8,9},{9,10},{10,1... | collective-permute-start | bytes 76808 | tf_op jit(solution)/shard_map/ppermute | solution.py:23
  49.5 9.4 %collective-permute-start.11 = (f32[5,16,16,5]{2,1,3,0:T(8,128)S(1)}, f32[5,16,16,5]{2,1,3,0:T(8,128)}, u32[]{:S(2)}, u32[]{:S(2)}) collective-permute-start(f32[5,16,16,5]{2,1,3,0:T(8,128)S(1)} %copy.83), channel_id=1, source_target_pairs={{1,0},{2,1},{3,2},{4,3},{5,4},{6,5},{7,6},{0,7},{9,8},{10,9},{11,1... | collective-permute-start | bytes 76808 | tf_op jit(solution)/shard_map/ppermute | solution.py:24
  51.5 12.7 %collective-permute-start.6 = (f32[5,5,16,128]{3,1,2,0:T(8,128)}, f32[5,5,16,128]{3,1,2,0:T(8,128)}, u32[]{:S(2)}, u32[]{:S(2)}) collective-permute-start(f32[5,5,16,128]{3,1,2,0:T(8,128)} %get-tuple-element.41), channel_id=1, source_target_pairs={{0,32},{32,64},{64,96},{96,0},{1,33},{33,65},{65,97},{97,1},{2,34}... | collective-permute-start | bytes 614408 | tf_op jit(solution)/shard_map/ppermute | solution.py:23
  55.6 9.9 %collective-permute-start.7 = (f32[5,5,16,128]{3,1,2,0:T(8,128)}, f32[5,5,16,128]{3,1,2,0:T(8,128)}, u32[]{:S(2)}, u32[]{:S(2)}) collective-permute-start(f32[5,5,16,128]{3,1,2,0:T(8,128)} %get-tuple-element.42), channel_id=1, source_target_pairs={{32,0},{64,32},{96,64},{0,96},{33,1},{65,33},{97,65},{1,97},{34,2}... | collective-permute-start | bytes 614408 | tf_op jit(solution)/shard_map/ppermute | solution.py:24
  62.9 2.6 %copy-start.1 = (f32[5,16,16,128]{3,2,1,0:T(8,128)S(1)}, f32[5,16,16,128]{3,2,1,0:T(8,128)}, u32[]{:S(2)}) copy-start(f32[5,16,16,128]{3,2,1,0:T(8,128)} %param.9) | copy-start | bytes 1966084
  68.1 12.9 %copy-start.6 = (f32[16,26,1,1]{1,0,3,2:T(8,128)S(1)}, f32[16,26,1,1]{1,0,3,2:T(8,128)}, u32[]{:S(2)}) copy-start(f32[16,26,1,1]{1,0,3,2:T(8,128)} %constant.28) | copy-start | bytes 4996
  68.2 6.0 %collective-permute-start.12 = (f32[5,5,16,128]{3,1,2,0:T(8,128)S(1)}, f32[5,5,16,128]{3,1,2,0:T(8,128)S(1)}, u32[]{:S(2)}, u32[]{:S(2)}) collective-permute-start(f32[5,5,16,128]{3,1,2,0:T(8,128)S(1)} %get-tuple-element.37), channel_id=1, source_target_pairs={{0,32},{32,64},{64,96},{96,0},{1,33},{33,65},{65,97},{97,1},{2,34}... | collective-permute-start | bytes 614408 | tf_op jit(solution)/shard_map/ppermute | solution.py:23
  70.2 10.8 %collective-permute-start.13 = (f32[5,5,16,128]{3,1,2,0:T(8,128)S(1)}, f32[5,5,16,128]{3,1,2,0:T(8,128)S(1)}, u32[]{:S(2)}, u32[]{:S(2)}) collective-permute-start(f32[5,5,16,128]{3,1,2,0:T(8,128)S(1)} %get-tuple-element.38), channel_id=1, source_target_pairs={{32,0},{64,32},{96,64},{0,96},{33,1},{65,33},{97,65},{1,97},{34,2}... | collective-permute-start | bytes 614408 | tf_op jit(solution)/shard_map/ppermute | solution.py:24
  82.1 8.0 %collective-permute-start.14 = (f32[5,16,5,128]{3,1,2,0:T(8,128)S(1)}, f32[5,16,5,128]{3,1,2,0:T(8,128)S(1)}, u32[]{:S(2)}, u32[]{:S(2)}) collective-permute-start(f32[5,16,5,128]{3,1,2,0:T(8,128)S(1)} %get-tuple-element.35), channel_id=1, source_target_pairs={{0,8},{8,16},{16,24},{24,0},{1,9},{9,17},{17,25},{25,1},{2,10},{10... | collective-permute-start | bytes 614408 | tf_op jit(solution)/shard_map/ppermute | solution.py:23
  82.3 7.8 %collective-permute-start.15 = (f32[5,16,5,128]{3,1,2,0:T(8,128)S(1)}, f32[5,16,5,128]{3,1,2,0:T(8,128)S(1)}, u32[]{:S(2)}, u32[]{:S(2)}) collective-permute-start(f32[5,16,5,128]{3,1,2,0:T(8,128)S(1)} %get-tuple-element.36), channel_id=1, source_target_pairs={{8,0},{16,8},{24,16},{0,24},{9,1},{17,9},{25,17},{1,25},{10,2},{18... | collective-permute-start | bytes 614408 | tf_op jit(solution)/shard_map/ppermute | solution.py:24
  92.3 8.0 %collective-permute-start.16 = (f32[5,16,16,5]{2,1,3,0:T(8,128)S(1)}, f32[5,16,16,5]{2,1,3,0:T(8,128)S(1)}, u32[]{:S(2)}, u32[]{:S(2)}) collective-permute-start(f32[5,16,16,5]{2,1,3,0:T(8,128)S(1)} %copy.90), channel_id=1, source_target_pairs={{0,1},{1,2},{2,3},{3,4},{4,5},{5,6},{6,7},{7,0},{8,9},{9,10},{10,1... | collective-permute-start | bytes 76808 | tf_op jit(solution)/shard_map/ppermute | solution.py:23
  92.4 11.7 %copy-start.5 = (f32[128,138,1,1]{0,1,3,2:T(8,128)S(1)}, f32[128,138,1,1]{0,1,3,2:T(8,128)}, u32[]{:S(2)}) copy-start(f32[128,138,1,1]{0,1,3,2:T(8,128)} %constant.29) | copy-start | bytes 211972
  93.0 10.6 %collective-permute-start.17 = (f32[5,16,16,5]{2,1,3,0:T(8,128)S(1)}, f32[5,16,16,5]{2,1,3,0:T(8,128)S(1)}, u32[]{:S(2)}, u32[]{:S(2)}) collective-permute-start(f32[5,16,16,5]{2,1,3,0:T(8,128)S(1)} %copy.91), channel_id=1, source_target_pairs={{1,0},{2,1},{3,2},{4,3},{5,4},{6,5},{7,6},{0,7},{9,8},{10,9},{11,1... | collective-permute-start | bytes 76808 | tf_op jit(solution)/shard_map/ppermute | solution.py:24
where the time goes:
time: 107 us; the launch traced here: 106 us
  waiting for transfers between devices  42.7 us (40%)
  starting transfers between devices  34.5 us (32%)
  matrix products  12.7 us (12%)
  local copies, waits for them, and re-layouts  11.5 us (11%)
  other arithmetic  4.49 us (4%)
    ppermute x9, waiting for transfers between devices, with_halo(): before = lax.ppermute(last, axis, up)  26.4 us
    ppermute x9, starting transfers between devices, with_halo(): after = lax.ppermute(initial, axis, down)  17.7 us
    ppermute x9, starting transfers between devices, with_halo(): before = lax.ppermute(last, axis, up)  16.8 us
    ppermute x9, waiting for transfers between devices, with_halo(): after = lax.ppermute(initial, axis, down)  16.3 us
    dot_general x9, matrix products, sweep_lines(): jnp.einsum(line_forms[dim], matrix, padded, precision=lax.Precision.HIGHEST)  12.7 us
    slice x8, local copies, waits for them, and re-layouts, with_halo(): last = lax.slice_in_dim(value, length - width, length, axis=dim)  4.1 us
    unnamed x16, local copies, waits for them, and re-layouts  2.5 us
  transfers between devices with their start and end apart: 18, of which 8 were waited for; matrix products, arithmetic and copies ran while one was open for 12% of the time, Pallas kernels for 0%

commit v1 on v0

--- a/solution.py
+++ b/solution.py
@@ -1,7 +1,11 @@
+import functools
+
 import jax
 import jax.numpy as jnp
 import numpy as np
 from jax import lax
+from jax.experimental import pallas as pl
+from jax.experimental.pallas import tpu as pltpu
 from jax.sharding import PartitionSpec as P
 
 WIDTH = 5
@@ -11,6 +15,71 @@
 conduction = 0.15 * 1.4 / (0.4 * 0.72)
 step_duration = 0.08
 line_forms = ("", "al,flyz->fayz", "al,fxlz->fxaz", "al,fxyl->fxya")
+MESH = pl.DeviceIdType.MESH
+AXES = ("xi", "eta", "zeta")
+
+
+def exchange_kernel(routes, sizes, *refs):
+    count = len(routes)
+    sources, targets = refs[:count], refs[count : 2 * count]
+    send_sems, recv_sems = refs[2 * count :]
+    here = [lax.axis_index(axis) for axis in AXES]
+
+    def device(axis, step):
+        place = list(here)
+        slot = AXES.index(axis)
+        place[slot] = lax.rem(here[slot] + step + sizes[slot], sizes[slot])
+        return tuple(place)
+
+    partners = []
+    for axis, step in routes:
+        for way in (step, -step):
+            if (axis, way) not in partners:
+                partners.append((axis, way))
+    barrier = pltpu.get_barrier_semaphore()
+    for axis, step in partners:
+        pl.semaphore_signal(barrier, inc=1, device_id=device(axis, step), device_id_type=MESH)
+    pl.semaphore_wait(barrier, len(partners))
+    copies = []
+    for index, (axis, step) in enumerate(routes):
+        copy = pltpu.make_async_remote_copy(
+            src_ref=sources[index],
+            dst_ref=targets[index],
+            send_sem=send_sems.at[index],
+            recv_sem=recv_sems.at[index],
+            device_id=device(axis, step),
+            device_id_type=MESH,
+        )
+        copy.start()
+        copies.append(copy)
+    for copy in copies:
+        copy.wait()
+
+
+def exchange_faces(items, tag):
+    sizes = tuple(lax.axis_size(axis) for axis in AXES)
+    sends, routes = [], []
+    for value, axis, dim in items:
+        length = value.shape[dim]
+        sends.append(lax.slice_in_dim(value, length - WIDTH, length, axis=dim))
+        routes.append((axis, 1))
+        sends.append(lax.slice_in_dim(value, 0, WIDTH, axis=dim))
+        routes.append((axis, -1))
+    received = pl.pallas_call(
+        functools.partial(exchange_kernel, tuple(routes), sizes),
+        out_shape=[jax.ShapeDtypeStruct(send.shape, send.dtype) for send in sends],
+        in_specs=[pl.BlockSpec(memory_space=pltpu.VMEM)] * len(sends),
+        out_specs=[pl.BlockSpec(memory_space=pltpu.VMEM)] * len(sends),
+        scratch_shapes=[
+            pltpu.SemaphoreType.DMA((len(sends),)),
+            pltpu.SemaphoreType.DMA((len(sends),)),
+        ],
+        compiler_params=pltpu.CompilerParams(collective_id=tag, has_side_effects=True),
+    )(*sends)
+    return [
+        jnp.concatenate([received[2 * index], value, received[2 * index + 1]], axis=dim)
+        for index, (value, axis, dim) in enumerate(items)
+    ]
 
 
 def with_halo(value, sides, width):
@@ -171,11 +240,10 @@
         conserved_solution
     )
     basic_quantity = jnp.concatenate([fluid_speed_vector, thermal_level[None]], axis=0)
-    slopes = [
-        sweep_lines(faces_xi(basic_quantity), derive[0], 1),
-        sweep_lines(faces_eta(basic_quantity), derive[1], 2),
-        sweep_lines(faces_zeta(basic_quantity), derive[2], 3),
-    ]
+    padded = exchange_faces(
+        [(basic_quantity, "xi", 1), (basic_quantity, "eta", 2), (basic_quantity, "zeta", 3)], 0
+    )
+    slopes = [sweep_lines(padded[k], derive[k], k + 1) for k in range(3)]
     contra = fluxes(
         conserved_solution,
         fluid_speed_vector,
@@ -184,13 +252,14 @@
         metrics,
         jacobian,
     )
-    divergence = sweep_lines(faces_xi(contra[0]), derive[0], 1)
-    divergence = divergence + sweep_lines(faces_eta(contra[1]), derive[1], 2)
-    divergence = divergence + sweep_lines(faces_zeta(contra[2]), derive[2], 3)
+    padded = exchange_faces([(contra[0], "xi", 1), (contra[1], "eta", 2), (contra[2], "zeta", 3)], 1)
+    divergence = sweep_lines(padded[0], derive[0], 1)
+    divergence = divergence + sweep_lines(padded[1], derive[1], 2)
+    divergence = divergence + sweep_lines(padded[2], derive[2], 3)
     sectioned = conserved_solution - step_duration * jacobian * divergence
-    result = sweep_lines(faces_xi(sectioned), smooth[0], 1)
-    result = sweep_lines(faces_eta(result), smooth[1], 2)
-    result = sweep_lines(faces_zeta(result), smooth[2], 3)
+    result = sweep_lines(exchange_faces([(sectioned, "xi", 1)], 2)[0], smooth[0], 1)
+    result = sweep_lines(exchange_faces([(result, "eta", 2)], 3)[0], smooth[1], 2)
+    result = sweep_lines(exchange_faces([(result, "zeta", 3)], 4)[0], smooth[2], 3)
     return result
 
 

time: 107 us -> 162 us (1.51); the launches traced: 106 us -> 159 us
  Pallas kernels: 0 us -> 128 us
  waiting for transfers between devices: 42.7 us -> 0 us
  starting transfers between devices: 34.5 us -> 0 us
  other arithmetic: 4.49 us -> 8.8 us
  local copies, waits for them, and re-layouts: 11.5 us -> 9.06 us
    pallas_call x0 -> x5, Pallas kernels: none -> 128 us  [exchange_faces(): pl.pallas_call(functools.partial(exchange_kernel, tuple(routes), sizes),...]
    ppermute x18 -> x0, waiting for transfers between devices: 42.7 us -> none  [the longest x9 26.4 us: with_halo(): before = lax.ppermute(last, axis, up)]
    ppermute x18 -> x0, starting transfers between devices: 34.5 us -> none  [the longest x9 17.7 us: with_halo(): after = lax.ppermute(initial, axis, down)]
    ppermute x4 -> x0, local copies, waits for them, and re-layouts: 3.11 us -> none  [the longest x2 2.02 us: with_halo(): after = lax.ppermute(initial, axis, down)]
    concatenate x3, other arithmetic: 0.28 us -> 2.7 us  [local(): jnp.concatenate([fluid_speed_vector, thermal_level[None]], axis=0)]
    concatenate x3, other arithmetic: 1.26 us -> 3.29 us  [exchange_faces(): jnp.concatenate([received[2 * index], value, received[2 * index + 1]], ax...]
    slice x11 -> x6, local copies, waits for them, and re-layouts: 5.36 us -> 5.88 us  [exchange_faces(): sends.append(lax.slice_in_dim(value, 0, WIDTH, axis=dim))]
  transfers between devices with their start and end apart: 18 -> 0, of which waited for: 8 -> 0; matrix products, arithmetic and copies ran while one was open for 12% -> 0% of each run, Pallas kernels for 0% -> 0%
where the time goes in v1:
time: 162 us; the launch traced here: 159 us
  Pallas kernels  128 us (79%)
  matrix products  13.7 us (8%)
  local copies, waits for them, and re-layouts  9.06 us (6%)
  other arithmetic  8.8 us (5%)
    pallas_call x5, Pallas kernels, exchange_faces(): pl.pallas_call(functools.partial(exchange_kernel, tuple(routes), sizes),...  128 us
    dot_general x9, matrix products, sweep_lines(): jnp.einsum(line_forms[dim], matrix, padded, precision=lax.Precision.HIGHEST)  13.7 us
    slice x6, local copies, waits for them, and re-layouts, exchange_faces(): sends.append(lax.slice_in_dim(value, 0, WIDTH, axis=dim))  5.88 us
    concatenate x3, other arithmetic, exchange_faces(): jnp.concatenate([received[2 * index], value, received[2 * index + 1]], ax...  3.29 us

profile of v1, /device:TPU:1, one launch (start us, length us, event | category | flops | bytes accessed | tf_op | source)
XLA Modules:
  0.0 159.5 jit_solution(11211653089215068680)
XLA Ops:
  0.0 1.0 slice_bitcast_fusion.24
  1.0 1.1 multiply_reduce_fusion
  2.1 1.1 pad_maximum_fusion.3
  3.2 0.8 fusion.65
  4.1 0.7 fusion.67
  4.8 33.8 %shard_map.91 = (f32[4,5,16,128]{3,2,1,0:T(8,128)}, f32[4,5,16,128]{3,2,1,0:T(8,128)}, f32[4,16,5,128]{3,2,1,0:T(8,128)}, f32[4,16,5,128]{3,2,1,0:T(8,128)}, f32...) custom-call(f32[4,5,16,128]{3,2,1,0:T(8,128)} %get-tuple-element.91.refs_0_, ...), custom_call_target="tpu_custom_call" | custom-call | tf_op jit(solution)/shard_map/pallas_call | solution.py:68
  38.6 0.0 copy-start.12
  38.6 1.1 pad_maximum_fusion.2
  39.7 1.0 fusion.61
  40.7 0.0 copy-start.11
  40.7 0.2 copy.30
  40.9 0.9 convolution_bitcast_fusion
  41.9 0.0 copy-done.8
  41.9 1.1 fusion.53
  43.1 0.1 copy-done
  43.1 0.2 bitcast_dynamic-update-slice_fusion.11
  43.3 0.1 bitcast_dynamic-update-slice_fusion.10
  43.5 0.1 bitcast_dynamic-update-slice_fusion.9
  43.6 0.2 bitcast_dynamic-update-slice_fusion.8
  43.8 0.1 bitcast_dynamic-update-slice_fusion.6
  43.9 0.1 bitcast_dynamic-update-slice_fusion.5
  44.1 0.6 copy-done.3
  44.6 0.1 bitcast_dynamic-update-slice_fusion.4
  44.8 0.1 bitcast_dynamic-update-slice_fusion.1
  44.9 0.1 bitcast_dynamic-update-slice_fusion
  45.0 0.0 copy-start.4
  45.0 0.1 slice_bitcast_fusion.21
  45.1 1.0 copy-done.4
  46.1 0.4 multiply_add_fusion
  46.6 1.3 fusion.93
  47.8 0.9 fusion.94
  48.7 0.8 fusion.95
  49.5 42.1 %shard_map.92 = (f32[5,5,16,128]{3,2,1,0:T(8,128)}, f32[5,5,16,128]{3,2,1,0:T(8,128)}, f32[5,16,5,128]{3,2,1,0:T(8,128)}, f32[5,16,5,128]{3,2,1,0:T(8,128)}, f32...) custom-call(f32[5,5,16,128]{3,2,1,0:T(8,128)} %get-tuple-element.80.refs_0_, ...), custom_call_target="tpu_custom_call" | custom-call | tf_op jit(solution)/shard_map/pallas_call | solution.py:68
  91.6 1.1 pad_maximum_fusion
  92.7 1.2 fusion.26
  94.0 1.2 fusion.43
  95.3 1.4 fusion.34
  96.7 0.8 fusion.92
  97.4 10.5 %shard_map.93 = (f32[5,5,16,128]{3,2,1,0:T(8,128)}, f32[5,5,16,128]{3,2,1,0:T(8,128)}) custom-call(f32[5,5,16,128]{3,2,1,0:T(8,128)} %get-tuple-element.74.refs_0_, f32[5,5,16,128]{3,2,1,0:T(8,128)} %get-tuple-element.73.refs_1_), custom_call_target="tpu_custom_call" | custom-call | tf_op jit(solution)/shard_map/pallas_call | solution.py:68
  108.0 1.1 pad_maximum_fusion.1
  109.1 1.2 fusion.24
  110.3 0.2 copy.29
  110.5 0.9 fusion.91
  111.4 8.9 %shard_map.94 = (f32[5,16,5,128]{3,2,1,0:T(8,128)}, f32[5,16,5,128]{3,2,1,0:T(8,128)}) custom-call(f32[5,16,5,128]{3,2,1,0:T(8,128)} %get-tuple-element.72.refs_0_, f32[5,16,5,128]{3,2,1,0:T(8,128)} %get-tuple-element.71.refs_1_), custom_call_target="tpu_custom_call" | custom-call | tf_op jit(solution)/shard_map/pallas_call | solution.py:68
  120.3 2.2 %fusion.37 = f32[5,16,16,128]{3,2,1,0:T(8,128)S(1)} fusion(f32[16,26,1,1]{1,0,3,2:T(8,128)S(1)} %copy-done.14, f32[5,16,5,128]{3,2,1,0:T(8,128)} %get-tuple-element.38, f32[5,16,16,128]{3,2,1,0:T(8,128)S(1)} %bitcast.425, f32[5,16,5,128]{3,2,1,0:T(8,128)} %get-tuple-element.37), kind=kOutput, calls=%fused_computation.31 | convolution fusion | flops 51650560 | bytes 1721984 | tf_op jit(solution)/shard_map/al,fxlz->fxaz/dot_general | solution.py:164
  122.4 1.3 fusion.90
  123.7 32.3 %shard_map.95 = (f32[5,16,16,5]{3,2,1,0:T(8,128)}, f32[5,16,16,5]{3,2,1,0:T(8,128)}) custom-call(f32[5,16,16,5]{3,2,1,0:T(8,128)} %get-tuple-element.70.refs_0_, f32[5,16,16,5]{3,2,1,0:T(8,128)} %get-tuple-element.69.refs_1_), custom_call_target="tpu_custom_call" | custom-call | tf_op jit(solution)/shard_map/pallas_call | solution.py:68
  156.0 3.5 %fusion.18 = f32[5,16,16,128]{3,2,1,0:T(8,128)} fusion(f32[128,138,1,1]{0,1,3,2:T(8,128)S(1)} %copy-done.13, f32[5,16,16,5]{3,2,1,0:T(8,128)} %get-tuple-element.40, f32[5,16,16,128]{3,2,1,0:T(8,128)S(1)} %fusion.37, f32[5,16,16,5]{3,2,1,0:T(8,128)} %get-tuple-element.39), kind=kOutput, calls=%fused_computation.18 | convolution fusion | flops 271672320 | bytes 1432576 | tf_op jit(solution)/shard_map/al,fxyl->fxya/dot_general | solution.py:164
  (31 shorter events, 0.2 us)
Async XLA Ops:
  0.0 2.1 %copy-start.1 = (f32[5,16,16,128]{3,2,1,0:T(8,128)S(1)}, f32[5,16,16,128]{3,2,1,0:T(8,128)}, u32[]{:S(2)}) copy-start(f32[5,16,16,128]{3,2,1,0:T(8,128)} %param.9) | copy-start | bytes 1966084
  38.6 1.1 copy-start.12
  39.7 1.2 copy-start.15
  39.7 1.2 copy-start.16
  40.7 1.2 copy-start.7
  40.7 1.2 copy-start.8
  40.7 1.2 copy-start.11
  41.8 1.3 copy-start
  41.8 1.3 copy-start.2
  43.8 0.8 copy-start.3
  45.0 1.1 copy-start.4
  92.7 1.2 copy-start.9
  92.7 1.2 copy-start.10
  94.0 1.3 copy-start.5
  94.0 1.3 copy-start.6
  97.4 11.6 %copy-start.14 = (f32[16,26,1,1]{1,0,3,2:T(8,128)S(1)}, f32[16,26,1,1]{1,0,3,2:T(8,128)}, u32[]{:S(2)}) copy-start(f32[16,26,1,1]{1,0,3,2:T(8,128)} %constant.28) | copy-start | bytes 4996
  123.7 32.3 %copy-start.13 = (f32[128,138,1,1]{0,1,3,2:T(8,128)S(1)}, f32[128,138,1,1]{0,1,3,2:T(8,128)}, u32[]{:S(2)}) copy-start(f32[128,138,1,1]{0,1,3,2:T(8,128)} %constant.29) | copy-start | bytes 211972

commit v2 on v1

--- a/solution.py
+++ b/solution.py
@@ -61,10 +61,12 @@
     sends, routes = [], []
     for value, axis, dim in items:
         length = value.shape[dim]
-        sends.append(lax.slice_in_dim(value, length - WIDTH, length, axis=dim))
-        routes.append((axis, 1))
-        sends.append(lax.slice_in_dim(value, 0, WIDTH, axis=dim))
-        routes.append((axis, -1))
+        for face, step in ((slice(length - WIDTH, length), 1), (slice(0, WIDTH), -1)):
+            part = lax.slice_in_dim(value, face.start, face.stop, axis=dim)
+            if dim == value.ndim - 1:
+                part = jnp.moveaxis(part, dim, 1).reshape(part.shape[0], WIDTH, -1)
+            sends.append(part)
+            routes.append((axis, step))
     received = pl.pallas_call(
         functools.partial(exchange_kernel, tuple(routes), sizes),
         out_shape=[jax.ShapeDtypeStruct(send.shape, send.dtype) for send in sends],
@@ -76,10 +78,15 @@
         ],
         compiler_params=pltpu.CompilerParams(collective_id=tag, has_side_effects=True),
     )(*sends)
-    return [
-        jnp.concatenate([received[2 * index], value, received[2 * index + 1]], axis=dim)
-        for index, (value, axis, dim) in enumerate(items)
-    ]
+    padded = []
+    for index, (value, axis, dim) in enumerate(items):
+        before, after = received[2 * index], received[2 * index + 1]
+        if dim == value.ndim - 1:
+            shape = (value.shape[0], WIDTH) + value.shape[1:dim]
+            before = jnp.moveaxis(before.reshape(shape), 1, dim)
+            after = jnp.moveaxis(after.reshape(shape), 1, dim)
+        padded.append(jnp.concatenate([before, value, after], axis=dim))
+    return padded
 
 
 def with_halo(value, sides, width):

time: 162 us -> 97.7 us (0.60)
  Pallas kernels: 128 us -> 55.4 us
  local copies, waits for them, and re-layouts: 9.06 us -> 16.9 us
    pallas_call x5, Pallas kernels: 128 us -> 55.4 us  [exchange_faces(): pl.pallas_call(functools.partial(exchange_kernel, tuple(routes), sizes),...]
    reshape x0 -> x8, local copies, waits for them, and re-layouts: none -> 8.09 us  [the longest x6 6.04 us: exchange_faces(): part = jnp.moveaxis(part, dim, 1).reshape(part.shape[0], WIDTH, -1)]
    pallas_call x0 -> x4, local copies, waits for them, and re-layouts: none -> 2.6 us  [exchange_faces(): pl.pallas_call(functools.partial(exchange_kernel, tuple(routes), sizes),...]
    unnamed x34 -> x30, local copies, waits for them, and re-layouts: 1.75 us -> 0.07 us
where the time goes in v2:
time: 97.7 us; the launch traced here: 96 us
  Pallas kernels  55.4 us (57%)
  local copies, waits for them, and re-layouts  16.9 us (17%)
  matrix products  14.7 us (15%)
  other arithmetic  8.53 us (9%)
    pallas_call x5, Pallas kernels, exchange_faces(): pl.pallas_call(functools.partial(exchange_kernel, tuple(routes), sizes),...  55.4 us
    dot_general x9, matrix products, sweep_lines(): jnp.einsum(line_forms[dim], matrix, padded, precision=lax.Precision.HIGHEST)  14.7 us
    reshape x6, local copies, waits for them, and re-layouts, exchange_faces(): part = jnp.moveaxis(part, dim, 1).reshape(part.shape[0], WIDTH, -1)  6.04 us
    slice x6, local copies, waits for them, and re-layouts, exchange_faces(): part = lax.slice_in_dim(value, face.start, face.stop, axis=dim)  4.65 us
    concatenate x3, other arithmetic, exchange_faces(): padded.append(jnp.concatenate([before, value, after], axis=dim))  3.29 us
    pallas_call x4, local copies, waits for them, and re-layouts, exchange_faces(): pl.pallas_call(functools.partial(exchange_kernel, tuple(routes), sizes),...  2.6 us

profile of v2, /device:TPU:1, one launch (start us, length us, event | category | flops | bytes accessed | tf_op | source)
XLA Modules:
  0.0 96.0 jit_solution(8976149555414324811)
XLA Ops:
  0.0 1.0 %slice_bitcast_fusion.24 = f32[16,16,128]{2,1,0:T(8,128)S(1)} fusion(f32[5,16,16,128]{3,2,1,0:T(8,128)} %param.9), kind=kLoop, calls=%fused_computation.151 | loop fusion | bytes 262144 | tf_op jit(solution)/shard_map/div | solution.py:188
  1.0 1.1 %multiply_reduce_fusion = (f32[16,16,128]{2,1,0:T(8,128)S(1)}, f32[3,16,16,128]{3,2,1,0:T(8,128)S(1)}) fusion(f32[5,16,16,128]{3,2,1,0:T(8,128)} %param.9, f32[16,16,128]{2,1,0:T(8,128)S(1)} %slice_bitcast_fusion.24), kind=kLoop, calls=%fused_computation.72 | loop fusion | flops 262144 | bytes 1048576 | tf_op jit(solution)/shard_map/reduce_sum | solution.py:190
  2.1 0.7 fusion.78
  2.8 0.2 pad_maximum_fusion.3
  3.0 0.8 copy.10.refs_4_
  3.8 0.8 copy.11.refs_5_
  4.6 0.8 fusion.65
  5.4 0.7 fusion.67
  6.1 15.4 %shard_map.91 = (f32[4,5,16,128]{3,2,1,0:T(8,128)}, f32[4,5,16,128]{3,2,1,0:T(8,128)}, f32[4,16,5,128]{3,2,1,0:T(8,128)}, f32[4,16,5,128]{3,2,1,0:T(8,128)}, f32[4,5,256]{2,1,0:T(8,128)}, /*index=5*/f32[4,5,256]{2,1,0:T(8,128)}) custom-call(f32[4,5,16,128]{3,2,1,0:T(8,128)} %get-tuple-element.91.refs_0_, f32[4,5,16,128]{3,2,1,0:T(8,128)} %get-tuple-element.90.refs_1_, ...), custom_call_target="tpu_custom_call" | custom-call | tf_op jit(solution)/shard_map/pallas_call | solution.py:70
  21.6 1.1 %pad_maximum_fusion.2 = f32[4,26,16,128]{3,2,1,0:T(8,128)S(1)} fusion(f32[4,5,16,128]{3,2,1,0:T(8,128)} %get-tuple-element.24, f32[1,16,16,128]{3,2,1,0:T(8,128)S(1)} %get-tuple-element.84, f32[3,16,16,128]{3,2,1,0:T(8,128)S(1)} %get-tuple-element.54, f32[4,5,16,128]{3,2,1,0:T(8,128)} %get-tuple-element.23), kind=kLoop, calls=%fused_computation.59 | loop fusion | flops 638976 | bytes 1703936 | tf_op jit(solution)/shard_map/concatenate | solution.py:88
  22.7 1.0 %fusion.61 = f32[4,16,128,16]{2,3,1,0:T(8,128)S(1)} fusion(f32[16,26,1,1]{1,0,3,2:T(8,128)S(1)} %copy-done.7, f32[4,26,16,128]{3,2,1,0:T(8,128)S(1)} %pad_maximum_fusion.2), kind=kOutput, calls=%fused_computation.57 | convolution fusion | flops 40894464 | bytes 1377920 | tf_op jit(solution)/shard_map/al,flyz->fayz/dot_general | solution.py:171
  23.7 0.2 copy.48
  23.9 0.9 convolution_bitcast_fusion
  24.8 0.2 copy.14
  25.0 0.2 copy.15
  25.3 2.2 %fusion.53 = f32[4,16,16,128]{3,2,1,0:T(8,128)S(1)} fusion(f32[128,138,1,1]{0,1,3,2:T(8,128)} %constant.27, f32[4,16,16,5]{3,2,1,0:T(8,128)S(1)} %bitcast.473, f32[1,16,16,128]{3,2,1,0:T(8,128)S(1)} %get-tuple-element.84, f32[3,16,16,128]{3,2,1,0:T(8,128)S(1)} %get-tuple-element.54, f32[4,16,16,5]{3,2,1,0:T(8,128)S(1)} %bitcast.472), kind=kOutput, calls=%fused_computation.49 | convolution fusion | flops 217479168 | bytes 1160192 | tf_op jit(solution)/shard_map/al,fxyl->fxya/dot_general | solution.py:171
  27.5 0.2 bitcast_dynamic-update-slice_fusion.11
  28.0 0.2 bitcast_dynamic-update-slice_fusion.8
  28.4 0.1 bitcast_dynamic-update-slice_fusion.4
  28.6 0.1 bitcast_dynamic-update-slice_fusion
  28.9 0.4 multiply_add_fusion
  29.3 1.1 %fusion.93 = (f32[5,16,16,5]{3,2,1,0:T(8,128)S(1)}, f32[5,16,16,5]{3,2,1,0:T(8,128)}) fusion(f32[5,16,16,128]{3,2,1,0:T(8,128)S(1)} %get-tuple-element.55), kind=kLoop, calls=%fused_computation.165 | loop fusion | bytes 102400 | tf_op jit(solution)/shard_map/slice | solution.py:65
  30.4 1.9 %copy.32.refs_4_ = f32[5,5,256]{2,1,0:T(8,128)} copy(f32[5,5,256]{1,2,0:T(8,128)} %bitcast.466) | data formatting | bytes 51200 | tf_op jit(solution)/shard_map/reshape | solution.py:67
  32.3 0.8 copy.33.refs_5_
  33.1 0.9 fusion.94
  34.0 0.8 fusion.95
  34.8 13.6 %shard_map.92 = (f32[5,5,16,128]{3,2,1,0:T(8,128)}, f32[5,5,16,128]{3,2,1,0:T(8,128)}, f32[5,16,5,128]{3,2,1,0:T(8,128)}, f32[5,16,5,128]{3,2,1,0:T(8,128)}, f32[5,5,256]{2,1,0:T(8,128)}, /*index=5*/f32[5,5,256]{2,1,0:T(8,128)}) custom-call(f32[5,5,16,128]{3,2,1,0:T(8,128)} %get-tuple-element.80.refs_0_, f32[5,5,16,128]{3,2,1,0:T(8,128)} %get-tuple-element.79.refs_1_, ...), custom_call_target="tpu_custom_call" | custom-call | tf_op jit(solution)/shard_map/pallas_call | solution.py:70
  48.4 1.1 %pad_maximum_fusion = f32[5,26,16,128]{3,2,1,0:T(8,128)S(1)} fusion(f32[5,5,16,128]{3,2,1,0:T(8,128)} %get-tuple-element.30, f32[5,16,16,128]{3,2,1,0:T(8,128)S(1)} %get-tuple-element.57, f32[5,5,16,128]{3,2,1,0:T(8,128)} %get-tuple-element.29), kind=kLoop, calls=%fused_computation.40 | loop fusion | flops 532480 | bytes 2129920 | tf_op jit(solution)/shard_map/concatenate | solution.py:88
  49.6 1.2 %fusion.26 = f32[5,16,128,16]{2,3,1,0:T(8,128)S(1)} fusion(f32[16,26,1,1]{1,0,3,2:T(8,128)S(1)} %copy-done.7, f32[5,26,16,128]{3,2,1,0:T(8,128)S(1)} %pad_maximum_fusion), kind=kOutput, calls=%fused_computation.26 | convolution fusion | flops 51118080 | bytes 1721984 | tf_op jit(solution)/shard_map/al,flyz->fayz/dot_general | solution.py:171
  50.8 1.2 %fusion.43 = f32[5,16,16,128]{3,2,1,0:T(8,128)S(1)} fusion(f32[16,26,1,1]{1,0,3,2:T(8,128)S(1)} %copy-done.7, f32[5,16,5,128]{3,2,1,0:T(8,128)S(1)} %copy-done.5, f32[5,16,16,128]{3,2,1,0:T(8,128)S(1)} %get-tuple-element.56, f32[5,16,5,128]{3,2,1,0:T(8,128)S(1)} %copy-done.4, f32[5,16,128,16]{2,3,1,0:T(8,128)S(1)} %fusion.26), kind=kOutput, calls=%fused_computation.33 | convolution fusion | flops 51814400 | bytes 2377344 | tf_op jit(solution)/shard_map/al,fxlz->fxaz/dot_general | solution.py:171
  52.0 1.1 %copy.20 = f32[5,5,256]{1,2,0:T(8,128)S(1)} copy(f32[5,5,256]{2,1,0:T(8,128)} %get-tuple-element.33) | data formatting | bytes 51200 | tf_op jit(solution)/shard_map/pallas_call | solution.py:70
  53.1 1.1 %copy.21 = f32[5,5,256]{1,2,0:T(8,128)} copy(f32[5,5,256]{2,1,0:T(8,128)S(1)} %copy-done.9) | data formatting | bytes 51200 | tf_op jit(solution)/shard_map/pallas_call | solution.py:70
  54.3 2.5 %fusion.34 = f32[5,16,16,128]{3,2,1,0:T(8,128)S(1)} fusion(f32[5,16,16,128]{3,2,1,0:T(8,128)S(1)} %copy-done.1, f32[5,16,16,128]{3,2,1,0:T(8,128)S(1)} %fusion.43, f32[128,138,1,1]{0,1,3,2:T(8,128)S(1)} %copy-done.6, f32[5,16,16,5]{3,2,1,0:T(8,128)} %bitcast.463, f32[5,16,16,128]{3,2,1,0:T(8,128)S(1)} %get-tuple-element.55, ...), kind=kOutput, calls=%fused_computation.30 | convolution fusion | flops 272163840 | bytes 2874368 | tf_op jit(solution)/shard_map/al,fxyl->fxya/dot_general | solution.py:171
  56.7 0.8 fusion.92
  57.5 10.4 %shard_map.93 = (f32[5,5,16,128]{3,2,1,0:T(8,128)}, f32[5,5,16,128]{3,2,1,0:T(8,128)}) custom-call(f32[5,5,16,128]{3,2,1,0:T(8,128)} %get-tuple-element.74.refs_0_, f32[5,5,16,128]{3,2,1,0:T(8,128)} %get-tuple-element.73.refs_1_), custom_call_target="tpu_custom_call" | custom-call | tf_op jit(solution)/shard_map/pallas_call | solution.py:70
  67.9 1.1 %pad_maximum_fusion.1 = f32[5,26,16,128]{3,2,1,0:T(8,128)S(1)} fusion(f32[5,5,16,128]{3,2,1,0:T(8,128)} %get-tuple-element.36, f32[5,16,16,128]{3,2,1,0:T(8,128)S(1)} %fusion.34, f32[5,5,16,128]{3,2,1,0:T(8,128)} %get-tuple-element.35), kind=kLoop, calls=%fused_computation.41 | loop fusion | flops 532480 | bytes 2129920 | tf_op jit(solution)/shard_map/concatenate | solution.py:88
  69.0 1.4 %fusion.24 = f32[5,16,128,16]{2,3,1,0:T(8,128)S(1)} fusion(f32[16,26,1,1]{1,0,3,2:T(8,128)S(1)} %copy-done.10, f32[5,26,16,128]{3,2,1,0:T(8,128)S(1)} %pad_maximum_fusion.1), kind=kOutput, calls=%fused_computation.24 | convolution fusion | flops 51118080 | bytes 1721984 | tf_op jit(solution)/shard_map/al,flyz->fayz/dot_general | solution.py:171
  70.4 0.2 copy.47
  70.7 0.9 fusion.91
  71.5 9.1 %shard_map.94 = (f32[5,16,5,128]{3,2,1,0:T(8,128)}, f32[5,16,5,128]{3,2,1,0:T(8,128)}) custom-call(f32[5,16,5,128]{3,2,1,0:T(8,128)} %get-tuple-element.72.refs_0_, f32[5,16,5,128]{3,2,1,0:T(8,128)} %get-tuple-element.71.refs_1_), custom_call_target="tpu_custom_call" | custom-call | tf_op jit(solution)/shard_map/pallas_call | solution.py:70
  80.6 2.2 %fusion.37 = f32[5,16,16,128]{3,2,1,0:T(8,128)S(1)} fusion(f32[16,26,1,1]{1,0,3,2:T(8,128)S(1)} %copy-done.10, f32[5,16,5,128]{3,2,1,0:T(8,128)} %get-tuple-element.38, f32[5,16,16,128]{3,2,1,0:T(8,128)S(1)} %bitcast.461, f32[5,16,5,128]{3,2,1,0:T(8,128)} %get-tuple-element.37), kind=kOutput, calls=%fused_computation.31 | convolution fusion | flops 51650560 | bytes 1721984 | tf_op jit(solution)/shard_map/al,fxlz->fxaz/dot_general | solution.py:171
  82.8 0.2 fusion.90
  83.1 0.8 copy.34.refs_0_
  83.9 0.8 copy.35.refs_1_
  84.7 6.9 %shard_map.95 = (f32[5,5,256]{2,1,0:T(8,128)}, f32[5,5,256]{2,1,0:T(8,128)}) custom-call(f32[5,5,256]{2,1,0:T(8,128)} %copy.34.refs_0_, f32[5,5,256]{2,1,0:T(8,128)} %copy.35.refs_1_), custom_call_target="tpu_custom_call" | custom-call | tf_op jit(solution)/shard_map/pallas_call | solution.py:70
  91.7 1.0 %copy.36 = f32[5,5,256]{1,2,0:T(8,128)S(1)} copy(f32[5,5,256]{2,1,0:T(8,128)} %get-tuple-element.39) | data formatting | bytes 51200 | tf_op jit(solution)/shard_map/reshape | solution.py:86
  92.7 1.0 %copy.37 = f32[5,5,256]{1,2,0:T(8,128)S(1)} copy(f32[5,5,256]{2,1,0:T(8,128)} %get-tuple-element.40) | data formatting | bytes 51200 | tf_op jit(solution)/shard_map/reshape | solution.py:87
  93.8 2.2 %fusion.18 = f32[5,16,16,128]{3,2,1,0:T(8,128)} fusion(f32[128,138,1,1]{0,1,3,2:T(8,128)S(1)} %copy-done.8, f32[5,16,16,5]{3,2,1,0:T(8,128)S(1)} %bitcast.469, f32[5,16,16,128]{3,2,1,0:T(8,128)S(1)} %fusion.37, f32[5,16,16,5]{3,2,1,0:T(8,128)S(1)} %bitcast.468), kind=kOutput, calls=%fused_computation.18 | convolution fusion | flops 271672320 | bytes 1432576 | tf_op jit(solution)/shard_map/al,fxyl->fxya/dot_general | solution.py:171
  (39 shorter events, 0.8 us)
Async XLA Ops:
  0.0 2.1 %copy-start.1 = (f32[5,16,16,128]{3,2,1,0:T(8,128)S(1)}, f32[5,16,16,128]{3,2,1,0:T(8,128)}, u32[]{:S(2)}) copy-start(f32[5,16,16,128]{3,2,1,0:T(8,128)} %param.9) | copy-start | bytes 1966084
  6.1 16.5 %copy-start.7 = (f32[16,26,1,1]{1,0,3,2:T(8,128)S(1)}, f32[16,26,1,1]{1,0,3,2:T(8,128)}, u32[]{:S(2)}) copy-start(f32[16,26,1,1]{1,0,3,2:T(8,128)} %constant.26) | copy-start | bytes 4996
  22.6 1.2 %copy-start.13 = (f32[4,16,5,128]{3,2,1,0:T(8,128)S(1)}, f32[4,16,5,128]{3,2,1,0:T(8,128)}, u32[]{:S(2)}) copy-start(f32[4,16,5,128]{3,2,1,0:T(8,128)} %get-tuple-element.25) | copy-start | bytes 491524
  22.7 1.2 %copy-start.14 = (f32[4,16,5,128]{3,2,1,0:T(8,128)S(1)}, f32[4,16,5,128]{3,2,1,0:T(8,128)}, u32[]{:S(2)}) copy-start(f32[4,16,5,128]{3,2,1,0:T(8,128)} %get-tuple-element.26) | copy-start | bytes 491524
  23.6 1.1 %copy-start.12 = (f32[4,5,256]{2,1,0:T(8,128)S(1)}, f32[4,5,256]{2,1,0:T(8,128)}, u32[]{:S(2)}) copy-start(f32[4,5,256]{2,1,0:T(8,128)} %get-tuple-element.27) | copy-start | bytes 61444
  23.8 1.2 %copy-start.11 = (f32[4,5,256]{2,1,0:T(8,128)S(1)}, f32[4,5,256]{2,1,0:T(8,128)}, u32[]{:S(2)}) copy-start(f32[4,5,256]{2,1,0:T(8,128)} %get-tuple-element.28) | copy-start | bytes 61444
  25.2 2.2 %copy-start = (f32[3,3,16,16,128]{4,3,2,1,0:T(8,128)S(1)}, f32[3,3,16,16,128]{4,3,2,1,0:T(8,128)}, u32[]{:S(2)}) copy-start(f32[3,3,16,16,128]{4,3,2,1,0:T(8,128)} %param.10) | copy-start | bytes 3538948
  25.2 2.2 %copy-start.2 = (f32[16,16,128]{2,1,0:T(8,128)S(1)}, f32[16,16,128]{2,1,0:T(8,128)}, u32[]{:S(2)}) copy-start(f32[16,16,128]{2,1,0:T(8,128)} %param.11) | copy-start | bytes 393220
  25.3 2.2 %copy-start.3 = (f32[5,16,16,128]{3,2,1,0:T(8,128)S(1)}, f32[5,16,16,128]{3,2,1,0:T(8,128)}, u32[]{:S(2)}) copy-start(f32[5,16,16,128]{3,2,1,0:T(8,128)} %get-tuple-element.85) | copy-start | bytes 1966084
  49.5 1.2 %copy-start.4 = (f32[5,16,5,128]{3,2,1,0:T(8,128)S(1)}, f32[5,16,5,128]{3,2,1,0:T(8,128)}, u32[]{:S(2)}) copy-start(f32[5,16,5,128]{3,2,1,0:T(8,128)} %get-tuple-element.31) | copy-start | bytes 614404
  49.6 1.2 %copy-start.5 = (f32[5,16,5,128]{3,2,1,0:T(8,128)S(1)}, f32[5,16,5,128]{3,2,1,0:T(8,128)}, u32[]{:S(2)}) copy-start(f32[5,16,5,128]{3,2,1,0:T(8,128)} %get-tuple-element.32) | copy-start | bytes 614404
  50.8 2.3 %copy-start.9 = (f32[5,5,256]{2,1,0:T(8,128)S(1)}, f32[5,5,256]{2,1,0:T(8,128)}, u32[]{:S(2)}) copy-start(f32[5,5,256]{2,1,0:T(8,128)} %get-tuple-element.34) | copy-start | bytes 76804
  52.0 2.2 %copy-start.6 = (f32[128,138,1,1]{0,1,3,2:T(8,128)S(1)}, f32[128,138,1,1]{0,1,3,2:T(8,128)}, u32[]{:S(2)}) copy-start(f32[128,138,1,1]{0,1,3,2:T(8,128)} %constant.27) | copy-start | bytes 211972
  57.5 11.5 %copy-start.10 = (f32[16,26,1,1]{1,0,3,2:T(8,128)S(1)}, f32[16,26,1,1]{1,0,3,2:T(8,128)}, u32[]{:S(2)}) copy-start(f32[16,26,1,1]{1,0,3,2:T(8,128)} %constant.28) | copy-start | bytes 4996
  83.9 9.8 %copy-start.8 = (f32[128,138,1,1]{0,1,3,2:T(8,128)S(1)}, f32[128,138,1,1]{0,1,3,2:T(8,128)}, u32[]{:S(2)}) copy-start(f32[128,138,1,1]{0,1,3,2:T(8,128)} %constant.29) | copy-start | bytes 211972

commit v3 on v2

--- a/solution.py
+++ b/solution.py
@@ -1,4 +1,5 @@
 import functools
+import itertools
 
 import jax
 import jax.numpy as jnp
@@ -25,29 +26,28 @@
     send_sems, recv_sems = refs[2 * count :]
     here = [lax.axis_index(axis) for axis in AXES]
 
-    def device(axis, step):
-        place = list(here)
-        slot = AXES.index(axis)
-        place[slot] = lax.rem(here[slot] + step + sizes[slot], sizes[slot])
-        return tuple(place)
+    def device(offset):
+        return tuple(
+            lax.rem(here[slot] + offset[slot] + sizes[slot], sizes[slot]) for slot in range(3)
+        )
 
     partners = []
-    for axis, step in routes:
-        for way in (step, -step):
-            if (axis, way) not in partners:
-                partners.append((axis, way))
+    for offset in routes:
+        for way in (offset, tuple(-step for step in offset)):
+            if way not in partners:
+                partners.append(way)
     barrier = pltpu.get_barrier_semaphore()
-    for axis, step in partners:
-        pl.semaphore_signal(barrier, inc=1, device_id=device(axis, step), device_id_type=MESH)
+    for offset in partners:
+        pl.semaphore_signal(barrier, inc=1, device_id=device(offset), device_id_type=MESH)
     pl.semaphore_wait(barrier, len(partners))
     copies = []
-    for index, (axis, step) in enumerate(routes):
+    for index, offset in enumerate(routes):
         copy = pltpu.make_async_remote_copy(
             src_ref=sources[index],
             dst_ref=targets[index],
             send_sem=send_sems.at[index],
             recv_sem=recv_sems.at[index],
-            device_id=device(axis, step),
+            device_id=device(offset),
             device_id_type=MESH,
         )
         copy.start()
@@ -56,18 +56,9 @@
         copy.wait()
 
 
-def exchange_faces(items, tag):
+def exchange(sends, routes, tag):
     sizes = tuple(lax.axis_size(axis) for axis in AXES)
-    sends, routes = [], []
-    for value, axis, dim in items:
-        length = value.shape[dim]
-        for face, step in ((slice(length - WIDTH, length), 1), (slice(0, WIDTH), -1)):
-            part = lax.slice_in_dim(value, face.start, face.stop, axis=dim)
-            if dim == value.ndim - 1:
-                part = jnp.moveaxis(part, dim, 1).reshape(part.shape[0], WIDTH, -1)
-            sends.append(part)
-            routes.append((axis, step))
-    received = pl.pallas_call(
+    return pl.pallas_call(
         functools.partial(exchange_kernel, tuple(routes), sizes),
         out_shape=[jax.ShapeDtypeStruct(send.shape, send.dtype) for send in sends],
         in_specs=[pl.BlockSpec(memory_space=pltpu.VMEM)] * len(sends),
@@ -78,6 +69,23 @@
         ],
         compiler_params=pltpu.CompilerParams(collective_id=tag, has_side_effects=True),
     )(*sends)
+
+
+def offset_along(axis, step):
+    return tuple(step if name == axis else 0 for name in AXES)
+
+
+def exchange_faces(items, tag):
+    sends, routes = [], []
+    for value, axis, dim in items:
+        length = value.shape[dim]
+        for face, step in ((slice(length - WIDTH, length), 1), (slice(0, WIDTH), -1)):
+            part = lax.slice_in_dim(value, face.start, face.stop, axis=dim)
+            if dim == value.ndim - 1:
+                part = jnp.moveaxis(part, dim, 1).reshape(part.shape[0], WIDTH, -1)
+            sends.append(part)
+            routes.append(offset_along(axis, step))
+    received = exchange(sends, routes, tag)
     padded = []
     for index, (value, axis, dim) in enumerate(items):
         before, after = received[2 * index], received[2 * index + 1]
@@ -87,6 +95,45 @@
             after = jnp.moveaxis(after.reshape(shape), 1, dim)
         padded.append(jnp.concatenate([before, value, after], axis=dim))
     return padded
+
+
+def exchange_box(value, tag):
+    fields = value.shape[0]
+    sends, routes, shapes = [], [], []
+    for offset in itertools.product((-1, 0, 1), repeat=3):
+        if offset == (0, 0, 0):
+            continue
+        part = value
+        for slot, step in enumerate(offset):
+            length = value.shape[slot + 1]
+            if step == 1:
+                part = lax.slice_in_dim(part, length - WIDTH, length, axis=slot + 1)
+            elif step == -1:
+                part = lax.slice_in_dim(part, 0, WIDTH, axis=slot + 1)
+        shapes.append(part.shape)
+        if offset[2] != 0:
+            part = jnp.moveaxis(part, 3, 1).reshape(fields, WIDTH, -1)
+        sends.append(part)
+        routes.append(offset)
+    received = exchange(sends, routes, tag)
+    pieces = {}
+    for index, offset in enumerate(routes):
+        piece = received[index]
+        if offset[2] != 0:
+            shape = shapes[index]
+            piece = jnp.moveaxis(piece.reshape((fields, WIDTH) + shape[1:3]), 1, 3)
+        pieces[tuple(1 - step for step in offset)] = piece
+    pieces[(1, 1, 1)] = value
+    return jnp.concatenate(
+        [
+            jnp.concatenate(
+                [jnp.concatenate([pieces[(ix, iy, iz)] for iz in range(3)], axis=3) for iy in range(3)],
+                axis=2,
+            )
+            for ix in range(3)
+        ],
+        axis=1,
+    )
 
 
 def with_halo(value, sides, width):
@@ -264,9 +311,9 @@
     divergence = divergence + sweep_lines(padded[1], derive[1], 2)
     divergence = divergence + sweep_lines(padded[2], derive[2], 3)
     sectioned = conserved_solution - step_duration * jacobian * divergence
-    result = sweep_lines(exchange_faces([(sectioned, "xi", 1)], 2)[0], smooth[0], 1)
-    result = sweep_lines(exchange_faces([(result, "eta", 2)], 3)[0], smooth[1], 2)
-    result = sweep_lines(exchange_faces([(result, "zeta", 3)], 4)[0], smooth[2], 3)
+    result = sweep_lines(exchange_box(sectioned, 2), smooth[0], 1)
+    result = sweep_lines(result, smooth[1], 2)
+    result = sweep_lines(result, smooth[2], 3)
     return result
 
 

time: 97.7 us -> 149 us (1.53)
  local copies, waits for them, and re-layouts: 16.9 us -> 54.1 us
  other arithmetic: 8.53 us -> 21.1 us
  matrix products: 14.7 us -> 20.6 us
  Pallas kernels: 55.4 us -> 51.6 us
    reshape x2 -> x54, local copies, waits for them, and re-layouts: 2.06 us -> 31.4 us  [the longest x24 18.1 us: exchange_box(): piece = jnp.moveaxis(piece.reshape((fields, WIDTH) + shape[1:3]), 1, 3)]
    pallas_call x4 -> x10, local copies, waits for them, and re-layouts: 2.6 us -> 10.3 us  [exchange(): pl.pallas_call(functools.partial(exchange_kernel, tuple(routes), sizes),...]
    concatenate x0 -> x1, other arithmetic: none -> 7.44 us  [exchange_box(): jnp.concatenate([jnp.concatenate([jnp.concatenate([pieces[ix, iy, iz] for...]
    dot_general x9, matrix products: 14.7 us -> 20.6 us  [sweep_lines(): jnp.einsum(line_forms[dim], matrix, padded, precision=lax.Precision.HIGHEST)]
    pallas_call x5 -> x3, Pallas kernels: 55.4 us -> 51.6 us  [exchange(): pl.pallas_call(functools.partial(exchange_kernel, tuple(routes), sizes),...]
    slice x0 -> x5, local copies, waits for them, and re-layouts: none -> 2.87 us  [exchange_box(): part = lax.slice_in_dim(part, length - WIDTH, length, axis=slot + 1)]
    unnamed x8, other arithmetic: 0.8 us -> 3.65 us
    slice x6 -> x3, local copies, waits for them, and re-layouts: 4.65 us -> 2.72 us  [exchange_faces(): part = lax.slice_in_dim(value, face.start, face.stop, axis=dim)]
where the time goes in v3:
time: 149 us; the launch traced here: 148 us
  local copies, waits for them, and re-layouts  54.1 us (36%)
  Pallas kernels  51.6 us (35%)
  other arithmetic  21.1 us (14%)
  matrix products  20.6 us (14%)
    pallas_call x3, Pallas kernels, exchange(): pl.pallas_call(functools.partial(exchange_kernel, tuple(routes), sizes),...  51.6 us
    dot_general x9, matrix products, sweep_lines(): jnp.einsum(line_forms[dim], matrix, padded, precision=lax.Precision.HIGHEST)  20.6 us
    reshape x24, local copies, waits for them, and re-layouts, exchange_box(): piece = jnp.moveaxis(piece.reshape((fields, WIDTH) + shape[1:3]), 1, 3)  18.1 us
    reshape x30, local copies, waits for them, and re-layouts, exchange_box(): part = jnp.moveaxis(part, 3, 1).reshape(fields, WIDTH, -1)  13.3 us
    pallas_call x10, local copies, waits for them, and re-layouts, exchange(): pl.pallas_call(functools.partial(exchange_kernel, tuple(routes), sizes),...  10.3 us
    concatenate x1, other arithmetic, exchange_box(): jnp.concatenate([jnp.concatenate([jnp.concatenate([pieces[ix, iy, iz] for...  7.44 us
    reshape x4, local copies, waits for them, and re-layouts, exchange_faces(): part = jnp.moveaxis(part, dim, 1).reshape(part.shape[0], WIDTH, -1)  4.37 us
    unnamed x8, other arithmetic  3.65 us

profile of v3, /device:TPU:1, one launch (start us, length us, event | category | flops | bytes accessed | tf_op | source)
XLA Modules:
  0.0 147.9 jit_solution(346383372981356374)
XLA Ops:
  0.0 1.6 %broadcast_multiply_fusion = f32[16,16,128]{2,1,0:T(8,128)} fusion(f32[16,16,128]{2,1,0:T(8,128)} %param.11), kind=kLoop, calls=%fused_computation.157 | loop fusion | flops 32768 | bytes 262144 | tf_op jit(solution)/shard_map/mul | solution.py:313
  1.6 0.9 slice_bitcast_fusion.28
  2.5 1.1 multiply_reduce_fusion
  3.6 1.8 %fusion.71 = (f32[1,16,16,128]{3,2,1,0:T(8,128)S(1)}, f32[5,16,16,128]{3,2,1,0:T(8,128)}) fusion(f32[16,16,128]{2,1,0:T(8,128)S(1)} %get-tuple-element.93, f32[5,16,16,128]{3,2,1,0:T(8,128)} %param.9), kind=kLoop, calls=%fused_computation.118 | loop fusion | flops 131071 | bytes 786432 | tf_op jit(solution)/shard_map/div | solution.py:239
  6.1 0.8 fusion.58
  8.8 15.4 %shard_map.91 = (f32[4,5,16,128]{3,2,1,0:T(8,128)}, f32[4,5,16,128]{3,2,1,0:T(8,128)}, f32[4,16,5,128]{3,2,1,0:T(8,128)}, f32[4,16,5,128]{3,2,1,0:T(8,128)}, f32[4,5,256]{2,1,0:T(8,128)}, /*index=5*/f32[4,5,256]{2,1,0:T(8,128)}) custom-call(f32[4,5,16,128]{3,2,1,0:T(8,128)} %get-tuple-element.151.refs_0_, f32[4,5,16,128]{3,2,1,0:T(8,128)} %get-tuple-element.150.refs_1_, ...), custom_call_target="tpu_custom_call" | custom-call | tf_op jit(solution)/shard_map/pallas_call | solution.py:61
  24.3 2.1 %convolution_bitcast_fusion = f32[4,16,16,128]{3,2,1,0:T(8,128)S(1)} fusion(f32[16,26,1,1]{1,0,3,2:T(8,128)S(1)} %copy-done.9, f32[4,16,5,128]{3,2,1,0:T(8,128)} %get-tuple-element.46, f32[1,16,16,128]{3,2,1,0:T(8,128)S(1)} %get-tuple-element.144, f32[3,16,16,128]{3,2,1,0:T(8,128)S(1)} %get-tuple-element.94, f32[4,16,5,128]{3,2,1,0:T(8,128)} %get-tuple-element.45), kind=kOutput, calls=%fused_computation.26 | convolution fusion | flops 41533440 | bytes 1377920 | tf_op jit(solution)/shard_map/al,fxlz->fxaz/dot_general | solution.py:218
  26.3 1.1 pad_maximum_fusion.1
  27.4 1.0 fusion.54
  28.6 1.8 %copy.110 = f32[4,5,256]{1,2,0:T(8,128)} copy(f32[4,5,256]{2,1,0:T(8,128)} %get-tuple-element.47) | data formatting | bytes 40960 | tf_op jit(solution)/shard_map/pallas_call | solution.py:61
  30.4 1.8 %copy.111 = f32[4,5,256]{1,2,0:T(8,128)} copy(f32[4,5,256]{2,1,0:T(8,128)} %get-tuple-element.48) | data formatting | bytes 40960 | tf_op jit(solution)/shard_map/pallas_call | solution.py:61
  32.2 2.3 %fusion.46 = f32[4,16,16,128]{3,2,1,0:T(8,128)S(1)} fusion(f32[128,138,1,1]{0,1,3,2:T(8,128)} %constant.27, f32[4,16,16,5]{3,2,1,0:T(8,128)} %bitcast.555, f32[1,16,16,128]{3,2,1,0:T(8,128)S(1)} %get-tuple-element.144, f32[3,16,16,128]{3,2,1,0:T(8,128)S(1)} %get-tuple-element.94, f32[4,16,16,5]{3,2,1,0:T(8,128)} %bitcast.554), kind=kOutput, calls=%fused_computation.40 | convolution fusion | flops 217479168 | bytes 1160192 | tf_op jit(solution)/shard_map/al,fxyl->fxya/dot_general | solution.py:218
  34.5 1.8 %bitcast_dynamic-update-slice_fusion.11 = (f32[5,16,16,128]{3,2,1,0:T(8,128)}, f32[16,16,128]{2,1,0:T(8,128)S(1)}, f32[16,16,128]{2,1,0:T(8,128)S(1)}, f32[16,16...) fusion(f32[5,16,16,128]{3,2,1,0:T(8,128)} %get-tuple-element.145, ...), kind=kLoop, calls=%fused_computation.112 | loop fusion | flops 983040 | bytes 3801088
  37.9 0.8 bitcast_dynamic-update-slice_fusion.8
  41.2 0.9 fusion.87
  42.1 1.0 fusion.86
  43.2 1.9 %copy.161.refs_5_ = f32[5,5,256]{2,1,0:T(8,128)} copy(f32[5,5,256]{1,2,0:T(8,128)} %bitcast.548) | data formatting | bytes 51200 | tf_op jit(solution)/shard_map/reshape | solution.py:85
  45.1 0.8 copy.160.refs_4_
  45.9 13.6 %shard_map.92 = (f32[5,5,16,128]{3,2,1,0:T(8,128)}, f32[5,5,16,128]{3,2,1,0:T(8,128)}, f32[5,16,5,128]{3,2,1,0:T(8,128)}, f32[5,16,5,128]{3,2,1,0:T(8,128)}, f32[5,5,256]{2,1,0:T(8,128)}, /*index=5*/f32[5,5,256]{2,1,0:T(8,128)}) custom-call(f32[5,5,16,128]{3,2,1,0:T(8,128)} %get-tuple-element.140.refs_0_, f32[5,5,16,128]{3,2,1,0:T(8,128)} %get-tuple-element.139.refs_1_, ...), custom_call_target="tpu_custom_call" | custom-call | tf_op jit(solution)/shard_map/pallas_call | solution.py:61
  59.6 1.2 pad_maximum_fusion
  60.8 1.2 fusion.22
  62.0 1.2 fusion.36
  63.2 1.0 copy.116
  64.3 1.1 copy.117
  65.4 2.5 %fusion.30 = f32[5,16,16,128]{3,2,1,0:T(8,128)S(1)} fusion(f32[5,16,16,128]{3,2,1,0:T(8,128)S(1)} %copy-done.1, f32[5,16,16,128]{3,2,1,0:T(8,128)S(1)} %fusion.36, f32[128,138,1,1]{0,1,3,2:T(8,128)S(1)} %copy-done.8, f32[5,16,16,5]{3,2,1,0:T(8,128)} %bitcast.545, f32[5,16,16,128]{3,2,1,0:T(8,128)S(1)} %get-tuple-element.95, ...), kind=kOutput, calls=%fused_computation.23 | convolution fusion | flops 272163840 | bytes 2874368 | tf_op jit(solution)/shard_map/al,fxyl->fxya/dot_general | solution.py:218
  69.4 0.9 fusion.84
  83.0 0.8 copy.133.refs_13_
  83.8 0.8 copy.132.refs_12_
  84.7 22.6 %shard_map.93 = (f32[5,5,25]{2,1,0:T(8,128)}, f32[5,5,5,128]{3,2,1,0:T(8,128)}, f32[5,5,25]{2,1,0:T(8,128)}, f32[5,5,80]{2,1,0:T(8,128)}, f32[5,5,16,128]{3,2,1,...) custom-call(f32[5,5,25]{2,1,0:T(8,128)} %copy.162.refs_0_, ...), custom_call_target="tpu_custom_call" | custom-call | tf_op jit(solution)/shard_map/pallas_call | solution.py:61
  107.3 0.8 reshape.177
  108.2 0.9 copy.136
  109.9 0.9 copy.137
  111.6 0.9 copy.140
  113.3 0.9 copy.141
  115.0 0.9 copy.148
  116.7 0.9 copy.149
  118.4 0.9 copy.152
  120.1 0.9 copy.153
  121.0 0.9 copy.138
  121.9 1.5 %copy.139 = f32[5,5,80]{1,2,0:T(8,128)} copy(f32[5,5,80]{2,1,0:T(8,128)} %get-tuple-element.60) | data formatting | bytes 16000 | tf_op jit(solution)/shard_map/pallas_call | solution.py:61
  123.4 0.9 reshape.183
  124.9 0.9 reshape.184
  127.9 0.8 copy.150
  128.7 0.8 copy.151
  130.1 7.4 %maximum_maximum_fusion = f32[5,26,26,138]{3,2,1,0:T(8,128)S(1)} fusion(f32[5,5,5,5]{3,2,1,0:T(8,128)} %bitcast.575, f32[5,5,5,128]{3,2,1,0:T(8,128)} %get-tuple-element.79, f32[5,5,5,5]{3,2,1,0:T(8,128)} %bitcast.574, f32[5,5,16,5]{3,2,1,0:T(8,128)} %bitcast.567, f32[5,5,16,128]{3,2,1,0:T(8,128)} %get-tuple-element.76, f32[5,5,16,5]{3,2,1,0:T(8,128)} %bitcast.566, ...), kind=kLoop, calls=%fused_computation | loop fusion | flops 12127440 | bytes 3731520 | tf_op jit(solution)/shard_map/concatenate | solution.py:127
  137.6 5.2 %fusion.4 = f32[5,16,26,138]{3,1,2,0:T(8,128)S(1)} fusion(f32[16,26,1,1]{1,0,3,2:T(8,128)S(1)} %copy-done.14, f32[5,26,26,138]{3,2,1,0:T(8,128)S(1)} %maximum_maximum_fusion), kind=kOutput, calls=%fused_computation.5 | convolution fusion | flops 89556480 | bytes 3015584 | tf_op jit(solution)/shard_map/al,flyz->fayz/dot_general | solution.py:218
  142.8 3.1 %fusion.7 = f32[5,16,16,138]{3,2,1,0:T(8,128)S(1)} fusion(f32[16,26,1,1]{1,0,3,2:T(8,128)S(1)} %copy-done.14, f32[5,16,26,138]{3,1,2,0:T(8,128)S(1)} %fusion.4), kind=kOutput, calls=%fused_computation.6 | convolution fusion | flops 55111680 | bytes 1856384 | tf_op jit(solution)/shard_map/al,fxlz->fxaz/dot_general | solution.py:218
  145.9 2.0 %fusion.89 = f32[5,16,16,128]{3,2,1,0:T(8,128)} fusion(f32[5,16,16,138]{3,2,1,0:T(8,128)S(1)} %fusion.7, f32[128,138,1,1]{0,1,3,2:T(8,128)S(1)} %copy-done.10), kind=kOutput, calls=%fused_computation.170 | convolution fusion | flops 271319040 | bytes 1432576 | tf_op jit(solution)/shard_map/al,fxyl->fxya/dot_general | solution.py:218
  (104 shorter events, 29.9 us)
Async XLA Ops:
  0.0 24.2 %copy-start.9 = (f32[16,26,1,1]{1,0,3,2:T(8,128)S(1)}, f32[16,26,1,1]{1,0,3,2:T(8,128)}, u32[]{:S(2)}) copy-start(f32[16,26,1,1]{1,0,3,2:T(8,128)} %constant.26) | copy-start | bytes 4996
  3.6 20.7 %copy-start.3 = (f32[16,16,128]{2,1,0:T(8,128)}, f32[16,16,128]{2,1,0:T(8,128)S(1)}, u32[]{:S(2)}) copy-start(f32[16,16,128]{2,1,0:T(8,128)S(1)} %get-tuple-element.93) | copy-start | bytes 393220
  24.2 10.3 %copy-start = (f32[3,3,16,16,128]{4,3,2,1,0:T(8,128)S(1)}, f32[3,3,16,16,128]{4,3,2,1,0:T(8,128)}, u32[]{:S(2)}) copy-start(f32[3,3,16,16,128]{4,3,2,1,0:T(8,128)} %param.10) | copy-start | bytes 3538948
  24.2 10.3 %copy-start.1 = (f32[5,16,16,128]{3,2,1,0:T(8,128)S(1)}, f32[5,16,16,128]{3,2,1,0:T(8,128)}, u32[]{:S(2)}) copy-start(f32[5,16,16,128]{3,2,1,0:T(8,128)} %param.9) | copy-start | bytes 1966084
  24.3 10.3 %copy-start.2 = (f32[16,16,128]{2,1,0:T(8,128)S(1)}, f32[16,16,128]{2,1,0:T(8,128)}, u32[]{:S(2)}) copy-start(f32[16,16,128]{2,1,0:T(8,128)} %param.11) | copy-start | bytes 393220
  38.9 1.1 copy-start.4
  59.5 2.4 %copy-start.6 = (f32[5,16,5,128]{3,2,1,0:T(8,128)S(1)}, f32[5,16,5,128]{3,2,1,0:T(8,128)}, u32[]{:S(2)}) copy-start(f32[5,16,5,128]{3,2,1,0:T(8,128)} %get-tuple-element.51) | copy-start | bytes 614404
  59.5 2.4 %copy-start.7 = (f32[5,16,5,128]{3,2,1,0:T(8,128)S(1)}, f32[5,16,5,128]{3,2,1,0:T(8,128)}, u32[]{:S(2)}) copy-start(f32[5,16,5,128]{3,2,1,0:T(8,128)} %get-tuple-element.52) | copy-start | bytes 614404
  59.5 4.7 %copy-start.13 = (f32[5,5,256]{2,1,0:T(8,128)S(1)}, f32[5,5,256]{2,1,0:T(8,128)}, u32[]{:S(2)}) copy-start(f32[5,5,256]{2,1,0:T(8,128)} %get-tuple-element.54) | copy-start | bytes 76804
  59.5 5.8 %copy-start.5 = (f32[16,16,128]{2,1,0:T(8,128)S(1)}, f32[16,16,128]{2,1,0:T(8,128)}, u32[]{:S(2)}) copy-start(f32[16,16,128]{2,1,0:T(8,128)} %broadcast_multiply_fusion) | copy-start | bytes 393220
  59.6 5.8 %copy-start.8 = (f32[128,138,1,1]{0,1,3,2:T(8,128)S(1)}, f32[128,138,1,1]{0,1,3,2:T(8,128)}, u32[]{:S(2)}) copy-start(f32[128,138,1,1]{0,1,3,2:T(8,128)} %constant.27) | copy-start | bytes 211972
  107.3 19.1 %copy-start.18 = (f32[5,5,80]{2,1,0:T(8,128)S(1)}, f32[5,5,80]{2,1,0:T(8,128)}, u32[]{:S(2)}) copy-start(f32[5,5,80]{2,1,0:T(8,128)} %get-tuple-element.69) | copy-start | bytes 24004
  107.3 19.9 %copy-start.17 = (f32[5,5,80]{2,1,0:T(8,128)S(1)}, f32[5,5,80]{2,1,0:T(8,128)}, u32[]{:S(2)}) copy-start(f32[5,5,80]{2,1,0:T(8,128)} %get-tuple-element.71) | copy-start | bytes 24004
  107.3 20.6 %copy-start.16 = (f32[5,5,80]{2,1,0:T(8,128)S(1)}, f32[5,5,80]{2,1,0:T(8,128)}, u32[]{:S(2)}) copy-start(f32[5,5,80]{2,1,0:T(8,128)} %get-tuple-element.75) | copy-start | bytes 24004
  107.3 21.4 %copy-start.15 = (f32[5,5,80]{2,1,0:T(8,128)S(1)}, f32[5,5,80]{2,1,0:T(8,128)}, u32[]{:S(2)}) copy-start(f32[5,5,80]{2,1,0:T(8,128)} %get-tuple-element.77) | copy-start | bytes 24004
  107.3 22.3 %copy-start.12 = (f32[5,5,256]{2,1,0:T(8,128)S(1)}, f32[5,5,256]{2,1,0:T(8,128)}, u32[]{:S(2)}) copy-start(f32[5,5,256]{2,1,0:T(8,128)} %get-tuple-element.67) | copy-start | bytes 76804
  107.3 22.5 %copy-start.11 = (f32[5,5,256]{2,1,0:T(8,128)S(1)}, f32[5,5,256]{2,1,0:T(8,128)}, u32[]{:S(2)}) copy-start(f32[5,5,256]{2,1,0:T(8,128)} %get-tuple-element.68) | copy-start | bytes 76804
  130.1 7.5 %copy-start.14 = (f32[16,26,1,1]{1,0,3,2:T(8,128)S(1)}, f32[16,26,1,1]{1,0,3,2:T(8,128)}, u32[]{:S(2)}) copy-start(f32[16,26,1,1]{1,0,3,2:T(8,128)} %constant.28) | copy-start | bytes 4996
  137.6 8.3 %copy-start.10 = (f32[128,138,1,1]{0,1,3,2:T(8,128)S(1)}, f32[128,138,1,1]{0,1,3,2:T(8,128)}, u32[]{:S(2)}) copy-start(f32[128,138,1,1]{0,1,3,2:T(8,128)} %constant.29) | copy-start | bytes 211972

commit v4 on v2

--- a/solution.py
+++ b/solution.py
@@ -70,8 +70,8 @@
     received = pl.pallas_call(
         functools.partial(exchange_kernel, tuple(routes), sizes),
         out_shape=[jax.ShapeDtypeStruct(send.shape, send.dtype) for send in sends],
-        in_specs=[pl.BlockSpec(memory_space=pltpu.VMEM)] * len(sends),
-        out_specs=[pl.BlockSpec(memory_space=pltpu.VMEM)] * len(sends),
+        in_specs=[pl.BlockSpec(memory_space=pl.ANY)] * len(sends),
+        out_specs=[pl.BlockSpec(memory_space=pl.ANY)] * len(sends),
         scratch_shapes=[
             pltpu.SemaphoreType.DMA((len(sends),)),
             pltpu.SemaphoreType.DMA((len(sends),)),

time: 97.7 us -> 89.5 us (0.916)
  Pallas kernels: 55.4 us -> 47.4 us
    pallas_call x5, Pallas kernels: 55.4 us -> 47.4 us  [exchange_faces(): pl.pallas_call(functools.partial(exchange_kernel, tuple(routes), sizes),...]
where the time goes in v4:
time: 89.5 us; the launch traced here: 87.9 us
  Pallas kernels  47.4 us (53%)
  local copies, waits for them, and re-layouts  16.9 us (19%)
  matrix products  14.7 us (16%)
  other arithmetic  8.53 us (10%)
    pallas_call x5, Pallas kernels, exchange_faces(): pl.pallas_call(functools.partial(exchange_kernel, tuple(routes), sizes),...  47.4 us
    dot_general x9, matrix products, sweep_lines(): jnp.einsum(line_forms[dim], matrix, padded, precision=lax.Precision.HIGHEST)  14.7 us
    reshape x6, local copies, waits for them, and re-layouts, exchange_faces(): part = jnp.moveaxis(part, dim, 1).reshape(part.shape[0], WIDTH, -1)  6.04 us
    slice x6, local copies, waits for them, and re-layouts, exchange_faces(): part = lax.slice_in_dim(value, face.start, face.stop, axis=dim)  4.65 us
    concatenate x3, other arithmetic, exchange_faces(): padded.append(jnp.concatenate([before, value, after], axis=dim))  3.29 us
    pallas_call x4, local copies, waits for them, and re-layouts, exchange_faces(): pl.pallas_call(functools.partial(exchange_kernel, tuple(routes), sizes),...  2.6 us

profile of v4, /device:TPU:1, one launch (start us, length us, event | category | flops | bytes accessed | tf_op | source)
XLA Modules:
  0.0 87.9 jit_solution(223888208088301665)
XLA Ops:
  0.0 1.0 %slice_bitcast_fusion.24 = f32[16,16,128]{2,1,0:T(8,128)S(1)} fusion(f32[5,16,16,128]{3,2,1,0:T(8,128)} %param.9), kind=kLoop, calls=%fused_computation.151 | loop fusion | bytes 262144 | tf_op jit(solution)/shard_map/div | solution.py:188
  1.0 1.1 %multiply_reduce_fusion = (f32[16,16,128]{2,1,0:T(8,128)S(1)}, f32[3,16,16,128]{3,2,1,0:T(8,128)S(1)}) fusion(f32[5,16,16,128]{3,2,1,0:T(8,128)} %param.9, f32[16,16,128]{2,1,0:T(8,128)S(1)} %slice_bitcast_fusion.24), kind=kLoop, calls=%fused_computation.72 | loop fusion | flops 262144 | bytes 1048576 | tf_op jit(solution)/shard_map/reduce_sum | solution.py:190
  2.1 0.7 fusion.78
  2.8 0.2 pad_maximum_fusion.3
  3.0 0.8 copy.10.refs_4_
  3.8 0.8 copy.11.refs_5_
  4.6 0.8 fusion.65
  5.4 0.7 fusion.67
  6.1 13.6 %shard_map.91 = (f32[4,5,16,128]{3,2,1,0:T(8,128)}, f32[4,5,16,128]{3,2,1,0:T(8,128)}, f32[4,16,5,128]{3,2,1,0:T(8,128)}, f32[4,16,5,128]{3,2,1,0:T(8,128)}, f32[4,5,256]{2,1,0:T(8,128)}, /*index=5*/f32[4,5,256]{2,1,0:T(8,128)}) custom-call(f32[4,5,16,128]{3,2,1,0:T(8,128)} %get-tuple-element.91.refs_0_, f32[4,5,16,128]{3,2,1,0:T(8,128)} %get-tuple-element.90.refs_1_, ...), custom_call_target="tpu_custom_call" | custom-call | tf_op jit(solution)/shard_map/pallas_call | solution.py:70
  19.7 1.1 %pad_maximum_fusion.2 = f32[4,26,16,128]{3,2,1,0:T(8,128)S(1)} fusion(f32[4,5,16,128]{3,2,1,0:T(8,128)} %get-tuple-element.24, f32[1,16,16,128]{3,2,1,0:T(8,128)S(1)} %get-tuple-element.84, f32[3,16,16,128]{3,2,1,0:T(8,128)S(1)} %get-tuple-element.54, f32[4,5,16,128]{3,2,1,0:T(8,128)} %get-tuple-element.23), kind=kLoop, calls=%fused_computation.59 | loop fusion | flops 638976 | bytes 1703936 | tf_op jit(solution)/shard_map/concatenate | solution.py:88
  20.8 1.0 %fusion.61 = f32[4,16,128,16]{2,3,1,0:T(8,128)S(1)} fusion(f32[16,26,1,1]{1,0,3,2:T(8,128)S(1)} %copy-done.7, f32[4,26,16,128]{3,2,1,0:T(8,128)S(1)} %pad_maximum_fusion.2), kind=kOutput, calls=%fused_computation.57 | convolution fusion | flops 40894464 | bytes 1377920 | tf_op jit(solution)/shard_map/al,flyz->fayz/dot_general | solution.py:171
  21.8 0.2 copy.48
  22.0 0.9 %convolution_bitcast_fusion = f32[4,16,16,128]{3,2,1,0:T(8,128)S(1)} fusion(f32[16,26,1,1]{1,0,3,2:T(8,128)S(1)} %copy-done.7, f32[4,16,5,128]{3,2,1,0:T(8,128)S(1)} %copy-done.14, f32[1,16,16,128]{3,2,1,0:T(8,128)S(1)} %get-tuple-element.84, f32[3,16,16,128]{3,2,1,0:T(8,128)S(1)} %get-tuple-element.54, f32[4,16,5,128]{3,2,1,0:T(8,128)S(1)} %copy-done.13), kind=kOutput, calls=%fused_computation.34 | convolution fusion | flops 41533440 | bytes 1377920 | tf_op jit(solution)/shard_map/al,fxlz->fxaz/dot_general | solution.py:171
  22.9 0.2 copy.14
  23.1 0.2 copy.15
  23.4 2.2 %fusion.53 = f32[4,16,16,128]{3,2,1,0:T(8,128)S(1)} fusion(f32[128,138,1,1]{0,1,3,2:T(8,128)} %constant.27, f32[4,16,16,5]{3,2,1,0:T(8,128)S(1)} %bitcast.473, f32[1,16,16,128]{3,2,1,0:T(8,128)S(1)} %get-tuple-element.84, f32[3,16,16,128]{3,2,1,0:T(8,128)S(1)} %get-tuple-element.54, f32[4,16,16,5]{3,2,1,0:T(8,128)S(1)} %bitcast.472), kind=kOutput, calls=%fused_computation.49 | convolution fusion | flops 217479168 | bytes 1160192 | tf_op jit(solution)/shard_map/al,fxyl->fxya/dot_general | solution.py:171
  25.6 0.2 bitcast_dynamic-update-slice_fusion.11
  26.1 0.2 bitcast_dynamic-update-slice_fusion.8
  26.5 0.1 bitcast_dynamic-update-slice_fusion.4
  26.8 0.1 bitcast_dynamic-update-slice_fusion
  27.0 0.4 multiply_add_fusion
  27.5 1.1 %fusion.93 = (f32[5,16,16,5]{3,2,1,0:T(8,128)S(1)}, f32[5,16,16,5]{3,2,1,0:T(8,128)}) fusion(f32[5,16,16,128]{3,2,1,0:T(8,128)S(1)} %get-tuple-element.55), kind=kLoop, calls=%fused_computation.165 | loop fusion | bytes 102400 | tf_op jit(solution)/shard_map/slice | solution.py:65
  28.5 1.9 %copy.32.refs_4_ = f32[5,5,256]{2,1,0:T(8,128)} copy(f32[5,5,256]{1,2,0:T(8,128)} %bitcast.466) | data formatting | bytes 51200 | tf_op jit(solution)/shard_map/reshape | solution.py:67
  30.5 0.8 copy.33.refs_5_
  31.3 0.9 %fusion.94 = (f32[5,16,5,128]{3,2,1,0:T(8,128)}, f32[5,16,5,128]{3,2,1,0:T(8,128)}) fusion(f32[5,16,16,128]{3,2,1,0:T(8,128)S(1)} %get-tuple-element.56), kind=kLoop, calls=%fused_computation.166 | loop fusion | bytes 819200 | tf_op jit(solution)/shard_map/slice | solution.py:65
  32.2 0.8 fusion.95
  33.0 11.6 %shard_map.92 = (f32[5,5,16,128]{3,2,1,0:T(8,128)}, f32[5,5,16,128]{3,2,1,0:T(8,128)}, f32[5,16,5,128]{3,2,1,0:T(8,128)}, f32[5,16,5,128]{3,2,1,0:T(8,128)}, f32[5,5,256]{2,1,0:T(8,128)}, /*index=5*/f32[5,5,256]{2,1,0:T(8,128)}) custom-call(f32[5,5,16,128]{3,2,1,0:T(8,128)} %get-tuple-element.80.refs_0_, f32[5,5,16,128]{3,2,1,0:T(8,128)} %get-tuple-element.79.refs_1_, ...), custom_call_target="tpu_custom_call" | custom-call | tf_op jit(solution)/shard_map/pallas_call | solution.py:70
  44.6 1.1 %pad_maximum_fusion = f32[5,26,16,128]{3,2,1,0:T(8,128)S(1)} fusion(f32[5,5,16,128]{3,2,1,0:T(8,128)} %get-tuple-element.30, f32[5,16,16,128]{3,2,1,0:T(8,128)S(1)} %get-tuple-element.57, f32[5,5,16,128]{3,2,1,0:T(8,128)} %get-tuple-element.29), kind=kLoop, calls=%fused_computation.40 | loop fusion | flops 532480 | bytes 2129920 | tf_op jit(solution)/shard_map/concatenate | solution.py:88
  45.7 1.2 %fusion.26 = f32[5,16,128,16]{2,3,1,0:T(8,128)S(1)} fusion(f32[16,26,1,1]{1,0,3,2:T(8,128)S(1)} %copy-done.7, f32[5,26,16,128]{3,2,1,0:T(8,128)S(1)} %pad_maximum_fusion), kind=kOutput, calls=%fused_computation.26 | convolution fusion | flops 51118080 | bytes 1721984 | tf_op jit(solution)/shard_map/al,flyz->fayz/dot_general | solution.py:171
  47.0 1.2 %fusion.43 = f32[5,16,16,128]{3,2,1,0:T(8,128)S(1)} fusion(f32[16,26,1,1]{1,0,3,2:T(8,128)S(1)} %copy-done.7, f32[5,16,5,128]{3,2,1,0:T(8,128)S(1)} %copy-done.5, f32[5,16,16,128]{3,2,1,0:T(8,128)S(1)} %get-tuple-element.56, f32[5,16,5,128]{3,2,1,0:T(8,128)S(1)} %copy-done.4, f32[5,16,128,16]{2,3,1,0:T(8,128)S(1)} %fusion.26), kind=kOutput, calls=%fused_computation.33 | convolution fusion | flops 51814400 | bytes 2377344 | tf_op jit(solution)/shard_map/al,fxlz->fxaz/dot_general | solution.py:171
  48.2 1.1 %copy.20 = f32[5,5,256]{1,2,0:T(8,128)S(1)} copy(f32[5,5,256]{2,1,0:T(8,128)} %get-tuple-element.33) | data formatting | bytes 51200 | tf_op jit(solution)/shard_map/pallas_call | solution.py:70
  49.3 1.1 %copy.21 = f32[5,5,256]{1,2,0:T(8,128)} copy(f32[5,5,256]{2,1,0:T(8,128)S(1)} %copy-done.9) | data formatting | bytes 51200 | tf_op jit(solution)/shard_map/pallas_call | solution.py:70
  50.4 2.5 %fusion.34 = f32[5,16,16,128]{3,2,1,0:T(8,128)S(1)} fusion(f32[5,16,16,128]{3,2,1,0:T(8,128)S(1)} %copy-done.1, f32[5,16,16,128]{3,2,1,0:T(8,128)S(1)} %fusion.43, f32[128,138,1,1]{0,1,3,2:T(8,128)S(1)} %copy-done.6, f32[5,16,16,5]{3,2,1,0:T(8,128)} %bitcast.463, f32[5,16,16,128]{3,2,1,0:T(8,128)S(1)} %get-tuple-element.55, ...), kind=kOutput, calls=%fused_computation.30 | convolution fusion | flops 272163840 | bytes 2874368 | tf_op jit(solution)/shard_map/al,fxyl->fxya/dot_general | solution.py:171
  52.9 0.8 fusion.92
  53.7 8.9 %shard_map.93 = (f32[5,5,16,128]{3,2,1,0:T(8,128)}, f32[5,5,16,128]{3,2,1,0:T(8,128)}) custom-call(f32[5,5,16,128]{3,2,1,0:T(8,128)} %get-tuple-element.74.refs_0_, f32[5,5,16,128]{3,2,1,0:T(8,128)} %get-tuple-element.73.refs_1_), custom_call_target="tpu_custom_call" | custom-call | tf_op jit(solution)/shard_map/pallas_call | solution.py:70
  62.6 1.1 %pad_maximum_fusion.1 = f32[5,26,16,128]{3,2,1,0:T(8,128)S(1)} fusion(f32[5,5,16,128]{3,2,1,0:T(8,128)} %get-tuple-element.36, f32[5,16,16,128]{3,2,1,0:T(8,128)S(1)} %fusion.34, f32[5,5,16,128]{3,2,1,0:T(8,128)} %get-tuple-element.35), kind=kLoop, calls=%fused_computation.41 | loop fusion | flops 532480 | bytes 2129920 | tf_op jit(solution)/shard_map/concatenate | solution.py:88
  63.7 1.4 %fusion.24 = f32[5,16,128,16]{2,3,1,0:T(8,128)S(1)} fusion(f32[16,26,1,1]{1,0,3,2:T(8,128)S(1)} %copy-done.10, f32[5,26,16,128]{3,2,1,0:T(8,128)S(1)} %pad_maximum_fusion.1), kind=kOutput, calls=%fused_computation.24 | convolution fusion | flops 51118080 | bytes 1721984 | tf_op jit(solution)/shard_map/al,flyz->fayz/dot_general | solution.py:171
  65.1 0.2 copy.47
  65.3 0.9 %fusion.91 = (f32[5,16,5,128]{3,2,1,0:T(8,128)}, f32[5,16,5,128]{3,2,1,0:T(8,128)}) fusion(f32[5,16,16,128]{3,2,1,0:T(8,128)S(1)} %bitcast.460), kind=kLoop, calls=%fused_computation.163 | loop fusion | bytes 819200 | tf_op jit(solution)/shard_map/slice | solution.py:65
  66.2 7.5 %shard_map.94 = (f32[5,16,5,128]{3,2,1,0:T(8,128)}, f32[5,16,5,128]{3,2,1,0:T(8,128)}) custom-call(f32[5,16,5,128]{3,2,1,0:T(8,128)} %get-tuple-element.72.refs_0_, f32[5,16,5,128]{3,2,1,0:T(8,128)} %get-tuple-element.71.refs_1_), custom_call_target="tpu_custom_call" | custom-call | tf_op jit(solution)/shard_map/pallas_call | solution.py:70
  73.7 2.2 %fusion.37 = f32[5,16,16,128]{3,2,1,0:T(8,128)S(1)} fusion(f32[16,26,1,1]{1,0,3,2:T(8,128)S(1)} %copy-done.10, f32[5,16,5,128]{3,2,1,0:T(8,128)} %get-tuple-element.38, f32[5,16,16,128]{3,2,1,0:T(8,128)S(1)} %bitcast.461, f32[5,16,5,128]{3,2,1,0:T(8,128)} %get-tuple-element.37), kind=kOutput, calls=%fused_computation.31 | convolution fusion | flops 51650560 | bytes 1721984 | tf_op jit(solution)/shard_map/al,fxlz->fxaz/dot_general | solution.py:171
  75.9 0.2 fusion.90
  76.1 0.8 copy.34.refs_0_
  77.0 0.8 copy.35.refs_1_
  77.8 5.8 %shard_map.95 = (f32[5,5,256]{2,1,0:T(8,128)}, f32[5,5,256]{2,1,0:T(8,128)}) custom-call(f32[5,5,256]{2,1,0:T(8,128)} %copy.34.refs_0_, f32[5,5,256]{2,1,0:T(8,128)} %copy.35.refs_1_), custom_call_target="tpu_custom_call" | custom-call | tf_op jit(solution)/shard_map/pallas_call | solution.py:70
  83.6 1.0 %copy.36 = f32[5,5,256]{1,2,0:T(8,128)S(1)} copy(f32[5,5,256]{2,1,0:T(8,128)} %get-tuple-element.39) | data formatting | bytes 51200 | tf_op jit(solution)/shard_map/reshape | solution.py:86
  84.7 1.0 %copy.37 = f32[5,5,256]{1,2,0:T(8,128)S(1)} copy(f32[5,5,256]{2,1,0:T(8,128)} %get-tuple-element.40) | data formatting | bytes 51200 | tf_op jit(solution)/shard_map/reshape | solution.py:87
  85.7 2.2 %fusion.18 = f32[5,16,16,128]{3,2,1,0:T(8,128)} fusion(f32[128,138,1,1]{0,1,3,2:T(8,128)S(1)} %copy-done.8, f32[5,16,16,5]{3,2,1,0:T(8,128)S(1)} %bitcast.469, f32[5,16,16,128]{3,2,1,0:T(8,128)S(1)} %fusion.37, f32[5,16,16,5]{3,2,1,0:T(8,128)S(1)} %bitcast.468), kind=kOutput, calls=%fused_computation.18 | convolution fusion | flops 271672320 | bytes 1432576 | tf_op jit(solution)/shard_map/al,fxyl->fxya/dot_general | solution.py:171
  (39 shorter events, 0.8 us)
Async XLA Ops:
  0.0 2.1 %copy-start.1 = (f32[5,16,16,128]{3,2,1,0:T(8,128)S(1)}, f32[5,16,16,128]{3,2,1,0:T(8,128)}, u32[]{:S(2)}) copy-start(f32[5,16,16,128]{3,2,1,0:T(8,128)} %param.9) | copy-start | bytes 1966084
  6.1 14.6 %copy-start.7 = (f32[16,26,1,1]{1,0,3,2:T(8,128)S(1)}, f32[16,26,1,1]{1,0,3,2:T(8,128)}, u32[]{:S(2)}) copy-start(f32[16,26,1,1]{1,0,3,2:T(8,128)} %constant.26) | copy-start | bytes 4996
  20.8 1.2 %copy-start.13 = (f32[4,16,5,128]{3,2,1,0:T(8,128)S(1)}, f32[4,16,5,128]{3,2,1,0:T(8,128)}, u32[]{:S(2)}) copy-start(f32[4,16,5,128]{3,2,1,0:T(8,128)} %get-tuple-element.25) | copy-start | bytes 491524
  20.8 1.2 %copy-start.14 = (f32[4,16,5,128]{3,2,1,0:T(8,128)S(1)}, f32[4,16,5,128]{3,2,1,0:T(8,128)}, u32[]{:S(2)}) copy-start(f32[4,16,5,128]{3,2,1,0:T(8,128)} %get-tuple-element.26) | copy-start | bytes 491524
  21.8 1.1 %copy-start.12 = (f32[4,5,256]{2,1,0:T(8,128)S(1)}, f32[4,5,256]{2,1,0:T(8,128)}, u32[]{:S(2)}) copy-start(f32[4,5,256]{2,1,0:T(8,128)} %get-tuple-element.27) | copy-start | bytes 61444
  22.0 1.2 %copy-start.11 = (f32[4,5,256]{2,1,0:T(8,128)S(1)}, f32[4,5,256]{2,1,0:T(8,128)}, u32[]{:S(2)}) copy-start(f32[4,5,256]{2,1,0:T(8,128)} %get-tuple-element.28) | copy-start | bytes 61444
  23.4 2.2 %copy-start = (f32[3,3,16,16,128]{4,3,2,1,0:T(8,128)S(1)}, f32[3,3,16,16,128]{4,3,2,1,0:T(8,128)}, u32[]{:S(2)}) copy-start(f32[3,3,16,16,128]{4,3,2,1,0:T(8,128)} %param.10) | copy-start | bytes 3538948
  23.4 2.2 %copy-start.2 = (f32[16,16,128]{2,1,0:T(8,128)S(1)}, f32[16,16,128]{2,1,0:T(8,128)}, u32[]{:S(2)}) copy-start(f32[16,16,128]{2,1,0:T(8,128)} %param.11) | copy-start | bytes 393220
  23.4 2.2 %copy-start.3 = (f32[5,16,16,128]{3,2,1,0:T(8,128)S(1)}, f32[5,16,16,128]{3,2,1,0:T(8,128)}, u32[]{:S(2)}) copy-start(f32[5,16,16,128]{3,2,1,0:T(8,128)} %get-tuple-element.85) | copy-start | bytes 1966084
  45.7 1.2 %copy-start.4 = (f32[5,16,5,128]{3,2,1,0:T(8,128)S(1)}, f32[5,16,5,128]{3,2,1,0:T(8,128)}, u32[]{:S(2)}) copy-start(f32[5,16,5,128]{3,2,1,0:T(8,128)} %get-tuple-element.31) | copy-start | bytes 614404
  45.7 1.2 %copy-start.5 = (f32[5,16,5,128]{3,2,1,0:T(8,128)S(1)}, f32[5,16,5,128]{3,2,1,0:T(8,128)}, u32[]{:S(2)}) copy-start(f32[5,16,5,128]{3,2,1,0:T(8,128)} %get-tuple-element.32) | copy-start | bytes 614404
  47.0 2.3 %copy-start.9 = (f32[5,5,256]{2,1,0:T(8,128)S(1)}, f32[5,5,256]{2,1,0:T(8,128)}, u32[]{:S(2)}) copy-start(f32[5,5,256]{2,1,0:T(8,128)} %get-tuple-element.34) | copy-start | bytes 76804
  48.2 2.2 %copy-start.6 = (f32[128,138,1,1]{0,1,3,2:T(8,128)S(1)}, f32[128,138,1,1]{0,1,3,2:T(8,128)}, u32[]{:S(2)}) copy-start(f32[128,138,1,1]{0,1,3,2:T(8,128)} %constant.27) | copy-start | bytes 211972
  53.7 10.1 %copy-start.10 = (f32[16,26,1,1]{1,0,3,2:T(8,128)S(1)}, f32[16,26,1,1]{1,0,3,2:T(8,128)}, u32[]{:S(2)}) copy-start(f32[16,26,1,1]{1,0,3,2:T(8,128)} %constant.28) | copy-start | bytes 4996
  77.0 8.7 %copy-start.8 = (f32[128,138,1,1]{0,1,3,2:T(8,128)S(1)}, f32[128,138,1,1]{0,1,3,2:T(8,128)}, u32[]{:S(2)}) copy-start(f32[128,138,1,1]{0,1,3,2:T(8,128)} %constant.29) | copy-start | bytes 211972

commit v5 on v1

--- a/solution.py
+++ b/solution.py
@@ -19,35 +19,33 @@
 AXES = ("xi", "eta", "zeta")
 
 
-def exchange_kernel(routes, sizes, *refs):
-    count = len(routes)
-    sources, targets = refs[:count], refs[count : 2 * count]
-    send_sems, recv_sems = refs[2 * count :]
+def exchange_kernel(routes, sizes, count, *refs):
+    sources, targets = refs[:count], refs[count:-2]
+    send_sems, recv_sems = refs[-2:]
     here = [lax.axis_index(axis) for axis in AXES]
 
-    def device(axis, step):
-        place = list(here)
-        slot = AXES.index(axis)
-        place[slot] = lax.rem(here[slot] + step + sizes[slot], sizes[slot])
-        return tuple(place)
+    def device(offset):
+        return tuple(
+            lax.rem(here[slot] + offset[slot] + sizes[slot], sizes[slot]) for slot in range(3)
+        )
 
     partners = []
-    for axis, step in routes:
-        for way in (step, -step):
-            if (axis, way) not in partners:
-                partners.append((axis, way))
+    for offset, *_ in routes:
+        for way in (offset, tuple(-step for step in offset)):
+            if way not in partners:
+                partners.append(way)
     barrier = pltpu.get_barrier_semaphore()
-    for axis, step in partners:
-        pl.semaphore_signal(barrier, inc=1, device_id=device(axis, step), device_id_type=MESH)
+    for offset in partners:
+        pl.semaphore_signal(barrier, inc=1, device_id=device(offset), device_id_type=MESH)
     pl.semaphore_wait(barrier, len(partners))
     copies = []
-    for index, (axis, step) in enumerate(routes):
+    for index, (offset, source, source_at, target, target_at) in enumerate(routes):
         copy = pltpu.make_async_remote_copy(
-            src_ref=sources[index],
-            dst_ref=targets[index],
+            src_ref=sources[source].at[source_at],
+            dst_ref=targets[target].at[target_at],
             send_sem=send_sems.at[index],
             recv_sem=recv_sems.at[index],
-            device_id=device(axis, step),
+            device_id=device(offset),
             device_id_type=MESH,
         )
         copy.start()
@@ -56,30 +54,77 @@
         copy.wait()
 
 
-def exchange_faces(items, tag):
+def exchange(arrays, routes, out_shapes, tag):
     sizes = tuple(lax.axis_size(axis) for axis in AXES)
-    sends, routes = [], []
-    for value, axis, dim in items:
-        length = value.shape[dim]
-        sends.append(lax.slice_in_dim(value, length - WIDTH, length, axis=dim))
-        routes.append((axis, 1))
-        sends.append(lax.slice_in_dim(value, 0, WIDTH, axis=dim))
-        routes.append((axis, -1))
-    received = pl.pallas_call(
-        functools.partial(exchange_kernel, tuple(routes), sizes),
-        out_shape=[jax.ShapeDtypeStruct(send.shape, send.dtype) for send in sends],
-        in_specs=[pl.BlockSpec(memory_space=pltpu.VMEM)] * len(sends),
-        out_specs=[pl.BlockSpec(memory_space=pltpu.VMEM)] * len(sends),
+    return pl.pallas_call(
+        functools.partial(exchange_kernel, tuple(routes), sizes, len(arrays)),
+        out_shape=out_shapes,
+        in_specs=[pl.BlockSpec(memory_space=pl.ANY)] * len(arrays),
+        out_specs=[pl.BlockSpec(memory_space=pl.ANY)] * len(out_shapes),
         scratch_shapes=[
-            pltpu.SemaphoreType.DMA((len(sends),)),
-            pltpu.SemaphoreType.DMA((len(sends),)),
+            pltpu.SemaphoreType.DMA((len(routes),)),
+            pltpu.SemaphoreType.DMA((len(routes),)),
         ],
         compiler_params=pltpu.CompilerParams(collective_id=tag, has_side_effects=True),
-    )(*sends)
-    return [
-        jnp.concatenate([received[2 * index], value, received[2 * index + 1]], axis=dim)
-        for index, (value, axis, dim) in enumerate(items)
-    ]
+    )(*arrays)
+
+
+def offset_along(axis, step):
+    return tuple(step if name == axis else 0 for name in AXES)
+
+
+def window(ndim, dim, start, stop):
+    return tuple(slice(start, stop) if axis == dim else slice(None) for axis in range(ndim))
+
+
+def exchange_faces(items, tag):
+    arrays, routes, out_shapes = [], [], []
+    for value, axis, dim in items:
+        ndim, length = value.ndim, value.shape[dim]
+        if dim == ndim - 1:
+            both = jnp.stack(
+                [
+                    lax.slice_in_dim(value, length - WIDTH, length, axis=dim),
+                    lax.slice_in_dim(value, 0, WIDTH, axis=dim),
+                ]
+            )
+            both = jnp.moveaxis(both, dim + 1, 2).reshape(2, value.shape[0], WIDTH, -1)
+            arrays.append(both)
+            out_shapes.append(jax.ShapeDtypeStruct(both.shape, both.dtype))
+            source, target = len(arrays) - 1, len(out_shapes) - 1
+            routes.append((offset_along(axis, 1), source, 0, target, 0))
+            routes.append((offset_along(axis, -1), source, 1, target, 1))
+        elif dim == ndim - 2:
+            face = value.shape[:dim] + (WIDTH,) + value.shape[dim + 1 :]
+            arrays.append(lax.slice_in_dim(value, length - WIDTH, length, axis=dim))
+            arrays.append(lax.slice_in_dim(value, 0, WIDTH, axis=dim))
+            out_shapes += [jax.ShapeDtypeStruct(face, value.dtype)] * 2
+            source, target = len(arrays) - 2, len(out_shapes) - 2
+            whole = window(ndim, dim, None, None)
+            routes.append((offset_along(axis, 1), source, whole, target, whole))
+            routes.append((offset_along(axis, -1), source + 1, whole, target + 1, whole))
+        else:
+            arrays.append(value)
+            face = value.shape[:dim] + (WIDTH,) + value.shape[dim + 1 :]
+            out_shapes += [jax.ShapeDtypeStruct(face, value.dtype)] * 2
+            source, target = len(arrays) - 1, len(out_shapes) - 2
+            whole = window(ndim, dim, None, None)
+            last, first = window(ndim, dim, length - WIDTH, length), window(ndim, dim, 0, WIDTH)
+            routes.append((offset_along(axis, 1), source, last, target, whole))
+            routes.append((offset_along(axis, -1), source, first, target + 1, whole))
+    received = exchange(arrays, routes, out_shapes, tag)
+    padded, place = [], 0
+    for value, axis, dim in items:
+        if dim == value.ndim - 1:
+            both = received[place].reshape((2, value.shape[0], WIDTH) + value.shape[1:dim])
+            both = jnp.moveaxis(both, 2, dim + 1)
+            before, after = both[0], both[1]
+            place += 1
+        else:
+            before, after = received[place], received[place + 1]
+            place += 2
+        padded.append(jnp.concatenate([before, value, after], axis=dim))
+    return padded
 
 
 def with_halo(value, sides, width):

time: 162 us -> 89.8 us (0.55)
  Pallas kernels: 128 us -> 47.4 us
  local copies, waits for them, and re-layouts: 9.06 us -> 17.6 us
    pallas_call x5, Pallas kernels: 128 us -> 47.4 us  [exchange(): pl.pallas_call(functools.partial(exchange_kernel, tuple(routes), sizes, l...]
    another operation x0 -> x8, local copies, waits for them, and re-layouts: none -> 4.5 us  [exchange_faces(): jnp.stack([lax.slice_in_dim(value, length - WIDTH, length, axis=dim), lax...]
    slice x6 -> x2, local copies, waits for them, and re-layouts: 5.88 us -> 1.77 us  [exchange_faces(): arrays.append(lax.slice_in_dim(value, 0, WIDTH, axis=dim))]
    reshape x0 -> x4, local copies, waits for them, and re-layouts: none -> 3.8 us  [the longest x3 2.48 us: exchange_faces(): both = jnp.moveaxis(both, dim + 1, 2).reshape(2, value.shape[0], WIDTH, -1)]
    pallas_call x0 -> x2, local copies, waits for them, and re-layouts: none -> 2.76 us  [exchange(): pl.pallas_call(functools.partial(exchange_kernel, tuple(routes), sizes, l...]
    squeeze x0 -> x3, local copies, waits for them, and re-layouts: none -> 1.69 us  [exchange_faces(): before, after = (both[0], both[1])]
where the time goes in v5:
time: 89.8 us; the launch traced here: 88.4 us
  Pallas kernels  47.4 us (53%)
  local copies, waits for them, and re-layouts  17.6 us (20%)
  matrix products  13.2 us (15%)
  other arithmetic  9.66 us (11%)
    pallas_call x5, Pallas kernels, exchange(): pl.pallas_call(functools.partial(exchange_kernel, tuple(routes), sizes, l...  47.4 us
    dot_general x9, matrix products, sweep_lines(): jnp.einsum(line_forms[dim], matrix, padded, precision=lax.Precision.HIGHEST)  13.2 us
    another operation x8, local copies, waits for them, and re-layouts, exchange_faces(): jnp.stack([lax.slice_in_dim(value, length - WIDTH, length, axis=dim), lax...  4.5 us
    pallas_call x2, local copies, waits for them, and re-layouts, exchange(): pl.pallas_call(functools.partial(exchange_kernel, tuple(routes), sizes, l...  2.76 us
    concatenate x3, other arithmetic, exchange_faces(): padded.append(jnp.concatenate([before, value, after], axis=dim))  2.49 us
    reshape x3, local copies, waits for them, and re-layouts, exchange_faces(): both = jnp.moveaxis(both, dim + 1, 2).reshape(2, value.shape[0], WIDTH, -1)  2.48 us

profile of v5, /device:TPU:1, one launch (start us, length us, event | category | flops | bytes accessed | tf_op | source)
XLA Modules:
  0.0 88.4 jit_solution(7381958451286628504)
XLA Ops:
  0.0 1.0 %slice_bitcast_fusion.34 = f32[16,16,128]{2,1,0:T(8,128)S(1)} fusion(f32[5,16,16,128]{3,2,1,0:T(8,128)} %param.9), kind=kLoop, calls=%fused_computation.163 | loop fusion | bytes 262144 | tf_op jit(solution)/shard_map/div | solution.py:226
  1.0 1.1 %multiply_reduce_fusion = (f32[16,16,128]{2,1,0:T(8,128)S(1)}, f32[3,16,16,128]{3,2,1,0:T(8,128)S(1)}) fusion(f32[5,16,16,128]{3,2,1,0:T(8,128)} %param.9, f32[16,16,128]{2,1,0:T(8,128)S(1)} %slice_bitcast_fusion.34), kind=kLoop, calls=%fused_computation.85 | loop fusion | flops 262144 | bytes 1048576 | tf_op jit(solution)/shard_map/reduce_sum | solution.py:228
  2.1 0.7 fusion.79
  2.8 0.2 fusion.64
  3.0 0.5 copy.57
  3.4 0.5 copy.58
  4.0 0.8 reshape.47.refs_3_
  4.8 0.8 fusion.68
  5.6 0.8 pad_maximum_fusion.refs_0_
  6.5 13.6 %shard_map.91 = (f32[4,5,16,128]{3,2,1,0:T(8,128)}, f32[4,5,16,128]{3,2,1,0:T(8,128)}, f32[4,16,5,128]{3,2,1,0:T(8,128)}, f32[4,16,5,128]{3,2,1,0:T(8,128)}, f32[2,4,5,256]{3,2,1,0:T(8,128)}) custom-call(f32[4,16,16,128]{3,2,1,0:T(8,128)} %pad_maximum_fusion.refs_0_, f32[4,16,5,128]{3,2,1,0:T(8,128)} %get-tuple-element.83.refs_1_, ...), custom_call_target="tpu_custom_call" | custom-call | tf_op jit(solution)/shard_map/pallas_call | solution.py:59
  20.0 1.1 %pad_maximum_fusion.3 = f32[4,26,16,128]{3,2,1,0:T(8,128)S(1)} fusion(f32[4,5,16,128]{3,2,1,0:T(8,128)} %get-tuple-element.20, f32[1,16,16,128]{3,2,1,0:T(8,128)S(1)} %get-tuple-element.78, f32[3,16,16,128]{3,2,1,0:T(8,128)S(1)} %get-tuple-element.46, f32[4,5,16,128]{3,2,1,0:T(8,128)} %get-tuple-element.19), kind=kLoop, calls=%fused_computation.59 | loop fusion | flops 638976 | bytes 1703936 | tf_op jit(solution)/shard_map/concatenate | solution.py:126
  21.1 1.0 %fusion.61 = f32[4,16,128,16]{2,3,1,0:T(8,128)S(1)} fusion(f32[16,26,1,1]{1,0,3,2:T(8,128)S(1)} %copy-done.11, f32[4,26,16,128]{3,2,1,0:T(8,128)S(1)} %pad_maximum_fusion.3), kind=kOutput, calls=%fused_computation.57 | convolution fusion | flops 40894464 | bytes 1377920 | tf_op jit(solution)/shard_map/al,flyz->fayz/dot_general | solution.py:209
  22.1 0.2 copy.99
  22.3 0.9 %convolution_bitcast_fusion = f32[4,16,16,128]{3,2,1,0:T(8,128)S(1)} fusion(f32[16,26,1,1]{1,0,3,2:T(8,128)S(1)} %copy-done.11, f32[4,16,5,128]{3,2,1,0:T(8,128)S(1)} %copy-done.16, f32[1,16,16,128]{3,2,1,0:T(8,128)S(1)} %get-tuple-element.78, f32[3,16,16,128]{3,2,1,0:T(8,128)S(1)} %get-tuple-element.46, f32[4,16,5,128]{3,2,1,0:T(8,128)S(1)} %copy-done.15), kind=kOutput, calls=%fused_computation.34 | convolution fusion | flops 41533440 | bytes 1377920 | tf_op jit(solution)/shard_map/al,fxlz->fxaz/dot_general | solution.py:209
  23.2 0.4 copy.63
  23.8 0.7 copy-done.7
  24.5 1.1 %fusion.53 = f32[4,16,16,128]{3,2,1,0:T(8,128)S(1)} fusion(f32[128,138,1,1]{0,1,3,2:T(8,128)S(1)} %copy-done.7, f32[4,16,16,5]{3,2,1,0:T(8,128)S(1)} %get-tuple-element.66, f32[1,16,16,128]{3,2,1,0:T(8,128)S(1)} %get-tuple-element.78, f32[3,16,16,128]{3,2,1,0:T(8,128)S(1)} %get-tuple-element.46, f32[4,16,16,5]{3,2,1,0:T(8,128)S(1)} %get-tuple-element.65), kind=kOutput, calls=%fused_computation.49 | convolution fusion | flops 217479168 | bytes 1160192 | tf_op jit(solution)/shard_map/al,fxyl->fxya/dot_general | solution.py:209
  25.7 0.2 bitcast_dynamic-update-slice_fusion.11
  26.2 0.2 bitcast_dynamic-update-slice_fusion.8
  26.6 0.1 bitcast_dynamic-update-slice_fusion.4
  27.1 1.2 %multiply_add_fusion = (f32[5,16,16,128]{3,2,1,0:T(8,128)S(1)}, f32[5,16,16,128]{3,2,1,0:T(8,128)S(1)}, f32[5,16,16,128]{3,2,1,0:T(8,128)}) fusion(f32[5,16,16,128]{3,2,1,0:T(8,128)S(1)} %bitcast_dynamic-update-slice_fusion, f32[5,16,16,128]{3,2,1,0:T(8,128)S(1)} %bitcast_dynamic-update-slice_fusion.4, f32[5,16,16,128]{3,2,1,0:T(8,128)S(1)} %get-tuple-element.75, ...), kind=kLoop, calls=%fused_computation.73 | loop fusion | flops 2457600 | bytes 5111808 | tf_op jit(solution)/shard_map/add | solution.py:273
  28.3 0.2 slice_bitcast_fusion.7
  28.5 1.3 %copy.64 = f32[1,5,16,16,5]{3,2,4,1,0:T(8,128)} copy(f32[1,5,16,16,5]{4,3,2,1,0:T(8,128)S(1)} %get-tuple-element.71) | data formatting | bytes 51200 | tf_op jit(solution)/shard_map/stack | solution.py:85
  29.8 0.6 copy.65
  30.3 1.0 %maximum_bitcast_fusion = f32[2,5,5,16,16]{4,3,2,1,0:T(8,128)S(1)} fusion(f32[1,5,16,16,5]{3,2,4,1,0:T(8,128)S(1)} %copy.65, f32[1,5,16,16,5]{3,2,4,1,0:T(8,128)} %copy.64), kind=kLoop, calls=%fused_computation.83 | loop fusion | flops 12800 | bytes 102400 | tf_op jit(solution)/shard_map/transpose | solution.py:91
  31.3 0.8 reshape.48.refs_3_
  32.2 0.9 %fusion.92 = (f32[5,16,5,128]{3,2,1,0:T(8,128)}, f32[5,16,5,128]{3,2,1,0:T(8,128)}) fusion(f32[5,16,16,128]{3,2,1,0:T(8,128)S(1)} %get-tuple-element.48), kind=kLoop, calls=%fused_computation.175 | loop fusion | bytes 819200 | tf_op jit(solution)/shard_map/slice | solution.py:100
  33.1 11.6 %shard_map.92 = (f32[5,5,16,128]{3,2,1,0:T(8,128)}, f32[5,5,16,128]{3,2,1,0:T(8,128)}, f32[5,16,5,128]{3,2,1,0:T(8,128)}, f32[5,16,5,128]{3,2,1,0:T(8,128)}, f32[2,5,5,256]{3,2,1,0:T(8,128)}) custom-call(f32[5,16,16,128]{3,2,1,0:T(8,128)} %get-tuple-element.49.refs_0_, f32[5,16,5,128]{3,2,1,0:T(8,128)} %get-tuple-element.74.refs_1_, ...), custom_call_target="tpu_custom_call" | custom-call | tf_op jit(solution)/shard_map/pallas_call | solution.py:59
  44.7 2.4 %copy.70 = f32[2,5,5,256]{2,3,1,0:T(8,128)} copy(f32[2,5,5,256]{3,2,1,0:T(8,128)} %get-tuple-element.28) | data formatting | bytes 102400 | tf_op jit(solution)/shard_map/pallas_call | solution.py:59
  47.1 1.5 %slice_bitcast_fusion.5 = (f32[5,16,16,5]{3,2,1,0:T(8,128)S(1)}, f32[5,16,16,5]{3,2,1,0:T(8,128)S(1)}) fusion(f32[2,5,16,16,5]{4,3,2,1,0:T(8,128)} %bitcast.471), kind=kLoop, calls=%fused_computation.69 | loop fusion | bytes 102400 | tf_op jit(solution)/shard_map/squeeze | solution.py:121
  48.8 1.2 %fusion.26 = f32[5,16,128,16]{2,3,1,0:T(8,128)S(1)} fusion(f32[16,26,1,1]{1,0,3,2:T(8,128)S(1)} %copy-done.11, f32[5,26,16,128]{3,2,1,0:T(8,128)S(1)} %pad_maximum_fusion.1), kind=kOutput, calls=%fused_computation.26 | convolution fusion | flops 51118080 | bytes 1721984 | tf_op jit(solution)/shard_map/al,flyz->fayz/dot_general | solution.py:209
  50.0 1.2 %fusion.43 = f32[5,16,16,128]{3,2,1,0:T(8,128)S(1)} fusion(f32[16,26,1,1]{1,0,3,2:T(8,128)S(1)} %copy-done.11, f32[5,16,5,128]{3,2,1,0:T(8,128)S(1)} %copy-done.6, f32[5,16,16,128]{3,2,1,0:T(8,128)S(1)} %get-tuple-element.48, f32[5,16,5,128]{3,2,1,0:T(8,128)S(1)} %copy-done.5, f32[5,16,128,16]{2,3,1,0:T(8,128)S(1)} %fusion.26), kind=kOutput, calls=%fused_computation.33 | convolution fusion | flops 51814400 | bytes 2377344 | tf_op jit(solution)/shard_map/al,fxlz->fxaz/dot_general | solution.py:209
  51.3 2.2 %fusion.34.refs_0_ = f32[5,16,16,128]{3,2,1,0:T(8,128)} fusion(f32[5,16,16,128]{3,2,1,0:T(8,128)S(1)} %copy-done.1, f32[5,16,16,128]{3,2,1,0:T(8,128)S(1)} %fusion.43, f32[128,138,1,1]{0,1,3,2:T(8,128)S(1)} %copy-done.8, f32[5,16,16,5]{3,2,1,0:T(8,128)S(1)} %get-tuple-element.53, f32[5,16,16,128]{3,2,1,0:T(8,128)S(1)} %get-tuple-element.47, ...), kind=kOutput, calls=%fused_computation.30 | convolution fusion | flops 272163840 | bytes 2874368 | tf_op jit(solution)/shard_map/al,fxyl->fxya/dot_general | solution.py:209
  53.5 8.9 %shard_map.93 = (f32[5,5,16,128]{3,2,1,0:T(8,128)}, f32[5,5,16,128]{3,2,1,0:T(8,128)}) custom-call(f32[5,16,16,128]{3,2,1,0:T(8,128)} %fusion.34.refs_0_), custom_call_target="tpu_custom_call" | custom-call | tf_op jit(solution)/shard_map/pallas_call | solution.py:59
  62.5 1.3 %pad_maximum_fusion.2 = f32[5,26,16,128]{3,2,1,0:T(8,128)S(1)} fusion(f32[5,5,16,128]{3,2,1,0:T(8,128)} %get-tuple-element.30, f32[5,16,16,128]{3,2,1,0:T(8,128)} %fusion.34.refs_0_, f32[5,5,16,128]{3,2,1,0:T(8,128)} %get-tuple-element.29), kind=kLoop, calls=%fused_computation.41 | loop fusion | flops 532480 | bytes 2129920 | tf_op jit(solution)/shard_map/concatenate | solution.py:126
  63.8 1.2 %fusion.24 = f32[5,16,128,16]{2,3,1,0:T(8,128)S(1)} fusion(f32[16,26,1,1]{1,0,3,2:T(8,128)S(1)} %copy-done.14, f32[5,26,16,128]{3,2,1,0:T(8,128)S(1)} %pad_maximum_fusion.2), kind=kOutput, calls=%fused_computation.24 | convolution fusion | flops 51118080 | bytes 1721984 | tf_op jit(solution)/shard_map/al,flyz->fayz/dot_general | solution.py:209
  65.0 0.2 copy.98
  65.2 0.9 fusion.91
  66.1 7.5 %shard_map.94 = (f32[5,16,5,128]{3,2,1,0:T(8,128)}, f32[5,16,5,128]{3,2,1,0:T(8,128)}) custom-call(f32[5,16,5,128]{3,2,1,0:T(8,128)} %get-tuple-element.70.refs_0_, f32[5,16,5,128]{3,2,1,0:T(8,128)} %get-tuple-element.69.refs_1_), custom_call_target="tpu_custom_call" | custom-call | tf_op jit(solution)/shard_map/pallas_call | solution.py:59
  73.6 2.2 %fusion.37 = f32[5,16,16,128]{3,2,1,0:T(8,128)S(1)} fusion(f32[16,26,1,1]{1,0,3,2:T(8,128)S(1)} %copy-done.14, f32[5,16,5,128]{3,2,1,0:T(8,128)} %get-tuple-element.32, f32[5,16,16,128]{3,2,1,0:T(8,128)S(1)} %bitcast.470, f32[5,16,5,128]{3,2,1,0:T(8,128)} %get-tuple-element.31), kind=kOutput, calls=%fused_computation.31 | convolution fusion | flops 51650560 | bytes 1721984 | tf_op jit(solution)/shard_map/al,fxlz->fxaz/dot_general | solution.py:209
  75.8 0.2 slice_bitcast_fusion.3
  76.0 0.6 copy.73
  76.6 0.6 copy.74
  77.3 0.8 reshape.49.refs_0_
  78.1 5.8 %shard_map.95 = f32[2,5,5,256]{3,2,1,0:T(8,128)} custom-call(f32[2,5,5,256]{3,2,1,0:T(8,128)} %reshape.49.refs_0_), custom_call_target="tpu_custom_call" | custom-call | tf_op jit(solution)/shard_map/pallas_call | solution.py:59
  83.9 1.3 %copy.88 = f32[2,5,5,256]{2,3,1,0:T(8,128)S(1)} copy(f32[2,5,5,256]{3,2,1,0:T(8,128)} %shard_map.95) | data formatting | bytes 102400 | tf_op jit(solution)/shard_map/reshape | solution.py:119
  85.4 0.7 copy-done.12
  86.1 2.2 %fusion.18 = f32[5,16,16,128]{3,2,1,0:T(8,128)} fusion(f32[128,138,1,1]{0,1,3,2:T(8,128)S(1)} %copy-done.12, f32[5,16,16,5]{3,2,1,0:T(8,128)S(1)} %get-tuple-element.51, f32[5,16,16,128]{3,2,1,0:T(8,128)S(1)} %fusion.37, f32[5,16,16,5]{3,2,1,0:T(8,128)S(1)} %get-tuple-element.50), kind=kOutput, calls=%fused_computation.18 | convolution fusion | flops 271672320 | bytes 1432576 | tf_op jit(solution)/shard_map/al,fxyl->fxya/dot_general | solution.py:209
  (47 shorter events, 1.4 us)
Async XLA Ops:
  0.0 2.1 %copy-start.1 = (f32[5,16,16,128]{3,2,1,0:T(8,128)S(1)}, f32[5,16,16,128]{3,2,1,0:T(8,128)}, u32[]{:S(2)}) copy-start(f32[5,16,16,128]{3,2,1,0:T(8,128)} %param.9) | copy-start | bytes 1966084
  6.5 14.6 %copy-start.11 = (f32[16,26,1,1]{1,0,3,2:T(8,128)S(1)}, f32[16,26,1,1]{1,0,3,2:T(8,128)}, u32[]{:S(2)}) copy-start(f32[16,26,1,1]{1,0,3,2:T(8,128)} %constant.26) | copy-start | bytes 4996
  21.1 1.2 %copy-start.15 = (f32[4,16,5,128]{3,2,1,0:T(8,128)S(1)}, f32[4,16,5,128]{3,2,1,0:T(8,128)}, u32[]{:S(2)}) copy-start(f32[4,16,5,128]{3,2,1,0:T(8,128)} %get-tuple-element.21) | copy-start | bytes 491524
  21.1 1.2 %copy-start.16 = (f32[4,16,5,128]{3,2,1,0:T(8,128)S(1)}, f32[4,16,5,128]{3,2,1,0:T(8,128)}, u32[]{:S(2)}) copy-start(f32[4,16,5,128]{3,2,1,0:T(8,128)} %get-tuple-element.22) | copy-start | bytes 491524
  22.1 1.1 %copy-start.13 = (f32[2,4,5,256]{3,2,1,0:T(8,128)S(1)}, f32[2,4,5,256]{3,2,1,0:T(8,128)}, u32[]{:S(2)}) copy-start(f32[2,4,5,256]{3,2,1,0:T(8,128)} %get-tuple-element.23) | copy-start | bytes 122884
  23.6 0.9 %copy-start.7 = (f32[128,138,1,1]{0,1,3,2:T(8,128)S(1)}, f32[128,138,1,1]{0,1,3,2:T(8,128)}, u32[]{:S(2)}) copy-start(f32[128,138,1,1]{0,1,3,2:T(8,128)} %constant.27) | copy-start | bytes 211972
  23.7 1.9 %copy-start = (f32[3,3,16,16,128]{4,3,2,1,0:T(8,128)S(1)}, f32[3,3,16,16,128]{4,3,2,1,0:T(8,128)}, u32[]{:S(2)}) copy-start(f32[3,3,16,16,128]{4,3,2,1,0:T(8,128)} %param.10) | copy-start | bytes 3538948
  23.7 1.9 %copy-start.2 = (f32[16,16,128]{2,1,0:T(8,128)S(1)}, f32[16,16,128]{2,1,0:T(8,128)}, u32[]{:S(2)}) copy-start(f32[16,16,128]{2,1,0:T(8,128)} %param.11) | copy-start | bytes 393220
  23.7 1.9 %copy-start.4 = (f32[5,16,16,128]{3,2,1,0:T(8,128)S(1)}, f32[5,16,16,128]{3,2,1,0:T(8,128)}, u32[]{:S(2)}) copy-start(f32[5,16,16,128]{3,2,1,0:T(8,128)} %get-tuple-element.79) | copy-start | bytes 1966084
  47.1 1.5 %copy-start.3 = (f32[5,16,16,128]{3,2,1,0:T(8,128)S(1)}, f32[5,16,16,128]{3,2,1,0:T(8,128)}, u32[]{:S(2)}) copy-start(f32[5,16,16,128]{3,2,1,0:T(8,128)} %get-tuple-element.49.refs_0_) | copy-start | bytes 1966084
  47.1 1.5 %copy-start.9 = (f32[5,5,16,128]{3,2,1,0:T(8,128)S(1)}, f32[5,5,16,128]{3,2,1,0:T(8,128)}, u32[]{:S(2)}) copy-start(f32[5,5,16,128]{3,2,1,0:T(8,128)} %get-tuple-element.24) | copy-start | bytes 614404
  47.1 1.6 %copy-start.10 = (f32[5,5,16,128]{3,2,1,0:T(8,128)S(1)}, f32[5,5,16,128]{3,2,1,0:T(8,128)}, u32[]{:S(2)}) copy-start(f32[5,5,16,128]{3,2,1,0:T(8,128)} %get-tuple-element.25) | copy-start | bytes 614404
  48.8 1.2 %copy-start.5 = (f32[5,16,5,128]{3,2,1,0:T(8,128)S(1)}, f32[5,16,5,128]{3,2,1,0:T(8,128)}, u32[]{:S(2)}) copy-start(f32[5,16,5,128]{3,2,1,0:T(8,128)} %get-tuple-element.26) | copy-start | bytes 614404
  48.8 1.2 %copy-start.6 = (f32[5,16,5,128]{3,2,1,0:T(8,128)S(1)}, f32[5,16,5,128]{3,2,1,0:T(8,128)}, u32[]{:S(2)}) copy-start(f32[5,16,5,128]{3,2,1,0:T(8,128)} %get-tuple-element.27) | copy-start | bytes 614404
  50.0 1.3 %copy-start.8 = (f32[128,138,1,1]{0,1,3,2:T(8,128)S(1)}, f32[128,138,1,1]{0,1,3,2:T(8,128)}, u32[]{:S(2)}) copy-start(f32[128,138,1,1]{0,1,3,2:T(8,128)} %constant.27) | copy-start | bytes 211972
  53.5 10.3 %copy-start.14 = (f32[16,26,1,1]{1,0,3,2:T(8,128)S(1)}, f32[16,26,1,1]{1,0,3,2:T(8,128)}, u32[]{:S(2)}) copy-start(f32[16,26,1,1]{1,0,3,2:T(8,128)} %constant.28) | copy-start | bytes 4996
  85.2 0.9 %copy-start.12 = (f32[128,138,1,1]{0,1,3,2:T(8,128)S(1)}, f32[128,138,1,1]{0,1,3,2:T(8,128)}, u32[]{:S(2)}) copy-start(f32[128,138,1,1]{0,1,3,2:T(8,128)} %constant.29) | copy-start | bytes 211972

commit v6 on v5

--- a/solution.py
+++ b/solution.py
@@ -127,6 +127,41 @@
     return padded
 
 
+def exchange_plane(value, tag):
+    length_x, length_y = value.shape[1], value.shape[2]
+    faces_y = jnp.stack(
+        [
+            lax.slice_in_dim(value, length_y - WIDTH, length_y, axis=2),
+            lax.slice_in_dim(value, 0, WIDTH, axis=2),
+        ]
+    )
+    last_x, first_x = slice(length_x - WIDTH, length_x), slice(0, WIDTH)
+    every = slice(None)
+    routes = [
+        ((1, 0, 0), 0, (every, last_x), 0, 0),
+        ((-1, 0, 0), 0, (every, first_x), 0, 1),
+        ((0, 1, 0), 1, 0, 1, 0),
+        ((0, -1, 0), 1, 1, 1, 1),
+        ((1, 1, 0), 1, (0, every, last_x), 2, (0, 0)),
+        ((-1, 1, 0), 1, (0, every, first_x), 2, (0, 1)),
+        ((1, -1, 0), 1, (1, every, last_x), 2, (1, 0)),
+        ((-1, -1, 0), 1, (1, every, first_x), 2, (1, 1)),
+    ]
+    fields, depth = value.shape[0], value.shape[3]
+    out_shapes = [
+        jax.ShapeDtypeStruct((2, fields, WIDTH, length_y, depth), value.dtype),
+        jax.ShapeDtypeStruct((2, fields, length_x, WIDTH, depth), value.dtype),
+        jax.ShapeDtypeStruct((2, 2, fields, WIDTH, WIDTH, depth), value.dtype),
+    ]
+    along_x, along_y, edges = exchange([value, faces_y], routes, out_shapes, tag)
+    sections = [
+        jnp.concatenate([edges[0, 0], along_x[0], edges[1, 0]], axis=2),
+        jnp.concatenate([along_y[0], value, along_y[1]], axis=2),
+        jnp.concatenate([edges[0, 1], along_x[1], edges[1, 1]], axis=2),
+    ]
+    return jnp.concatenate(sections, axis=1)
+
+
 def with_halo(value, sides, width):
     for axis, dim in sides:
         count, length = (lax.axis_size(axis), value.shape[dim])
@@ -302,8 +337,8 @@
     divergence = divergence + sweep_lines(padded[1], derive[1], 2)
     divergence = divergence + sweep_lines(padded[2], derive[2], 3)
     sectioned = conserved_solution - step_duration * jacobian * divergence
-    result = sweep_lines(exchange_faces([(sectioned, "xi", 1)], 2)[0], smooth[0], 1)
-    result = sweep_lines(exchange_faces([(result, "eta", 2)], 3)[0], smooth[1], 2)
+    result = sweep_lines(exchange_plane(sectioned, 2), smooth[0], 1)
+    result = sweep_lines(result, smooth[1], 2)
     result = sweep_lines(exchange_faces([(result, "zeta", 3)], 4)[0], smooth[2], 3)
     return result
 

time: 89.8 us -> 86.4 us (0.962)
  Pallas kernels: 47.4 us -> 43.9 us
  local copies, waits for them, and re-layouts: 17.6 us -> 19.9 us
  other arithmetic: 9.66 us -> 8.65 us
    pallas_call x5 -> x4, Pallas kernels: 47.4 us -> 43.9 us  [exchange(): pl.pallas_call(functools.partial(exchange_kernel, tuple(routes), sizes, l...]
    concatenate x3 -> x2, other arithmetic: 2.49 us -> 1.15 us  [exchange_faces(): padded.append(jnp.concatenate([before, value, after], axis=dim))]
    squeeze x0 -> x3, local copies, waits for them, and re-layouts: none -> 1.28 us  [the longest x1 1.22 us: exchange_plane(): along_y[0]]
    another operation x8, local copies, waits for them, and re-layouts: 4.5 us -> 5.76 us  [exchange_faces(): jnp.stack([lax.slice_in_dim(value, length - WIDTH, length, axis=dim), lax...]
    transpose x3, other arithmetic: 1.07 us -> 0.13 us  [exchange_faces(): both = jnp.moveaxis(both, dim + 1, 2).reshape(2, value.shape[0], WIDTH, -1)]
    another operation x0 -> x1, other arithmetic: none -> 0.9 us  [exchange_plane(): jnp.stack([lax.slice_in_dim(value, length_y - WIDTH, length_y, axis=2), l...]
    unnamed x34 -> x42, local copies, waits for them, and re-layouts: 1.65 us -> 2.22 us
where the time goes in v6:
time: 86.4 us; the launch traced here: 85.6 us
  Pallas kernels  43.9 us (51%)
  local copies, waits for them, and re-layouts  19.9 us (23%)
  matrix products  12.6 us (15%)
  other arithmetic  8.65 us (10%)
    pallas_call x4, Pallas kernels, exchange(): pl.pallas_call(functools.partial(exchange_kernel, tuple(routes), sizes, l...  43.9 us
    dot_general x9, matrix products, sweep_lines(): jnp.einsum(line_forms[dim], matrix, padded, precision=lax.Precision.HIGHEST)  12.6 us
    another operation x8, local copies, waits for them, and re-layouts, exchange_faces(): jnp.stack([lax.slice_in_dim(value, length - WIDTH, length, axis=dim), lax...  5.76 us
    pallas_call x2, local copies, waits for them, and re-layouts, exchange(): pl.pallas_call(functools.partial(exchange_kernel, tuple(routes), sizes, l...  2.79 us
    reshape x3, local copies, waits for them, and re-layouts, exchange_faces(): both = jnp.moveaxis(both, dim + 1, 2).reshape(2, value.shape[0], WIDTH, -1)  2.48 us
    unnamed x42, local copies, waits for them, and re-layouts  2.22 us

profile of v6, /device:TPU:1, one launch (start us, length us, event | category | flops | bytes accessed | tf_op | source)
XLA Modules:
  0.0 85.6 jit_solution(15935213428789925424)
XLA Ops:
  0.0 1.0 %slice_bitcast_fusion.40 = f32[16,16,128]{2,1,0:T(8,128)S(1)} fusion(f32[5,16,16,128]{3,2,1,0:T(8,128)} %param.9), kind=kLoop, calls=%fused_computation.166 | loop fusion | bytes 262144 | tf_op jit(solution)/shard_map/div | solution.py:261
  1.0 1.1 %multiply_reduce_fusion = (f32[16,16,128]{2,1,0:T(8,128)S(1)}, f32[3,16,16,128]{3,2,1,0:T(8,128)S(1)}) fusion(f32[5,16,16,128]{3,2,1,0:T(8,128)} %param.9, f32[16,16,128]{2,1,0:T(8,128)S(1)} %slice_bitcast_fusion.40), kind=kLoop, calls=%fused_computation.82 | loop fusion | flops 262144 | bytes 1048576 | tf_op jit(solution)/shard_map/reduce_sum | solution.py:263
  2.1 0.7 fusion.78
  2.8 0.2 fusion.63
  3.0 0.5 copy.53
  3.4 0.5 copy.54
  4.0 0.8 reshape.47.refs_3_
  4.8 0.9 fusion.67
  5.6 0.8 pad_maximum_fusion.refs_0_
  6.5 13.6 %shard_map.91 = (f32[4,5,16,128]{3,2,1,0:T(8,128)}, f32[4,5,16,128]{3,2,1,0:T(8,128)}, f32[4,16,5,128]{3,2,1,0:T(8,128)}, f32[4,16,5,128]{3,2,1,0:T(8,128)}, f32[2,4,5,256]{3,2,1,0:T(8,128)}) custom-call(f32[4,16,16,128]{3,2,1,0:T(8,128)} %pad_maximum_fusion.refs_0_, f32[4,16,5,128]{3,2,1,0:T(8,128)} %get-tuple-element.83.refs_1_, ...), custom_call_target="tpu_custom_call" | custom-call | tf_op jit(solution)/shard_map/pallas_call | solution.py:59
  20.0 1.1 %pad_maximum_fusion.2 = f32[4,26,16,128]{3,2,1,0:T(8,128)S(1)} fusion(f32[4,5,16,128]{3,2,1,0:T(8,128)} %get-tuple-element.19, f32[1,16,16,128]{3,2,1,0:T(8,128)S(1)} %get-tuple-element.78, f32[3,16,16,128]{3,2,1,0:T(8,128)S(1)} %get-tuple-element.44, f32[4,5,16,128]{3,2,1,0:T(8,128)} %get-tuple-element.18), kind=kLoop, calls=%fused_computation.56 | loop fusion | flops 638976 | bytes 1703936 | tf_op jit(solution)/shard_map/concatenate | solution.py:126
  21.1 1.0 %fusion.60 = f32[4,16,128,16]{2,3,1,0:T(8,128)S(1)} fusion(f32[16,26,1,1]{1,0,3,2:T(8,128)S(1)} %copy-done.15, f32[4,26,16,128]{3,2,1,0:T(8,128)S(1)} %pad_maximum_fusion.2), kind=kOutput, calls=%fused_computation.54 | convolution fusion | flops 40894464 | bytes 1377920 | tf_op jit(solution)/shard_map/al,flyz->fayz/dot_general | solution.py:244
  22.1 0.2 copy.99
  22.3 0.9 %convolution_bitcast_fusion = f32[4,16,16,128]{3,2,1,0:T(8,128)S(1)} fusion(f32[16,26,1,1]{1,0,3,2:T(8,128)S(1)} %copy-done.15, f32[4,16,5,128]{3,2,1,0:T(8,128)S(1)} %copy-done.20, f32[1,16,16,128]{3,2,1,0:T(8,128)S(1)} %get-tuple-element.78, f32[3,16,16,128]{3,2,1,0:T(8,128)S(1)} %get-tuple-element.44, f32[4,16,5,128]{3,2,1,0:T(8,128)S(1)} %copy-done.19), kind=kOutput, calls=%fused_computation.32 | convolution fusion | flops 41533440 | bytes 1377920 | tf_op jit(solution)/shard_map/al,fxlz->fxaz/dot_general | solution.py:244
  23.2 0.4 copy.59
  23.7 0.7 copy-done.11
  24.5 1.1 %fusion.52 = f32[4,16,16,128]{3,2,1,0:T(8,128)S(1)} fusion(f32[128,138,1,1]{0,1,3,2:T(8,128)S(1)} %copy-done.11, f32[4,16,16,5]{3,2,1,0:T(8,128)S(1)} %get-tuple-element.64, f32[1,16,16,128]{3,2,1,0:T(8,128)S(1)} %get-tuple-element.78, f32[3,16,16,128]{3,2,1,0:T(8,128)S(1)} %get-tuple-element.44, f32[4,16,16,5]{3,2,1,0:T(8,128)S(1)} %get-tuple-element.63), kind=kOutput, calls=%fused_computation.46 | convolution fusion | flops 217479168 | bytes 1160192 | tf_op jit(solution)/shard_map/al,fxyl->fxya/dot_general | solution.py:244
  25.7 0.2 bitcast_dynamic-update-slice_fusion.11
  26.1 0.2 bitcast_dynamic-update-slice_fusion.8
  27.0 1.2 %multiply_add_fusion = (f32[5,16,16,128]{3,2,1,0:T(8,128)S(1)}, f32[5,16,16,128]{3,2,1,0:T(8,128)S(1)}, f32[5,16,16,128]{3,2,1,0:T(8,128)}) fusion(f32[5,16,16,128]{3,2,1,0:T(8,128)S(1)} %bitcast_dynamic-update-slice_fusion, f32[5,16,16,128]{3,2,1,0:T(8,128)S(1)} %bitcast_dynamic-update-slice_fusion.4, f32[5,16,16,128]{3,2,1,0:T(8,128)S(1)} %get-tuple-element.75, ...), kind=kLoop, calls=%fused_computation.70 | loop fusion | flops 2457600 | bytes 5111808 | tf_op jit(solution)/shard_map/add | solution.py:308
  28.2 1.1 %slice_bitcast_fusion.7 = (f32[1,5,16,16,5]{4,3,2,1,0:T(8,128)}, f32[1,5,16,16,5]{4,3,2,1,0:T(8,128)S(1)}) fusion(f32[5,16,16,128]{3,2,1,0:T(8,128)S(1)} %get-tuple-element.45), kind=kLoop, calls=%fused_computation.68 | loop fusion | bytes 102400 | tf_op jit(solution)/shard_map/stack | solution.py:85
  29.3 1.7 %copy.60 = f32[1,5,16,16,5]{3,2,4,1,0:T(8,128)S(1)} copy(f32[1,5,16,16,5]{4,3,2,1,0:T(8,128)} %get-tuple-element.71) | data formatting | bytes 51200 | tf_op jit(solution)/shard_map/stack | solution.py:85
  31.0 0.6 copy.61
  31.7 0.8 reshape.48.refs_3_
  32.5 0.9 %fusion.89 = (f32[5,16,5,128]{3,2,1,0:T(8,128)}, f32[5,16,5,128]{3,2,1,0:T(8,128)}) fusion(f32[5,16,16,128]{3,2,1,0:T(8,128)S(1)} %get-tuple-element.46), kind=kLoop, calls=%fused_computation.180 | loop fusion | bytes 819200 | tf_op jit(solution)/shard_map/slice | solution.py:100
  33.4 11.6 %shard_map.92 = (f32[5,5,16,128]{3,2,1,0:T(8,128)}, f32[5,5,16,128]{3,2,1,0:T(8,128)}, f32[5,16,5,128]{3,2,1,0:T(8,128)}, f32[5,16,5,128]{3,2,1,0:T(8,128)}, f32[2,5,5,256]{3,2,1,0:T(8,128)}) custom-call(f32[5,16,16,128]{3,2,1,0:T(8,128)} %get-tuple-element.47.refs_0_, f32[5,16,5,128]{3,2,1,0:T(8,128)} %get-tuple-element.74.refs_1_, ...), custom_call_target="tpu_custom_call" | custom-call | tf_op jit(solution)/shard_map/pallas_call | solution.py:59
  45.0 2.4 %copy.66 = f32[2,5,5,256]{2,3,1,0:T(8,128)} copy(f32[2,5,5,256]{3,2,1,0:T(8,128)} %get-tuple-element.27) | data formatting | bytes 102400 | tf_op jit(solution)/shard_map/pallas_call | solution.py:59
  47.4 1.5 %slice_bitcast_fusion.5 = (f32[5,16,16,5]{3,2,1,0:T(8,128)S(1)}, f32[5,16,16,5]{3,2,1,0:T(8,128)S(1)}) fusion(f32[2,5,16,16,5]{4,3,2,1,0:T(8,128)} %bitcast.488), kind=kLoop, calls=%fused_computation.66 | loop fusion | bytes 102400 | tf_op jit(solution)/shard_map/squeeze | solution.py:121
  49.1 1.2 %fusion.25 = f32[5,16,128,16]{2,3,1,0:T(8,128)S(1)} fusion(f32[16,26,1,1]{1,0,3,2:T(8,128)S(1)} %copy-done.15, f32[5,26,16,128]{3,2,1,0:T(8,128)S(1)} %pad_maximum_fusion.1), kind=kOutput, calls=%fused_computation.24 | convolution fusion | flops 51118080 | bytes 1721984 | tf_op jit(solution)/shard_map/al,flyz->fayz/dot_general | solution.py:244
  50.4 1.2 %fusion.42 = f32[5,16,16,128]{3,2,1,0:T(8,128)S(1)} fusion(f32[16,26,1,1]{1,0,3,2:T(8,128)S(1)} %copy-done.15, f32[5,16,5,128]{3,2,1,0:T(8,128)S(1)} %copy-done.10, f32[5,16,16,128]{3,2,1,0:T(8,128)S(1)} %get-tuple-element.46, f32[5,16,5,128]{3,2,1,0:T(8,128)S(1)} %copy-done.9, f32[5,16,128,16]{2,3,1,0:T(8,128)S(1)} %fusion.25), kind=kOutput, calls=%fused_computation.31 | convolution fusion | flops 51814400 | bytes 2377344 | tf_op jit(solution)/shard_map/al,fxlz->fxaz/dot_general | solution.py:244
  51.7 1.4 %fusion.36.refs_0_ = f32[5,16,16,128]{3,2,1,0:T(8,128)S(1)} fusion(f32[5,16,16,128]{3,2,1,0:T(8,128)S(1)} %copy-done.1, f32[5,16,16,128]{3,2,1,0:T(8,128)S(1)} %fusion.42, f32[128,138,1,1]{0,1,3,2:T(8,128)S(1)} %copy-done.12, f32[5,16,16,5]{3,2,1,0:T(8,128)S(1)} %get-tuple-element.51, f32[5,16,16,128]{3,2,1,0:T(8,128)S(1)} %get-tuple-element.45, ...), kind=kOutput, calls=%fused_computation.29 | convolution fusion | flops 272163840 | bytes 2874368 | tf_op jit(solution)/shard_map/al,fxyl->fxya/dot_general | solution.py:244
  53.1 0.2 slice_bitcast_fusion.11
  53.3 0.9 %pad_maximum_fusion.3.refs_1_ = f32[2,5,16,5,128]{4,3,2,1,0:T(8,128)} fusion(f32[1,5,16,5,128]{4,3,2,1,0:T(8,128)S(1)} %get-tuple-element.70, f32[1,5,16,5,128]{4,3,2,1,0:T(8,128)S(1)} %get-tuple-element.69), kind=kLoop, calls=%fused_computation.69 | loop fusion | flops 102400 | bytes 819200 | tf_op jit(solution)/shard_map/stack | solution.py:132
  54.2 13.4 %shard_map.93 = (f32[2,5,5,16,128]{4,3,2,1,0:T(8,128)}, f32[2,5,16,5,128]{4,3,2,1,0:T(8,128)}, f32[2,2,5,5,5,128]{5,4,3,2,1,0:T(8,128)}) custom-call(f32[5,16,16,128]{3,2,1,0:T(8,128)} %copy-done.2, f32[2,5,16,5,128]{4,3,2,1,0:T(8,128)} %pad_maximum_fusion.3.refs_1_), custom_call_target="tpu_custom_call" | custom-call | tf_op jit(solution)/shard_map/pallas_call | solution.py:59
  67.6 1.2 %slice_bitcast_fusion.13 = (f32[5,16,5,128]{3,2,1,0:T(8,128)S(1)}, f32[5,16,5,128]{3,2,1,0:T(8,128)S(1)}) fusion(f32[2,5,16,5,128]{4,3,2,1,0:T(8,128)} %get-tuple-element.30), kind=kLoop, calls=%fused_computation.88 | loop fusion | bytes 819200 | tf_op jit(solution)/shard_map/squeeze | solution.py:159
  69.0 0.2 copy-done.3
  69.1 0.4 maximum_maximum_fusion
  69.5 0.3 copy-done.18
  69.8 2.4 %fusion.2 = f32[5,16,26,128]{3,1,2,0:T(8,128)S(1)} fusion(f32[16,26,1,1]{1,0,3,2:T(8,128)S(1)} %copy-done.18, f32[5,26,26,128]{3,2,1,0:T(8,128)S(1)} %maximum_maximum_fusion), kind=kOutput, calls=%fused_computation.3 | convolution fusion | flops 83066880 | bytes 2797184 | tf_op jit(solution)/shard_map/al,flyz->fayz/dot_general | solution.py:244
  72.3 1.2 %fusion.27 = f32[5,16,16,128]{3,2,1,0:T(8,128)S(1)} fusion(f32[16,26,1,1]{1,0,3,2:T(8,128)S(1)} %copy-done.18, f32[5,16,26,128]{3,1,2,0:T(8,128)S(1)} %fusion.2), kind=kOutput, calls=%fused_computation.26 | convolution fusion | flops 51118080 | bytes 1721984 | tf_op jit(solution)/shard_map/al,fxlz->fxaz/dot_general | solution.py:244
  73.5 0.2 slice_bitcast_fusion.3
  73.7 0.6 copy.69
  74.3 0.6 copy.70
  75.0 0.8 reshape.49.refs_0_
  75.8 5.3 %shard_map.94 = f32[2,5,5,256]{3,2,1,0:T(8,128)} custom-call(f32[2,5,5,256]{3,2,1,0:T(8,128)} %reshape.49.refs_0_), custom_call_target="tpu_custom_call" | custom-call | tf_op jit(solution)/shard_map/pallas_call | solution.py:59
  81.1 1.3 %copy.84 = f32[2,5,5,256]{2,3,1,0:T(8,128)S(1)} copy(f32[2,5,5,256]{3,2,1,0:T(8,128)} %shard_map.94) | data formatting | bytes 102400 | tf_op jit(solution)/shard_map/reshape | solution.py:119
  82.6 0.8 copy-done.16
  83.3 2.2 %fusion.17 = f32[5,16,16,128]{3,2,1,0:T(8,128)} fusion(f32[128,138,1,1]{0,1,3,2:T(8,128)S(1)} %copy-done.16, f32[5,16,16,5]{3,2,1,0:T(8,128)S(1)} %get-tuple-element.49, f32[5,16,16,128]{3,2,1,0:T(8,128)S(1)} %fusion.27, f32[5,16,16,5]{3,2,1,0:T(8,128)S(1)} %get-tuple-element.48), kind=kOutput, calls=%fused_computation.16 | convolution fusion | flops 271672320 | bytes 1432576 | tf_op jit(solution)/shard_map/al,fxyl->fxya/dot_general | solution.py:244
  (57 shorter events, 1.7 us)
Async XLA Ops:
  0.0 2.1 %copy-start.1 = (f32[5,16,16,128]{3,2,1,0:T(8,128)S(1)}, f32[5,16,16,128]{3,2,1,0:T(8,128)}, u32[]{:S(2)}) copy-start(f32[5,16,16,128]{3,2,1,0:T(8,128)} %param.9) | copy-start | bytes 1966084
  6.5 14.6 %copy-start.15 = (f32[16,26,1,1]{1,0,3,2:T(8,128)S(1)}, f32[16,26,1,1]{1,0,3,2:T(8,128)}, u32[]{:S(2)}) copy-start(f32[16,26,1,1]{1,0,3,2:T(8,128)} %constant.26) | copy-start | bytes 4996
  21.1 1.2 %copy-start.19 = (f32[4,16,5,128]{3,2,1,0:T(8,128)S(1)}, f32[4,16,5,128]{3,2,1,0:T(8,128)}, u32[]{:S(2)}) copy-start(f32[4,16,5,128]{3,2,1,0:T(8,128)} %get-tuple-element.20) | copy-start | bytes 491524
  21.1 1.2 %copy-start.20 = (f32[4,16,5,128]{3,2,1,0:T(8,128)S(1)}, f32[4,16,5,128]{3,2,1,0:T(8,128)}, u32[]{:S(2)}) copy-start(f32[4,16,5,128]{3,2,1,0:T(8,128)} %get-tuple-element.21) | copy-start | bytes 491524
  22.1 1.1 %copy-start.17 = (f32[2,4,5,256]{3,2,1,0:T(8,128)S(1)}, f32[2,4,5,256]{3,2,1,0:T(8,128)}, u32[]{:S(2)}) copy-start(f32[2,4,5,256]{3,2,1,0:T(8,128)} %get-tuple-element.22) | copy-start | bytes 122884
  23.6 0.9 %copy-start.11 = (f32[128,138,1,1]{0,1,3,2:T(8,128)S(1)}, f32[128,138,1,1]{0,1,3,2:T(8,128)}, u32[]{:S(2)}) copy-start(f32[128,138,1,1]{0,1,3,2:T(8,128)} %constant.27) | copy-start | bytes 211972
  23.7 1.9 %copy-start = (f32[3,3,16,16,128]{4,3,2,1,0:T(8,128)S(1)}, f32[3,3,16,16,128]{4,3,2,1,0:T(8,128)}, u32[]{:S(2)}) copy-start(f32[3,3,16,16,128]{4,3,2,1,0:T(8,128)} %param.10) | copy-start | bytes 3538948
  23.7 1.9 %copy-start.4 = (f32[16,16,128]{2,1,0:T(8,128)S(1)}, f32[16,16,128]{2,1,0:T(8,128)}, u32[]{:S(2)}) copy-start(f32[16,16,128]{2,1,0:T(8,128)} %param.11) | copy-start | bytes 393220
  23.7 1.9 %copy-start.6 = (f32[5,16,16,128]{3,2,1,0:T(8,128)S(1)}, f32[5,16,16,128]{3,2,1,0:T(8,128)}, u32[]{:S(2)}) copy-start(f32[5,16,16,128]{3,2,1,0:T(8,128)} %get-tuple-element.79) | copy-start | bytes 1966084
  47.4 1.5 %copy-start.5 = (f32[5,16,16,128]{3,2,1,0:T(8,128)S(1)}, f32[5,16,16,128]{3,2,1,0:T(8,128)}, u32[]{:S(2)}) copy-start(f32[5,16,16,128]{3,2,1,0:T(8,128)} %get-tuple-element.47.refs_0_) | copy-start | bytes 1966084
  47.4 1.5 %copy-start.13 = (f32[5,5,16,128]{3,2,1,0:T(8,128)S(1)}, f32[5,5,16,128]{3,2,1,0:T(8,128)}, u32[]{:S(2)}) copy-start(f32[5,5,16,128]{3,2,1,0:T(8,128)} %get-tuple-element.23) | copy-start | bytes 614404
  47.4 1.6 %copy-start.14 = (f32[5,5,16,128]{3,2,1,0:T(8,128)S(1)}, f32[5,5,16,128]{3,2,1,0:T(8,128)}, u32[]{:S(2)}) copy-start(f32[5,5,16,128]{3,2,1,0:T(8,128)} %get-tuple-element.24) | copy-start | bytes 614404
  49.1 1.2 %copy-start.9 = (f32[5,16,5,128]{3,2,1,0:T(8,128)S(1)}, f32[5,16,5,128]{3,2,1,0:T(8,128)}, u32[]{:S(2)}) copy-start(f32[5,16,5,128]{3,2,1,0:T(8,128)} %get-tuple-element.25) | copy-start | bytes 614404
  49.1 1.2 %copy-start.10 = (f32[5,16,5,128]{3,2,1,0:T(8,128)S(1)}, f32[5,16,5,128]{3,2,1,0:T(8,128)}, u32[]{:S(2)}) copy-start(f32[5,16,5,128]{3,2,1,0:T(8,128)} %get-tuple-element.26) | copy-start | bytes 614404
  50.4 1.3 %copy-start.12 = (f32[128,138,1,1]{0,1,3,2:T(8,128)S(1)}, f32[128,138,1,1]{0,1,3,2:T(8,128)}, u32[]{:S(2)}) copy-start(f32[128,138,1,1]{0,1,3,2:T(8,128)} %constant.27) | copy-start | bytes 211972
  53.0 1.1 %copy-start.2 = (f32[5,16,16,128]{3,2,1,0:T(8,128)}, f32[5,16,16,128]{3,2,1,0:T(8,128)S(1)}, u32[]{:S(2)}) copy-start(f32[5,16,16,128]{3,2,1,0:T(8,128)S(1)} %fusion.36.refs_0_) | copy-start | bytes 1966084
  67.6 1.3 %copy-start.8 = (f32[2,2,5,5,5,128]{5,4,3,2,1,0:T(8,128)S(1)}, f32[2,2,5,5,5,128]{5,4,3,2,1,0:T(8,128)}, u32[]{:S(2)}) copy-start(f32[2,2,5,5,5,128]{5,4,3,2,1,0:T(8,128)} %get-tuple-element.28) | copy-start | bytes 768004
  67.6 1.3 %copy-start.7 = (f32[2,5,5,16,128]{4,3,2,1,0:T(8,128)S(1)}, f32[2,5,5,16,128]{4,3,2,1,0:T(8,128)}, u32[]{:S(2)}) copy-start(f32[2,5,5,16,128]{4,3,2,1,0:T(8,128)} %get-tuple-element.29) | copy-start | bytes 1228804
  67.6 1.5 %copy-start.3 = (f32[5,16,16,128]{3,2,1,0:T(8,128)S(1)}, f32[5,16,16,128]{3,2,1,0:T(8,128)}, u32[]{:S(2)}) copy-start(f32[5,16,16,128]{3,2,1,0:T(8,128)} %copy-done.2) | copy-start | bytes 1966084
  69.1 0.7 copy-start.18
  82.4 0.9 %copy-start.16 = (f32[128,138,1,1]{0,1,3,2:T(8,128)S(1)}, f32[128,138,1,1]{0,1,3,2:T(8,128)}, u32[]{:S(2)}) copy-start(f32[128,138,1,1]{0,1,3,2:T(8,128)} %constant.29) | copy-start | bytes 211972

commit v7 on v6

--- a/solution.py
+++ b/solution.py
@@ -60,7 +60,7 @@
         functools.partial(exchange_kernel, tuple(routes), sizes, len(arrays)),
         out_shape=out_shapes,
         in_specs=[pl.BlockSpec(memory_space=pl.ANY)] * len(arrays),
-        out_specs=[pl.BlockSpec(memory_space=pl.ANY)] * len(out_shapes),
+        out_specs=[pl.BlockSpec(memory_space=pltpu.VMEM)] * len(out_shapes),
         scratch_shapes=[
             pltpu.SemaphoreType.DMA((len(routes),)),
             pltpu.SemaphoreType.DMA((len(routes),)),

time: 86.4 us -> 89.8 us (1.039)
  Pallas kernels: 43.9 us -> 47.2 us
    pallas_call x4, Pallas kernels: 43.9 us -> 47.2 us  [exchange(): pl.pallas_call(functools.partial(exchange_kernel, tuple(routes), sizes, l...]
where the time goes in v7:
time: 89.8 us; the launch traced here: 88.9 us
  Pallas kernels  47.2 us (53%)
  local copies, waits for them, and re-layouts  19.9 us (22%)
  matrix products  12.6 us (14%)
  other arithmetic  8.65 us (10%)
    pallas_call x4, Pallas kernels, exchange(): pl.pallas_call(functools.partial(exchange_kernel, tuple(routes), sizes, l...  47.2 us
    dot_general x9, matrix products, sweep_lines(): jnp.einsum(line_forms[dim], matrix, padded, precision=lax.Precision.HIGHEST)  12.6 us
    another operation x8, local copies, waits for them, and re-layouts, exchange_faces(): jnp.stack([lax.slice_in_dim(value, length - WIDTH, length, axis=dim), lax...  5.76 us
    pallas_call x2, local copies, waits for them, and re-layouts, exchange(): pl.pallas_call(functools.partial(exchange_kernel, tuple(routes), sizes, l...  2.79 us
    reshape x3, local copies, waits for them, and re-layouts, exchange_faces(): both = jnp.moveaxis(both, dim + 1, 2).reshape(2, value.shape[0], WIDTH, -1)  2.48 us
    unnamed x42, local copies, waits for them, and re-layouts  2.22 us

profile of v7, /device:TPU:1, one launch (start us, length us, event | category | flops | bytes accessed | tf_op | source)
XLA Modules:
  0.0 88.9 jit_solution(15715289768292470122)
XLA Ops:
  0.0 1.0 %slice_bitcast_fusion.40 = f32[16,16,128]{2,1,0:T(8,128)S(1)} fusion(f32[5,16,16,128]{3,2,1,0:T(8,128)} %param.9), kind=kLoop, calls=%fused_computation.166 | loop fusion | bytes 262144 | tf_op jit(solution)/shard_map/div | solution.py:261
  1.0 1.1 %multiply_reduce_fusion = (f32[16,16,128]{2,1,0:T(8,128)S(1)}, f32[3,16,16,128]{3,2,1,0:T(8,128)S(1)}) fusion(f32[5,16,16,128]{3,2,1,0:T(8,128)} %param.9, f32[16,16,128]{2,1,0:T(8,128)S(1)} %slice_bitcast_fusion.40), kind=kLoop, calls=%fused_computation.82 | loop fusion | flops 262144 | bytes 1048576 | tf_op jit(solution)/shard_map/reduce_sum | solution.py:263
  2.1 0.7 fusion.78
  2.8 0.2 fusion.63
  3.0 0.5 copy.53
  3.4 0.5 copy.54
  4.0 0.8 reshape.47.refs_3_
  4.8 0.9 fusion.67
  5.6 0.8 pad_maximum_fusion.refs_0_
  6.5 14.4 %shard_map.91 = (f32[4,5,16,128]{3,2,1,0:T(8,128)}, f32[4,5,16,128]{3,2,1,0:T(8,128)}, f32[4,16,5,128]{3,2,1,0:T(8,128)}, f32[4,16,5,128]{3,2,1,0:T(8,128)}, f32[2,4,5,256]{3,2,1,0:T(8,128)}) custom-call(f32[4,16,16,128]{3,2,1,0:T(8,128)} %pad_maximum_fusion.refs_0_, f32[4,16,5,128]{3,2,1,0:T(8,128)} %get-tuple-element.83.refs_1_, ...), custom_call_target="tpu_custom_call" | custom-call | tf_op jit(solution)/shard_map/pallas_call | solution.py:59
  20.9 1.1 %pad_maximum_fusion.2 = f32[4,26,16,128]{3,2,1,0:T(8,128)S(1)} fusion(f32[4,5,16,128]{3,2,1,0:T(8,128)} %get-tuple-element.19, f32[1,16,16,128]{3,2,1,0:T(8,128)S(1)} %get-tuple-element.78, f32[3,16,16,128]{3,2,1,0:T(8,128)S(1)} %get-tuple-element.44, f32[4,5,16,128]{3,2,1,0:T(8,128)} %get-tuple-element.18), kind=kLoop, calls=%fused_computation.56 | loop fusion | flops 638976 | bytes 1703936 | tf_op jit(solution)/shard_map/concatenate | solution.py:126
  22.0 1.0 %fusion.60 = f32[4,16,128,16]{2,3,1,0:T(8,128)S(1)} fusion(f32[16,26,1,1]{1,0,3,2:T(8,128)S(1)} %copy-done.15, f32[4,26,16,128]{3,2,1,0:T(8,128)S(1)} %pad_maximum_fusion.2), kind=kOutput, calls=%fused_computation.54 | convolution fusion | flops 40894464 | bytes 1377920 | tf_op jit(solution)/shard_map/al,flyz->fayz/dot_general | solution.py:244
  22.9 0.2 copy.99
  23.1 0.9 %convolution_bitcast_fusion = f32[4,16,16,128]{3,2,1,0:T(8,128)S(1)} fusion(f32[16,26,1,1]{1,0,3,2:T(8,128)S(1)} %copy-done.15, f32[4,16,5,128]{3,2,1,0:T(8,128)S(1)} %copy-done.20, f32[1,16,16,128]{3,2,1,0:T(8,128)S(1)} %get-tuple-element.78, f32[3,16,16,128]{3,2,1,0:T(8,128)S(1)} %get-tuple-element.44, f32[4,16,5,128]{3,2,1,0:T(8,128)S(1)} %copy-done.19), kind=kOutput, calls=%fused_computation.32 | convolution fusion | flops 41533440 | bytes 1377920 | tf_op jit(solution)/shard_map/al,fxlz->fxaz/dot_general | solution.py:244
  24.0 0.4 copy.59
  24.6 0.7 copy-done.11
  25.3 1.1 %fusion.52 = f32[4,16,16,128]{3,2,1,0:T(8,128)S(1)} fusion(f32[128,138,1,1]{0,1,3,2:T(8,128)S(1)} %copy-done.11, f32[4,16,16,5]{3,2,1,0:T(8,128)S(1)} %get-tuple-element.64, f32[1,16,16,128]{3,2,1,0:T(8,128)S(1)} %get-tuple-element.78, f32[3,16,16,128]{3,2,1,0:T(8,128)S(1)} %get-tuple-element.44, f32[4,16,16,5]{3,2,1,0:T(8,128)S(1)} %get-tuple-element.63), kind=kOutput, calls=%fused_computation.46 | convolution fusion | flops 217479168 | bytes 1160192 | tf_op jit(solution)/shard_map/al,fxyl->fxya/dot_general | solution.py:244
  26.5 0.2 bitcast_dynamic-update-slice_fusion.11
  27.0 0.2 bitcast_dynamic-update-slice_fusion.8
  27.9 1.2 %multiply_add_fusion = (f32[5,16,16,128]{3,2,1,0:T(8,128)S(1)}, f32[5,16,16,128]{3,2,1,0:T(8,128)S(1)}, f32[5,16,16,128]{3,2,1,0:T(8,128)}) fusion(f32[5,16,16,128]{3,2,1,0:T(8,128)S(1)} %bitcast_dynamic-update-slice_fusion, f32[5,16,16,128]{3,2,1,0:T(8,128)S(1)} %bitcast_dynamic-update-slice_fusion.4, f32[5,16,16,128]{3,2,1,0:T(8,128)S(1)} %get-tuple-element.75, ...), kind=kLoop, calls=%fused_computation.70 | loop fusion | flops 2457600 | bytes 5111808 | tf_op jit(solution)/shard_map/add | solution.py:308
  29.1 1.1 %slice_bitcast_fusion.7 = (f32[1,5,16,16,5]{4,3,2,1,0:T(8,128)}, f32[1,5,16,16,5]{4,3,2,1,0:T(8,128)S(1)}) fusion(f32[5,16,16,128]{3,2,1,0:T(8,128)S(1)} %get-tuple-element.45), kind=kLoop, calls=%fused_computation.68 | loop fusion | bytes 102400 | tf_op jit(solution)/shard_map/stack | solution.py:85
  30.2 1.7 %copy.60 = f32[1,5,16,16,5]{3,2,4,1,0:T(8,128)S(1)} copy(f32[1,5,16,16,5]{4,3,2,1,0:T(8,128)} %get-tuple-element.71) | data formatting | bytes 51200 | tf_op jit(solution)/shard_map/stack | solution.py:85
  31.8 0.6 copy.61
  32.5 0.8 reshape.48.refs_3_
  33.3 0.9 fusion.89
  34.2 12.6 %shard_map.92 = (f32[5,5,16,128]{3,2,1,0:T(8,128)}, f32[5,5,16,128]{3,2,1,0:T(8,128)}, f32[5,16,5,128]{3,2,1,0:T(8,128)}, f32[5,16,5,128]{3,2,1,0:T(8,128)}, f32[2,5,5,256]{3,2,1,0:T(8,128)}) custom-call(f32[5,16,16,128]{3,2,1,0:T(8,128)} %get-tuple-element.47.refs_0_, f32[5,16,5,128]{3,2,1,0:T(8,128)} %get-tuple-element.74.refs_1_, ...), custom_call_target="tpu_custom_call" | custom-call | tf_op jit(solution)/shard_map/pallas_call | solution.py:59
  46.8 2.4 %copy.66 = f32[2,5,5,256]{2,3,1,0:T(8,128)} copy(f32[2,5,5,256]{3,2,1,0:T(8,128)} %get-tuple-element.27) | data formatting | bytes 102400 | tf_op jit(solution)/shard_map/pallas_call | solution.py:59
  49.2 1.5 %slice_bitcast_fusion.5 = (f32[5,16,16,5]{3,2,1,0:T(8,128)S(1)}, f32[5,16,16,5]{3,2,1,0:T(8,128)S(1)}) fusion(f32[2,5,16,16,5]{4,3,2,1,0:T(8,128)} %bitcast.488), kind=kLoop, calls=%fused_computation.66 | loop fusion | bytes 102400 | tf_op jit(solution)/shard_map/squeeze | solution.py:121
  50.9 1.2 %fusion.25 = f32[5,16,128,16]{2,3,1,0:T(8,128)S(1)} fusion(f32[16,26,1,1]{1,0,3,2:T(8,128)S(1)} %copy-done.15, f32[5,26,16,128]{3,2,1,0:T(8,128)S(1)} %pad_maximum_fusion.1), kind=kOutput, calls=%fused_computation.24 | convolution fusion | flops 51118080 | bytes 1721984 | tf_op jit(solution)/shard_map/al,flyz->fayz/dot_general | solution.py:244
  52.2 1.2 %fusion.42 = f32[5,16,16,128]{3,2,1,0:T(8,128)S(1)} fusion(f32[16,26,1,1]{1,0,3,2:T(8,128)S(1)} %copy-done.15, f32[5,16,5,128]{3,2,1,0:T(8,128)S(1)} %copy-done.10, f32[5,16,16,128]{3,2,1,0:T(8,128)S(1)} %get-tuple-element.46, f32[5,16,5,128]{3,2,1,0:T(8,128)S(1)} %copy-done.9, f32[5,16,128,16]{2,3,1,0:T(8,128)S(1)} %fusion.25), kind=kOutput, calls=%fused_computation.31 | convolution fusion | flops 51814400 | bytes 2377344 | tf_op jit(solution)/shard_map/al,fxlz->fxaz/dot_general | solution.py:244
  53.5 1.4 %fusion.36.refs_0_ = f32[5,16,16,128]{3,2,1,0:T(8,128)S(1)} fusion(f32[5,16,16,128]{3,2,1,0:T(8,128)S(1)} %copy-done.1, f32[5,16,16,128]{3,2,1,0:T(8,128)S(1)} %fusion.42, f32[128,138,1,1]{0,1,3,2:T(8,128)S(1)} %copy-done.12, f32[5,16,16,5]{3,2,1,0:T(8,128)S(1)} %get-tuple-element.51, f32[5,16,16,128]{3,2,1,0:T(8,128)S(1)} %get-tuple-element.45, ...), kind=kOutput, calls=%fused_computation.29 | convolution fusion | flops 272163840 | bytes 2874368 | tf_op jit(solution)/shard_map/al,fxyl->fxya/dot_general | solution.py:244
  54.9 0.2 slice_bitcast_fusion.11
  55.1 0.9 %pad_maximum_fusion.3.refs_1_ = f32[2,5,16,5,128]{4,3,2,1,0:T(8,128)} fusion(f32[1,5,16,5,128]{4,3,2,1,0:T(8,128)S(1)} %get-tuple-element.70, f32[1,5,16,5,128]{4,3,2,1,0:T(8,128)S(1)} %get-tuple-element.69), kind=kLoop, calls=%fused_computation.69 | loop fusion | flops 102400 | bytes 819200 | tf_op jit(solution)/shard_map/stack | solution.py:132
  56.0 14.4 %shard_map.93 = (f32[2,5,5,16,128]{4,3,2,1,0:T(8,128)}, f32[2,5,16,5,128]{4,3,2,1,0:T(8,128)}, f32[2,2,5,5,5,128]{5,4,3,2,1,0:T(8,128)}) custom-call(f32[5,16,16,128]{3,2,1,0:T(8,128)} %copy-done.2, f32[2,5,16,5,128]{4,3,2,1,0:T(8,128)} %pad_maximum_fusion.3.refs_1_), custom_call_target="tpu_custom_call" | custom-call | tf_op jit(solution)/shard_map/pallas_call | solution.py:59
  70.5 1.2 %slice_bitcast_fusion.13 = (f32[5,16,5,128]{3,2,1,0:T(8,128)S(1)}, f32[5,16,5,128]{3,2,1,0:T(8,128)S(1)}) fusion(f32[2,5,16,5,128]{4,3,2,1,0:T(8,128)} %get-tuple-element.30), kind=kLoop, calls=%fused_computation.88 | loop fusion | bytes 819200 | tf_op jit(solution)/shard_map/squeeze | solution.py:159
  71.8 0.2 copy-done.3
  72.0 0.4 maximum_maximum_fusion
  72.3 0.3 copy-done.18
  72.7 2.4 %fusion.2 = f32[5,16,26,128]{3,1,2,0:T(8,128)S(1)} fusion(f32[16,26,1,1]{1,0,3,2:T(8,128)S(1)} %copy-done.18, f32[5,26,26,128]{3,2,1,0:T(8,128)S(1)} %maximum_maximum_fusion), kind=kOutput, calls=%fused_computation.3 | convolution fusion | flops 83066880 | bytes 2797184 | tf_op jit(solution)/shard_map/al,flyz->fayz/dot_general | solution.py:244
  75.1 1.2 %fusion.27 = f32[5,16,16,128]{3,2,1,0:T(8,128)S(1)} fusion(f32[16,26,1,1]{1,0,3,2:T(8,128)S(1)} %copy-done.18, f32[5,16,26,128]{3,1,2,0:T(8,128)S(1)} %fusion.2), kind=kOutput, calls=%fused_computation.26 | convolution fusion | flops 51118080 | bytes 1721984 | tf_op jit(solution)/shard_map/al,fxlz->fxaz/dot_general | solution.py:244
  76.3 0.2 slice_bitcast_fusion.3
  76.5 0.6 copy.69
  77.1 0.6 copy.70
  77.8 0.8 reshape.49.refs_0_
  78.6 5.8 %shard_map.94 = f32[2,5,5,256]{3,2,1,0:T(8,128)} custom-call(f32[2,5,5,256]{3,2,1,0:T(8,128)} %reshape.49.refs_0_), custom_call_target="tpu_custom_call" | custom-call | tf_op jit(solution)/shard_map/pallas_call | solution.py:59
  84.5 1.3 %copy.84 = f32[2,5,5,256]{2,3,1,0:T(8,128)S(1)} copy(f32[2,5,5,256]{3,2,1,0:T(8,128)} %shard_map.94) | data formatting | bytes 102400 | tf_op jit(solution)/shard_map/reshape | solution.py:119
  85.9 0.8 copy-done.16
  86.7 2.2 %fusion.17 = f32[5,16,16,128]{3,2,1,0:T(8,128)} fusion(f32[128,138,1,1]{0,1,3,2:T(8,128)S(1)} %copy-done.16, f32[5,16,16,5]{3,2,1,0:T(8,128)S(1)} %get-tuple-element.49, f32[5,16,16,128]{3,2,1,0:T(8,128)S(1)} %fusion.27, f32[5,16,16,5]{3,2,1,0:T(8,128)S(1)} %get-tuple-element.48), kind=kOutput, calls=%fused_computation.16 | convolution fusion | flops 271672320 | bytes 1432576 | tf_op jit(solution)/shard_map/al,fxyl->fxya/dot_general | solution.py:244
  (57 shorter events, 1.7 us)
Async XLA Ops:
  0.0 2.1 %copy-start.1 = (f32[5,16,16,128]{3,2,1,0:T(8,128)S(1)}, f32[5,16,16,128]{3,2,1,0:T(8,128)}, u32[]{:S(2)}) copy-start(f32[5,16,16,128]{3,2,1,0:T(8,128)} %param.9) | copy-start | bytes 1966084
  6.5 15.5 %copy-start.15 = (f32[16,26,1,1]{1,0,3,2:T(8,128)S(1)}, f32[16,26,1,1]{1,0,3,2:T(8,128)}, u32[]{:S(2)}) copy-start(f32[16,26,1,1]{1,0,3,2:T(8,128)} %constant.26) | copy-start | bytes 4996
  21.9 1.2 %copy-start.19 = (f32[4,16,5,128]{3,2,1,0:T(8,128)S(1)}, f32[4,16,5,128]{3,2,1,0:T(8,128)}, u32[]{:S(2)}) copy-start(f32[4,16,5,128]{3,2,1,0:T(8,128)} %get-tuple-element.20) | copy-start | bytes 491524
  21.9 1.2 %copy-start.20 = (f32[4,16,5,128]{3,2,1,0:T(8,128)S(1)}, f32[4,16,5,128]{3,2,1,0:T(8,128)}, u32[]{:S(2)}) copy-start(f32[4,16,5,128]{3,2,1,0:T(8,128)} %get-tuple-element.21) | copy-start | bytes 491524
  22.9 1.1 %copy-start.17 = (f32[2,4,5,256]{3,2,1,0:T(8,128)S(1)}, f32[2,4,5,256]{3,2,1,0:T(8,128)}, u32[]{:S(2)}) copy-start(f32[2,4,5,256]{3,2,1,0:T(8,128)} %get-tuple-element.22) | copy-start | bytes 122884
  24.4 0.9 %copy-start.11 = (f32[128,138,1,1]{0,1,3,2:T(8,128)S(1)}, f32[128,138,1,1]{0,1,3,2:T(8,128)}, u32[]{:S(2)}) copy-start(f32[128,138,1,1]{0,1,3,2:T(8,128)} %constant.27) | copy-start | bytes 211972
  24.5 1.9 %copy-start = (f32[3,3,16,16,128]{4,3,2,1,0:T(8,128)S(1)}, f32[3,3,16,16,128]{4,3,2,1,0:T(8,128)}, u32[]{:S(2)}) copy-start(f32[3,3,16,16,128]{4,3,2,1,0:T(8,128)} %param.10) | copy-start | bytes 3538948
  24.6 1.9 %copy-start.4 = (f32[16,16,128]{2,1,0:T(8,128)S(1)}, f32[16,16,128]{2,1,0:T(8,128)}, u32[]{:S(2)}) copy-start(f32[16,16,128]{2,1,0:T(8,128)} %param.11) | copy-start | bytes 393220
  24.6 1.9 %copy-start.6 = (f32[5,16,16,128]{3,2,1,0:T(8,128)S(1)}, f32[5,16,16,128]{3,2,1,0:T(8,128)}, u32[]{:S(2)}) copy-start(f32[5,16,16,128]{3,2,1,0:T(8,128)} %get-tuple-element.79) | copy-start | bytes 1966084
  49.2 1.5 %copy-start.5 = (f32[5,16,16,128]{3,2,1,0:T(8,128)S(1)}, f32[5,16,16,128]{3,2,1,0:T(8,128)}, u32[]{:S(2)}) copy-start(f32[5,16,16,128]{3,2,1,0:T(8,128)} %get-tuple-element.47.refs_0_) | copy-start | bytes 1966084
  49.2 1.5 %copy-start.13 = (f32[5,5,16,128]{3,2,1,0:T(8,128)S(1)}, f32[5,5,16,128]{3,2,1,0:T(8,128)}, u32[]{:S(2)}) copy-start(f32[5,5,16,128]{3,2,1,0:T(8,128)} %get-tuple-element.23) | copy-start | bytes 614404
  49.2 1.6 %copy-start.14 = (f32[5,5,16,128]{3,2,1,0:T(8,128)S(1)}, f32[5,5,16,128]{3,2,1,0:T(8,128)}, u32[]{:S(2)}) copy-start(f32[5,5,16,128]{3,2,1,0:T(8,128)} %get-tuple-element.24) | copy-start | bytes 614404
  50.9 1.2 %copy-start.9 = (f32[5,16,5,128]{3,2,1,0:T(8,128)S(1)}, f32[5,16,5,128]{3,2,1,0:T(8,128)}, u32[]{:S(2)}) copy-start(f32[5,16,5,128]{3,2,1,0:T(8,128)} %get-tuple-element.25) | copy-start | bytes 614404
  50.9 1.2 %copy-start.10 = (f32[5,16,5,128]{3,2,1,0:T(8,128)S(1)}, f32[5,16,5,128]{3,2,1,0:T(8,128)}, u32[]{:S(2)}) copy-start(f32[5,16,5,128]{3,2,1,0:T(8,128)} %get-tuple-element.26) | copy-start | bytes 614404
  52.2 1.3 %copy-start.12 = (f32[128,138,1,1]{0,1,3,2:T(8,128)S(1)}, f32[128,138,1,1]{0,1,3,2:T(8,128)}, u32[]{:S(2)}) copy-start(f32[128,138,1,1]{0,1,3,2:T(8,128)} %constant.27) | copy-start | bytes 211972
  54.8 1.1 %copy-start.2 = (f32[5,16,16,128]{3,2,1,0:T(8,128)}, f32[5,16,16,128]{3,2,1,0:T(8,128)S(1)}, u32[]{:S(2)}) copy-start(f32[5,16,16,128]{3,2,1,0:T(8,128)S(1)} %fusion.36.refs_0_) | copy-start | bytes 1966084
  70.4 1.3 %copy-start.8 = (f32[2,2,5,5,5,128]{5,4,3,2,1,0:T(8,128)S(1)}, f32[2,2,5,5,5,128]{5,4,3,2,1,0:T(8,128)}, u32[]{:S(2)}) copy-start(f32[2,2,5,5,5,128]{5,4,3,2,1,0:T(8,128)} %get-tuple-element.28) | copy-start | bytes 768004
  70.4 1.3 %copy-start.7 = (f32[2,5,5,16,128]{4,3,2,1,0:T(8,128)S(1)}, f32[2,5,5,16,128]{4,3,2,1,0:T(8,128)}, u32[]{:S(2)}) copy-start(f32[2,5,5,16,128]{4,3,2,1,0:T(8,128)} %get-tuple-element.29) | copy-start | bytes 1228804
  70.5 1.5 %copy-start.3 = (f32[5,16,16,128]{3,2,1,0:T(8,128)S(1)}, f32[5,16,16,128]{3,2,1,0:T(8,128)}, u32[]{:S(2)}) copy-start(f32[5,16,16,128]{3,2,1,0:T(8,128)} %copy-done.2) | copy-start | bytes 1966084
  72.0 0.7 copy-start.18
  85.8 0.9 %copy-start.16 = (f32[128,138,1,1]{0,1,3,2:T(8,128)S(1)}, f32[128,138,1,1]{0,1,3,2:T(8,128)}, u32[]{:S(2)}) copy-start(f32[128,138,1,1]{0,1,3,2:T(8,128)} %constant.29) | copy-start | bytes 211972

commit v8 on v6

--- a/solution.py
+++ b/solution.py
@@ -162,6 +162,66 @@
     return jnp.concatenate(sections, axis=1)
 
 
+def sweep_zeta_kernel(sizes, block_ref, middle_ref, lower_ref, upper_ref, out_ref,
+                      turned, before, after, send_sems, recv_sems):
+    fields, length_x, length_y, depth = block_ref.shape
+    rows = fields * length_x * length_y
+    here = [lax.axis_index(axis) for axis in AXES]
+    up = tuple(here[:2]) + (lax.rem(here[2] + 1, sizes[2]),)
+    down = tuple(here[:2]) + (lax.rem(here[2] + sizes[2] - 1, sizes[2]),)
+    turned[...] = block_ref[...].reshape(rows, depth).T
+    barrier = pltpu.get_barrier_semaphore()
+    for partner in (up, down):
+        pl.semaphore_signal(barrier, inc=1, device_id=partner, device_id_type=MESH)
+    pl.semaphore_wait(barrier, 2)
+    copies = [
+        pltpu.make_async_remote_copy(
+            src_ref=turned.at[pl.ds(depth - 8, 8)], dst_ref=before,
+            send_sem=send_sems.at[0], recv_sem=recv_sems.at[0],
+            device_id=up, device_id_type=MESH,
+        ),
+        pltpu.make_async_remote_copy(
+            src_ref=turned.at[pl.ds(0, 8)], dst_ref=after,
+            send_sem=send_sems.at[1], recv_sem=recv_sems.at[1],
+            device_id=down, device_id_type=MESH,
+        ),
+    ]
+    for copy in copies:
+        copy.start()
+    total = jnp.dot(middle_ref[...], turned[...], precision=lax.Precision.HIGHEST,
+                    preferred_element_type=jnp.float32)
+    for copy in copies:
+        copy.wait()
+    total = total + jnp.dot(lower_ref[...], before[...], precision=lax.Precision.HIGHEST,
+                            preferred_element_type=jnp.float32)
+    total = total + jnp.dot(upper_ref[...], after[...], precision=lax.Precision.HIGHEST,
+                            preferred_element_type=jnp.float32)
+    out_ref[...] = total.T.reshape(fields, length_x, length_y, depth)
+
+
+def sweep_zeta(value, matrix, tag):
+    sizes = tuple(lax.axis_size(axis) for axis in AXES)
+    fields, length_x, length_y, depth = value.shape
+    rows = fields * length_x * length_y
+    middle = matrix[:, WIDTH : WIDTH + depth]
+    lower = jnp.concatenate([jnp.zeros((depth, 8 - WIDTH), matrix.dtype), matrix[:, :WIDTH]], axis=1)
+    upper = jnp.concatenate([matrix[:, WIDTH + depth :], jnp.zeros((depth, 8 - WIDTH), matrix.dtype)], axis=1)
+    return pl.pallas_call(
+        functools.partial(sweep_zeta_kernel, sizes),
+        out_shape=jax.ShapeDtypeStruct(value.shape, value.dtype),
+        in_specs=[pl.BlockSpec(memory_space=pltpu.VMEM)] * 4,
+        out_specs=pl.BlockSpec(memory_space=pltpu.VMEM),
+        scratch_shapes=[
+            pltpu.VMEM((depth, rows), jnp.float32),
+            pltpu.VMEM((8, rows), jnp.float32),
+            pltpu.VMEM((8, rows), jnp.float32),
+            pltpu.SemaphoreType.DMA((2,)),
+            pltpu.SemaphoreType.DMA((2,)),
+        ],
+        compiler_params=pltpu.CompilerParams(collective_id=tag, has_side_effects=True),
+    )(value, middle, lower, upper)
+
+
 def with_halo(value, sides, width):
     for axis, dim in sides:
         count, length = (lax.axis_size(axis), value.shape[dim])
@@ -339,7 +399,7 @@
     sectioned = conserved_solution - step_duration * jacobian * divergence
     result = sweep_lines(exchange_plane(sectioned, 2), smooth[0], 1)
     result = sweep_lines(result, smooth[1], 2)
-    result = sweep_lines(exchange_faces([(result, "zeta", 3)], 4)[0], smooth[2], 3)
+    result = sweep_zeta(result, smooth[2], 4)
     return result
 
 

time: 86.4 us -> 84.4 us (0.977)
  local copies, waits for them, and re-layouts: 19.9 us -> 14.6 us
  Pallas kernels: 43.9 us -> 47.6 us
  matrix products: 12.6 us -> 11.3 us
  other arithmetic: 8.65 us -> 9.61 us
    pallas_call x0 -> x1, Pallas kernels: none -> 8.98 us  [sweep_zeta(): pl.pallas_call(functools.partial(sweep_zeta_kernel, sizes), out_shape=jax...]
    pallas_call x4 -> x3, Pallas kernels: 43.9 us -> 38.6 us  [exchange(): pl.pallas_call(functools.partial(exchange_kernel, tuple(routes), sizes, l...]
    another operation x8 -> x5, local copies, waits for them, and re-layouts: 5.76 us -> 3.08 us  [exchange_faces(): jnp.stack([lax.slice_in_dim(value, length - WIDTH, length, axis=dim), lax...]
    unnamed x42 -> x41, local copies, waits for them, and re-layouts: 2.22 us -> 4.44 us
    squeeze x3 -> x2, local copies, waits for them, and re-layouts: 1.68 us -> 0.16 us  [exchange_faces(): before, after = (both[0], both[1])]
    dot_general x9 -> x8, matrix products: 12.6 us -> 11.3 us  [sweep_lines(): jnp.einsum(line_forms[dim], matrix, padded, precision=lax.Precision.HIGHEST)]
    reshape x1 -> x0, local copies, waits for them, and re-layouts: 1.32 us -> none  [exchange_faces(): received[place].reshape((2, value.shape[0], WIDTH) + value.shape[1:dim])]
    pallas_call x2, local copies, waits for them, and re-layouts: 2.79 us -> 1.67 us  [exchange(): pl.pallas_call(functools.partial(exchange_kernel, tuple(routes), sizes, l...]
where the time goes in v8:
time: 84.4 us; the launch traced here: 83.6 us
  Pallas kernels  47.6 us (56%)
  local copies, waits for them, and re-layouts  14.6 us (17%)
  matrix products  11.3 us (13%)
  other arithmetic  9.61 us (11%)
    pallas_call x3, Pallas kernels, exchange(): pl.pallas_call(functools.partial(exchange_kernel, tuple(routes), sizes, l...  38.6 us
    dot_general x8, matrix products, sweep_lines(): jnp.einsum(line_forms[dim], matrix, padded, precision=lax.Precision.HIGHEST)  11.3 us
    pallas_call x1, Pallas kernels, sweep_zeta(): pl.pallas_call(functools.partial(sweep_zeta_kernel, sizes), out_shape=jax...  8.98 us
    unnamed x41, local copies, waits for them, and re-layouts  4.44 us
    another operation x5, local copies, waits for them, and re-layouts, exchange_faces(): jnp.stack([lax.slice_in_dim(value, length - WIDTH, length, axis=dim), lax...  3.08 us

profile of v8, /device:TPU:1, one launch (start us, length us, event | category | flops | bytes accessed | tf_op | source)
XLA Modules:
  0.0 83.6 jit_solution(2829383469220418645)
XLA Ops:
  0.0 1.0 %slice_bitcast_fusion.36 = f32[16,16,128]{2,1,0:T(8,128)S(1)} fusion(f32[5,16,16,128]{3,2,1,0:T(8,128)} %param.9), kind=kLoop, calls=%fused_computation.155 | loop fusion | bytes 262144 | tf_op jit(solution)/shard_map/div | solution.py:321
  1.0 1.1 %multiply_reduce_fusion = (f32[16,16,128]{2,1,0:T(8,128)S(1)}, f32[3,16,16,128]{3,2,1,0:T(8,128)S(1)}) fusion(f32[5,16,16,128]{3,2,1,0:T(8,128)} %param.9, f32[16,16,128]{2,1,0:T(8,128)S(1)} %slice_bitcast_fusion.36), kind=kLoop, calls=%fused_computation.71 | loop fusion | flops 262144 | bytes 1048576 | tf_op jit(solution)/shard_map/reduce_sum | solution.py:323
  2.1 0.7 fusion.72
  2.8 0.2 fusion.57
  3.0 0.5 copy.41
  3.4 0.5 copy.42
  4.0 0.8 reshape.38.refs_3_
  4.8 0.8 %fusion.61 = (f32[4,16,5,128]{3,2,1,0:T(8,128)}, f32[4,16,5,128]{3,2,1,0:T(8,128)}) fusion(f32[3,16,16,128]{3,2,1,0:T(8,128)S(1)} %get-tuple-element.44, f32[1,16,16,128]{3,2,1,0:T(8,128)S(1)} %get-tuple-element.74), kind=kLoop, calls=%fused_computation.79 | loop fusion | flops 81920 | bytes 851968 | tf_op jit(solution)/shard_map/concatenate | solution.py:382
  5.6 0.8 %pad_maximum_fusion.refs_0_ = f32[4,16,16,128]{3,2,1,0:T(8,128)} fusion(f32[1,16,16,128]{3,2,1,0:T(8,128)S(1)} %get-tuple-element.74, f32[3,16,16,128]{3,2,1,0:T(8,128)S(1)} %get-tuple-element.44), kind=kLoop, calls=%fused_computation.31 | loop fusion | flops 131072 | bytes 1048576 | tf_op jit(solution)/shard_map/concatenate | solution.py:382
  6.5 13.6 %shard_map.91 = (f32[4,5,16,128]{3,2,1,0:T(8,128)}, f32[4,5,16,128]{3,2,1,0:T(8,128)}, f32[4,16,5,128]{3,2,1,0:T(8,128)}, f32[4,16,5,128]{3,2,1,0:T(8,128)}, f32[2,4,5,256]{3,2,1,0:T(8,128)}) custom-call(f32[4,16,16,128]{3,2,1,0:T(8,128)} %pad_maximum_fusion.refs_0_, f32[4,16,5,128]{3,2,1,0:T(8,128)} %get-tuple-element.79.refs_1_, ...), custom_call_target="tpu_custom_call" | custom-call | tf_op jit(solution)/shard_map/pallas_call | solution.py:59
  20.0 1.1 %pad_maximum_fusion.2 = f32[4,26,16,128]{3,2,1,0:T(8,128)S(1)} fusion(f32[4,5,16,128]{3,2,1,0:T(8,128)} %get-tuple-element.19, f32[1,16,16,128]{3,2,1,0:T(8,128)S(1)} %get-tuple-element.74, f32[3,16,16,128]{3,2,1,0:T(8,128)S(1)} %get-tuple-element.44, f32[4,5,16,128]{3,2,1,0:T(8,128)} %get-tuple-element.18), kind=kLoop, calls=%fused_computation.50 | loop fusion | flops 638976 | bytes 1703936 | tf_op jit(solution)/shard_map/concatenate | solution.py:126
  21.2 1.0 %fusion.54 = f32[4,16,128,16]{2,3,1,0:T(8,128)S(1)} fusion(f32[16,26,1,1]{1,0,3,2:T(8,128)S(1)} %copy-done.15, f32[4,26,16,128]{3,2,1,0:T(8,128)S(1)} %pad_maximum_fusion.2), kind=kOutput, calls=%fused_computation.48 | convolution fusion | flops 40894464 | bytes 1377920 | tf_op jit(solution)/shard_map/al,flyz->fayz/dot_general | solution.py:304
  22.1 0.2 copy.76
  22.3 0.9 %convolution_bitcast_fusion = f32[4,16,16,128]{3,2,1,0:T(8,128)S(1)} fusion(f32[16,26,1,1]{1,0,3,2:T(8,128)S(1)} %copy-done.15, f32[4,16,5,128]{3,2,1,0:T(8,128)S(1)} %copy-done.19, f32[1,16,16,128]{3,2,1,0:T(8,128)S(1)} %get-tuple-element.74, f32[3,16,16,128]{3,2,1,0:T(8,128)S(1)} %get-tuple-element.44, f32[4,16,5,128]{3,2,1,0:T(8,128)S(1)} %copy-done.18), kind=kOutput, calls=%fused_computation.26 | convolution fusion | flops 41533440 | bytes 1377920 | tf_op jit(solution)/shard_map/al,fxlz->fxaz/dot_general | solution.py:304
  23.2 0.4 copy.47
  23.7 0.8 copy-done.11
  24.5 1.1 %fusion.46 = f32[4,16,16,128]{3,2,1,0:T(8,128)S(1)} fusion(f32[128,138,1,1]{0,1,3,2:T(8,128)S(1)} %copy-done.11, f32[4,16,16,5]{3,2,1,0:T(8,128)S(1)} %get-tuple-element.62, f32[1,16,16,128]{3,2,1,0:T(8,128)S(1)} %get-tuple-element.74, f32[3,16,16,128]{3,2,1,0:T(8,128)S(1)} %get-tuple-element.44, f32[4,16,16,5]{3,2,1,0:T(8,128)S(1)} %get-tuple-element.61), kind=kOutput, calls=%fused_computation.40 | convolution fusion | flops 217479168 | bytes 1160192 | tf_op jit(solution)/shard_map/al,fxyl->fxya/dot_general | solution.py:304
  25.7 0.2 bitcast_dynamic-update-slice_fusion.11
  25.9 0.1 bitcast_dynamic-update-slice_fusion.10
  26.0 0.1 bitcast_dynamic-update-slice_fusion.9
  26.2 0.2 bitcast_dynamic-update-slice_fusion.8
  26.5 0.1 bitcast_dynamic-update-slice_fusion.5
  26.6 0.1 bitcast_dynamic-update-slice_fusion.4
  26.8 0.1 bitcast_dynamic-update-slice_fusion
  27.1 1.3 %multiply_add_fusion = (f32[5,16,16,128]{3,2,1,0:T(8,128)S(1)}, f32[5,16,16,128]{3,2,1,0:T(8,128)S(1)}, f32[5,16,16,128]{3,2,1,0:T(8,128)}) fusion(f32[5,16,16,128]{3,2,1,0:T(8,128)S(1)} %bitcast_dynamic-update-slice_fusion, f32[5,16,16,128]{3,2,1,0:T(8,128)S(1)} %bitcast_dynamic-update-slice_fusion.4, f32[5,16,16,128]{3,2,1,0:T(8,128)S(1)} %get-tuple-element.71, ...), kind=kLoop, calls=%fused_computation.60 | loop fusion | flops 2457600 | bytes 5111808 | tf_op jit(solution)/shard_map/add | solution.py:368
  28.3 0.2 slice_bitcast_fusion.3
  28.6 1.3 %copy.48 = f32[1,5,16,16,5]{3,2,4,1,0:T(8,128)} copy(f32[1,5,16,16,5]{4,3,2,1,0:T(8,128)S(1)} %get-tuple-element.67) | data formatting | bytes 51200 | tf_op jit(solution)/shard_map/stack | solution.py:85
  29.8 0.6 copy.49
  30.4 1.0 %maximum_bitcast_fusion = f32[2,5,5,16,16]{4,3,2,1,0:T(8,128)S(1)} fusion(f32[1,5,16,16,5]{3,2,4,1,0:T(8,128)S(1)} %copy.49, f32[1,5,16,16,5]{3,2,4,1,0:T(8,128)} %copy.48), kind=kLoop, calls=%fused_computation.70 | loop fusion | flops 12800 | bytes 102400 | tf_op jit(solution)/shard_map/transpose | solution.py:91
  31.4 0.8 %reshape.39.refs_3_ = f32[2,5,5,256]{3,2,1,0:T(8,128)} reshape(f32[2,5,5,16,16]{4,3,2,1,0:T(8,128)S(1)} %maximum_bitcast_fusion) | data formatting | bytes 102400 | tf_op jit(solution)/shard_map/reshape | solution.py:91
  32.2 0.9 %fusion.82 = (f32[5,16,5,128]{3,2,1,0:T(8,128)}, f32[5,16,5,128]{3,2,1,0:T(8,128)}) fusion(f32[5,16,16,128]{3,2,1,0:T(8,128)S(1)} %get-tuple-element.46), kind=kLoop, calls=%fused_computation.168 | loop fusion | bytes 819200 | tf_op jit(solution)/shard_map/slice | solution.py:100
  33.2 11.6 %shard_map.92 = (f32[5,5,16,128]{3,2,1,0:T(8,128)}, f32[5,5,16,128]{3,2,1,0:T(8,128)}, f32[5,16,5,128]{3,2,1,0:T(8,128)}, f32[5,16,5,128]{3,2,1,0:T(8,128)}, f32[2,5,5,256]{3,2,1,0:T(8,128)}) custom-call(f32[5,16,16,128]{3,2,1,0:T(8,128)} %get-tuple-element.47.refs_0_, f32[5,16,5,128]{3,2,1,0:T(8,128)} %get-tuple-element.70.refs_1_, ...), custom_call_target="tpu_custom_call" | custom-call | tf_op jit(solution)/shard_map/pallas_call | solution.py:59
  44.8 1.3 %copy.54 = f32[2,5,5,256]{2,3,1,0:T(8,128)S(1)} copy(f32[2,5,5,256]{3,2,1,0:T(8,128)} %get-tuple-element.27) | data formatting | bytes 102400 | tf_op jit(solution)/shard_map/pallas_call | solution.py:59
  46.2 1.0 %copy-done.5 = f32[5,16,16,128]{3,2,1,0:T(8,128)S(1)} copy-done((f32[5,16,16,128]{3,2,1,0:T(8,128)S(1)}, f32[5,16,16,128]{3,2,1,0:T(8,128)}, u32[]{:S(2)}) %copy-start.5) | copy-done | bytes 655384
  47.4 1.2 %fusion.19 = f32[5,16,128,16]{2,3,1,0:T(8,128)S(1)} fusion(f32[16,26,1,1]{1,0,3,2:T(8,128)S(1)} %copy-done.15, f32[5,26,16,128]{3,2,1,0:T(8,128)S(1)} %pad_maximum_fusion.1), kind=kOutput, calls=%fused_computation.18 | convolution fusion | flops 51118080 | bytes 1721984 | tf_op jit(solution)/shard_map/al,flyz->fayz/dot_general | solution.py:304
  48.7 1.2 %fusion.36 = f32[5,16,16,128]{3,2,1,0:T(8,128)S(1)} fusion(f32[16,26,1,1]{1,0,3,2:T(8,128)S(1)} %copy-done.15, f32[5,16,5,128]{3,2,1,0:T(8,128)S(1)} %copy-done.10, f32[5,16,16,128]{3,2,1,0:T(8,128)S(1)} %get-tuple-element.46, f32[5,16,5,128]{3,2,1,0:T(8,128)S(1)} %copy-done.9, f32[5,16,128,16]{2,3,1,0:T(8,128)S(1)} %fusion.19), kind=kOutput, calls=%fused_computation.25 | convolution fusion | flops 51814400 | bytes 2377344 | tf_op jit(solution)/shard_map/al,fxlz->fxaz/dot_general | solution.py:304
  49.9 1.4 %fusion.30.refs_0_ = f32[5,16,16,128]{3,2,1,0:T(8,128)S(1)} fusion(f32[5,16,16,128]{3,2,1,0:T(8,128)S(1)} %copy-done.1, f32[5,16,16,128]{3,2,1,0:T(8,128)S(1)} %fusion.36, f32[128,138,1,1]{0,1,3,2:T(8,128)S(1)} %copy-done.12, f32[5,16,16,5]{3,2,1,0:T(8,128)S(1)} %get-tuple-element.49, f32[5,16,16,128]{3,2,1,0:T(8,128)S(1)} %get-tuple-element.45, ...), kind=kOutput, calls=%fused_computation.23 | convolution fusion | flops 272163840 | bytes 2874368 | tf_op jit(solution)/shard_map/al,fxyl->fxya/dot_general | solution.py:304
  51.3 0.2 slice_bitcast_fusion.7
  51.6 0.9 %pad_maximum_fusion.3.refs_1_ = f32[2,5,16,5,128]{4,3,2,1,0:T(8,128)} fusion(f32[1,5,16,5,128]{4,3,2,1,0:T(8,128)S(1)} %get-tuple-element.66, f32[1,5,16,5,128]{4,3,2,1,0:T(8,128)S(1)} %get-tuple-element.65), kind=kLoop, calls=%fused_computation.59 | loop fusion | flops 102400 | bytes 819200 | tf_op jit(solution)/shard_map/stack | solution.py:132
  52.5 13.4 %shard_map.93 = (f32[2,5,5,16,128]{4,3,2,1,0:T(8,128)}, f32[2,5,16,5,128]{4,3,2,1,0:T(8,128)}, f32[2,2,5,5,5,128]{5,4,3,2,1,0:T(8,128)}) custom-call(f32[5,16,16,128]{3,2,1,0:T(8,128)} %copy-done.2, f32[2,5,16,5,128]{4,3,2,1,0:T(8,128)} %pad_maximum_fusion.3.refs_1_), custom_call_target="tpu_custom_call" | custom-call | tf_op jit(solution)/shard_map/pallas_call | solution.py:59
  65.9 1.2 %slice_bitcast_fusion.9 = (f32[5,16,5,128]{3,2,1,0:T(8,128)S(1)}, f32[5,16,5,128]{3,2,1,0:T(8,128)S(1)}) fusion(f32[2,5,16,5,128]{4,3,2,1,0:T(8,128)} %get-tuple-element.30), kind=kLoop, calls=%fused_computation.77 | loop fusion | bytes 819200 | tf_op jit(solution)/shard_map/squeeze | solution.py:159
  67.2 0.2 copy-done.3
  67.4 0.4 maximum_maximum_fusion
  67.8 0.3 copy-done.17
  68.1 2.4 %fusion.2 = f32[5,16,26,128]{3,1,2,0:T(8,128)S(1)} fusion(f32[16,26,1,1]{1,0,3,2:T(8,128)S(1)} %copy-done.17, f32[5,26,26,128]{3,2,1,0:T(8,128)S(1)} %maximum_maximum_fusion), kind=kOutput, calls=%fused_computation.3 | convolution fusion | flops 83066880 | bytes 2797184 | tf_op jit(solution)/shard_map/al,flyz->fayz/dot_general | solution.py:304
  70.5 2.0 %fusion.21.block_ref = f32[5,16,16,128]{3,2,1,0:T(8,128)} fusion(f32[16,26,1,1]{1,0,3,2:T(8,128)S(1)} %copy-done.17, f32[5,16,26,128]{3,1,2,0:T(8,128)S(1)} %fusion.2), kind=kOutput, calls=%fused_computation.20 | convolution fusion | flops 51118080 | bytes 1721984 | tf_op jit(solution)/shard_map/al,fxlz->fxaz/dot_general | solution.py:304
  72.6 9.0 %shard_map.94 = f32[5,16,16,128]{3,2,1,0:T(8,128)} custom-call(f32[5,16,16,128]{3,2,1,0:T(8,128)} %fusion.21.block_ref, f32[128,128]{1,0:T(8,128)} %constant.31.middle_ref, f32[128,8]{1,0:T(8,128)} %constant.33.lower_ref, f32[128,8]{1,0:T(8,128)} %constant.35.upper_ref), custom_call_target="tpu_custom_call" | custom-call | tf_op jit(solution)/shard_map/pallas_call | solution.py:209
  81.6 2.0 %copy.90 = f32[5,16,16,128]{3,2,1,0:T(8,128)} copy(f32[5,16,16,128]{3,2,1,0:T(8,128)} %shard_map.94) | data formatting | bytes 1310720
  (48 shorter events, 0.8 us)
Async XLA Ops:
  0.0 2.1 %copy-start.1 = (f32[5,16,16,128]{3,2,1,0:T(8,128)S(1)}, f32[5,16,16,128]{3,2,1,0:T(8,128)}, u32[]{:S(2)}) copy-start(f32[5,16,16,128]{3,2,1,0:T(8,128)} %param.9) | copy-start | bytes 1966084
  6.5 14.6 %copy-start.15 = (f32[16,26,1,1]{1,0,3,2:T(8,128)S(1)}, f32[16,26,1,1]{1,0,3,2:T(8,128)}, u32[]{:S(2)}) copy-start(f32[16,26,1,1]{1,0,3,2:T(8,128)} %constant.36) | copy-start | bytes 4996
  21.1 1.2 %copy-start.18 = (f32[4,16,5,128]{3,2,1,0:T(8,128)S(1)}, f32[4,16,5,128]{3,2,1,0:T(8,128)}, u32[]{:S(2)}) copy-start(f32[4,16,5,128]{3,2,1,0:T(8,128)} %get-tuple-element.20) | copy-start | bytes 491524
  21.1 1.2 %copy-start.19 = (f32[4,16,5,128]{3,2,1,0:T(8,128)S(1)}, f32[4,16,5,128]{3,2,1,0:T(8,128)}, u32[]{:S(2)}) copy-start(f32[4,16,5,128]{3,2,1,0:T(8,128)} %get-tuple-element.21) | copy-start | bytes 491524
  22.1 1.1 %copy-start.16 = (f32[2,4,5,256]{3,2,1,0:T(8,128)S(1)}, f32[2,4,5,256]{3,2,1,0:T(8,128)}, u32[]{:S(2)}) copy-start(f32[2,4,5,256]{3,2,1,0:T(8,128)} %get-tuple-element.22) | copy-start | bytes 122884
  23.6 0.9 %copy-start.11 = (f32[128,138,1,1]{0,1,3,2:T(8,128)S(1)}, f32[128,138,1,1]{0,1,3,2:T(8,128)}, u32[]{:S(2)}) copy-start(f32[128,138,1,1]{0,1,3,2:T(8,128)} %constant.37) | copy-start | bytes 211972
  23.7 2.0 %copy-start = (f32[3,3,16,16,128]{4,3,2,1,0:T(8,128)S(1)}, f32[3,3,16,16,128]{4,3,2,1,0:T(8,128)}, u32[]{:S(2)}) copy-start(f32[3,3,16,16,128]{4,3,2,1,0:T(8,128)} %param.10) | copy-start | bytes 3538948
  23.7 2.0 %copy-start.4 = (f32[16,16,128]{2,1,0:T(8,128)S(1)}, f32[16,16,128]{2,1,0:T(8,128)}, u32[]{:S(2)}) copy-start(f32[16,16,128]{2,1,0:T(8,128)} %param.11) | copy-start | bytes 393220
  23.7 2.0 %copy-start.6 = (f32[5,16,16,128]{3,2,1,0:T(8,128)S(1)}, f32[5,16,16,128]{3,2,1,0:T(8,128)}, u32[]{:S(2)}) copy-start(f32[5,16,16,128]{3,2,1,0:T(8,128)} %get-tuple-element.75) | copy-start | bytes 1966084
  46.1 1.1 %copy-start.5 = (f32[5,16,16,128]{3,2,1,0:T(8,128)S(1)}, f32[5,16,16,128]{3,2,1,0:T(8,128)}, u32[]{:S(2)}) copy-start(f32[5,16,16,128]{3,2,1,0:T(8,128)} %get-tuple-element.47.refs_0_) | copy-start | bytes 1966084
  46.1 1.1 %copy-start.13 = (f32[5,5,16,128]{3,2,1,0:T(8,128)S(1)}, f32[5,5,16,128]{3,2,1,0:T(8,128)}, u32[]{:S(2)}) copy-start(f32[5,5,16,128]{3,2,1,0:T(8,128)} %get-tuple-element.23) | copy-start | bytes 614404
  46.1 1.2 %copy-start.14 = (f32[5,5,16,128]{3,2,1,0:T(8,128)S(1)}, f32[5,5,16,128]{3,2,1,0:T(8,128)}, u32[]{:S(2)}) copy-start(f32[5,5,16,128]{3,2,1,0:T(8,128)} %get-tuple-element.24) | copy-start | bytes 614404
  47.4 1.2 %copy-start.9 = (f32[5,16,5,128]{3,2,1,0:T(8,128)S(1)}, f32[5,16,5,128]{3,2,1,0:T(8,128)}, u32[]{:S(2)}) copy-start(f32[5,16,5,128]{3,2,1,0:T(8,128)} %get-tuple-element.25) | copy-start | bytes 614404
  47.4 1.2 %copy-start.10 = (f32[5,16,5,128]{3,2,1,0:T(8,128)S(1)}, f32[5,16,5,128]{3,2,1,0:T(8,128)}, u32[]{:S(2)}) copy-start(f32[5,16,5,128]{3,2,1,0:T(8,128)} %get-tuple-element.26) | copy-start | bytes 614404
  48.6 1.3 %copy-start.12 = (f32[128,138,1,1]{0,1,3,2:T(8,128)S(1)}, f32[128,138,1,1]{0,1,3,2:T(8,128)}, u32[]{:S(2)}) copy-start(f32[128,138,1,1]{0,1,3,2:T(8,128)} %constant.37) | copy-start | bytes 211972
  51.3 1.2 %copy-start.2 = (f32[5,16,16,128]{3,2,1,0:T(8,128)}, f32[5,16,16,128]{3,2,1,0:T(8,128)S(1)}, u32[]{:S(2)}) copy-start(f32[5,16,16,128]{3,2,1,0:T(8,128)S(1)} %fusion.30.refs_0_) | copy-start | bytes 1966084
  65.9 1.3 %copy-start.8 = (f32[2,2,5,5,5,128]{5,4,3,2,1,0:T(8,128)S(1)}, f32[2,2,5,5,5,128]{5,4,3,2,1,0:T(8,128)}, u32[]{:S(2)}) copy-start(f32[2,2,5,5,5,128]{5,4,3,2,1,0:T(8,128)} %get-tuple-element.28) | copy-start | bytes 768004
  65.9 1.3 %copy-start.7 = (f32[2,5,5,16,128]{4,3,2,1,0:T(8,128)S(1)}, f32[2,5,5,16,128]{4,3,2,1,0:T(8,128)}, u32[]{:S(2)}) copy-start(f32[2,5,5,16,128]{4,3,2,1,0:T(8,128)} %get-tuple-element.29) | copy-start | bytes 1228804
  65.9 1.5 %copy-start.3 = (f32[5,16,16,128]{3,2,1,0:T(8,128)S(1)}, f32[5,16,16,128]{3,2,1,0:T(8,128)}, u32[]{:S(2)}) copy-start(f32[5,16,16,128]{3,2,1,0:T(8,128)} %copy-done.2) | copy-start | bytes 1966084
  67.4 0.7 copy-start.17

commit v9 on v7

--- a/solution.py
+++ b/solution.py
@@ -19,9 +19,18 @@
 AXES = ("xi", "eta", "zeta")
 
 
-def exchange_kernel(routes, sizes, count, *refs):
-    sources, targets = refs[:count], refs[count:-2]
-    send_sems, recv_sems = refs[-2:]
+def exchange_kernel(routes, sizes, count, zeta, *refs):
+    sources = refs[:count]
+    refs = refs[count:]
+    if zeta:
+        block_ref, middle_ref, lower_ref, upper_ref = refs[:4]
+        refs = refs[4:]
+    targets = refs[: len(refs) - 2 - (4 if zeta else 0)]
+    refs = refs[len(targets) :]
+    if zeta:
+        out_ref, turned, before, after = refs[:4]
+        refs = refs[4:]
+    send_sems, recv_sems = refs
     here = [lax.axis_index(axis) for axis in AXES]
 
     def device(offset):
@@ -29,8 +38,13 @@
             lax.rem(here[slot] + offset[slot] + sizes[slot], sizes[slot]) for slot in range(3)
         )
 
+    if zeta:
+        fields, length_x, length_y, depth = block_ref.shape
+        rows = fields * length_x * length_y
+        turned[...] = block_ref[...].reshape(rows, depth).T
+    offsets = [route[0] for route in routes] + ([(0, 0, 1), (0, 0, -1)] if zeta else [])
     partners = []
-    for offset, *_ in routes:
+    for offset in offsets:
         for way in (offset, tuple(-step for step in offset)):
             if way not in partners:
                 partners.append(way)
@@ -40,33 +54,81 @@
     pl.semaphore_wait(barrier, len(partners))
     copies = []
     for index, (offset, source, source_at, target, target_at) in enumerate(routes):
-        copy = pltpu.make_async_remote_copy(
-            src_ref=sources[source].at[source_at],
-            dst_ref=targets[target].at[target_at],
-            send_sem=send_sems.at[index],
-            recv_sem=recv_sems.at[index],
-            device_id=device(offset),
-            device_id_type=MESH,
+        copies.append(
+            pltpu.make_async_remote_copy(
+                src_ref=sources[source].at[source_at],
+                dst_ref=targets[target].at[target_at],
+                send_sem=send_sems.at[index],
+                recv_sem=recv_sems.at[index],
+                device_id=device(offset),
+                device_id_type=MESH,
+            )
         )
+    if zeta:
+        for index, (rows_at, landing, offset) in enumerate(
+            ((pl.ds(depth - 8, 8), before, (0, 0, 1)), (pl.ds(0, 8), after, (0, 0, -1)))
+        ):
+            copies.append(
+                pltpu.make_async_remote_copy(
+                    src_ref=turned.at[rows_at],
+                    dst_ref=landing,
+                    send_sem=send_sems.at[len(routes) + index],
+                    recv_sem=recv_sems.at[len(routes) + index],
+                    device_id=device(offset),
+                    device_id_type=MESH,
+                )
+            )
+    for copy in copies:
         copy.start()
-        copies.append(copy)
+    if zeta:
+        total = jnp.dot(middle_ref[...], turned[...], precision=lax.Precision.HIGHEST,
+                        preferred_element_type=jnp.float32)
     for copy in copies:
         copy.wait()
-
-
-def exchange(arrays, routes, out_shapes, tag):
+    if zeta:
+        total = total + jnp.dot(lower_ref[...], before[...], precision=lax.Precision.HIGHEST,
+                                preferred_element_type=jnp.float32)
+        total = total + jnp.dot(upper_ref[...], after[...], precision=lax.Precision.HIGHEST,
+                                preferred_element_type=jnp.float32)
+        out_ref[...] = total.T.reshape(fields, length_x, length_y, depth)
+
+
+def exchange(arrays, routes, out_shapes, tag, zeta=None):
     sizes = tuple(lax.axis_size(axis) for axis in AXES)
+    operands = list(arrays)
+    in_specs = [pl.BlockSpec(memory_space=pl.ANY)] * len(arrays)
+    out_specs = [pl.BlockSpec(memory_space=pl.ANY)] * len(out_shapes)
+    out_shapes = list(out_shapes)
+    scratch = []
+    copies = len(routes)
+    if zeta is not None:
+        value, matrix = zeta
+        fields, length_x, length_y, depth = value.shape
+        rows = fields * length_x * length_y
+        padding = jnp.zeros((depth, 8 - WIDTH), matrix.dtype)
+        operands += [
+            value,
+            matrix[:, WIDTH : WIDTH + depth],
+            jnp.concatenate([padding, matrix[:, :WIDTH]], axis=1),
+            jnp.concatenate([matrix[:, WIDTH + depth :], padding], axis=1),
+        ]
+        in_specs += [pl.BlockSpec(memory_space=pltpu.VMEM)] * 4
+        out_shapes.append(jax.ShapeDtypeStruct(value.shape, value.dtype))
+        out_specs.append(pl.BlockSpec(memory_space=pltpu.VMEM))
+        scratch = [pltpu.VMEM((depth, rows), jnp.float32), pltpu.VMEM((8, rows), jnp.float32),
+                   pltpu.VMEM((8, rows), jnp.float32)]
+        copies += 2
     return pl.pallas_call(
-        functools.partial(exchange_kernel, tuple(routes), sizes, len(arrays)),
+        functools.partial(exchange_kernel, tuple(routes), sizes, len(arrays), zeta is not None),
         out_shape=out_shapes,
-        in_specs=[pl.BlockSpec(memory_space=pl.ANY)] * len(arrays),
-        out_specs=[pl.BlockSpec(memory_space=pltpu.VMEM)] * len(out_shapes),
-        scratch_shapes=[
-            pltpu.SemaphoreType.DMA((len(routes),)),
-            pltpu.SemaphoreType.DMA((len(routes),)),
+        in_specs=in_specs,
+        out_specs=out_specs,
+        scratch_shapes=scratch + [
+            pltpu.SemaphoreType.DMA((copies,)),
+            pltpu.SemaphoreType.DMA((copies,)),
         ],
         compiler_params=pltpu.CompilerParams(collective_id=tag, has_side_effects=True),
-    )(*arrays)
+    )(*operands)
 
 
 def offset_along(axis, step):
@@ -77,7 +139,7 @@
     return tuple(slice(start, stop) if axis == dim else slice(None) for axis in range(ndim))
 
 
-def exchange_faces(items, tag):
+def exchange_faces(items, tag, zeta=None):
     arrays, routes, out_shapes = [], [], []
     for value, axis, dim in items:
         ndim, length = value.ndim, value.shape[dim]
@@ -112,7 +174,7 @@
             last, first = window(ndim, dim, length - WIDTH, length), window(ndim, dim, 0, WIDTH)
             routes.append((offset_along(axis, 1), source, last, target, whole))
             routes.append((offset_along(axis, -1), source, first, target + 1, whole))
-    received = exchange(arrays, routes, out_shapes, tag)
+    received = exchange(arrays, routes, out_shapes, tag, zeta)
     padded, place = [], 0
     for value, axis, dim in items:
         if dim == value.ndim - 1:
@@ -124,6 +186,8 @@
             before, after = received[place], received[place + 1]
             place += 2
         padded.append(jnp.concatenate([before, value, after], axis=dim))
+    if zeta is not None:
+        padded.append(received[-1])
     return padded
 
 
@@ -160,6 +224,10 @@
         jnp.concatenate([edges[0, 1], along_x[1], edges[1, 1]], axis=2),
     ]
     return jnp.concatenate(sections, axis=1)
+
+
+def sweep_zeta(value, matrix, tag):
+    return exchange([], [], [], tag, (value, matrix))[-1]
 
 
 def with_halo(value, sides, width):
@@ -321,9 +389,9 @@
     )
     basic_quantity = jnp.concatenate([fluid_speed_vector, thermal_level[None]], axis=0)
     padded = exchange_faces(
-        [(basic_quantity, "xi", 1), (basic_quantity, "eta", 2), (basic_quantity, "zeta", 3)], 0
-    )
-    slopes = [sweep_lines(padded[k], derive[k], k + 1) for k in range(3)]
+        [(basic_quantity, "xi", 1), (basic_quantity, "eta", 2)], 0, (basic_quantity, derive[2])
+    )
+    slopes = [sweep_lines(padded[k], derive[k], k + 1) for k in range(2)] + [padded[2]]
     contra = fluxes(
         conserved_solution,
         fluid_speed_vector,
@@ -332,14 +400,14 @@
         metrics,
         jacobian,
     )
-    padded = exchange_faces([(contra[0], "xi", 1), (contra[1], "eta", 2), (contra[2], "zeta", 3)], 1)
+    padded = exchange_faces([(contra[0], "xi", 1), (contra[1], "eta", 2)], 1, (contra[2], derive[2]))
     divergence = sweep_lines(padded[0], derive[0], 1)
     divergence = divergence + sweep_lines(padded[1], derive[1], 2)
-    divergence = divergence + sweep_lines(padded[2], derive[2], 3)
+    divergence = divergence + padded[2]
     sectioned = conserved_solution - step_duration * jacobian * divergence
     result = sweep_lines(exchange_plane(sectioned, 2), smooth[0], 1)
     result = sweep_lines(result, smooth[1], 2)
-    result = sweep_lines(exchange_faces([(result, "zeta", 3)], 4)[0], smooth[2], 3)
+    result = sweep_zeta(result, smooth[2], 4)
     return result
 
 

time: 89.8 us -> 80.5 us (0.90)
  local copies, waits for them, and re-layouts: 19.9 us -> 6.34 us
  Pallas kernels: 47.2 us -> 55 us
  matrix products: 12.6 us -> 8.98 us
    pallas_call x4, Pallas kernels: 47.2 us -> 55 us  [exchange(): pl.pallas_call(functools.partial(exchange_kernel, tuple(routes), sizes, l...]
    another operation x8 -> x0, local copies, waits for them, and re-layouts: 5.76 us -> none  [exchange_faces(): jnp.stack([lax.slice_in_dim(value, length - WIDTH, length, axis=dim), lax...]
    reshape x4 -> x0, local copies, waits for them, and re-layouts: 3.79 us -> none  [the longest x3 2.48 us: exchange_faces(): both = jnp.moveaxis(both, dim + 1, 2).reshape(2, value.shape[0], WIDTH, -1)]
    dot_general x9 -> x6, matrix products: 12.6 us -> 8.98 us  [sweep_lines(): jnp.einsum(line_forms[dim], matrix, padded, precision=lax.Precision.HIGHEST)]
    pallas_call x2 -> x0, local copies, waits for them, and re-layouts: 2.79 us -> none  [exchange(): pl.pallas_call(functools.partial(exchange_kernel, tuple(routes), sizes, l...]
    squeeze x3 -> x0, local copies, waits for them, and re-layouts: 1.68 us -> none  [exchange_faces(): before, after = (both[0], both[1])]
    concatenate x2, other arithmetic: 1.15 us -> 2.18 us  [exchange_faces(): padded.append(jnp.concatenate([before, value, after], axis=dim))]
    unnamed x42 -> x33, local copies, waits for them, and re-layouts: 2.22 us -> 2.88 us
where the time goes in v9:
time: 80.5 us; the launch traced here: 79.7 us
  Pallas kernels  55 us (68%)
  other arithmetic  9 us (11%)
  matrix products  8.98 us (11%)
  local copies, waits for them, and re-layouts  6.34 us (8%)
    pallas_call x4, Pallas kernels, exchange(): pl.pallas_call(functools.partial(exchange_kernel, tuple(routes), sizes, l...  55 us
    dot_general x6, matrix products, sweep_lines(): jnp.einsum(line_forms[dim], matrix, padded, precision=lax.Precision.HIGHEST)  8.98 us
    unnamed x33, local copies, waits for them, and re-layouts  2.88 us
    concatenate x2, other arithmetic, exchange_faces(): padded.append(jnp.concatenate([before, value, after], axis=dim))  2.18 us
    concatenate x2, other arithmetic, local(): jnp.concatenate([fluid_speed_vector, thermal_level[None]], axis=0)  1.68 us

profile of v9, /device:TPU:1, one launch (start us, length us, event | category | flops | bytes accessed | tf_op | source)
XLA Modules:
  0.0 79.7 jit_solution(5436617553835240363)
XLA Ops:
  0.0 1.0 %slice_bitcast_fusion.26 = f32[16,16,128]{2,1,0:T(8,128)S(1)} fusion(f32[5,16,16,128]{3,2,1,0:T(8,128)} %param.9), kind=kLoop, calls=%fused_computation.160 | loop fusion | bytes 262144 | tf_op jit(solution)/shard_map/div | solution.py:329
  1.0 1.1 %multiply_reduce_fusion = (f32[16,16,128]{2,1,0:T(8,128)S(1)}, f32[3,16,16,128]{3,2,1,0:T(8,128)S(1)}) fusion(f32[5,16,16,128]{3,2,1,0:T(8,128)} %param.9, f32[16,16,128]{2,1,0:T(8,128)S(1)} %slice_bitcast_fusion.26), kind=kLoop, calls=%fused_computation.42 | loop fusion | flops 262144 | bytes 1048576 | tf_op jit(solution)/shard_map/reduce_sum | solution.py:331
  2.1 0.9 %fusion.41 = (f32[4,16,5,128]{3,2,1,0:T(8,128)}, f32[4,16,5,128]{3,2,1,0:T(8,128)}) fusion(f32[3,16,16,128]{3,2,1,0:T(8,128)S(1)} %get-tuple-element.44, f32[1,16,16,128]{3,2,1,0:T(8,128)S(1)} %get-tuple-element.68), kind=kLoop, calls=%fused_computation.49 | loop fusion | flops 81920 | bytes 851968 | tf_op jit(solution)/shard_map/concatenate | solution.py:390
  3.0 0.8 %pad_maximum_fusion.1.refs_0_.refs_3_ = f32[4,16,16,128]{3,2,1,0:T(8,128)} fusion(f32[1,16,16,128]{3,2,1,0:T(8,128)S(1)} %get-tuple-element.68, f32[3,16,16,128]{3,2,1,0:T(8,128)S(1)} %get-tuple-element.44), kind=kLoop, calls=%fused_computation.33 | loop fusion | flops 131072 | bytes 1048576 | tf_op jit(solution)/shard_map/concatenate | solution.py:390
  3.8 17.2 %shard_map.91 = (f32[4,5,16,128]{3,2,1,0:T(8,128)}, f32[4,5,16,128]{3,2,1,0:T(8,128)}, f32[4,16,5,128]{3,2,1,0:T(8,128)}, f32[4,16,5,128]{3,2,1,0:T(8,128)}, f32[4,16,16,128]{3,2,1,0:T(8,128)}) custom-call(f32[4,16,16,128]{3,2,1,0:T(8,128)} %pad_maximum_fusion.1.refs_0_.refs_3_, f32[4,16,5,128]{3,2,1,0:T(8,128)} %get-tuple-element.71.refs_1_, ...), custom_call_target="tpu_custom_call" | custom-call | tf_op jit(solution)/shard_map/pallas_call | solution.py:121
  21.0 1.1 %pad_maximum_fusion.2 = f32[4,26,16,128]{3,2,1,0:T(8,128)S(1)} fusion(f32[4,5,16,128]{3,2,1,0:T(8,128)} %get-tuple-element.19, f32[1,16,16,128]{3,2,1,0:T(8,128)S(1)} %get-tuple-element.68, f32[3,16,16,128]{3,2,1,0:T(8,128)S(1)} %get-tuple-element.44, f32[4,5,16,128]{3,2,1,0:T(8,128)} %get-tuple-element.18), kind=kLoop, calls=%fused_computation.34 | loop fusion | flops 638976 | bytes 1703936 | tf_op jit(solution)/shard_map/concatenate | solution.py:188
  22.0 0.0 copy-done.12
  22.1 0.0 copy-start.14
  22.1 0.0 copy-start.15
  22.1 1.0 %fusion.38 = f32[4,16,128,16]{2,3,1,0:T(8,128)S(1)} fusion(f32[16,26,1,1]{1,0,3,2:T(8,128)S(1)} %copy-done.12, f32[4,26,16,128]{3,2,1,0:T(8,128)S(1)} %pad_maximum_fusion.2), kind=kOutput, calls=%fused_computation.29 | convolution fusion | flops 40894464 | bytes 1377920 | tf_op jit(solution)/shard_map/al,flyz->fayz/dot_general | solution.py:312
  23.1 0.0 copy-start
  23.1 0.0 copy-start.4
  23.1 0.0 copy-start.6
  23.1 0.2 copy.32
  23.3 0.9 %convolution_bitcast_fusion = f32[4,16,16,128]{3,2,1,0:T(8,128)S(1)} fusion(f32[16,26,1,1]{1,0,3,2:T(8,128)S(1)} %copy-done.12, f32[4,16,5,128]{3,2,1,0:T(8,128)S(1)} %copy-done.15, f32[1,16,16,128]{3,2,1,0:T(8,128)S(1)} %get-tuple-element.68, f32[3,16,16,128]{3,2,1,0:T(8,128)S(1)} %get-tuple-element.44, f32[4,16,5,128]{3,2,1,0:T(8,128)S(1)} %copy-done.14), kind=kOutput, calls=%fused_computation.20 | convolution fusion | flops 41533440 | bytes 1377920 | tf_op jit(solution)/shard_map/al,fxlz->fxaz/dot_general | solution.py:312
  24.2 0.1 copy-done
  24.3 0.0 copy-done.4
  24.3 0.2 copy-done.6
  24.5 0.2 bitcast_dynamic-update-slice_fusion.11
  24.7 0.1 bitcast_dynamic-update-slice_fusion.10
  24.8 0.1 bitcast_dynamic-update-slice_fusion.9
  25.0 0.2 bitcast_dynamic-update-slice_fusion.8
  25.2 0.1 bitcast_dynamic-update-slice_fusion.6
  25.3 0.1 bitcast_dynamic-update-slice_fusion.5
  25.4 0.1 bitcast_dynamic-update-slice_fusion.4
  25.6 0.1 bitcast_dynamic-update-slice_fusion.1
  25.6 0.1 bitcast_dynamic-update-slice_fusion
  25.8 0.1 slice_bitcast_fusion.23
  25.9 1.4 %multiply_add_fusion = (f32[5,16,16,128]{3,2,1,0:T(8,128)}, f32[5,16,16,128]{3,2,1,0:T(8,128)S(1)}, f32[5,16,16,128]{3,2,1,0:T(8,128)}) fusion(f32[5,16,16,128]{3,2,1,0:T(8,128)S(1)} %bitcast_dynamic-update-slice_fusion, f32[5,16,16,128]{3,2,1,0:T(8,128)S(1)} %bitcast_dynamic-update-slice_fusion.4, f32[5,16,16,128]{3,2,1,0:T(8,128)S(1)} %get-tuple-element.65, ...), kind=kLoop, calls=%fused_computation.36 | loop fusion | flops 2457600 | bytes 5111808 | tf_op jit(solution)/shard_map/add | solution.py:376
  27.3 0.9 %fusion.99 = (f32[5,16,5,128]{3,2,1,0:T(8,128)}, f32[5,16,5,128]{3,2,1,0:T(8,128)}) fusion(f32[5,16,16,128]{3,2,1,0:T(8,128)S(1)} %get-tuple-element.46), kind=kLoop, calls=%fused_computation.171 | loop fusion | bytes 819200 | tf_op jit(solution)/shard_map/slice | solution.py:162
  28.2 15.4 %shard_map.92 = (f32[5,5,16,128]{3,2,1,0:T(8,128)}, f32[5,5,16,128]{3,2,1,0:T(8,128)}, f32[5,16,5,128]{3,2,1,0:T(8,128)}, f32[5,16,5,128]{3,2,1,0:T(8,128)}, f32[5,16,16,128]{3,2,1,0:T(8,128)}) custom-call(f32[5,16,16,128]{3,2,1,0:T(8,128)} %get-tuple-element.47.refs_0_, f32[5,16,5,128]{3,2,1,0:T(8,128)} %get-tuple-element.64.refs_1_, ...), custom_call_target="tpu_custom_call" | custom-call | tf_op jit(solution)/shard_map/pallas_call | solution.py:121
  43.7 1.1 %pad_maximum_fusion = f32[5,26,16,128]{3,2,1,0:T(8,128)S(1)} fusion(f32[5,5,16,128]{3,2,1,0:T(8,128)} %get-tuple-element.24, f32[5,16,16,128]{3,2,1,0:T(8,128)S(1)} %copy-done.5, f32[5,5,16,128]{3,2,1,0:T(8,128)} %get-tuple-element.23), kind=kLoop, calls=%fused_computation.21 | loop fusion | flops 532480 | bytes 2129920 | tf_op jit(solution)/shard_map/concatenate | solution.py:188
  44.8 0.0 copy-start.7
  44.8 1.2 %fusion.11 = f32[5,16,128,16]{2,3,1,0:T(8,128)S(1)} fusion(f32[16,26,1,1]{1,0,3,2:T(8,128)S(1)} %copy-done.12, f32[5,26,16,128]{3,2,1,0:T(8,128)S(1)} %pad_maximum_fusion), kind=kOutput, calls=%fused_computation.12 | convolution fusion | flops 51118080 | bytes 1721984 | tf_op jit(solution)/shard_map/al,flyz->fayz/dot_general | solution.py:312
  46.1 1.3 %fusion.28.refs_0_ = f32[5,16,16,128]{3,2,1,0:T(8,128)S(1)} fusion(f32[5,16,16,128]{3,2,1,0:T(8,128)S(1)} %copy-done.1, f32[5,16,16,128]{3,2,1,0:T(8,128)S(1)} %copy-done.7, f32[16,26,1,1]{1,0,3,2:T(8,128)S(1)} %copy-done.12, f32[5,16,5,128]{3,2,1,0:T(8,128)S(1)} %copy-done.11, f32[5,16,16,128]{3,2,1,0:T(8,128)S(1)} %get-tuple-element.46, ...), kind=kOutput, calls=%fused_computation.19 | convolution fusion | flops 52305920 | bytes 3819136 | tf_op jit(solution)/shard_map/al,fxlz->fxaz/dot_general | solution.py:312
  47.4 0.0 copy-start.2
  47.4 1.0 %pad_maximum_fusion.3.refs_1_ = f32[2,5,16,5,128]{4,3,2,1,0:T(8,128)} fusion(f32[1,5,16,5,128]{4,3,2,1,0:T(8,128)S(1)} %get-tuple-element.62, f32[1,5,16,5,128]{4,3,2,1,0:T(8,128)S(1)} %get-tuple-element.61), kind=kLoop, calls=%fused_computation.35 | loop fusion | flops 102400 | bytes 819200 | tf_op jit(solution)/shard_map/stack | solution.py:196
  48.4 13.4 %shard_map.93 = (f32[2,5,5,16,128]{4,3,2,1,0:T(8,128)}, f32[2,5,16,5,128]{4,3,2,1,0:T(8,128)}, f32[2,2,5,5,5,128]{5,4,3,2,1,0:T(8,128)}) custom-call(f32[5,16,16,128]{3,2,1,0:T(8,128)} %copy-done.2, f32[2,5,16,5,128]{4,3,2,1,0:T(8,128)} %pad_maximum_fusion.3.refs_1_), custom_call_target="tpu_custom_call" | custom-call | tf_op jit(solution)/shard_map/pallas_call | solution.py:121
  61.9 0.0 copy-start.3
  61.9 1.2 %slice_bitcast_fusion.3 = (f32[5,16,5,128]{3,2,1,0:T(8,128)S(1)}, f32[5,16,5,128]{3,2,1,0:T(8,128)S(1)}) fusion(f32[2,5,16,5,128]{4,3,2,1,0:T(8,128)} %get-tuple-element.30), kind=kLoop, calls=%fused_computation.47 | loop fusion | bytes 819200 | tf_op jit(solution)/shard_map/squeeze | solution.py:223
  63.2 0.0 copy-done.8
  63.2 0.2 copy-done.3
  63.4 0.4 maximum_maximum_fusion
  63.8 0.3 copy-done.13
  64.1 2.6 %fusion = f32[5,26,128,16]{2,3,1,0:T(8,128)S(1)} fusion(f32[16,26,1,1]{1,0,3,2:T(8,128)S(1)} %copy-done.13, f32[5,26,26,128]{3,2,1,0:T(8,128)S(1)} %maximum_maximum_fusion), kind=kOutput, calls=%fused_computation.1 | convolution fusion | flops 83066880 | bytes 2797184 | tf_op jit(solution)/shard_map/al,flyz->fayz/dot_general | solution.py:312
  66.7 2.0 %fusion.13.refs_0_ = f32[5,16,16,128]{3,2,1,0:T(8,128)} fusion(f32[16,26,1,1]{1,0,3,2:T(8,128)S(1)} %copy-done.13, f32[5,26,128,16]{2,3,1,0:T(8,128)S(1)} %fusion), kind=kOutput, calls=%fused_computation.14 | convolution fusion | flops 51118080 | bytes 1721984 | tf_op jit(solution)/shard_map/al,fxlz->fxaz/dot_general | solution.py:312
  68.7 9.0 %shard_map.94 = f32[5,16,16,128]{3,2,1,0:T(8,128)} custom-call(f32[5,16,16,128]{3,2,1,0:T(8,128)} %fusion.13.refs_0_, f32[128,128]{1,0:T(8,128)} %constant.40.refs_1_, f32[128,8]{1,0:T(8,128)} %constant.42.refs_2_, f32[128,8]{1,0:T(8,128)} %constant.44.refs_3_), custom_call_target="tpu_custom_call" | custom-call | tf_op jit(solution)/shard_map/pallas_call | solution.py:121
  77.7 2.0 %copy.46 = f32[5,16,16,128]{3,2,1,0:T(8,128)} copy(f32[5,16,16,128]{3,2,1,0:T(8,128)} %shard_map.94) | data formatting | bytes 1310720
  (24 shorter events, 0.2 us)
Async XLA Ops:
  0.0 2.1 %copy-start.1 = (f32[5,16,16,128]{3,2,1,0:T(8,128)S(1)}, f32[5,16,16,128]{3,2,1,0:T(8,128)}, u32[]{:S(2)}) copy-start(f32[5,16,16,128]{3,2,1,0:T(8,128)} %param.9) | copy-start | bytes 1966084
  3.8 18.2 %copy-start.12 = (f32[16,26,1,1]{1,0,3,2:T(8,128)S(1)}, f32[16,26,1,1]{1,0,3,2:T(8,128)}, u32[]{:S(2)}) copy-start(f32[16,26,1,1]{1,0,3,2:T(8,128)} %constant.45) | copy-start | bytes 4996
  22.1 1.2 %copy-start.14 = (f32[4,16,5,128]{3,2,1,0:T(8,128)S(1)}, f32[4,16,5,128]{3,2,1,0:T(8,128)}, u32[]{:S(2)}) copy-start(f32[4,16,5,128]{3,2,1,0:T(8,128)} %get-tuple-element.20) | copy-start | bytes 491524
  22.1 1.2 %copy-start.15 = (f32[4,16,5,128]{3,2,1,0:T(8,128)S(1)}, f32[4,16,5,128]{3,2,1,0:T(8,128)}, u32[]{:S(2)}) copy-start(f32[4,16,5,128]{3,2,1,0:T(8,128)} %get-tuple-element.21) | copy-start | bytes 491524
  23.1 1.3 %copy-start = (f32[3,3,16,16,128]{4,3,2,1,0:T(8,128)S(1)}, f32[3,3,16,16,128]{4,3,2,1,0:T(8,128)}, u32[]{:S(2)}) copy-start(f32[3,3,16,16,128]{4,3,2,1,0:T(8,128)} %param.10) | copy-start | bytes 3538948
  23.1 1.3 %copy-start.4 = (f32[16,16,128]{2,1,0:T(8,128)S(1)}, f32[16,16,128]{2,1,0:T(8,128)}, u32[]{:S(2)}) copy-start(f32[16,16,128]{2,1,0:T(8,128)} %param.11) | copy-start | bytes 393220
  23.1 1.4 %copy-start.6 = (f32[4,16,16,128]{3,2,1,0:T(8,128)S(1)}, f32[4,16,16,128]{3,2,1,0:T(8,128)}, u32[]{:S(2)}) copy-start(f32[4,16,16,128]{3,2,1,0:T(8,128)} %get-tuple-element.22) | copy-start | bytes 1572868
  28.2 15.5 %copy-start.5 = (f32[5,16,16,128]{3,2,1,0:T(8,128)S(1)}, f32[5,16,16,128]{3,2,1,0:T(8,128)}, u32[]{:S(2)}) copy-start(f32[5,16,16,128]{3,2,1,0:T(8,128)} %get-tuple-element.47.refs_0_) | copy-start | bytes 1966084
  44.8 1.3 %copy-start.7 = (f32[5,16,16,128]{3,2,1,0:T(8,128)S(1)}, f32[5,16,16,128]{3,2,1,0:T(8,128)}, u32[]{:S(2)}) copy-start(f32[5,16,16,128]{3,2,1,0:T(8,128)} %get-tuple-element.27) | copy-start | bytes 1966084
  44.8 1.3 %copy-start.10 = (f32[5,16,5,128]{3,2,1,0:T(8,128)S(1)}, f32[5,16,5,128]{3,2,1,0:T(8,128)}, u32[]{:S(2)}) copy-start(f32[5,16,5,128]{3,2,1,0:T(8,128)} %get-tuple-element.25) | copy-start | bytes 614404
  44.8 1.3 %copy-start.11 = (f32[5,16,5,128]{3,2,1,0:T(8,128)S(1)}, f32[5,16,5,128]{3,2,1,0:T(8,128)}, u32[]{:S(2)}) copy-start(f32[5,16,5,128]{3,2,1,0:T(8,128)} %get-tuple-element.26) | copy-start | bytes 614404
  47.4 1.1 %copy-start.2 = (f32[5,16,16,128]{3,2,1,0:T(8,128)}, f32[5,16,16,128]{3,2,1,0:T(8,128)S(1)}, u32[]{:S(2)}) copy-start(f32[5,16,16,128]{3,2,1,0:T(8,128)S(1)} %fusion.28.refs_0_) | copy-start | bytes 1966084
  61.8 1.3 %copy-start.9 = (f32[2,2,5,5,5,128]{5,4,3,2,1,0:T(8,128)S(1)}, f32[2,2,5,5,5,128]{5,4,3,2,1,0:T(8,128)}, u32[]{:S(2)}) copy-start(f32[2,2,5,5,5,128]{5,4,3,2,1,0:T(8,128)} %get-tuple-element.28) | copy-start | bytes 768004
  61.9 1.3 %copy-start.8 = (f32[2,5,5,16,128]{4,3,2,1,0:T(8,128)S(1)}, f32[2,5,5,16,128]{4,3,2,1,0:T(8,128)}, u32[]{:S(2)}) copy-start(f32[2,5,5,16,128]{4,3,2,1,0:T(8,128)} %get-tuple-element.29) | copy-start | bytes 1228804
  61.9 1.5 %copy-start.3 = (f32[5,16,16,128]{3,2,1,0:T(8,128)S(1)}, f32[5,16,16,128]{3,2,1,0:T(8,128)}, u32[]{:S(2)}) copy-start(f32[5,16,16,128]{3,2,1,0:T(8,128)} %copy-done.2) | copy-start | bytes 1966084
  63.4 0.7 copy-start.13

commit v10 on v9

--- a/solution.py
+++ b/solution.py
@@ -38,10 +38,6 @@
             lax.rem(here[slot] + offset[slot] + sizes[slot], sizes[slot]) for slot in range(3)
         )
 
-    if zeta:
-        fields, length_x, length_y, depth = block_ref.shape
-        rows = fields * length_x * length_y
-        turned[...] = block_ref[...].reshape(rows, depth).T
     offsets = [route[0] for route in routes] + ([(0, 0, 1), (0, 0, -1)] if zeta else [])
     partners = []
     for offset in offsets:
@@ -51,6 +47,10 @@
     barrier = pltpu.get_barrier_semaphore()
     for offset in partners:
         pl.semaphore_signal(barrier, inc=1, device_id=device(offset), device_id_type=MESH)
+    if zeta:
+        fields, length_x, length_y, depth = block_ref.shape
+        rows = fields * length_x * length_y
+        turned[...] = block_ref[...].reshape(rows, depth).T
     pl.semaphore_wait(barrier, len(partners))
     copies = []
     for index, (offset, source, source_at, target, target_at) in enumerate(routes):

time: 80.5 us -> 79.8 us (level)
  no operation moved by 1% of the time
where the time goes in v10:
time: 79.8 us; the launch traced here: 79 us
  Pallas kernels  54.3 us (68%)
  other arithmetic  9 us (11%)
  matrix products  8.98 us (11%)
  local copies, waits for them, and re-layouts  6.34 us (8%)
    pallas_call x4, Pallas kernels, exchange(): pl.pallas_call(functools.partial(exchange_kernel, tuple(routes), sizes, l...  54.3 us
    dot_general x6, matrix products, sweep_lines(): jnp.einsum(line_forms[dim], matrix, padded, precision=lax.Precision.HIGHEST)  8.98 us
    unnamed x33, local copies, waits for them, and re-layouts  2.88 us
    concatenate x2, other arithmetic, exchange_faces(): padded.append(jnp.concatenate([before, value, after], axis=dim))  2.18 us
    concatenate x2, other arithmetic, local(): jnp.concatenate([fluid_speed_vector, thermal_level[None]], axis=0)  1.68 us

profile of v10, /device:TPU:1, one launch (start us, length us, event | category | flops | bytes accessed | tf_op | source)
XLA Modules:
  0.0 79.0 jit_solution(7437490169846025568)
XLA Ops:
  0.0 1.0 %slice_bitcast_fusion.26 = f32[16,16,128]{2,1,0:T(8,128)S(1)} fusion(f32[5,16,16,128]{3,2,1,0:T(8,128)} %param.9), kind=kLoop, calls=%fused_computation.160 | loop fusion | bytes 262144 | tf_op jit(solution)/shard_map/div | solution.py:329
  1.0 1.1 %multiply_reduce_fusion = (f32[16,16,128]{2,1,0:T(8,128)S(1)}, f32[3,16,16,128]{3,2,1,0:T(8,128)S(1)}) fusion(f32[5,16,16,128]{3,2,1,0:T(8,128)} %param.9, f32[16,16,128]{2,1,0:T(8,128)S(1)} %slice_bitcast_fusion.26), kind=kLoop, calls=%fused_computation.42 | loop fusion | flops 262144 | bytes 1048576 | tf_op jit(solution)/shard_map/reduce_sum | solution.py:331
  2.1 0.0 copy-done.1
  2.1 0.9 %fusion.41 = (f32[4,16,5,128]{3,2,1,0:T(8,128)}, f32[4,16,5,128]{3,2,1,0:T(8,128)}) fusion(f32[3,16,16,128]{3,2,1,0:T(8,128)S(1)} %get-tuple-element.44, f32[1,16,16,128]{3,2,1,0:T(8,128)S(1)} %get-tuple-element.68), kind=kLoop, calls=%fused_computation.49 | loop fusion | flops 81920 | bytes 851968 | tf_op jit(solution)/shard_map/concatenate | solution.py:390
  3.0 0.8 %pad_maximum_fusion.1.refs_0_.refs_3_ = f32[4,16,16,128]{3,2,1,0:T(8,128)} fusion(f32[1,16,16,128]{3,2,1,0:T(8,128)S(1)} %get-tuple-element.68, f32[3,16,16,128]{3,2,1,0:T(8,128)S(1)} %get-tuple-element.44), kind=kLoop, calls=%fused_computation.33 | loop fusion | flops 131072 | bytes 1048576 | tf_op jit(solution)/shard_map/concatenate | solution.py:390
  3.8 16.9 %shard_map.91 = (f32[4,5,16,128]{3,2,1,0:T(8,128)}, f32[4,5,16,128]{3,2,1,0:T(8,128)}, f32[4,16,5,128]{3,2,1,0:T(8,128)}, f32[4,16,5,128]{3,2,1,0:T(8,128)}, f32[4,16,16,128]{3,2,1,0:T(8,128)}) custom-call(f32[4,16,16,128]{3,2,1,0:T(8,128)} %pad_maximum_fusion.1.refs_0_.refs_3_, f32[4,16,5,128]{3,2,1,0:T(8,128)} %get-tuple-element.71.refs_1_, ...), custom_call_target="tpu_custom_call" | custom-call | tf_op jit(solution)/shard_map/pallas_call | solution.py:121
  20.7 1.1 %pad_maximum_fusion.2 = f32[4,26,16,128]{3,2,1,0:T(8,128)S(1)} fusion(f32[4,5,16,128]{3,2,1,0:T(8,128)} %get-tuple-element.19, f32[1,16,16,128]{3,2,1,0:T(8,128)S(1)} %get-tuple-element.68, f32[3,16,16,128]{3,2,1,0:T(8,128)S(1)} %get-tuple-element.44, f32[4,5,16,128]{3,2,1,0:T(8,128)} %get-tuple-element.18), kind=kLoop, calls=%fused_computation.34 | loop fusion | flops 638976 | bytes 1703936 | tf_op jit(solution)/shard_map/concatenate | solution.py:188
  21.8 0.0 copy-done.12
  21.8 0.0 copy-start.14
  21.8 1.0 %fusion.38 = f32[4,16,128,16]{2,3,1,0:T(8,128)S(1)} fusion(f32[16,26,1,1]{1,0,3,2:T(8,128)S(1)} %copy-done.12, f32[4,26,16,128]{3,2,1,0:T(8,128)S(1)} %pad_maximum_fusion.2), kind=kOutput, calls=%fused_computation.29 | convolution fusion | flops 40894464 | bytes 1377920 | tf_op jit(solution)/shard_map/al,flyz->fayz/dot_general | solution.py:312
  22.8 0.0 copy-start
  22.8 0.0 copy-start.4
  22.8 0.2 copy.32
  23.0 0.9 %convolution_bitcast_fusion = f32[4,16,16,128]{3,2,1,0:T(8,128)S(1)} fusion(f32[16,26,1,1]{1,0,3,2:T(8,128)S(1)} %copy-done.12, f32[4,16,5,128]{3,2,1,0:T(8,128)S(1)} %copy-done.15, f32[1,16,16,128]{3,2,1,0:T(8,128)S(1)} %get-tuple-element.68, f32[3,16,16,128]{3,2,1,0:T(8,128)S(1)} %get-tuple-element.44, f32[4,16,5,128]{3,2,1,0:T(8,128)S(1)} %copy-done.14), kind=kOutput, calls=%fused_computation.20 | convolution fusion | flops 41533440 | bytes 1377920 | tf_op jit(solution)/shard_map/al,fxlz->fxaz/dot_general | solution.py:312
  23.9 0.1 copy-done
  24.1 0.0 copy-done.4
  24.1 0.2 copy-done.6
  24.3 0.2 bitcast_dynamic-update-slice_fusion.11
  24.5 0.1 bitcast_dynamic-update-slice_fusion.10
  24.6 0.1 bitcast_dynamic-update-slice_fusion.9
  24.7 0.2 bitcast_dynamic-update-slice_fusion.8
  24.9 0.1 bitcast_dynamic-update-slice_fusion.6
  25.0 0.1 bitcast_dynamic-update-slice_fusion.5
  25.2 0.1 bitcast_dynamic-update-slice_fusion.4
  25.3 0.1 bitcast_dynamic-update-slice_fusion.1
  25.4 0.1 bitcast_dynamic-update-slice_fusion
  25.5 0.1 slice_bitcast_fusion.23
  25.6 1.4 %multiply_add_fusion = (f32[5,16,16,128]{3,2,1,0:T(8,128)}, f32[5,16,16,128]{3,2,1,0:T(8,128)S(1)}, f32[5,16,16,128]{3,2,1,0:T(8,128)}) fusion(f32[5,16,16,128]{3,2,1,0:T(8,128)S(1)} %bitcast_dynamic-update-slice_fusion, f32[5,16,16,128]{3,2,1,0:T(8,128)S(1)} %bitcast_dynamic-update-slice_fusion.4, f32[5,16,16,128]{3,2,1,0:T(8,128)S(1)} %get-tuple-element.65, ...), kind=kLoop, calls=%fused_computation.36 | loop fusion | flops 2457600 | bytes 5111808 | tf_op jit(solution)/shard_map/add | solution.py:376
  27.0 0.9 %fusion.99 = (f32[5,16,5,128]{3,2,1,0:T(8,128)}, f32[5,16,5,128]{3,2,1,0:T(8,128)}) fusion(f32[5,16,16,128]{3,2,1,0:T(8,128)S(1)} %get-tuple-element.46), kind=kLoop, calls=%fused_computation.171 | loop fusion | bytes 819200 | tf_op jit(solution)/shard_map/slice | solution.py:162
  27.9 15.2 %shard_map.92 = (f32[5,5,16,128]{3,2,1,0:T(8,128)}, f32[5,5,16,128]{3,2,1,0:T(8,128)}, f32[5,16,5,128]{3,2,1,0:T(8,128)}, f32[5,16,5,128]{3,2,1,0:T(8,128)}, f32[5,16,16,128]{3,2,1,0:T(8,128)}) custom-call(f32[5,16,16,128]{3,2,1,0:T(8,128)} %get-tuple-element.47.refs_0_, f32[5,16,5,128]{3,2,1,0:T(8,128)} %get-tuple-element.64.refs_1_, ...), custom_call_target="tpu_custom_call" | custom-call | tf_op jit(solution)/shard_map/pallas_call | solution.py:121
  43.2 1.1 %pad_maximum_fusion = f32[5,26,16,128]{3,2,1,0:T(8,128)S(1)} fusion(f32[5,5,16,128]{3,2,1,0:T(8,128)} %get-tuple-element.24, f32[5,16,16,128]{3,2,1,0:T(8,128)S(1)} %copy-done.5, f32[5,5,16,128]{3,2,1,0:T(8,128)} %get-tuple-element.23), kind=kLoop, calls=%fused_computation.21 | loop fusion | flops 532480 | bytes 2129920 | tf_op jit(solution)/shard_map/concatenate | solution.py:188
  44.3 1.2 %fusion.11 = f32[5,16,128,16]{2,3,1,0:T(8,128)S(1)} fusion(f32[16,26,1,1]{1,0,3,2:T(8,128)S(1)} %copy-done.12, f32[5,26,16,128]{3,2,1,0:T(8,128)S(1)} %pad_maximum_fusion), kind=kOutput, calls=%fused_computation.12 | convolution fusion | flops 51118080 | bytes 1721984 | tf_op jit(solution)/shard_map/al,flyz->fayz/dot_general | solution.py:312
  45.6 1.3 %fusion.28.refs_0_ = f32[5,16,16,128]{3,2,1,0:T(8,128)S(1)} fusion(f32[5,16,16,128]{3,2,1,0:T(8,128)S(1)} %copy-done.1, f32[5,16,16,128]{3,2,1,0:T(8,128)S(1)} %copy-done.7, f32[16,26,1,1]{1,0,3,2:T(8,128)S(1)} %copy-done.12, f32[5,16,5,128]{3,2,1,0:T(8,128)S(1)} %copy-done.11, f32[5,16,16,128]{3,2,1,0:T(8,128)S(1)} %get-tuple-element.46, ...), kind=kOutput, calls=%fused_computation.19 | convolution fusion | flops 52305920 | bytes 3819136 | tf_op jit(solution)/shard_map/al,fxlz->fxaz/dot_general | solution.py:312
  46.9 0.0 copy-start.2
  47.0 1.0 %pad_maximum_fusion.3.refs_1_ = f32[2,5,16,5,128]{4,3,2,1,0:T(8,128)} fusion(f32[1,5,16,5,128]{4,3,2,1,0:T(8,128)S(1)} %get-tuple-element.62, f32[1,5,16,5,128]{4,3,2,1,0:T(8,128)S(1)} %get-tuple-element.61), kind=kLoop, calls=%fused_computation.35 | loop fusion | flops 102400 | bytes 819200 | tf_op jit(solution)/shard_map/stack | solution.py:196
  48.0 13.4 %shard_map.93 = (f32[2,5,5,16,128]{4,3,2,1,0:T(8,128)}, f32[2,5,16,5,128]{4,3,2,1,0:T(8,128)}, f32[2,2,5,5,5,128]{5,4,3,2,1,0:T(8,128)}) custom-call(f32[5,16,16,128]{3,2,1,0:T(8,128)} %copy-done.2, f32[2,5,16,5,128]{4,3,2,1,0:T(8,128)} %pad_maximum_fusion.3.refs_1_), custom_call_target="tpu_custom_call" | custom-call | tf_op jit(solution)/shard_map/pallas_call | solution.py:121
  61.4 0.0 copy-start.9
  61.4 0.0 copy-start.8
  61.4 0.0 copy-start.3
  61.4 1.2 %slice_bitcast_fusion.3 = (f32[5,16,5,128]{3,2,1,0:T(8,128)S(1)}, f32[5,16,5,128]{3,2,1,0:T(8,128)S(1)}) fusion(f32[2,5,16,5,128]{4,3,2,1,0:T(8,128)} %get-tuple-element.30), kind=kLoop, calls=%fused_computation.47 | loop fusion | bytes 819200 | tf_op jit(solution)/shard_map/squeeze | solution.py:223
  62.7 0.0 copy-done.8
  62.8 0.2 copy-done.3
  62.9 0.4 maximum_maximum_fusion
  63.3 0.3 copy-done.13
  63.6 2.6 %fusion = f32[5,26,128,16]{2,3,1,0:T(8,128)S(1)} fusion(f32[16,26,1,1]{1,0,3,2:T(8,128)S(1)} %copy-done.13, f32[5,26,26,128]{3,2,1,0:T(8,128)S(1)} %maximum_maximum_fusion), kind=kOutput, calls=%fused_computation.1 | convolution fusion | flops 83066880 | bytes 2797184 | tf_op jit(solution)/shard_map/al,flyz->fayz/dot_general | solution.py:312
  66.2 2.0 %fusion.13.refs_0_ = f32[5,16,16,128]{3,2,1,0:T(8,128)} fusion(f32[16,26,1,1]{1,0,3,2:T(8,128)S(1)} %copy-done.13, f32[5,26,128,16]{2,3,1,0:T(8,128)S(1)} %fusion), kind=kOutput, calls=%fused_computation.14 | convolution fusion | flops 51118080 | bytes 1721984 | tf_op jit(solution)/shard_map/al,fxlz->fxaz/dot_general | solution.py:312
  68.3 8.7 %shard_map.94 = f32[5,16,16,128]{3,2,1,0:T(8,128)} custom-call(f32[5,16,16,128]{3,2,1,0:T(8,128)} %fusion.13.refs_0_, f32[128,128]{1,0:T(8,128)} %constant.40.refs_1_, f32[128,8]{1,0:T(8,128)} %constant.42.refs_2_, f32[128,8]{1,0:T(8,128)} %constant.44.refs_3_), custom_call_target="tpu_custom_call" | custom-call | tf_op jit(solution)/shard_map/pallas_call | solution.py:121
  77.0 2.0 %copy.46 = f32[5,16,16,128]{3,2,1,0:T(8,128)} copy(f32[5,16,16,128]{3,2,1,0:T(8,128)} %shard_map.94) | data formatting | bytes 1310720
  (24 shorter events, 0.2 us)
Async XLA Ops:
  0.0 2.1 %copy-start.1 = (f32[5,16,16,128]{3,2,1,0:T(8,128)S(1)}, f32[5,16,16,128]{3,2,1,0:T(8,128)}, u32[]{:S(2)}) copy-start(f32[5,16,16,128]{3,2,1,0:T(8,128)} %param.9) | copy-start | bytes 1966084
  3.8 18.0 %copy-start.12 = (f32[16,26,1,1]{1,0,3,2:T(8,128)S(1)}, f32[16,26,1,1]{1,0,3,2:T(8,128)}, u32[]{:S(2)}) copy-start(f32[16,26,1,1]{1,0,3,2:T(8,128)} %constant.45) | copy-start | bytes 4996
  21.8 1.2 %copy-start.14 = (f32[4,16,5,128]{3,2,1,0:T(8,128)S(1)}, f32[4,16,5,128]{3,2,1,0:T(8,128)}, u32[]{:S(2)}) copy-start(f32[4,16,5,128]{3,2,1,0:T(8,128)} %get-tuple-element.20) | copy-start | bytes 491524
  21.8 1.2 %copy-start.15 = (f32[4,16,5,128]{3,2,1,0:T(8,128)S(1)}, f32[4,16,5,128]{3,2,1,0:T(8,128)}, u32[]{:S(2)}) copy-start(f32[4,16,5,128]{3,2,1,0:T(8,128)} %get-tuple-element.21) | copy-start | bytes 491524
  22.8 1.3 %copy-start = (f32[3,3,16,16,128]{4,3,2,1,0:T(8,128)S(1)}, f32[3,3,16,16,128]{4,3,2,1,0:T(8,128)}, u32[]{:S(2)}) copy-start(f32[3,3,16,16,128]{4,3,2,1,0:T(8,128)} %param.10) | copy-start | bytes 3538948
  22.8 1.3 %copy-start.4 = (f32[16,16,128]{2,1,0:T(8,128)S(1)}, f32[16,16,128]{2,1,0:T(8,128)}, u32[]{:S(2)}) copy-start(f32[16,16,128]{2,1,0:T(8,128)} %param.11) | copy-start | bytes 393220
  22.8 1.4 %copy-start.6 = (f32[4,16,16,128]{3,2,1,0:T(8,128)S(1)}, f32[4,16,16,128]{3,2,1,0:T(8,128)}, u32[]{:S(2)}) copy-start(f32[4,16,16,128]{3,2,1,0:T(8,128)} %get-tuple-element.22) | copy-start | bytes 1572868
  27.9 15.2 %copy-start.5 = (f32[5,16,16,128]{3,2,1,0:T(8,128)S(1)}, f32[5,16,16,128]{3,2,1,0:T(8,128)}, u32[]{:S(2)}) copy-start(f32[5,16,16,128]{3,2,1,0:T(8,128)} %get-tuple-element.47.refs_0_) | copy-start | bytes 1966084
  44.3 1.3 %copy-start.7 = (f32[5,16,16,128]{3,2,1,0:T(8,128)S(1)}, f32[5,16,16,128]{3,2,1,0:T(8,128)}, u32[]{:S(2)}) copy-start(f32[5,16,16,128]{3,2,1,0:T(8,128)} %get-tuple-element.27) | copy-start | bytes 1966084
  44.3 1.3 %copy-start.10 = (f32[5,16,5,128]{3,2,1,0:T(8,128)S(1)}, f32[5,16,5,128]{3,2,1,0:T(8,128)}, u32[]{:S(2)}) copy-start(f32[5,16,5,128]{3,2,1,0:T(8,128)} %get-tuple-element.25) | copy-start | bytes 614404
  44.3 1.3 %copy-start.11 = (f32[5,16,5,128]{3,2,1,0:T(8,128)S(1)}, f32[5,16,5,128]{3,2,1,0:T(8,128)}, u32[]{:S(2)}) copy-start(f32[5,16,5,128]{3,2,1,0:T(8,128)} %get-tuple-element.26) | copy-start | bytes 614404
  46.9 1.1 %copy-start.2 = (f32[5,16,16,128]{3,2,1,0:T(8,128)}, f32[5,16,16,128]{3,2,1,0:T(8,128)S(1)}, u32[]{:S(2)}) copy-start(f32[5,16,16,128]{3,2,1,0:T(8,128)S(1)} %fusion.28.refs_0_) | copy-start | bytes 1966084
  61.4 1.3 %copy-start.9 = (f32[2,2,5,5,5,128]{5,4,3,2,1,0:T(8,128)S(1)}, f32[2,2,5,5,5,128]{5,4,3,2,1,0:T(8,128)}, u32[]{:S(2)}) copy-start(f32[2,2,5,5,5,128]{5,4,3,2,1,0:T(8,128)} %get-tuple-element.28) | copy-start | bytes 768004
  61.4 1.3 %copy-start.8 = (f32[2,5,5,16,128]{4,3,2,1,0:T(8,128)S(1)}, f32[2,5,5,16,128]{4,3,2,1,0:T(8,128)}, u32[]{:S(2)}) copy-start(f32[2,5,5,16,128]{4,3,2,1,0:T(8,128)} %get-tuple-element.29) | copy-start | bytes 1228804
  61.4 1.5 %copy-start.3 = (f32[5,16,16,128]{3,2,1,0:T(8,128)S(1)}, f32[5,16,16,128]{3,2,1,0:T(8,128)}, u32[]{:S(2)}) copy-start(f32[5,16,16,128]{3,2,1,0:T(8,128)} %copy-done.2) | copy-start | bytes 1966084
  62.9 0.7 copy-start.13

commit v11 on v10

--- a/solution.py
+++ b/solution.py
@@ -405,9 +405,9 @@
     divergence = divergence + sweep_lines(padded[1], derive[1], 2)
     divergence = divergence + padded[2]
     sectioned = conserved_solution - step_duration * jacobian * divergence
-    result = sweep_lines(exchange_plane(sectioned, 2), smooth[0], 1)
+    result = sweep_zeta(sectioned, smooth[2], 4)
+    result = sweep_lines(exchange_plane(result, 2), smooth[0], 1)
     result = sweep_lines(result, smooth[1], 2)
-    result = sweep_zeta(result, smooth[2], 4)
     return result
 
 

time: 79.8 us -> 80.3 us (level)
  Pallas kernels: 54.3 us -> 55.6 us
  local copies, waits for them, and re-layouts: 6.34 us -> 5.43 us
    unnamed x33 -> x30, local copies, waits for them, and re-layouts: 2.88 us -> 0.9 us
    pallas_call x4, Pallas kernels: 54.3 us -> 55.6 us  [exchange(): pl.pallas_call(functools.partial(exchange_kernel, tuple(routes), sizes, l...]
    another operation x1, local copies, waits for them, and re-layouts: 0.05 us -> 1.12 us  [exchange_plane(): jnp.stack([lax.slice_in_dim(value, length_y - WIDTH, length_y, axis=2), l...]
where the time goes in v11:
time: 80.3 us; the launch traced here: 80 us
  Pallas kernels  55.6 us (69%)
  matrix products  9.65 us (12%)
  other arithmetic  8.9 us (11%)
  local copies, waits for them, and re-layouts  5.43 us (7%)
    pallas_call x4, Pallas kernels, exchange(): pl.pallas_call(functools.partial(exchange_kernel, tuple(routes), sizes, l...  55.6 us
    dot_general x6, matrix products, sweep_lines(): jnp.einsum(line_forms[dim], matrix, padded, precision=lax.Precision.HIGHEST)  9.65 us
    concatenate x2, other arithmetic, exchange_faces(): padded.append(jnp.concatenate([before, value, after], axis=dim))  2.18 us
    concatenate x2, other arithmetic, local(): jnp.concatenate([fluid_speed_vector, thermal_level[None]], axis=0)  1.69 us

profile of v11, /device:TPU:1, one launch (start us, length us, event | category | flops | bytes accessed | tf_op | source)
XLA Modules:
  0.0 80.0 jit_solution(3447834592423408260)
XLA Ops:
  0.0 1.0 %slice_bitcast_fusion.26 = f32[16,16,128]{2,1,0:T(8,128)S(1)} fusion(f32[5,16,16,128]{3,2,1,0:T(8,128)} %param.9), kind=kLoop, calls=%fused_computation.160 | loop fusion | bytes 262144 | tf_op jit(solution)/shard_map/div | solution.py:329
  1.0 1.1 %multiply_reduce_fusion = (f32[16,16,128]{2,1,0:T(8,128)S(1)}, f32[3,16,16,128]{3,2,1,0:T(8,128)S(1)}) fusion(f32[5,16,16,128]{3,2,1,0:T(8,128)} %param.9, f32[16,16,128]{2,1,0:T(8,128)S(1)} %slice_bitcast_fusion.26), kind=kLoop, calls=%fused_computation.42 | loop fusion | flops 262144 | bytes 1048576 | tf_op jit(solution)/shard_map/reduce_sum | solution.py:331
  2.1 0.0 copy-done.1
  2.1 0.9 %fusion.41 = (f32[4,16,5,128]{3,2,1,0:T(8,128)}, f32[4,16,5,128]{3,2,1,0:T(8,128)}) fusion(f32[3,16,16,128]{3,2,1,0:T(8,128)S(1)} %get-tuple-element.44, f32[1,16,16,128]{3,2,1,0:T(8,128)S(1)} %get-tuple-element.68), kind=kLoop, calls=%fused_computation.49 | loop fusion | flops 81920 | bytes 851968 | tf_op jit(solution)/shard_map/concatenate | solution.py:390
  3.0 0.8 %pad_maximum_fusion.1.refs_0_.refs_3_ = f32[4,16,16,128]{3,2,1,0:T(8,128)} fusion(f32[1,16,16,128]{3,2,1,0:T(8,128)S(1)} %get-tuple-element.68, f32[3,16,16,128]{3,2,1,0:T(8,128)S(1)} %get-tuple-element.44), kind=kLoop, calls=%fused_computation.33 | loop fusion | flops 131072 | bytes 1048576 | tf_op jit(solution)/shard_map/concatenate | solution.py:390
  3.8 16.9 %shard_map.91 = (f32[4,5,16,128]{3,2,1,0:T(8,128)}, f32[4,5,16,128]{3,2,1,0:T(8,128)}, f32[4,16,5,128]{3,2,1,0:T(8,128)}, f32[4,16,5,128]{3,2,1,0:T(8,128)}, f32[4,16,16,128]{3,2,1,0:T(8,128)}) custom-call(f32[4,16,16,128]{3,2,1,0:T(8,128)} %pad_maximum_fusion.1.refs_0_.refs_3_, f32[4,16,5,128]{3,2,1,0:T(8,128)} %get-tuple-element.71.refs_1_, ...), custom_call_target="tpu_custom_call" | custom-call | tf_op jit(solution)/shard_map/pallas_call | solution.py:121
  20.7 1.1 %pad_maximum_fusion.2 = f32[4,26,16,128]{3,2,1,0:T(8,128)S(1)} fusion(f32[4,5,16,128]{3,2,1,0:T(8,128)} %get-tuple-element.19, f32[1,16,16,128]{3,2,1,0:T(8,128)S(1)} %get-tuple-element.68, f32[3,16,16,128]{3,2,1,0:T(8,128)S(1)} %get-tuple-element.44, f32[4,5,16,128]{3,2,1,0:T(8,128)} %get-tuple-element.18), kind=kLoop, calls=%fused_computation.34 | loop fusion | flops 638976 | bytes 1703936 | tf_op jit(solution)/shard_map/concatenate | solution.py:188
  21.8 0.0 copy-done.11
  21.8 0.0 copy-start.13
  21.8 0.0 copy-start.14
  21.8 1.0 %fusion.38 = f32[4,16,128,16]{2,3,1,0:T(8,128)S(1)} fusion(f32[16,26,1,1]{1,0,3,2:T(8,128)S(1)} %copy-done.11, f32[4,26,16,128]{3,2,1,0:T(8,128)S(1)} %pad_maximum_fusion.2), kind=kOutput, calls=%fused_computation.29 | convolution fusion | flops 40894464 | bytes 1377920 | tf_op jit(solution)/shard_map/al,flyz->fayz/dot_general | solution.py:312
  22.8 0.0 copy-start
  22.8 0.0 copy-start.3
  22.8 0.0 copy-start.5
  22.9 0.2 copy.32
  23.0 0.0 copy-done.13
  23.0 0.9 %convolution_bitcast_fusion = f32[4,16,16,128]{3,2,1,0:T(8,128)S(1)} fusion(f32[16,26,1,1]{1,0,3,2:T(8,128)S(1)} %copy-done.11, f32[4,16,5,128]{3,2,1,0:T(8,128)S(1)} %copy-done.14, f32[1,16,16,128]{3,2,1,0:T(8,128)S(1)} %get-tuple-element.68, f32[3,16,16,128]{3,2,1,0:T(8,128)S(1)} %get-tuple-element.44, f32[4,16,5,128]{3,2,1,0:T(8,128)S(1)} %copy-done.13), kind=kOutput, calls=%fused_computation.20 | convolution fusion | flops 41533440 | bytes 1377920 | tf_op jit(solution)/shard_map/al,fxlz->fxaz/dot_general | solution.py:312
  23.9 0.2 copy-done
  24.1 0.2 copy-done.5
  24.3 0.2 bitcast_dynamic-update-slice_fusion.11
  24.5 0.1 bitcast_dynamic-update-slice_fusion.10
  24.6 0.1 bitcast_dynamic-update-slice_fusion.9
  24.7 0.2 bitcast_dynamic-update-slice_fusion.8
  24.9 0.1 bitcast_dynamic-update-slice_fusion.6
  25.0 0.1 bitcast_dynamic-update-slice_fusion.5
  25.2 0.1 bitcast_dynamic-update-slice_fusion.4
  25.3 0.1 bitcast_dynamic-update-slice_fusion.1
  25.4 0.1 bitcast_dynamic-update-slice_fusion
  25.5 0.1 slice_bitcast_fusion.23
  25.6 1.4 %multiply_add_fusion = (f32[5,16,16,128]{3,2,1,0:T(8,128)}, f32[5,16,16,128]{3,2,1,0:T(8,128)S(1)}, f32[5,16,16,128]{3,2,1,0:T(8,128)}) fusion(f32[5,16,16,128]{3,2,1,0:T(8,128)S(1)} %bitcast_dynamic-update-slice_fusion, f32[5,16,16,128]{3,2,1,0:T(8,128)S(1)} %bitcast_dynamic-update-slice_fusion.4, f32[5,16,16,128]{3,2,1,0:T(8,128)S(1)} %get-tuple-element.65, ...), kind=kLoop, calls=%fused_computation.36 | loop fusion | flops 2457600 | bytes 5111808 | tf_op jit(solution)/shard_map/add | solution.py:376
  27.0 0.9 %fusion.99 = (f32[5,16,5,128]{3,2,1,0:T(8,128)}, f32[5,16,5,128]{3,2,1,0:T(8,128)}) fusion(f32[5,16,16,128]{3,2,1,0:T(8,128)S(1)} %get-tuple-element.46), kind=kLoop, calls=%fused_computation.171 | loop fusion | bytes 819200 | tf_op jit(solution)/shard_map/slice | solution.py:162
  28.0 15.2 %shard_map.92 = (f32[5,5,16,128]{3,2,1,0:T(8,128)}, f32[5,5,16,128]{3,2,1,0:T(8,128)}, f32[5,16,5,128]{3,2,1,0:T(8,128)}, f32[5,16,5,128]{3,2,1,0:T(8,128)}, f32[5,16,16,128]{3,2,1,0:T(8,128)}) custom-call(f32[5,16,16,128]{3,2,1,0:T(8,128)} %get-tuple-element.47.refs_0_, f32[5,16,5,128]{3,2,1,0:T(8,128)} %get-tuple-element.64.refs_1_, ...), custom_call_target="tpu_custom_call" | custom-call | tf_op jit(solution)/shard_map/pallas_call | solution.py:121
  43.2 0.0 copy-done.4
  43.2 1.1 %pad_maximum_fusion = f32[5,26,16,128]{3,2,1,0:T(8,128)S(1)} fusion(f32[5,5,16,128]{3,2,1,0:T(8,128)} %get-tuple-element.24, f32[5,16,16,128]{3,2,1,0:T(8,128)S(1)} %copy-done.4, f32[5,5,16,128]{3,2,1,0:T(8,128)} %get-tuple-element.23), kind=kLoop, calls=%fused_computation.21 | loop fusion | flops 532480 | bytes 2129920 | tf_op jit(solution)/shard_map/concatenate | solution.py:188
  44.4 1.2 %fusion.11 = f32[5,16,128,16]{2,3,1,0:T(8,128)S(1)} fusion(f32[16,26,1,1]{1,0,3,2:T(8,128)S(1)} %copy-done.11, f32[5,26,16,128]{3,2,1,0:T(8,128)S(1)} %pad_maximum_fusion), kind=kOutput, calls=%fused_computation.12 | convolution fusion | flops 51118080 | bytes 1721984 | tf_op jit(solution)/shard_map/al,flyz->fayz/dot_general | solution.py:312
  45.6 2.1 %fusion.28.refs_0_ = f32[5,16,16,128]{3,2,1,0:T(8,128)} fusion(f32[5,16,16,128]{3,2,1,0:T(8,128)S(1)} %copy-done.1, f32[5,16,16,128]{3,2,1,0:T(8,128)S(1)} %copy-done.6, f32[16,26,1,1]{1,0,3,2:T(8,128)S(1)} %copy-done.11, f32[5,16,5,128]{3,2,1,0:T(8,128)S(1)} %copy-done.10, f32[5,16,16,128]{3,2,1,0:T(8,128)S(1)} %get-tuple-element.46, ...), kind=kOutput, calls=%fused_computation.19 | convolution fusion | flops 52305920 | bytes 3819136 | tf_op jit(solution)/shard_map/al,fxlz->fxaz/dot_general | solution.py:312
  47.8 8.9 %shard_map.93.refs_0_ = f32[5,16,16,128]{3,2,1,0:T(8,128)} custom-call(f32[5,16,16,128]{3,2,1,0:T(8,128)} %fusion.28.refs_0_, f32[128,128]{1,0:T(8,128)} %constant.40.refs_1_, f32[128,8]{1,0:T(8,128)} %constant.42.refs_2_, f32[128,8]{1,0:T(8,128)} %constant.44.refs_3_), custom_call_target="tpu_custom_call" | custom-call | tf_op jit(solution)/shard_map/pallas_call | solution.py:121
  56.7 1.1 %slice_bitcast_fusion.3 = (f32[1,5,16,5,128]{4,3,2,1,0:T(8,128)S(1)}, f32[1,5,16,5,128]{4,3,2,1,0:T(8,128)S(1)}) fusion(f32[5,16,16,128]{3,2,1,0:T(8,128)} %shard_map.93.refs_0_), kind=kLoop, calls=%fused_computation.47 | loop fusion | bytes 819200 | tf_op jit(solution)/shard_map/stack | solution.py:196
  57.8 0.9 %pad_maximum_fusion.3.refs_1_ = f32[2,5,16,5,128]{4,3,2,1,0:T(8,128)} fusion(f32[1,5,16,5,128]{4,3,2,1,0:T(8,128)S(1)} %get-tuple-element.62, f32[1,5,16,5,128]{4,3,2,1,0:T(8,128)S(1)} %get-tuple-element.61), kind=kLoop, calls=%fused_computation.35 | loop fusion | flops 102400 | bytes 819200 | tf_op jit(solution)/shard_map/stack | solution.py:196
  58.7 14.6 %shard_map.94 = (f32[2,5,5,16,128]{4,3,2,1,0:T(8,128)}, f32[2,5,16,5,128]{4,3,2,1,0:T(8,128)}, f32[2,2,5,5,5,128]{5,4,3,2,1,0:T(8,128)}) custom-call(f32[5,16,16,128]{3,2,1,0:T(8,128)} %shard_map.93.refs_0_, f32[2,5,16,5,128]{4,3,2,1,0:T(8,128)} %pad_maximum_fusion.3.refs_1_), custom_call_target="tpu_custom_call" | custom-call | tf_op jit(solution)/shard_map/pallas_call | solution.py:121
  73.3 1.2 %slice_bitcast_fusion.1 = (f32[5,16,5,128]{3,2,1,0:T(8,128)S(1)}, f32[5,16,5,128]{3,2,1,0:T(8,128)S(1)}) fusion(f32[2,5,16,5,128]{4,3,2,1,0:T(8,128)} %get-tuple-element.30), kind=kLoop, calls=%fused_computation.45 | loop fusion | bytes 819200 | tf_op jit(solution)/shard_map/squeeze | solution.py:223
  74.5 0.0 copy-done.8
  74.6 0.0 copy-done.7
  74.6 0.2 copy-done.2
  74.8 0.4 maximum_maximum_fusion
  75.2 0.3 copy-done.12
  75.5 2.4 %fusion = f32[5,26,128,16]{2,3,1,0:T(8,128)S(1)} fusion(f32[16,26,1,1]{1,0,3,2:T(8,128)S(1)} %copy-done.12, f32[5,26,26,128]{3,2,1,0:T(8,128)S(1)} %maximum_maximum_fusion), kind=kOutput, calls=%fused_computation.1 | convolution fusion | flops 83066880 | bytes 2797184 | tf_op jit(solution)/shard_map/al,flyz->fayz/dot_general | solution.py:312
  77.9 2.0 %fusion.13 = f32[5,16,16,128]{3,2,1,0:T(8,128)} fusion(f32[16,26,1,1]{1,0,3,2:T(8,128)S(1)} %copy-done.12, f32[5,26,128,16]{2,3,1,0:T(8,128)S(1)} %fusion), kind=kOutput, calls=%fused_computation.14 | convolution fusion | flops 51118080 | bytes 1721984 | tf_op jit(solution)/shard_map/al,fxlz->fxaz/dot_general | solution.py:312
  (21 shorter events, 0.2 us)
Async XLA Ops:
  0.0 2.1 %copy-start.1 = (f32[5,16,16,128]{3,2,1,0:T(8,128)S(1)}, f32[5,16,16,128]{3,2,1,0:T(8,128)}, u32[]{:S(2)}) copy-start(f32[5,16,16,128]{3,2,1,0:T(8,128)} %param.9) | copy-start | bytes 1966084
  3.8 18.0 %copy-start.11 = (f32[16,26,1,1]{1,0,3,2:T(8,128)S(1)}, f32[16,26,1,1]{1,0,3,2:T(8,128)}, u32[]{:S(2)}) copy-start(f32[16,26,1,1]{1,0,3,2:T(8,128)} %constant.45) | copy-start | bytes 4996
  21.8 1.2 %copy-start.13 = (f32[4,16,5,128]{3,2,1,0:T(8,128)S(1)}, f32[4,16,5,128]{3,2,1,0:T(8,128)}, u32[]{:S(2)}) copy-start(f32[4,16,5,128]{3,2,1,0:T(8,128)} %get-tuple-element.20) | copy-start | bytes 491524
  21.8 1.2 %copy-start.14 = (f32[4,16,5,128]{3,2,1,0:T(8,128)S(1)}, f32[4,16,5,128]{3,2,1,0:T(8,128)}, u32[]{:S(2)}) copy-start(f32[4,16,5,128]{3,2,1,0:T(8,128)} %get-tuple-element.21) | copy-start | bytes 491524
  22.8 1.3 %copy-start = (f32[3,3,16,16,128]{4,3,2,1,0:T(8,128)S(1)}, f32[3,3,16,16,128]{4,3,2,1,0:T(8,128)}, u32[]{:S(2)}) copy-start(f32[3,3,16,16,128]{4,3,2,1,0:T(8,128)} %param.10) | copy-start | bytes 3538948
  22.8 1.3 %copy-start.3 = (f32[16,16,128]{2,1,0:T(8,128)S(1)}, f32[16,16,128]{2,1,0:T(8,128)}, u32[]{:S(2)}) copy-start(f32[16,16,128]{2,1,0:T(8,128)} %param.11) | copy-start | bytes 393220
  22.8 1.4 %copy-start.5 = (f32[4,16,16,128]{3,2,1,0:T(8,128)S(1)}, f32[4,16,16,128]{3,2,1,0:T(8,128)}, u32[]{:S(2)}) copy-start(f32[4,16,16,128]{3,2,1,0:T(8,128)} %get-tuple-element.22) | copy-start | bytes 1572868
  28.0 15.3 %copy-start.4 = (f32[5,16,16,128]{3,2,1,0:T(8,128)S(1)}, f32[5,16,16,128]{3,2,1,0:T(8,128)}, u32[]{:S(2)}) copy-start(f32[5,16,16,128]{3,2,1,0:T(8,128)} %get-tuple-element.47.refs_0_) | copy-start | bytes 1966084
  44.3 1.3 %copy-start.6 = (f32[5,16,16,128]{3,2,1,0:T(8,128)S(1)}, f32[5,16,16,128]{3,2,1,0:T(8,128)}, u32[]{:S(2)}) copy-start(f32[5,16,16,128]{3,2,1,0:T(8,128)} %get-tuple-element.27) | copy-start | bytes 1966084
  44.3 1.3 %copy-start.9 = (f32[5,16,5,128]{3,2,1,0:T(8,128)S(1)}, f32[5,16,5,128]{3,2,1,0:T(8,128)}, u32[]{:S(2)}) copy-start(f32[5,16,5,128]{3,2,1,0:T(8,128)} %get-tuple-element.25) | copy-start | bytes 614404
  44.4 1.3 %copy-start.10 = (f32[5,16,5,128]{3,2,1,0:T(8,128)S(1)}, f32[5,16,5,128]{3,2,1,0:T(8,128)}, u32[]{:S(2)}) copy-start(f32[5,16,5,128]{3,2,1,0:T(8,128)} %get-tuple-element.26) | copy-start | bytes 614404
  73.3 1.3 %copy-start.8 = (f32[2,2,5,5,5,128]{5,4,3,2,1,0:T(8,128)S(1)}, f32[2,2,5,5,5,128]{5,4,3,2,1,0:T(8,128)}, u32[]{:S(2)}) copy-start(f32[2,2,5,5,5,128]{5,4,3,2,1,0:T(8,128)} %get-tuple-element.28) | copy-start | bytes 768004
  73.3 1.3 %copy-start.7 = (f32[2,5,5,16,128]{4,3,2,1,0:T(8,128)S(1)}, f32[2,5,5,16,128]{4,3,2,1,0:T(8,128)}, u32[]{:S(2)}) copy-start(f32[2,5,5,16,128]{4,3,2,1,0:T(8,128)} %get-tuple-element.29) | copy-start | bytes 1228804
  73.3 1.5 %copy-start.2 = (f32[5,16,16,128]{3,2,1,0:T(8,128)S(1)}, f32[5,16,16,128]{3,2,1,0:T(8,128)}, u32[]{:S(2)}) copy-start(f32[5,16,16,128]{3,2,1,0:T(8,128)} %shard_map.93.refs_0_) | copy-start | bytes 1966084
  74.8 0.7 copy-start.12

commit v12 on v10

--- a/solution.py
+++ b/solution.py
@@ -95,8 +95,8 @@
 
 def exchange(arrays, routes, out_shapes, tag, zeta=None):
     sizes = tuple(lax.axis_size(axis) for axis in AXES)
-    operands = list(arrays)
-    in_specs = [pl.BlockSpec(memory_space=pl.ANY)] * len(arrays)
+    operands = [array for array, _ in arrays]
+    in_specs = [pl.BlockSpec(memory_space=space) for _, space in arrays]
     out_specs = [pl.BlockSpec(memory_space=pl.ANY)] * len(out_shapes)
     out_shapes = list(out_shapes)
     scratch = []
@@ -151,22 +151,22 @@
                 ]
             )
             both = jnp.moveaxis(both, dim + 1, 2).reshape(2, value.shape[0], WIDTH, -1)
-            arrays.append(both)
+            arrays.append((both, pl.ANY))
             out_shapes.append(jax.ShapeDtypeStruct(both.shape, both.dtype))
             source, target = len(arrays) - 1, len(out_shapes) - 1
             routes.append((offset_along(axis, 1), source, 0, target, 0))
             routes.append((offset_along(axis, -1), source, 1, target, 1))
         elif dim == ndim - 2:
             face = value.shape[:dim] + (WIDTH,) + value.shape[dim + 1 :]
-            arrays.append(lax.slice_in_dim(value, length - WIDTH, length, axis=dim))
-            arrays.append(lax.slice_in_dim(value, 0, WIDTH, axis=dim))
+            arrays.append((value, pltpu.VMEM))
             out_shapes += [jax.ShapeDtypeStruct(face, value.dtype)] * 2
-            source, target = len(arrays) - 2, len(out_shapes) - 2
+            source, target = len(arrays) - 1, len(out_shapes) - 2
             whole = window(ndim, dim, None, None)
-            routes.append((offset_along(axis, 1), source, whole, target, whole))
-            routes.append((offset_along(axis, -1), source + 1, whole, target + 1, whole))
+            last, first = window(ndim, dim, length - WIDTH, length), window(ndim, dim, 0, WIDTH)
+            routes.append((offset_along(axis, 1), source, last, target, whole))
+            routes.append((offset_along(axis, -1), source, first, target + 1, whole))
         else:
-            arrays.append(value)
+            arrays.append((value, pl.ANY))
             face = value.shape[:dim] + (WIDTH,) + value.shape[dim + 1 :]
             out_shapes += [jax.ShapeDtypeStruct(face, value.dtype)] * 2
             source, target = len(arrays) - 1, len(out_shapes) - 2
@@ -217,7 +217,7 @@
         jax.ShapeDtypeStruct((2, fields, length_x, WIDTH, depth), value.dtype),
         jax.ShapeDtypeStruct((2, 2, fields, WIDTH, WIDTH, depth), value.dtype),
     ]
-    along_x, along_y, edges = exchange([value, faces_y], routes, out_shapes, tag)
+    along_x, along_y, edges = exchange([(value, pl.ANY), (faces_y, pl.ANY)], routes, out_shapes, tag)
     sections = [
         jnp.concatenate([edges[0, 0], along_x[0], edges[1, 0]], axis=2),
         jnp.concatenate([along_y[0], value, along_y[1]], axis=2),

time: 79.8 us -> 78.8 us (0.987)
    slice x1 -> x0, local copies, waits for them, and re-layouts: 0.9 us -> none  [exchange_faces(): arrays.append(lax.slice_in_dim(value, 0, WIDTH, axis=dim))]
    concatenate x2 -> x1, other arithmetic: 1.68 us -> 0.83 us  [local(): jnp.concatenate([fluid_speed_vector, thermal_level[None]], axis=0)]
    unnamed x33 -> x35, local copies, waits for them, and re-layouts: 2.88 us -> 3.07 us
where the time goes in v12:
time: 78.8 us; the launch traced here: 77.9 us
  Pallas kernels  54.7 us (69%)
  matrix products  9.03 us (11%)
  other arithmetic  8.25 us (10%)
  local copies, waits for them, and re-layouts  5.62 us (7%)
    pallas_call x4, Pallas kernels, exchange(): pl.pallas_call(functools.partial(exchange_kernel, tuple(routes), sizes, l...  54.7 us
    dot_general x6, matrix products, sweep_lines(): jnp.einsum(line_forms[dim], matrix, padded, precision=lax.Precision.HIGHEST)  9.03 us
    unnamed x35, local copies, waits for them, and re-layouts  3.07 us
    concatenate x2, other arithmetic, exchange_faces(): padded.append(jnp.concatenate([before, value, after], axis=dim))  2.18 us

profile of v12, /device:TPU:1, one launch (start us, length us, event | category | flops | bytes accessed | tf_op | source)
XLA Modules:
  0.0 77.9 jit_solution(5650953286882934921)
XLA Ops:
  0.0 1.0 %slice_bitcast_fusion.26 = f32[16,16,128]{2,1,0:T(8,128)S(1)} fusion(f32[5,16,16,128]{3,2,1,0:T(8,128)} %param.9), kind=kLoop, calls=%fused_computation.154 | loop fusion | bytes 262144 | tf_op jit(solution)/shard_map/div | solution.py:329
  1.0 1.1 %multiply_reduce_fusion = (f32[16,16,128]{2,1,0:T(8,128)S(1)}, f32[3,16,16,128]{3,2,1,0:T(8,128)S(1)}) fusion(f32[5,16,16,128]{3,2,1,0:T(8,128)} %param.9, f32[16,16,128]{2,1,0:T(8,128)S(1)} %slice_bitcast_fusion.26), kind=kLoop, calls=%fused_computation.38 | loop fusion | flops 262144 | bytes 1048576 | tf_op jit(solution)/shard_map/reduce_sum | solution.py:331
  2.1 0.0 copy-done.1
  2.1 0.8 %pad_maximum_fusion.3.refs_0_.refs_1_.refs_2_ = f32[4,16,16,128]{3,2,1,0:T(8,128)} fusion(f32[1,16,16,128]{3,2,1,0:T(8,128)S(1)} %get-tuple-element.66, f32[3,16,16,128]{3,2,1,0:T(8,128)S(1)} %get-tuple-element.44), kind=kLoop, calls=%fused_computation.36 | loop fusion | flops 131072 | bytes 1048576 | tf_op jit(solution)/shard_map/concatenate | solution.py:390
  3.0 17.1 %shard_map.91 = (f32[4,5,16,128]{3,2,1,0:T(8,128)}, f32[4,5,16,128]{3,2,1,0:T(8,128)}, f32[4,16,5,128]{3,2,1,0:T(8,128)}, f32[4,16,5,128]{3,2,1,0:T(8,128)}, f32[4,16,16,128]{3,2,1,0:T(8,128)}) custom-call(f32[4,16,16,128]{3,2,1,0:T(8,128)} %pad_maximum_fusion.3.refs_0_.refs_1_.refs_2_, f32[4,16,16,128]{3,2,1,0:T(8,128)} %pad_maximum_fusion.3.refs_0_.refs_1_.refs_2_, ...), custom_call_target="tpu_custom_call" | custom-call | tf_op jit(solution)/shard_map/pallas_call | solution.py:121
  20.1 1.1 %pad_maximum_fusion.1 = f32[4,26,16,128]{3,2,1,0:T(8,128)S(1)} fusion(f32[4,5,16,128]{3,2,1,0:T(8,128)} %get-tuple-element.19, f32[1,16,16,128]{3,2,1,0:T(8,128)S(1)} %get-tuple-element.66, f32[3,16,16,128]{3,2,1,0:T(8,128)S(1)} %get-tuple-element.44, f32[4,5,16,128]{3,2,1,0:T(8,128)} %get-tuple-element.18), kind=kLoop, calls=%fused_computation.31 | loop fusion | flops 638976 | bytes 1703936 | tf_op jit(solution)/shard_map/concatenate | solution.py:188
  21.2 0.0 copy-done.13
  21.2 1.0 %fusion.38 = f32[4,16,128,16]{2,3,1,0:T(8,128)S(1)} fusion(f32[16,26,1,1]{1,0,3,2:T(8,128)S(1)} %copy-done.13, f32[4,26,16,128]{3,2,1,0:T(8,128)S(1)} %pad_maximum_fusion.1), kind=kOutput, calls=%fused_computation.29 | convolution fusion | flops 40894464 | bytes 1377920 | tf_op jit(solution)/shard_map/al,flyz->fayz/dot_general | solution.py:312
  22.2 0.0 copy-start
  22.2 0.0 copy-start.4
  22.2 0.2 copy.32
  22.4 0.9 %convolution_bitcast_fusion = f32[4,16,16,128]{3,2,1,0:T(8,128)S(1)} fusion(f32[16,26,1,1]{1,0,3,2:T(8,128)S(1)} %copy-done.13, f32[4,16,5,128]{3,2,1,0:T(8,128)S(1)} %copy-done.16, f32[1,16,16,128]{3,2,1,0:T(8,128)S(1)} %get-tuple-element.66, f32[3,16,16,128]{3,2,1,0:T(8,128)S(1)} %get-tuple-element.44, f32[4,16,5,128]{3,2,1,0:T(8,128)S(1)} %copy-done.15), kind=kOutput, calls=%fused_computation.20 | convolution fusion | flops 41533440 | bytes 1377920 | tf_op jit(solution)/shard_map/al,fxlz->fxaz/dot_general | solution.py:312
  23.3 0.1 copy-done
  23.5 0.0 copy-done.4
  23.5 0.2 copy-done.7
  23.6 0.2 bitcast_dynamic-update-slice_fusion.11
  23.8 0.1 bitcast_dynamic-update-slice_fusion.10
  24.0 0.1 bitcast_dynamic-update-slice_fusion.9
  24.1 0.2 bitcast_dynamic-update-slice_fusion.8
  24.3 0.1 bitcast_dynamic-update-slice_fusion.6
  24.4 0.1 bitcast_dynamic-update-slice_fusion.5
  24.5 0.1 bitcast_dynamic-update-slice_fusion.4
  24.7 0.1 bitcast_dynamic-update-slice_fusion.1
  24.8 0.1 bitcast_dynamic-update-slice_fusion
  24.9 0.1 slice_bitcast_fusion.23
  25.0 1.5 %multiply_add_fusion = (f32[5,16,16,128]{3,2,1,0:T(8,128)}, f32[5,16,16,128]{3,2,1,0:T(8,128)}, f32[5,16,16,128]{3,2,1,0:T(8,128)}) fusion(f32[5,16,16,128]{3,2,1,0:T(8,128)S(1)} %bitcast_dynamic-update-slice_fusion, f32[5,16,16,128]{3,2,1,0:T(8,128)S(1)} %bitcast_dynamic-update-slice_fusion.4, f32[5,16,16,128]{3,2,1,0:T(8,128)S(1)} %get-tuple-element.63, ...), kind=kLoop, calls=%fused_computation.33 | loop fusion | flops 2457600 | bytes 5111808 | tf_op jit(solution)/shard_map/add | solution.py:376
  26.5 15.4 %shard_map.92 = (f32[5,5,16,128]{3,2,1,0:T(8,128)}, f32[5,5,16,128]{3,2,1,0:T(8,128)}, f32[5,16,5,128]{3,2,1,0:T(8,128)}, f32[5,16,5,128]{3,2,1,0:T(8,128)}, f32[5,16,16,128]{3,2,1,0:T(8,128)}) custom-call(f32[5,16,16,128]{3,2,1,0:T(8,128)} %get-tuple-element.47.refs_0_, f32[5,16,16,128]{3,2,1,0:T(8,128)} %get-tuple-element.46.refs_1_, ...), custom_call_target="tpu_custom_call" | custom-call | tf_op jit(solution)/shard_map/pallas_call | solution.py:121
  41.9 1.1 %pad_maximum_fusion = f32[5,26,16,128]{3,2,1,0:T(8,128)S(1)} fusion(f32[5,5,16,128]{3,2,1,0:T(8,128)} %get-tuple-element.24, f32[5,16,16,128]{3,2,1,0:T(8,128)S(1)} %copy-done.6, f32[5,5,16,128]{3,2,1,0:T(8,128)} %get-tuple-element.23), kind=kLoop, calls=%fused_computation.21 | loop fusion | flops 532480 | bytes 2129920 | tf_op jit(solution)/shard_map/concatenate | solution.py:188
  43.1 1.2 %fusion.11 = f32[5,16,128,16]{2,3,1,0:T(8,128)S(1)} fusion(f32[16,26,1,1]{1,0,3,2:T(8,128)S(1)} %copy-done.13, f32[5,26,16,128]{3,2,1,0:T(8,128)S(1)} %pad_maximum_fusion), kind=kOutput, calls=%fused_computation.12 | convolution fusion | flops 51118080 | bytes 1721984 | tf_op jit(solution)/shard_map/al,flyz->fayz/dot_general | solution.py:312
  44.3 0.0 copy-done.5
  44.3 0.0 copy-done.8
  44.3 0.1 copy-done.11
  44.4 0.1 copy-done.12
  44.5 1.3 %fusion.28.refs_0_ = f32[5,16,16,128]{3,2,1,0:T(8,128)S(1)} fusion(f32[5,16,16,128]{3,2,1,0:T(8,128)S(1)} %copy-done.1, f32[5,16,16,128]{3,2,1,0:T(8,128)S(1)} %copy-done.8, f32[16,26,1,1]{1,0,3,2:T(8,128)S(1)} %copy-done.13, f32[5,16,5,128]{3,2,1,0:T(8,128)S(1)} %copy-done.12, f32[5,16,16,128]{3,2,1,0:T(8,128)S(1)} %copy-done.5, ...), kind=kOutput, calls=%fused_computation.19 | convolution fusion | flops 52305920 | bytes 3819136 | tf_op jit(solution)/shard_map/al,fxlz->fxaz/dot_general | solution.py:312
  45.9 0.0 copy-start.2
  45.9 1.0 %pad_maximum_fusion.2.refs_1_ = f32[2,5,16,5,128]{4,3,2,1,0:T(8,128)} fusion(f32[1,5,16,5,128]{4,3,2,1,0:T(8,128)S(1)} %get-tuple-element.62, f32[1,5,16,5,128]{4,3,2,1,0:T(8,128)S(1)} %get-tuple-element.61), kind=kLoop, calls=%fused_computation.32 | loop fusion | flops 102400 | bytes 819200 | tf_op jit(solution)/shard_map/stack | solution.py:196
  46.9 13.4 %shard_map.93 = (f32[2,5,5,16,128]{4,3,2,1,0:T(8,128)}, f32[2,5,16,5,128]{4,3,2,1,0:T(8,128)}, f32[2,2,5,5,5,128]{5,4,3,2,1,0:T(8,128)}) custom-call(f32[5,16,16,128]{3,2,1,0:T(8,128)} %copy-done.2, f32[2,5,16,5,128]{4,3,2,1,0:T(8,128)} %pad_maximum_fusion.2.refs_1_), custom_call_target="tpu_custom_call" | custom-call | tf_op jit(solution)/shard_map/pallas_call | solution.py:121
  60.4 0.0 copy-start.3
  60.4 1.2 %slice_bitcast_fusion.3 = (f32[5,16,5,128]{3,2,1,0:T(8,128)S(1)}, f32[5,16,5,128]{3,2,1,0:T(8,128)S(1)}) fusion(f32[2,5,16,5,128]{4,3,2,1,0:T(8,128)} %get-tuple-element.30), kind=kLoop, calls=%fused_computation.43 | loop fusion | bytes 819200 | tf_op jit(solution)/shard_map/squeeze | solution.py:223
  61.6 0.0 copy-done.10
  61.6 0.0 copy-done.9
  61.7 0.2 copy-done.3
  61.9 0.4 maximum_maximum_fusion
  62.2 0.3 copy-done.14
  62.6 2.6 %fusion = f32[5,26,128,16]{2,3,1,0:T(8,128)S(1)} fusion(f32[16,26,1,1]{1,0,3,2:T(8,128)S(1)} %copy-done.14, f32[5,26,26,128]{3,2,1,0:T(8,128)S(1)} %maximum_maximum_fusion), kind=kOutput, calls=%fused_computation.1 | convolution fusion | flops 83066880 | bytes 2797184 | tf_op jit(solution)/shard_map/al,flyz->fayz/dot_general | solution.py:312
  65.2 2.0 %fusion.13.refs_0_ = f32[5,16,16,128]{3,2,1,0:T(8,128)} fusion(f32[16,26,1,1]{1,0,3,2:T(8,128)S(1)} %copy-done.14, f32[5,26,128,16]{2,3,1,0:T(8,128)S(1)} %fusion), kind=kOutput, calls=%fused_computation.14 | convolution fusion | flops 51118080 | bytes 1721984 | tf_op jit(solution)/shard_map/al,fxlz->fxaz/dot_general | solution.py:312
  67.2 8.7 %shard_map.94 = f32[5,16,16,128]{3,2,1,0:T(8,128)} custom-call(f32[5,16,16,128]{3,2,1,0:T(8,128)} %fusion.13.refs_0_, f32[128,128]{1,0:T(8,128)} %constant.40.refs_1_, f32[128,8]{1,0:T(8,128)} %constant.42.refs_2_, f32[128,8]{1,0:T(8,128)} %constant.44.refs_3_), custom_call_target="tpu_custom_call" | custom-call | tf_op jit(solution)/shard_map/pallas_call | solution.py:121
  75.9 2.0 %copy.46 = f32[5,16,16,128]{3,2,1,0:T(8,128)} copy(f32[5,16,16,128]{3,2,1,0:T(8,128)} %shard_map.94) | data formatting | bytes 1310720
  (24 shorter events, 0.2 us)
Async XLA Ops:
  0.0 2.1 %copy-start.1 = (f32[5,16,16,128]{3,2,1,0:T(8,128)S(1)}, f32[5,16,16,128]{3,2,1,0:T(8,128)}, u32[]{:S(2)}) copy-start(f32[5,16,16,128]{3,2,1,0:T(8,128)} %param.9) | copy-start | bytes 1966084
  3.0 18.2 %copy-start.13 = (f32[16,26,1,1]{1,0,3,2:T(8,128)S(1)}, f32[16,26,1,1]{1,0,3,2:T(8,128)}, u32[]{:S(2)}) copy-start(f32[16,26,1,1]{1,0,3,2:T(8,128)} %constant.45) | copy-start | bytes 4996
  21.2 1.2 %copy-start.15 = (f32[4,16,5,128]{3,2,1,0:T(8,128)S(1)}, f32[4,16,5,128]{3,2,1,0:T(8,128)}, u32[]{:S(2)}) copy-start(f32[4,16,5,128]{3,2,1,0:T(8,128)} %get-tuple-element.20) | copy-start | bytes 491524
  21.2 1.2 %copy-start.16 = (f32[4,16,5,128]{3,2,1,0:T(8,128)S(1)}, f32[4,16,5,128]{3,2,1,0:T(8,128)}, u32[]{:S(2)}) copy-start(f32[4,16,5,128]{3,2,1,0:T(8,128)} %get-tuple-element.21) | copy-start | bytes 491524
  22.2 1.3 %copy-start = (f32[3,3,16,16,128]{4,3,2,1,0:T(8,128)S(1)}, f32[3,3,16,16,128]{4,3,2,1,0:T(8,128)}, u32[]{:S(2)}) copy-start(f32[3,3,16,16,128]{4,3,2,1,0:T(8,128)} %param.10) | copy-start | bytes 3538948
  22.2 1.3 %copy-start.4 = (f32[16,16,128]{2,1,0:T(8,128)S(1)}, f32[16,16,128]{2,1,0:T(8,128)}, u32[]{:S(2)}) copy-start(f32[16,16,128]{2,1,0:T(8,128)} %param.11) | copy-start | bytes 393220
  22.2 1.4 %copy-start.7 = (f32[4,16,16,128]{3,2,1,0:T(8,128)S(1)}, f32[4,16,16,128]{3,2,1,0:T(8,128)}, u32[]{:S(2)}) copy-start(f32[4,16,16,128]{3,2,1,0:T(8,128)} %get-tuple-element.22) | copy-start | bytes 1572868
  26.5 15.4 %copy-start.6 = (f32[5,16,16,128]{3,2,1,0:T(8,128)S(1)}, f32[5,16,16,128]{3,2,1,0:T(8,128)}, u32[]{:S(2)}) copy-start(f32[5,16,16,128]{3,2,1,0:T(8,128)} %get-tuple-element.47.refs_0_) | copy-start | bytes 1966084
  43.0 1.3 %copy-start.5 = (f32[5,16,16,128]{3,2,1,0:T(8,128)S(1)}, f32[5,16,16,128]{3,2,1,0:T(8,128)}, u32[]{:S(2)}) copy-start(f32[5,16,16,128]{3,2,1,0:T(8,128)} %get-tuple-element.46.refs_1_) | copy-start | bytes 1966084
  43.0 1.3 %copy-start.8 = (f32[5,16,16,128]{3,2,1,0:T(8,128)S(1)}, f32[5,16,16,128]{3,2,1,0:T(8,128)}, u32[]{:S(2)}) copy-start(f32[5,16,16,128]{3,2,1,0:T(8,128)} %get-tuple-element.27) | copy-start | bytes 1966084
  43.1 1.3 %copy-start.11 = (f32[5,16,5,128]{3,2,1,0:T(8,128)S(1)}, f32[5,16,5,128]{3,2,1,0:T(8,128)}, u32[]{:S(2)}) copy-start(f32[5,16,5,128]{3,2,1,0:T(8,128)} %get-tuple-element.25) | copy-start | bytes 614404
  43.1 1.4 %copy-start.12 = (f32[5,16,5,128]{3,2,1,0:T(8,128)S(1)}, f32[5,16,5,128]{3,2,1,0:T(8,128)}, u32[]{:S(2)}) copy-start(f32[5,16,5,128]{3,2,1,0:T(8,128)} %get-tuple-element.26) | copy-start | bytes 614404
  45.9 1.1 %copy-start.2 = (f32[5,16,16,128]{3,2,1,0:T(8,128)}, f32[5,16,16,128]{3,2,1,0:T(8,128)S(1)}, u32[]{:S(2)}) copy-start(f32[5,16,16,128]{3,2,1,0:T(8,128)S(1)} %fusion.28.refs_0_) | copy-start | bytes 1966084
  60.3 1.3 %copy-start.10 = (f32[2,2,5,5,5,128]{5,4,3,2,1,0:T(8,128)S(1)}, f32[2,2,5,5,5,128]{5,4,3,2,1,0:T(8,128)}, u32[]{:S(2)}) copy-start(f32[2,2,5,5,5,128]{5,4,3,2,1,0:T(8,128)} %get-tuple-element.28) | copy-start | bytes 768004
  60.3 1.3 %copy-start.9 = (f32[2,5,5,16,128]{4,3,2,1,0:T(8,128)S(1)}, f32[2,5,5,16,128]{4,3,2,1,0:T(8,128)}, u32[]{:S(2)}) copy-start(f32[2,5,5,16,128]{4,3,2,1,0:T(8,128)} %get-tuple-element.29) | copy-start | bytes 1228804
  60.4 1.5 %copy-start.3 = (f32[5,16,16,128]{3,2,1,0:T(8,128)S(1)}, f32[5,16,16,128]{3,2,1,0:T(8,128)}, u32[]{:S(2)}) copy-start(f32[5,16,16,128]{3,2,1,0:T(8,128)} %copy-done.2) | copy-start | bytes 1966084
  61.9 0.7 copy-start.14

commit v13 on v12

--- a/solution.py
+++ b/solution.py
@@ -193,23 +193,18 @@
 
 def exchange_plane(value, tag):
     length_x, length_y = value.shape[1], value.shape[2]
-    faces_y = jnp.stack(
-        [
-            lax.slice_in_dim(value, length_y - WIDTH, length_y, axis=2),
-            lax.slice_in_dim(value, 0, WIDTH, axis=2),
-        ]
-    )
     last_x, first_x = slice(length_x - WIDTH, length_x), slice(0, WIDTH)
+    last_y, first_y = slice(length_y - WIDTH, length_y), slice(0, WIDTH)
     every = slice(None)
     routes = [
         ((1, 0, 0), 0, (every, last_x), 0, 0),
         ((-1, 0, 0), 0, (every, first_x), 0, 1),
-        ((0, 1, 0), 1, 0, 1, 0),
-        ((0, -1, 0), 1, 1, 1, 1),
-        ((1, 1, 0), 1, (0, every, last_x), 2, (0, 0)),
-        ((-1, 1, 0), 1, (0, every, first_x), 2, (0, 1)),
-        ((1, -1, 0), 1, (1, every, last_x), 2, (1, 0)),
-        ((-1, -1, 0), 1, (1, every, first_x), 2, (1, 1)),
+        ((0, 1, 0), 1, (every, every, last_y), 1, 0),
+        ((0, -1, 0), 1, (every, every, first_y), 1, 1),
+        ((1, 1, 0), 1, (every, last_x, last_y), 2, (0, 0)),
+        ((-1, 1, 0), 1, (every, first_x, last_y), 2, (0, 1)),
+        ((1, -1, 0), 1, (every, last_x, first_y), 2, (1, 0)),
+        ((-1, -1, 0), 1, (every, first_x, first_y), 2, (1, 1)),
     ]
     fields, depth = value.shape[0], value.shape[3]
     out_shapes = [
@@ -217,7 +212,9 @@
         jax.ShapeDtypeStruct((2, fields, length_x, WIDTH, depth), value.dtype),
         jax.ShapeDtypeStruct((2, 2, fields, WIDTH, WIDTH, depth), value.dtype),
     ]
-    along_x, along_y, edges = exchange([(value, pl.ANY), (faces_y, pl.ANY)], routes, out_shapes, tag)
+    along_x, along_y, edges = exchange(
+        [(value, pl.ANY), (value, pltpu.VMEM)], routes, out_shapes, tag
+    )
     sections = [
         jnp.concatenate([edges[0, 0], along_x[0], edges[1, 0]], axis=2),
         jnp.concatenate([along_y[0], value, along_y[1]], axis=2),

time: 78.8 us -> 79.7 us (1.011)
  Pallas kernels: 54.7 us -> 55.8 us
  other arithmetic: 8.25 us -> 7.26 us
  matrix products: 9.03 us -> 9.87 us
    pallas_call x4, Pallas kernels: 54.7 us -> 55.8 us  [exchange(): pl.pallas_call(functools.partial(exchange_kernel, tuple(routes), sizes, l...]
    another operation x1 -> x0, other arithmetic: 0.98 us -> none  [exchange_plane(): jnp.stack([lax.slice_in_dim(value, length_y - WIDTH, length_y, axis=2), l...]
    dot_general x6, matrix products: 9.03 us -> 9.87 us  [sweep_lines(): jnp.einsum(line_forms[dim], matrix, padded, precision=lax.Precision.HIGHEST)]
    unnamed x35 -> x33, local copies, waits for them, and re-layouts: 3.07 us -> 3.06 us
where the time goes in v13:
time: 79.7 us; the launch traced here: 78.8 us
  Pallas kernels  55.8 us (70%)
  matrix products  9.87 us (12%)
  other arithmetic  7.26 us (9%)
  local copies, waits for them, and re-layouts  5.57 us (7%)
    pallas_call x4, Pallas kernels, exchange(): pl.pallas_call(functools.partial(exchange_kernel, tuple(routes), sizes, l...  55.8 us
    dot_general x6, matrix products, sweep_lines(): jnp.einsum(line_forms[dim], matrix, padded, precision=lax.Precision.HIGHEST)  9.87 us
    unnamed x33, local copies, waits for them, and re-layouts  3.06 us
    concatenate x2, other arithmetic, exchange_faces(): padded.append(jnp.concatenate([before, value, after], axis=dim))  2.18 us

profile of v13, /device:TPU:1, one launch (start us, length us, event | category | flops | bytes accessed | tf_op | source)
XLA Modules:
  0.0 78.8 jit_solution(7152049757250830250)
XLA Ops:
  0.0 1.0 %slice_bitcast_fusion.24 = f32[16,16,128]{2,1,0:T(8,128)S(1)} fusion(f32[5,16,16,128]{3,2,1,0:T(8,128)} %param.9), kind=kLoop, calls=%fused_computation.151 | loop fusion | bytes 262144 | tf_op jit(solution)/shard_map/div | solution.py:326
  1.0 1.1 %multiply_reduce_fusion = (f32[16,16,128]{2,1,0:T(8,128)S(1)}, f32[3,16,16,128]{3,2,1,0:T(8,128)S(1)}) fusion(f32[5,16,16,128]{3,2,1,0:T(8,128)} %param.9, f32[16,16,128]{2,1,0:T(8,128)S(1)} %slice_bitcast_fusion.24), kind=kLoop, calls=%fused_computation.37 | loop fusion | flops 262144 | bytes 1048576 | tf_op jit(solution)/shard_map/reduce_sum | solution.py:328
  2.1 0.0 copy-done.1
  2.1 0.8 %pad_maximum_fusion.2.refs_0_.refs_1_.refs_2_ = f32[4,16,16,128]{3,2,1,0:T(8,128)} fusion(f32[1,16,16,128]{3,2,1,0:T(8,128)S(1)} %get-tuple-element.64, f32[3,16,16,128]{3,2,1,0:T(8,128)S(1)} %get-tuple-element.44), kind=kLoop, calls=%fused_computation.35 | loop fusion | flops 131072 | bytes 1048576 | tf_op jit(solution)/shard_map/concatenate | solution.py:387
  3.0 17.2 %shard_map.91 = (f32[4,5,16,128]{3,2,1,0:T(8,128)}, f32[4,5,16,128]{3,2,1,0:T(8,128)}, f32[4,16,5,128]{3,2,1,0:T(8,128)}, f32[4,16,5,128]{3,2,1,0:T(8,128)}, f32[4,16,16,128]{3,2,1,0:T(8,128)}) custom-call(f32[4,16,16,128]{3,2,1,0:T(8,128)} %pad_maximum_fusion.2.refs_0_.refs_1_.refs_2_, f32[4,16,16,128]{3,2,1,0:T(8,128)} %pad_maximum_fusion.2.refs_0_.refs_1_.refs_2_, ...), custom_call_target="tpu_custom_call" | custom-call | tf_op jit(solution)/shard_map/pallas_call | solution.py:121
  20.1 1.1 %pad_maximum_fusion.1 = f32[4,26,16,128]{3,2,1,0:T(8,128)S(1)} fusion(f32[4,5,16,128]{3,2,1,0:T(8,128)} %get-tuple-element.19, f32[1,16,16,128]{3,2,1,0:T(8,128)S(1)} %get-tuple-element.64, f32[3,16,16,128]{3,2,1,0:T(8,128)S(1)} %get-tuple-element.44, f32[4,5,16,128]{3,2,1,0:T(8,128)} %get-tuple-element.18), kind=kLoop, calls=%fused_computation.31 | loop fusion | flops 638976 | bytes 1703936 | tf_op jit(solution)/shard_map/concatenate | solution.py:188
  21.2 0.0 copy-done.12
  21.2 0.0 copy-start.14
  21.2 0.0 copy-start.15
  21.2 1.0 %fusion.38 = f32[4,16,128,16]{2,3,1,0:T(8,128)S(1)} fusion(f32[16,26,1,1]{1,0,3,2:T(8,128)S(1)} %copy-done.12, f32[4,26,16,128]{3,2,1,0:T(8,128)S(1)} %pad_maximum_fusion.1), kind=kOutput, calls=%fused_computation.29 | convolution fusion | flops 40894464 | bytes 1377920 | tf_op jit(solution)/shard_map/al,flyz->fayz/dot_general | solution.py:309
  22.2 0.0 copy-start
  22.2 0.0 copy-start.3
  22.2 0.0 copy-start.6
  22.2 0.2 copy.32
  22.4 0.0 copy-done.14
  22.4 0.0 copy-done.15
  22.4 0.9 %convolution_bitcast_fusion = f32[4,16,16,128]{3,2,1,0:T(8,128)S(1)} fusion(f32[16,26,1,1]{1,0,3,2:T(8,128)S(1)} %copy-done.12, f32[4,16,5,128]{3,2,1,0:T(8,128)S(1)} %copy-done.15, f32[1,16,16,128]{3,2,1,0:T(8,128)S(1)} %get-tuple-element.64, f32[3,16,16,128]{3,2,1,0:T(8,128)S(1)} %get-tuple-element.44, f32[4,16,5,128]{3,2,1,0:T(8,128)S(1)} %copy-done.14), kind=kOutput, calls=%fused_computation.20 | convolution fusion | flops 41533440 | bytes 1377920 | tf_op jit(solution)/shard_map/al,fxlz->fxaz/dot_general | solution.py:309
  23.3 0.1 copy-done
  23.5 0.2 copy-done.6
  23.7 0.2 bitcast_dynamic-update-slice_fusion.11
  23.9 0.1 bitcast_dynamic-update-slice_fusion.10
  24.0 0.1 bitcast_dynamic-update-slice_fusion.9
  24.1 0.2 bitcast_dynamic-update-slice_fusion.8
  24.3 0.1 bitcast_dynamic-update-slice_fusion.6
  24.4 0.1 bitcast_dynamic-update-slice_fusion.5
  24.6 0.1 bitcast_dynamic-update-slice_fusion.4
  24.7 0.1 bitcast_dynamic-update-slice_fusion.1
  24.8 0.1 bitcast_dynamic-update-slice_fusion
  24.9 0.1 slice_bitcast_fusion.21
  25.0 1.5 %multiply_add_fusion = (f32[5,16,16,128]{3,2,1,0:T(8,128)}, f32[5,16,16,128]{3,2,1,0:T(8,128)}, f32[5,16,16,128]{3,2,1,0:T(8,128)}) fusion(f32[5,16,16,128]{3,2,1,0:T(8,128)S(1)} %bitcast_dynamic-update-slice_fusion, f32[5,16,16,128]{3,2,1,0:T(8,128)S(1)} %bitcast_dynamic-update-slice_fusion.4, f32[5,16,16,128]{3,2,1,0:T(8,128)S(1)} %get-tuple-element.61, ...), kind=kLoop, calls=%fused_computation.32 | loop fusion | flops 2457600 | bytes 5111808 | tf_op jit(solution)/shard_map/add | solution.py:373
  26.5 15.4 %shard_map.92 = (f32[5,5,16,128]{3,2,1,0:T(8,128)}, f32[5,5,16,128]{3,2,1,0:T(8,128)}, f32[5,16,5,128]{3,2,1,0:T(8,128)}, f32[5,16,5,128]{3,2,1,0:T(8,128)}, f32[5,16,16,128]{3,2,1,0:T(8,128)}) custom-call(f32[5,16,16,128]{3,2,1,0:T(8,128)} %get-tuple-element.47.refs_0_, f32[5,16,16,128]{3,2,1,0:T(8,128)} %get-tuple-element.46.refs_1_, ...), custom_call_target="tpu_custom_call" | custom-call | tf_op jit(solution)/shard_map/pallas_call | solution.py:121
  42.0 1.1 %pad_maximum_fusion = f32[5,26,16,128]{3,2,1,0:T(8,128)S(1)} fusion(f32[5,5,16,128]{3,2,1,0:T(8,128)} %get-tuple-element.24, f32[5,16,16,128]{3,2,1,0:T(8,128)S(1)} %copy-done.5, f32[5,5,16,128]{3,2,1,0:T(8,128)} %get-tuple-element.23), kind=kLoop, calls=%fused_computation.21 | loop fusion | flops 532480 | bytes 2129920 | tf_op jit(solution)/shard_map/concatenate | solution.py:188
  43.1 1.2 %fusion.11 = f32[5,16,128,16]{2,3,1,0:T(8,128)S(1)} fusion(f32[16,26,1,1]{1,0,3,2:T(8,128)S(1)} %copy-done.12, f32[5,26,16,128]{3,2,1,0:T(8,128)S(1)} %pad_maximum_fusion), kind=kOutput, calls=%fused_computation.12 | convolution fusion | flops 51118080 | bytes 1721984 | tf_op jit(solution)/shard_map/al,flyz->fayz/dot_general | solution.py:309
  44.3 0.0 copy-done.7
  44.4 0.1 copy-done.10
  44.4 0.1 copy-done.11
  44.5 2.2 %fusion.28.refs_0_.refs_1_ = f32[5,16,16,128]{3,2,1,0:T(8,128)} fusion(f32[5,16,16,128]{3,2,1,0:T(8,128)S(1)} %copy-done.1, f32[5,16,16,128]{3,2,1,0:T(8,128)S(1)} %copy-done.7, f32[16,26,1,1]{1,0,3,2:T(8,128)S(1)} %copy-done.12, f32[5,16,5,128]{3,2,1,0:T(8,128)S(1)} %copy-done.11, f32[5,16,16,128]{3,2,1,0:T(8,128)S(1)} %copy-done.4, ...), kind=kOutput, calls=%fused_computation.19 | convolution fusion | flops 52305920 | bytes 3819136 | tf_op jit(solution)/shard_map/al,fxlz->fxaz/dot_general | solution.py:309
  46.7 14.5 %shard_map.93 = (f32[2,5,5,16,128]{4,3,2,1,0:T(8,128)}, f32[2,5,16,5,128]{4,3,2,1,0:T(8,128)}, f32[2,2,5,5,5,128]{5,4,3,2,1,0:T(8,128)}) custom-call(f32[5,16,16,128]{3,2,1,0:T(8,128)} %fusion.28.refs_0_.refs_1_, f32[5,16,16,128]{3,2,1,0:T(8,128)} %fusion.28.refs_0_.refs_1_), custom_call_target="tpu_custom_call" | custom-call | tf_op jit(solution)/shard_map/pallas_call | solution.py:121
  61.3 0.0 copy-start.2
  61.3 1.2 %slice_bitcast_fusion.1 = (f32[5,16,5,128]{3,2,1,0:T(8,128)S(1)}, f32[5,16,5,128]{3,2,1,0:T(8,128)S(1)}) fusion(f32[2,5,16,5,128]{4,3,2,1,0:T(8,128)} %get-tuple-element.30), kind=kLoop, calls=%fused_computation.40 | loop fusion | bytes 819200 | tf_op jit(solution)/shard_map/squeeze | solution.py:220
  62.5 0.0 copy-done.8
  62.6 0.2 copy-done.2
  62.8 0.4 maximum_maximum_fusion
  63.1 0.3 copy-done.13
  63.5 2.6 %fusion = f32[5,26,128,16]{2,3,1,0:T(8,128)S(1)} fusion(f32[16,26,1,1]{1,0,3,2:T(8,128)S(1)} %copy-done.13, f32[5,26,26,128]{3,2,1,0:T(8,128)S(1)} %maximum_maximum_fusion), kind=kOutput, calls=%fused_computation.1 | convolution fusion | flops 83066880 | bytes 2797184 | tf_op jit(solution)/shard_map/al,flyz->fayz/dot_general | solution.py:309
  66.1 2.0 %fusion.13.refs_0_ = f32[5,16,16,128]{3,2,1,0:T(8,128)} fusion(f32[16,26,1,1]{1,0,3,2:T(8,128)S(1)} %copy-done.13, f32[5,26,128,16]{2,3,1,0:T(8,128)S(1)} %fusion), kind=kOutput, calls=%fused_computation.14 | convolution fusion | flops 51118080 | bytes 1721984 | tf_op jit(solution)/shard_map/al,fxlz->fxaz/dot_general | solution.py:309
  68.1 8.7 %shard_map.94 = f32[5,16,16,128]{3,2,1,0:T(8,128)} custom-call(f32[5,16,16,128]{3,2,1,0:T(8,128)} %fusion.13.refs_0_, f32[128,128]{1,0:T(8,128)} %constant.40.refs_1_, f32[128,8]{1,0:T(8,128)} %constant.42.refs_2_, f32[128,8]{1,0:T(8,128)} %constant.44.refs_3_), custom_call_target="tpu_custom_call" | custom-call | tf_op jit(solution)/shard_map/pallas_call | solution.py:121
  76.8 2.0 %copy.46 = f32[5,16,16,128]{3,2,1,0:T(8,128)} copy(f32[5,16,16,128]{3,2,1,0:T(8,128)} %shard_map.94) | data formatting | bytes 1310720
  (20 shorter events, 0.2 us)
Async XLA Ops:
  0.0 2.1 %copy-start.1 = (f32[5,16,16,128]{3,2,1,0:T(8,128)S(1)}, f32[5,16,16,128]{3,2,1,0:T(8,128)}, u32[]{:S(2)}) copy-start(f32[5,16,16,128]{3,2,1,0:T(8,128)} %param.9) | copy-start | bytes 1966084
  3.0 18.3 %copy-start.12 = (f32[16,26,1,1]{1,0,3,2:T(8,128)S(1)}, f32[16,26,1,1]{1,0,3,2:T(8,128)}, u32[]{:S(2)}) copy-start(f32[16,26,1,1]{1,0,3,2:T(8,128)} %constant.45) | copy-start | bytes 4996
  21.2 1.2 %copy-start.14 = (f32[4,16,5,128]{3,2,1,0:T(8,128)S(1)}, f32[4,16,5,128]{3,2,1,0:T(8,128)}, u32[]{:S(2)}) copy-start(f32[4,16,5,128]{3,2,1,0:T(8,128)} %get-tuple-element.20) | copy-start | bytes 491524
  21.2 1.2 %copy-start.15 = (f32[4,16,5,128]{3,2,1,0:T(8,128)S(1)}, f32[4,16,5,128]{3,2,1,0:T(8,128)}, u32[]{:S(2)}) copy-start(f32[4,16,5,128]{3,2,1,0:T(8,128)} %get-tuple-element.21) | copy-start | bytes 491524
  22.2 1.3 %copy-start = (f32[3,3,16,16,128]{4,3,2,1,0:T(8,128)S(1)}, f32[3,3,16,16,128]{4,3,2,1,0:T(8,128)}, u32[]{:S(2)}) copy-start(f32[3,3,16,16,128]{4,3,2,1,0:T(8,128)} %param.10) | copy-start | bytes 3538948
  22.2 1.3 %copy-start.3 = (f32[16,16,128]{2,1,0:T(8,128)S(1)}, f32[16,16,128]{2,1,0:T(8,128)}, u32[]{:S(2)}) copy-start(f32[16,16,128]{2,1,0:T(8,128)} %param.11) | copy-start | bytes 393220
  22.2 1.4 %copy-start.6 = (f32[4,16,16,128]{3,2,1,0:T(8,128)S(1)}, f32[4,16,16,128]{3,2,1,0:T(8,128)}, u32[]{:S(2)}) copy-start(f32[4,16,16,128]{3,2,1,0:T(8,128)} %get-tuple-element.22) | copy-start | bytes 1572868
  26.5 15.4 %copy-start.5 = (f32[5,16,16,128]{3,2,1,0:T(8,128)S(1)}, f32[5,16,16,128]{3,2,1,0:T(8,128)}, u32[]{:S(2)}) copy-start(f32[5,16,16,128]{3,2,1,0:T(8,128)} %get-tuple-element.47.refs_0_) | copy-start | bytes 1966084
  43.1 1.3 %copy-start.4 = (f32[5,16,16,128]{3,2,1,0:T(8,128)S(1)}, f32[5,16,16,128]{3,2,1,0:T(8,128)}, u32[]{:S(2)}) copy-start(f32[5,16,16,128]{3,2,1,0:T(8,128)} %get-tuple-element.46.refs_1_) | copy-start | bytes 1966084
  43.1 1.3 %copy-start.7 = (f32[5,16,16,128]{3,2,1,0:T(8,128)S(1)}, f32[5,16,16,128]{3,2,1,0:T(8,128)}, u32[]{:S(2)}) copy-start(f32[5,16,16,128]{3,2,1,0:T(8,128)} %get-tuple-element.27) | copy-start | bytes 1966084
  43.1 1.3 %copy-start.10 = (f32[5,16,5,128]{3,2,1,0:T(8,128)S(1)}, f32[5,16,5,128]{3,2,1,0:T(8,128)}, u32[]{:S(2)}) copy-start(f32[5,16,5,128]{3,2,1,0:T(8,128)} %get-tuple-element.25) | copy-start | bytes 614404
  43.1 1.4 %copy-start.11 = (f32[5,16,5,128]{3,2,1,0:T(8,128)S(1)}, f32[5,16,5,128]{3,2,1,0:T(8,128)}, u32[]{:S(2)}) copy-start(f32[5,16,5,128]{3,2,1,0:T(8,128)} %get-tuple-element.26) | copy-start | bytes 614404
  61.2 1.3 %copy-start.9 = (f32[2,2,5,5,5,128]{5,4,3,2,1,0:T(8,128)S(1)}, f32[2,2,5,5,5,128]{5,4,3,2,1,0:T(8,128)}, u32[]{:S(2)}) copy-start(f32[2,2,5,5,5,128]{5,4,3,2,1,0:T(8,128)} %get-tuple-element.28) | copy-start | bytes 768004
  61.2 1.3 %copy-start.8 = (f32[2,5,5,16,128]{4,3,2,1,0:T(8,128)S(1)}, f32[2,5,5,16,128]{4,3,2,1,0:T(8,128)}, u32[]{:S(2)}) copy-start(f32[2,5,5,16,128]{4,3,2,1,0:T(8,128)} %get-tuple-element.29) | copy-start | bytes 1228804
  61.3 1.5 %copy-start.2 = (f32[5,16,16,128]{3,2,1,0:T(8,128)S(1)}, f32[5,16,16,128]{3,2,1,0:T(8,128)}, u32[]{:S(2)}) copy-start(f32[5,16,16,128]{3,2,1,0:T(8,128)} %fusion.28.refs_0_.refs_1_) | copy-start | bytes 1966084
  62.8 0.7 copy-start.13

commit v14 on v12

--- a/solution.py
+++ b/solution.py
@@ -19,17 +19,35 @@
 AXES = ("xi", "eta", "zeta")
 
 
-def exchange_kernel(routes, sizes, count, zeta, *refs):
-    sources = refs[:count]
+def primitive_state(conserved):
+    density = conserved[0]
+    speed = conserved[1:4] / density
+    pressure = 0.4 * (conserved[4] - 0.5 * jnp.sum(conserved[1:4] * speed, axis=0))
+    return speed, pressure / density
+
+
+def exchange_kernel(routes, sizes, count, zeta, prepare, *refs):
+    sources = list(refs[:count])
     refs = refs[count:]
-    if zeta:
-        block_ref, middle_ref, lower_ref, upper_ref = refs[:4]
-        refs = refs[4:]
-    targets = refs[: len(refs) - 2 - (4 if zeta else 0)]
+    if prepare:
+        conserved_ref = sources.pop()
+    if zeta:
+        if not prepare:
+            block_ref = refs[0]
+            refs = refs[1:]
+        middle_ref, lower_ref, upper_ref = refs[:3]
+        refs = refs[3:]
+    targets = refs[: len(refs) - 2 - (4 if zeta else 0) - (1 if prepare else 0)]
     refs = refs[len(targets) :]
     if zeta:
         out_ref, turned, before, after = refs[:4]
         refs = refs[4:]
+    if prepare:
+        made = refs[0]
+        refs = refs[1:]
+        sources.append(made)
+        if zeta:
+            block_ref = made
     send_sems, recv_sems = refs
     here = [lax.axis_index(axis) for axis in AXES]
 
@@ -47,6 +65,10 @@
     barrier = pltpu.get_barrier_semaphore()
     for offset in partners:
         pl.semaphore_signal(barrier, inc=1, device_id=device(offset), device_id_type=MESH)
+    if prepare:
+        speed, temperature = primitive_state(conserved_ref[...])
+        made[0:3] = speed
+        made[3] = temperature
     if zeta:
         fields, length_x, length_y, depth = block_ref.shape
         rows = fields * length_x * length_y
@@ -93,7 +115,7 @@
         out_ref[...] = total.T.reshape(fields, length_x, length_y, depth)
 
 
-def exchange(arrays, routes, out_shapes, tag, zeta=None):
+def exchange(arrays, routes, out_shapes, tag, zeta=None, prepare=None):
     sizes = tuple(lax.axis_size(axis) for axis in AXES)
     operands = [array for array, _ in arrays]
     in_specs = [pl.BlockSpec(memory_space=space) for _, space in arrays]
@@ -101,25 +123,35 @@
     out_shapes = list(out_shapes)
     scratch = []
     copies = len(routes)
+    if prepare is not None:
+        operands.append(prepare)
+        in_specs.append(pl.BlockSpec(memory_space=pltpu.VMEM))
     if zeta is not None:
         value, matrix = zeta
         fields, length_x, length_y, depth = value.shape
         rows = fields * length_x * length_y
         padding = jnp.zeros((depth, 8 - WIDTH), matrix.dtype)
+        if prepare is None:
+            operands.append(value)
+            in_specs.append(pl.BlockSpec(memory_space=pltpu.VMEM))
         operands += [
-            value,
             matrix[:, WIDTH : WIDTH + depth],
             jnp.concatenate([padding, matrix[:, :WIDTH]], axis=1),
             jnp.concatenate([matrix[:, WIDTH + depth :], padding], axis=1),
         ]
-        in_specs += [pl.BlockSpec(memory_space=pltpu.VMEM)] * 4
+        in_specs += [pl.BlockSpec(memory_space=pltpu.VMEM)] * 3
         out_shapes.append(jax.ShapeDtypeStruct(value.shape, value.dtype))
         out_specs.append(pl.BlockSpec(memory_space=pltpu.VMEM))
         scratch = [pltpu.VMEM((depth, rows), jnp.float32), pltpu.VMEM((8, rows), jnp.float32),
                    pltpu.VMEM((8, rows), jnp.float32)]
         copies += 2
+    if prepare is not None:
+        scratch.append(pltpu.VMEM(zeta[0].shape, jnp.float32))
     return pl.pallas_call(
-        functools.partial(exchange_kernel, tuple(routes), sizes, len(arrays), zeta is not None),
+        functools.partial(
+            exchange_kernel, tuple(routes), sizes, len(arrays) + (prepare is not None),
+            zeta is not None, prepare is not None,
+        ),
         out_shape=out_shapes,
         in_specs=in_specs,
         out_specs=out_specs,
@@ -191,6 +223,28 @@
     return padded
 
 
+def exchange_primitive(conserved, primitive, matrix, tag):
+    length_x, length_y = primitive.shape[1], primitive.shape[2]
+    every = slice(None)
+    routes = [
+        ((1, 0, 0), 0, (every, slice(length_x - WIDTH, length_x)), 0, every),
+        ((-1, 0, 0), 0, (every, slice(0, WIDTH)), 1, every),
+        ((0, 1, 0), 0, (every, every, slice(length_y - WIDTH, length_y)), 2, every),
+        ((0, -1, 0), 0, (every, every, slice(0, WIDTH)), 3, every),
+    ]
+    face_x = (primitive.shape[0], WIDTH) + primitive.shape[2:]
+    face_y = primitive.shape[:2] + (WIDTH,) + primitive.shape[3:]
+    out_shapes = [jax.ShapeDtypeStruct(face, primitive.dtype) for face in (face_x, face_x, face_y, face_y)]
+    before_x, after_x, before_y, after_y, swept = exchange(
+        [], routes, out_shapes, tag, (primitive, matrix), conserved
+    )
+    return (
+        jnp.concatenate([before_x, primitive, after_x], axis=1),
+        jnp.concatenate([before_y, primitive, after_y], axis=2),
+        swept,
+    )
+
+
 def exchange_plane(value, tag):
     length_x, length_y = value.shape[1], value.shape[2]
     faces_y = jnp.stack(
@@ -388,9 +442,7 @@
         conserved_solution
     )
     basic_quantity = jnp.concatenate([fluid_speed_vector, thermal_level[None]], axis=0)
-    padded = exchange_faces(
-        [(basic_quantity, "xi", 1), (basic_quantity, "eta", 2)], 0, (basic_quantity, derive[2])
-    )
+    padded = exchange_primitive(conserved_solution, basic_quantity, derive[2], 0)
     slopes = [sweep_lines(padded[k], derive[k], k + 1) for k in range(2)] + [padded[2]]
     contra = fluxes(
         conserved_solution,

time: 78.8 us -> 77.9 us (0.989)
  other arithmetic: 8.25 us -> 7.42 us
    concatenate x2 -> x1, other arithmetic: 2.18 us -> 1.11 us  [exchange_faces(): padded.append(jnp.concatenate([before, value, after], axis=dim))]
    unnamed x35 -> x37, local copies, waits for them, and re-layouts: 3.07 us -> 3.26 us
where the time goes in v14:
time: 77.9 us; the launch traced here: 77 us
  Pallas kernels  54.3 us (70%)
  matrix products  9.03 us (12%)
  other arithmetic  7.42 us (10%)
  local copies, waits for them, and re-layouts  5.81 us (7%)
    pallas_call x4, Pallas kernels, exchange(): pl.pallas_call(functools.partial(exchange_kernel, tuple(routes), sizes, l...  54.3 us
    dot_general x6, matrix products, sweep_lines(): jnp.einsum(line_forms[dim], matrix, padded, precision=lax.Precision.HIGHEST)  9.03 us
    unnamed x37, local copies, waits for them, and re-layouts  3.26 us

profile of v14, /device:TPU:1, one launch (start us, length us, event | category | flops | bytes accessed | tf_op | source)
XLA Modules:
  0.0 77.0 jit_solution(11433207884313806887)
XLA Ops:
  0.0 1.0 %slice_bitcast_fusion.26 = f32[16,16,128]{2,1,0:T(8,128)S(1)} fusion(f32[5,16,16,128]{3,2,1,0:T(8,128)} %refs_0_.1), kind=kLoop, calls=%fused_computation.153 | loop fusion | bytes 262144 | tf_op jit(solution)/shard_map/div | solution.py:383
  1.0 1.1 %multiply_reduce_fusion = (f32[16,16,128]{2,1,0:T(8,128)S(1)}, f32[3,16,16,128]{3,2,1,0:T(8,128)S(1)}) fusion(f32[5,16,16,128]{3,2,1,0:T(8,128)} %refs_0_.1, f32[16,16,128]{2,1,0:T(8,128)S(1)} %slice_bitcast_fusion.26), kind=kLoop, calls=%fused_computation.37 | loop fusion | flops 262144 | bytes 1048576 | tf_op jit(solution)/shard_map/reduce_sum | solution.py:385
  2.1 0.0 copy-start.14
  2.1 16.8 %shard_map.91 = (f32[4,5,16,128]{3,2,1,0:T(8,128)}, f32[4,5,16,128]{3,2,1,0:T(8,128)}, f32[4,16,5,128]{3,2,1,0:T(8,128)}, f32[4,16,5,128]{3,2,1,0:T(8,128)}, f32[4,16,16,128]{3,2,1,0:T(8,128)}) custom-call(f32[5,16,16,128]{3,2,1,0:T(8,128)} %refs_0_.1, f32[128,128]{1,0:T(8,128)} %constant.35.refs_1_.refs_3_, f32[128,8]{1,0:T(8,128)} %constant.37.refs_2_.refs_4_, ...), custom_call_target="tpu_custom_call" | custom-call | tf_op jit(solution)/shard_map/pallas_call | solution.py:150
  19.0 1.1 %pad_maximum_fusion.1 = f32[4,26,16,128]{3,2,1,0:T(8,128)S(1)} fusion(f32[4,5,16,128]{3,2,1,0:T(8,128)} %get-tuple-element.19, f32[1,16,16,128]{3,2,1,0:T(8,128)S(1)} %get-tuple-element.66, f32[3,16,16,128]{3,2,1,0:T(8,128)S(1)} %get-tuple-element.44, f32[4,5,16,128]{3,2,1,0:T(8,128)} %get-tuple-element.18), kind=kLoop, calls=%fused_computation.31 | loop fusion | flops 638976 | bytes 1703936 | tf_op jit(solution)/shard_map/concatenate | solution.py:242
  20.1 1.0 %fusion.38 = f32[4,16,128,16]{2,3,1,0:T(8,128)S(1)} fusion(f32[16,26,1,1]{1,0,3,2:T(8,128)S(1)} %copy-done.14, f32[4,26,16,128]{3,2,1,0:T(8,128)S(1)} %pad_maximum_fusion.1), kind=kOutput, calls=%fused_computation.29 | convolution fusion | flops 40894464 | bytes 1377920 | tf_op jit(solution)/shard_map/al,flyz->fayz/dot_general | solution.py:366
  21.0 0.0 copy-start
  21.1 0.0 copy-start.2
  21.1 0.0 copy-start.5
  21.1 0.2 copy.32
  21.3 0.9 %convolution_bitcast_fusion = f32[4,16,16,128]{3,2,1,0:T(8,128)S(1)} fusion(f32[16,26,1,1]{1,0,3,2:T(8,128)S(1)} %copy-done.14, f32[4,16,5,128]{3,2,1,0:T(8,128)S(1)} %copy-done.17, f32[1,16,16,128]{3,2,1,0:T(8,128)S(1)} %get-tuple-element.66, f32[3,16,16,128]{3,2,1,0:T(8,128)S(1)} %get-tuple-element.44, f32[4,16,5,128]{3,2,1,0:T(8,128)S(1)} %copy-done.16), kind=kOutput, calls=%fused_computation.20 | convolution fusion | flops 41533440 | bytes 1377920 | tf_op jit(solution)/shard_map/al,fxlz->fxaz/dot_general | solution.py:366
  22.2 0.1 copy-done
  22.3 0.2 copy-done.2
  22.5 0.0 copy-done.5
  22.5 0.2 copy-done.8
  22.7 0.2 bitcast_dynamic-update-slice_fusion.11
  22.9 0.1 bitcast_dynamic-update-slice_fusion.10
  23.0 0.1 bitcast_dynamic-update-slice_fusion.9
  23.2 0.2 bitcast_dynamic-update-slice_fusion.8
  23.4 0.1 bitcast_dynamic-update-slice_fusion.6
  23.4 0.1 bitcast_dynamic-update-slice_fusion.5
  23.6 0.1 bitcast_dynamic-update-slice_fusion.4
  23.8 0.1 bitcast_dynamic-update-slice_fusion.1
  23.8 0.1 bitcast_dynamic-update-slice_fusion
  24.0 0.1 slice_bitcast_fusion.23
  24.1 1.5 %multiply_add_fusion = (f32[5,16,16,128]{3,2,1,0:T(8,128)}, f32[5,16,16,128]{3,2,1,0:T(8,128)}, f32[5,16,16,128]{3,2,1,0:T(8,128)}) fusion(f32[5,16,16,128]{3,2,1,0:T(8,128)S(1)} %bitcast_dynamic-update-slice_fusion, f32[5,16,16,128]{3,2,1,0:T(8,128)S(1)} %bitcast_dynamic-update-slice_fusion.4, f32[5,16,16,128]{3,2,1,0:T(8,128)S(1)} %get-tuple-element.63, ...), kind=kLoop, calls=%fused_computation.33 | loop fusion | flops 2457600 | bytes 5111808 | tf_op jit(solution)/shard_map/add | solution.py:430
  25.6 15.4 %shard_map.92 = (f32[5,5,16,128]{3,2,1,0:T(8,128)}, f32[5,5,16,128]{3,2,1,0:T(8,128)}, f32[5,16,5,128]{3,2,1,0:T(8,128)}, f32[5,16,5,128]{3,2,1,0:T(8,128)}, f32[5,16,16,128]{3,2,1,0:T(8,128)}) custom-call(f32[5,16,16,128]{3,2,1,0:T(8,128)} %get-tuple-element.47.refs_0_, f32[5,16,16,128]{3,2,1,0:T(8,128)} %get-tuple-element.46.refs_1_, ...), custom_call_target="tpu_custom_call" | custom-call | tf_op jit(solution)/shard_map/pallas_call | solution.py:150
  41.0 1.1 %pad_maximum_fusion = f32[5,26,16,128]{3,2,1,0:T(8,128)S(1)} fusion(f32[5,5,16,128]{3,2,1,0:T(8,128)} %get-tuple-element.24, f32[5,16,16,128]{3,2,1,0:T(8,128)S(1)} %copy-done.7, f32[5,5,16,128]{3,2,1,0:T(8,128)} %get-tuple-element.23), kind=kLoop, calls=%fused_computation.21 | loop fusion | flops 532480 | bytes 2129920 | tf_op jit(solution)/shard_map/concatenate | solution.py:220
  42.1 0.0 copy-start.6
  42.1 0.0 copy-start.9
  42.1 1.2 %fusion.11 = f32[5,16,128,16]{2,3,1,0:T(8,128)S(1)} fusion(f32[16,26,1,1]{1,0,3,2:T(8,128)S(1)} %copy-done.14, f32[5,26,16,128]{3,2,1,0:T(8,128)S(1)} %pad_maximum_fusion), kind=kOutput, calls=%fused_computation.12 | convolution fusion | flops 51118080 | bytes 1721984 | tf_op jit(solution)/shard_map/al,flyz->fayz/dot_general | solution.py:366
  43.4 0.0 copy-done.9
  43.4 0.1 copy-done.12
  43.5 0.1 copy-done.13
  43.6 1.3 %fusion.28.refs_0_ = f32[5,16,16,128]{3,2,1,0:T(8,128)S(1)} fusion(f32[5,16,16,128]{3,2,1,0:T(8,128)S(1)} %copy-done.2, f32[5,16,16,128]{3,2,1,0:T(8,128)S(1)} %copy-done.9, f32[16,26,1,1]{1,0,3,2:T(8,128)S(1)} %copy-done.14, f32[5,16,5,128]{3,2,1,0:T(8,128)S(1)} %copy-done.13, f32[5,16,16,128]{3,2,1,0:T(8,128)S(1)} %copy-done.6, ...), kind=kOutput, calls=%fused_computation.19 | convolution fusion | flops 52305920 | bytes 3819136 | tf_op jit(solution)/shard_map/al,fxlz->fxaz/dot_general | solution.py:366
  44.9 0.0 copy-start.3
  45.0 1.0 %pad_maximum_fusion.2.refs_1_ = f32[2,5,16,5,128]{4,3,2,1,0:T(8,128)} fusion(f32[1,5,16,5,128]{4,3,2,1,0:T(8,128)S(1)} %get-tuple-element.62, f32[1,5,16,5,128]{4,3,2,1,0:T(8,128)S(1)} %get-tuple-element.61), kind=kLoop, calls=%fused_computation.32 | loop fusion | flops 102400 | bytes 819200 | tf_op jit(solution)/shard_map/stack | solution.py:250
  46.0 13.4 %shard_map.93 = (f32[2,5,5,16,128]{4,3,2,1,0:T(8,128)}, f32[2,5,16,5,128]{4,3,2,1,0:T(8,128)}, f32[2,2,5,5,5,128]{5,4,3,2,1,0:T(8,128)}) custom-call(f32[5,16,16,128]{3,2,1,0:T(8,128)} %copy-done.3, f32[2,5,16,5,128]{4,3,2,1,0:T(8,128)} %pad_maximum_fusion.2.refs_1_), custom_call_target="tpu_custom_call" | custom-call | tf_op jit(solution)/shard_map/pallas_call | solution.py:150
  59.4 0.0 copy-start.4
  59.4 1.2 %slice_bitcast_fusion.3 = (f32[5,16,5,128]{3,2,1,0:T(8,128)S(1)}, f32[5,16,5,128]{3,2,1,0:T(8,128)S(1)}) fusion(f32[2,5,16,5,128]{4,3,2,1,0:T(8,128)} %get-tuple-element.30), kind=kLoop, calls=%fused_computation.42 | loop fusion | bytes 819200 | tf_op jit(solution)/shard_map/squeeze | solution.py:277
  60.7 0.0 copy-done.10
  60.7 0.2 copy-done.4
  60.9 0.4 maximum_maximum_fusion
  61.3 0.3 copy-done.15
  61.6 2.6 %fusion = f32[5,26,128,16]{2,3,1,0:T(8,128)S(1)} fusion(f32[16,26,1,1]{1,0,3,2:T(8,128)S(1)} %copy-done.15, f32[5,26,26,128]{3,2,1,0:T(8,128)S(1)} %maximum_maximum_fusion), kind=kOutput, calls=%fused_computation.1 | convolution fusion | flops 83066880 | bytes 2797184 | tf_op jit(solution)/shard_map/al,flyz->fayz/dot_general | solution.py:366
  64.2 2.0 %fusion.13.refs_0_ = f32[5,16,16,128]{3,2,1,0:T(8,128)} fusion(f32[16,26,1,1]{1,0,3,2:T(8,128)S(1)} %copy-done.15, f32[5,26,128,16]{2,3,1,0:T(8,128)S(1)} %fusion), kind=kOutput, calls=%fused_computation.14 | convolution fusion | flops 51118080 | bytes 1721984 | tf_op jit(solution)/shard_map/al,fxlz->fxaz/dot_general | solution.py:366
  66.3 8.7 %shard_map.94 = f32[5,16,16,128]{3,2,1,0:T(8,128)} custom-call(f32[5,16,16,128]{3,2,1,0:T(8,128)} %fusion.13.refs_0_, f32[128,128]{1,0:T(8,128)} %constant.40.refs_1_, f32[128,8]{1,0:T(8,128)} %constant.42.refs_2_, f32[128,8]{1,0:T(8,128)} %constant.44.refs_3_), custom_call_target="tpu_custom_call" | custom-call | tf_op jit(solution)/shard_map/pallas_call | solution.py:150
  75.0 2.0 %copy.46 = f32[5,16,16,128]{3,2,1,0:T(8,128)} copy(f32[5,16,16,128]{3,2,1,0:T(8,128)} %shard_map.94) | data formatting | bytes 1310720
  (25 shorter events, 0.2 us)
Async XLA Ops:
  0.0 2.1 %copy-start.1 = (f32[5,16,16,128]{3,2,1,0:T(8,128)S(1)}, f32[5,16,16,128]{3,2,1,0:T(8,128)}, u32[]{:S(2)}) copy-start(f32[5,16,16,128]{3,2,1,0:T(8,128)} %refs_0_.1) | copy-start | bytes 1966084
  2.1 17.9 %copy-start.14 = (f32[16,26,1,1]{1,0,3,2:T(8,128)S(1)}, f32[16,26,1,1]{1,0,3,2:T(8,128)}, u32[]{:S(2)}) copy-start(f32[16,26,1,1]{1,0,3,2:T(8,128)} %constant.45) | copy-start | bytes 4996
  20.0 1.2 %copy-start.16 = (f32[4,16,5,128]{3,2,1,0:T(8,128)S(1)}, f32[4,16,5,128]{3,2,1,0:T(8,128)}, u32[]{:S(2)}) copy-start(f32[4,16,5,128]{3,2,1,0:T(8,128)} %get-tuple-element.20) | copy-start | bytes 491524
  20.1 1.2 %copy-start.17 = (f32[4,16,5,128]{3,2,1,0:T(8,128)S(1)}, f32[4,16,5,128]{3,2,1,0:T(8,128)}, u32[]{:S(2)}) copy-start(f32[4,16,5,128]{3,2,1,0:T(8,128)} %get-tuple-element.21) | copy-start | bytes 491524
  21.0 1.3 %copy-start = (f32[3,3,16,16,128]{4,3,2,1,0:T(8,128)S(1)}, f32[3,3,16,16,128]{4,3,2,1,0:T(8,128)}, u32[]{:S(2)}) copy-start(f32[3,3,16,16,128]{4,3,2,1,0:T(8,128)} %param.10) | copy-start | bytes 3538948
  21.1 1.4 %copy-start.2 = (f32[5,16,16,128]{3,2,1,0:T(8,128)S(1)}, f32[5,16,16,128]{3,2,1,0:T(8,128)}, u32[]{:S(2)}) copy-start(f32[5,16,16,128]{3,2,1,0:T(8,128)} %refs_0_.1) | copy-start | bytes 1966084
  21.1 1.4 %copy-start.5 = (f32[16,16,128]{2,1,0:T(8,128)S(1)}, f32[16,16,128]{2,1,0:T(8,128)}, u32[]{:S(2)}) copy-start(f32[16,16,128]{2,1,0:T(8,128)} %param.11) | copy-start | bytes 393220
  21.1 1.6 %copy-start.8 = (f32[4,16,16,128]{3,2,1,0:T(8,128)S(1)}, f32[4,16,16,128]{3,2,1,0:T(8,128)}, u32[]{:S(2)}) copy-start(f32[4,16,16,128]{3,2,1,0:T(8,128)} %get-tuple-element.22) | copy-start | bytes 1572868
  25.6 15.4 %copy-start.7 = (f32[5,16,16,128]{3,2,1,0:T(8,128)S(1)}, f32[5,16,16,128]{3,2,1,0:T(8,128)}, u32[]{:S(2)}) copy-start(f32[5,16,16,128]{3,2,1,0:T(8,128)} %get-tuple-element.47.refs_0_) | copy-start | bytes 1966084
  42.1 1.3 %copy-start.6 = (f32[5,16,16,128]{3,2,1,0:T(8,128)S(1)}, f32[5,16,16,128]{3,2,1,0:T(8,128)}, u32[]{:S(2)}) copy-start(f32[5,16,16,128]{3,2,1,0:T(8,128)} %get-tuple-element.46.refs_1_) | copy-start | bytes 1966084
  42.1 1.3 %copy-start.9 = (f32[5,16,16,128]{3,2,1,0:T(8,128)S(1)}, f32[5,16,16,128]{3,2,1,0:T(8,128)}, u32[]{:S(2)}) copy-start(f32[5,16,16,128]{3,2,1,0:T(8,128)} %get-tuple-element.27) | copy-start | bytes 1966084
  42.1 1.3 %copy-start.12 = (f32[5,16,5,128]{3,2,1,0:T(8,128)S(1)}, f32[5,16,5,128]{3,2,1,0:T(8,128)}, u32[]{:S(2)}) copy-start(f32[5,16,5,128]{3,2,1,0:T(8,128)} %get-tuple-element.25) | copy-start | bytes 614404
  42.1 1.4 %copy-start.13 = (f32[5,16,5,128]{3,2,1,0:T(8,128)S(1)}, f32[5,16,5,128]{3,2,1,0:T(8,128)}, u32[]{:S(2)}) copy-start(f32[5,16,5,128]{3,2,1,0:T(8,128)} %get-tuple-element.26) | copy-start | bytes 614404
  44.9 1.1 %copy-start.3 = (f32[5,16,16,128]{3,2,1,0:T(8,128)}, f32[5,16,16,128]{3,2,1,0:T(8,128)S(1)}, u32[]{:S(2)}) copy-start(f32[5,16,16,128]{3,2,1,0:T(8,128)S(1)} %fusion.28.refs_0_) | copy-start | bytes 1966084
  59.4 1.3 %copy-start.11 = (f32[2,2,5,5,5,128]{5,4,3,2,1,0:T(8,128)S(1)}, f32[2,2,5,5,5,128]{5,4,3,2,1,0:T(8,128)}, u32[]{:S(2)}) copy-start(f32[2,2,5,5,5,128]{5,4,3,2,1,0:T(8,128)} %get-tuple-element.28) | copy-start | bytes 768004
  59.4 1.3 %copy-start.10 = (f32[2,5,5,16,128]{4,3,2,1,0:T(8,128)S(1)}, f32[2,5,5,16,128]{4,3,2,1,0:T(8,128)}, u32[]{:S(2)}) copy-start(f32[2,5,5,16,128]{4,3,2,1,0:T(8,128)} %get-tuple-element.29) | copy-start | bytes 1228804
  59.4 1.5 %copy-start.4 = (f32[5,16,16,128]{3,2,1,0:T(8,128)S(1)}, f32[5,16,16,128]{3,2,1,0:T(8,128)}, u32[]{:S(2)}) copy-start(f32[5,16,16,128]{3,2,1,0:T(8,128)} %copy-done.3) | copy-start | bytes 1966084
  60.9 0.7 copy-start.15

commit v15 on v14

--- a/solution.py
+++ b/solution.py
@@ -23,7 +23,7 @@
     density = conserved[0]
     speed = conserved[1:4] / density
     pressure = 0.4 * (conserved[4] - 0.5 * jnp.sum(conserved[1:4] * speed, axis=0))
-    return speed, pressure / density
+    return speed, pressure, pressure / density
 
 
 def exchange_kernel(routes, sizes, count, zeta, prepare, *refs):
@@ -37,17 +37,21 @@
             refs = refs[1:]
         middle_ref, lower_ref, upper_ref = refs[:3]
         refs = refs[3:]
-    targets = refs[: len(refs) - 2 - (4 if zeta else 0) - (1 if prepare else 0)]
+    extra = (1 if zeta else 0) + (2 if prepare else 0)
+    targets = refs[: len(refs) - 2 - (3 if zeta else 0) - extra]
     refs = refs[len(targets) :]
     if zeta:
-        out_ref, turned, before, after = refs[:4]
-        refs = refs[4:]
+        out_ref = refs[0]
+        refs = refs[1:]
     if prepare:
-        made = refs[0]
-        refs = refs[1:]
+        made, pressure_ref = refs[:2]
+        refs = refs[2:]
         sources.append(made)
         if zeta:
             block_ref = made
+    if zeta:
+        turned, before, after = refs[:3]
+        refs = refs[3:]
     send_sems, recv_sems = refs
     here = [lax.axis_index(axis) for axis in AXES]
 
@@ -66,9 +70,10 @@
     for offset in partners:
         pl.semaphore_signal(barrier, inc=1, device_id=device(offset), device_id_type=MESH)
     if prepare:
-        speed, temperature = primitive_state(conserved_ref[...])
+        speed, pressure, temperature = primitive_state(conserved_ref[...])
         made[0:3] = speed
         made[3] = temperature
+        pressure_ref[...] = pressure
     if zeta:
         fields, length_x, length_y, depth = block_ref.shape
         rows = fields * length_x * length_y
@@ -146,7 +151,11 @@
                    pltpu.VMEM((8, rows), jnp.float32)]
         copies += 2
     if prepare is not None:
-        scratch.append(pltpu.VMEM(zeta[0].shape, jnp.float32))
+        out_shapes += [
+            jax.ShapeDtypeStruct(zeta[0].shape, jnp.float32),
+            jax.ShapeDtypeStruct(prepare.shape[1:], jnp.float32),
+        ]
+        out_specs += [pl.BlockSpec(memory_space=pltpu.VMEM)] * 2
     return pl.pallas_call(
         functools.partial(
             exchange_kernel, tuple(routes), sizes, len(arrays) + (prepare is not None),
@@ -223,7 +232,8 @@
     return padded
 
 
-def exchange_primitive(conserved, primitive, matrix, tag):
+def exchange_primitive(conserved, matrix, tag):
+    primitive = jax.ShapeDtypeStruct((4,) + conserved.shape[1:], conserved.dtype)
     length_x, length_y = primitive.shape[1], primitive.shape[2]
     every = slice(None)
     routes = [
@@ -235,13 +245,15 @@
     face_x = (primitive.shape[0], WIDTH) + primitive.shape[2:]
     face_y = primitive.shape[:2] + (WIDTH,) + primitive.shape[3:]
     out_shapes = [jax.ShapeDtypeStruct(face, primitive.dtype) for face in (face_x, face_x, face_y, face_y)]
-    before_x, after_x, before_y, after_y, swept = exchange(
+    before_x, after_x, before_y, after_y, swept, primitive, pressure = exchange(
         [], routes, out_shapes, tag, (primitive, matrix), conserved
     )
     return (
         jnp.concatenate([before_x, primitive, after_x], axis=1),
         jnp.concatenate([before_y, primitive, after_y], axis=2),
         swept,
+        primitive,
+        pressure,
     )
 
 
@@ -438,12 +450,9 @@
     lengths = conserved_solution.shape[1:]
     derive = [jnp.asarray(derivative_table(length), dtype=jnp.float32) for length in lengths]
     smooth = [jnp.asarray(filter_table(length), dtype=jnp.float32) for length in lengths]
-    fluid_speed_vector, thermodynamic_stress_scalar, thermal_level = basic_quantities(
-        conserved_solution
-    )
-    basic_quantity = jnp.concatenate([fluid_speed_vector, thermal_level[None]], axis=0)
-    padded = exchange_primitive(conserved_solution, basic_quantity, derive[2], 0)
+    padded = exchange_primitive(conserved_solution, derive[2], 0)
     slopes = [sweep_lines(padded[k], derive[k], k + 1) for k in range(2)] + [padded[2]]
+    fluid_speed_vector, thermodynamic_stress_scalar = padded[3][0:3], padded[4]
     contra = fluxes(
         conserved_solution,
         fluid_speed_vector,

time: 77.9 us -> 75.8 us (0.973)
  other arithmetic: 7.42 us -> 6.43 us
  local copies, waits for them, and re-layouts: 5.81 us -> 4.87 us
    reduce_sum x1 -> x0, other arithmetic: 1.06 us -> none  [basic_quantities(): jnp.sum(conserved_solution[1:4] * fluid_speed_vector, axis=0)]
    div x1 -> x0, local copies, waits for them, and re-layouts: 0.98 us -> none  [basic_quantities(): fluid_speed_vector = conserved_solution[1:4] / density]
    unnamed x37 -> x40, local copies, waits for them, and re-layouts: 3.26 us -> 3.29 us
where the time goes in v15:
time: 75.8 us; the launch traced here: 75 us
  Pallas kernels  54.2 us (72%)
  matrix products  9.03 us (12%)
  other arithmetic  6.43 us (8%)
  local copies, waits for them, and re-layouts  4.87 us (6%)
    pallas_call x4, Pallas kernels, exchange(): pl.pallas_call(functools.partial(exchange_kernel, tuple(routes), sizes, l...  54.2 us
    dot_general x6, matrix products, sweep_lines(): jnp.einsum(line_forms[dim], matrix, padded, precision=lax.Precision.HIGHEST)  9.03 us
    unnamed x40, local copies, waits for them, and re-layouts  3.29 us

profile of v15, /device:TPU:1, one launch (start us, length us, event | category | flops | bytes accessed | tf_op | source)
XLA Modules:
  0.0 75.0 jit_solution(8545718080922671930)
XLA Ops:
  0.0 16.7 %shard_map.91 = (f32[4,5,16,128]{3,2,1,0:T(8,128)}, f32[4,5,16,128]{3,2,1,0:T(8,128)}, f32[4,16,5,128]{3,2,1,0:T(8,128)}, f32[4,16,5,128]{3,2,1,0:T(8,128)}, f32...) custom-call(f32[5,16,16,128]{3,2,1,0:T(8,128)} %refs_0_.1, ...), custom_call_target="tpu_custom_call" | custom-call | tf_op jit(solution)/shard_map/pallas_call | solution.py:159
  16.7 1.2 %pad_maximum_fusion.1 = f32[4,26,16,128]{3,2,1,0:T(8,128)S(1)} fusion(f32[4,5,16,128]{3,2,1,0:T(8,128)} %get-tuple-element.22, f32[4,16,16,128]{3,2,1,0:T(8,128)} %get-tuple-element.20, f32[4,5,16,128]{3,2,1,0:T(8,128)} %get-tuple-element.21), kind=kLoop, calls=%fused_computation.29 | loop fusion | flops 425984 | bytes 1703936 | tf_op jit(solution)/shard_map/concatenate | solution.py:252
  18.0 0.0 copy-done.17
  18.0 0.0 copy-start.1
  18.0 0.0 copy-start.15
  18.0 0.0 copy-start.16
  18.0 1.0 %fusion.36 = f32[4,16,128,16]{2,3,1,0:T(8,128)S(1)} fusion(f32[16,26,1,1]{1,0,3,2:T(8,128)S(1)} %copy-done.17, f32[4,26,16,128]{3,2,1,0:T(8,128)S(1)} %pad_maximum_fusion.1), kind=kOutput, calls=%fused_computation.27 | convolution fusion | flops 40894464 | bytes 1377920 | tf_op jit(solution)/shard_map/al,flyz->fayz/dot_general | solution.py:378
  19.0 0.0 copy-start.2
  19.0 0.0 copy-start
  19.0 0.0 copy-start.5
  19.1 0.2 copy.32
  19.3 0.9 %convolution_bitcast_fusion = f32[4,16,16,128]{3,2,1,0:T(8,128)S(1)} fusion(f32[16,26,1,1]{1,0,3,2:T(8,128)S(1)} %copy-done.17, f32[4,16,5,128]{3,2,1,0:T(8,128)S(1)} %copy-done.16, f32[4,16,16,128]{3,2,1,0:T(8,128)S(1)} %copy-done.1, f32[4,16,5,128]{3,2,1,0:T(8,128)S(1)} %copy-done.15), kind=kOutput, calls=%fused_computation.20 | convolution fusion | flops 41320448 | bytes 1377920 | tf_op jit(solution)/shard_map/al,fxlz->fxaz/dot_general | solution.py:378
  20.2 0.3 copy-done
  20.5 0.0 copy-done.8
  20.5 0.2 copy-done.9
  20.7 0.2 bitcast_dynamic-update-slice_fusion.11
  20.9 0.1 bitcast_dynamic-update-slice_fusion.10
  21.0 0.1 bitcast_dynamic-update-slice_fusion.9
  21.2 0.2 bitcast_dynamic-update-slice_fusion.8
  21.4 0.1 bitcast_dynamic-update-slice_fusion.6
  21.5 0.1 bitcast_dynamic-update-slice_fusion.5
  21.6 0.1 bitcast_dynamic-update-slice_fusion.4
  21.8 0.1 bitcast_dynamic-update-slice_fusion
  22.0 0.1 slice_bitcast_fusion.20
  22.1 1.5 %multiply_add_fusion = (f32[5,16,16,128]{3,2,1,0:T(8,128)}, f32[5,16,16,128]{3,2,1,0:T(8,128)}, f32[5,16,16,128]{3,2,1,0:T(8,128)}) fusion(f32[5,16,16,128]{3,2,1,0:T(8,128)S(1)} %bitcast_dynamic-update-slice_fusion, f32[5,16,16,128]{3,2,1,0:T(8,128)S(1)} %bitcast_dynamic-update-slice_fusion.4, f32[5,16,16,128]{3,2,1,0:T(8,128)S(1)} %get-tuple-element.64, ...), kind=kLoop, calls=%fused_computation.31 | loop fusion | flops 2457600 | bytes 5111808 | tf_op jit(solution)/shard_map/add | solution.py:442
  23.6 15.4 %shard_map.92 = (f32[5,5,16,128]{3,2,1,0:T(8,128)}, f32[5,5,16,128]{3,2,1,0:T(8,128)}, f32[5,16,5,128]{3,2,1,0:T(8,128)}, f32[5,16,5,128]{3,2,1,0:T(8,128)}, f32[5,16,16,128]{3,2,1,0:T(8,128)}) custom-call(f32[5,16,16,128]{3,2,1,0:T(8,128)} %get-tuple-element.48.refs_0_, f32[5,16,16,128]{3,2,1,0:T(8,128)} %get-tuple-element.47.refs_1_, ...), custom_call_target="tpu_custom_call" | custom-call | tf_op jit(solution)/shard_map/pallas_call | solution.py:159
  39.0 1.1 %pad_maximum_fusion = f32[5,26,16,128]{3,2,1,0:T(8,128)S(1)} fusion(f32[5,5,16,128]{3,2,1,0:T(8,128)} %get-tuple-element.28, f32[5,16,16,128]{3,2,1,0:T(8,128)S(1)} %copy-done.7, f32[5,5,16,128]{3,2,1,0:T(8,128)} %get-tuple-element.27), kind=kLoop, calls=%fused_computation.21 | loop fusion | flops 532480 | bytes 2129920 | tf_op jit(solution)/shard_map/concatenate | solution.py:229
  40.1 1.2 %fusion.11 = f32[5,16,128,16]{2,3,1,0:T(8,128)S(1)} fusion(f32[16,26,1,1]{1,0,3,2:T(8,128)S(1)} %copy-done.17, f32[5,26,16,128]{3,2,1,0:T(8,128)S(1)} %pad_maximum_fusion), kind=kOutput, calls=%fused_computation.12 | convolution fusion | flops 51118080 | bytes 1721984 | tf_op jit(solution)/shard_map/al,flyz->fayz/dot_general | solution.py:378
  41.3 0.0 copy-done.6
  41.4 0.0 copy-done.10
  41.4 0.1 copy-done.13
  41.4 0.1 copy-done.14
  41.5 1.3 %fusion.28.refs_0_ = f32[5,16,16,128]{3,2,1,0:T(8,128)S(1)} fusion(f32[5,16,16,128]{3,2,1,0:T(8,128)S(1)} %copy-done.2, f32[5,16,16,128]{3,2,1,0:T(8,128)S(1)} %copy-done.10, f32[16,26,1,1]{1,0,3,2:T(8,128)S(1)} %copy-done.17, f32[5,16,5,128]{3,2,1,0:T(8,128)S(1)} %copy-done.14, f32[5,16,16,128]{3,2,1,0:T(8,128)S(1)} %copy-done.6, ...), kind=kOutput, calls=%fused_computation.19 | convolution fusion | flops 52305920 | bytes 3819136 | tf_op jit(solution)/shard_map/al,fxlz->fxaz/dot_general | solution.py:378
  42.9 0.0 copy-start.3
  43.0 1.0 %pad_maximum_fusion.2.refs_1_ = f32[2,5,16,5,128]{4,3,2,1,0:T(8,128)} fusion(f32[1,5,16,5,128]{4,3,2,1,0:T(8,128)S(1)} %get-tuple-element.63, f32[1,5,16,5,128]{4,3,2,1,0:T(8,128)S(1)} %get-tuple-element.62), kind=kLoop, calls=%fused_computation.30 | loop fusion | flops 102400 | bytes 819200 | tf_op jit(solution)/shard_map/stack | solution.py:262
  44.0 13.4 %shard_map.93 = (f32[2,5,5,16,128]{4,3,2,1,0:T(8,128)}, f32[2,5,16,5,128]{4,3,2,1,0:T(8,128)}, f32[2,2,5,5,5,128]{5,4,3,2,1,0:T(8,128)}) custom-call(f32[5,16,16,128]{3,2,1,0:T(8,128)} %copy-done.3, f32[2,5,16,5,128]{4,3,2,1,0:T(8,128)} %pad_maximum_fusion.2.refs_1_), custom_call_target="tpu_custom_call" | custom-call | tf_op jit(solution)/shard_map/pallas_call | solution.py:159
  57.4 0.0 copy-start.12
  57.4 0.0 copy-start.11
  57.4 0.0 copy-start.4
  57.4 1.2 %slice_bitcast_fusion.3 = (f32[5,16,5,128]{3,2,1,0:T(8,128)S(1)}, f32[5,16,5,128]{3,2,1,0:T(8,128)S(1)}) fusion(f32[2,5,16,5,128]{4,3,2,1,0:T(8,128)} %get-tuple-element.34), kind=kLoop, calls=%fused_computation.38 | loop fusion | bytes 819200 | tf_op jit(solution)/shard_map/squeeze | solution.py:289
  58.7 0.0 copy-done.11
  58.7 0.2 copy-done.4
  58.9 0.4 maximum_maximum_fusion
  59.3 0.3 copy-done.18
  59.6 2.6 %fusion = f32[5,26,128,16]{2,3,1,0:T(8,128)S(1)} fusion(f32[16,26,1,1]{1,0,3,2:T(8,128)S(1)} %copy-done.18, f32[5,26,26,128]{3,2,1,0:T(8,128)S(1)} %maximum_maximum_fusion), kind=kOutput, calls=%fused_computation.1 | convolution fusion | flops 83066880 | bytes 2797184 | tf_op jit(solution)/shard_map/al,flyz->fayz/dot_general | solution.py:378
  62.2 2.0 %fusion.13.refs_0_ = f32[5,16,16,128]{3,2,1,0:T(8,128)} fusion(f32[16,26,1,1]{1,0,3,2:T(8,128)S(1)} %copy-done.18, f32[5,26,128,16]{2,3,1,0:T(8,128)S(1)} %fusion), kind=kOutput, calls=%fused_computation.14 | convolution fusion | flops 51118080 | bytes 1721984 | tf_op jit(solution)/shard_map/al,fxlz->fxaz/dot_general | solution.py:378
  64.2 8.7 %shard_map.94 = f32[5,16,16,128]{3,2,1,0:T(8,128)} custom-call(f32[5,16,16,128]{3,2,1,0:T(8,128)} %fusion.13.refs_0_, f32[128,128]{1,0:T(8,128)} %constant.35.refs_1_, f32[128,8]{1,0:T(8,128)} %constant.37.refs_2_, f32[128,8]{1,0:T(8,128)} %constant.39.refs_3_), custom_call_target="tpu_custom_call" | custom-call | tf_op jit(solution)/shard_map/pallas_call | solution.py:159
  73.0 2.0 %copy.46 = f32[5,16,16,128]{3,2,1,0:T(8,128)} copy(f32[5,16,16,128]{3,2,1,0:T(8,128)} %shard_map.94) | data formatting | bytes 1310720
  (25 shorter events, 0.3 us)
Async XLA Ops:
  0.0 18.0 %copy-start.17 = (f32[16,26,1,1]{1,0,3,2:T(8,128)S(1)}, f32[16,26,1,1]{1,0,3,2:T(8,128)}, u32[]{:S(2)}) copy-start(f32[16,26,1,1]{1,0,3,2:T(8,128)} %constant.40) | copy-start | bytes 4996
  18.0 1.2 %copy-start.1 = (f32[4,16,16,128]{3,2,1,0:T(8,128)S(1)}, f32[4,16,16,128]{3,2,1,0:T(8,128)}, u32[]{:S(2)}) copy-start(f32[4,16,16,128]{3,2,1,0:T(8,128)} %get-tuple-element.20) | copy-start | bytes 1572868
  18.0 1.2 %copy-start.15 = (f32[4,16,5,128]{3,2,1,0:T(8,128)S(1)}, f32[4,16,5,128]{3,2,1,0:T(8,128)}, u32[]{:S(2)}) copy-start(f32[4,16,5,128]{3,2,1,0:T(8,128)} %get-tuple-element.23) | copy-start | bytes 491524
  18.0 1.2 %copy-start.16 = (f32[4,16,5,128]{3,2,1,0:T(8,128)S(1)}, f32[4,16,5,128]{3,2,1,0:T(8,128)}, u32[]{:S(2)}) copy-start(f32[4,16,5,128]{3,2,1,0:T(8,128)} %get-tuple-element.24) | copy-start | bytes 491524
  19.0 1.2 %copy-start.2 = (f32[5,16,16,128]{3,2,1,0:T(8,128)S(1)}, f32[5,16,16,128]{3,2,1,0:T(8,128)}, u32[]{:S(2)}) copy-start(f32[5,16,16,128]{3,2,1,0:T(8,128)} %refs_0_.1) | copy-start | bytes 1966084
  19.0 1.5 %copy-start = (f32[3,3,16,16,128]{4,3,2,1,0:T(8,128)S(1)}, f32[3,3,16,16,128]{4,3,2,1,0:T(8,128)}, u32[]{:S(2)}) copy-start(f32[3,3,16,16,128]{4,3,2,1,0:T(8,128)} %param.10) | copy-start | bytes 3538948
  19.0 1.5 %copy-start.5 = (f32[16,16,128]{2,1,0:T(8,128)S(1)}, f32[16,16,128]{2,1,0:T(8,128)}, u32[]{:S(2)}) copy-start(f32[16,16,128]{2,1,0:T(8,128)} %param.11) | copy-start | bytes 393220
  19.0 1.5 %copy-start.8 = (f32[16,16,128]{2,1,0:T(8,128)S(1)}, f32[16,16,128]{2,1,0:T(8,128)}, u32[]{:S(2)}) copy-start(f32[16,16,128]{2,1,0:T(8,128)} %get-tuple-element.26) | copy-start | bytes 393220
  19.1 1.7 %copy-start.9 = (f32[4,16,16,128]{3,2,1,0:T(8,128)S(1)}, f32[4,16,16,128]{3,2,1,0:T(8,128)}, u32[]{:S(2)}) copy-start(f32[4,16,16,128]{3,2,1,0:T(8,128)} %get-tuple-element.25) | copy-start | bytes 1572868
  23.6 15.4 %copy-start.7 = (f32[5,16,16,128]{3,2,1,0:T(8,128)S(1)}, f32[5,16,16,128]{3,2,1,0:T(8,128)}, u32[]{:S(2)}) copy-start(f32[5,16,16,128]{3,2,1,0:T(8,128)} %get-tuple-element.48.refs_0_) | copy-start | bytes 1966084
  40.1 1.3 %copy-start.6 = (f32[5,16,16,128]{3,2,1,0:T(8,128)S(1)}, f32[5,16,16,128]{3,2,1,0:T(8,128)}, u32[]{:S(2)}) copy-start(f32[5,16,16,128]{3,2,1,0:T(8,128)} %get-tuple-element.47.refs_1_) | copy-start | bytes 1966084
  40.1 1.3 %copy-start.10 = (f32[5,16,16,128]{3,2,1,0:T(8,128)S(1)}, f32[5,16,16,128]{3,2,1,0:T(8,128)}, u32[]{:S(2)}) copy-start(f32[5,16,16,128]{3,2,1,0:T(8,128)} %get-tuple-element.31) | copy-start | bytes 1966084
  40.1 1.3 %copy-start.13 = (f32[5,16,5,128]{3,2,1,0:T(8,128)S(1)}, f32[5,16,5,128]{3,2,1,0:T(8,128)}, u32[]{:S(2)}) copy-start(f32[5,16,5,128]{3,2,1,0:T(8,128)} %get-tuple-element.29) | copy-start | bytes 614404
  40.1 1.4 %copy-start.14 = (f32[5,16,5,128]{3,2,1,0:T(8,128)S(1)}, f32[5,16,5,128]{3,2,1,0:T(8,128)}, u32[]{:S(2)}) copy-start(f32[5,16,5,128]{3,2,1,0:T(8,128)} %get-tuple-element.30) | copy-start | bytes 614404
  42.9 1.1 %copy-start.3 = (f32[5,16,16,128]{3,2,1,0:T(8,128)}, f32[5,16,16,128]{3,2,1,0:T(8,128)S(1)}, u32[]{:S(2)}) copy-start(f32[5,16,16,128]{3,2,1,0:T(8,128)S(1)} %fusion.28.refs_0_) | copy-start | bytes 1966084
  57.4 1.3 %copy-start.12 = (f32[2,2,5,5,5,128]{5,4,3,2,1,0:T(8,128)S(1)}, f32[2,2,5,5,5,128]{5,4,3,2,1,0:T(8,128)}, u32[]{:S(2)}) copy-start(f32[2,2,5,5,5,128]{5,4,3,2,1,0:T(8,128)} %get-tuple-element.32) | copy-start | bytes 768004
  57.4 1.3 %copy-start.11 = (f32[2,5,5,16,128]{4,3,2,1,0:T(8,128)S(1)}, f32[2,5,5,16,128]{4,3,2,1,0:T(8,128)}, u32[]{:S(2)}) copy-start(f32[2,5,5,16,128]{4,3,2,1,0:T(8,128)} %get-tuple-element.33) | copy-start | bytes 1228804
  57.4 1.5 %copy-start.4 = (f32[5,16,16,128]{3,2,1,0:T(8,128)S(1)}, f32[5,16,16,128]{3,2,1,0:T(8,128)}, u32[]{:S(2)}) copy-start(f32[5,16,16,128]{3,2,1,0:T(8,128)} %copy-done.3) | copy-start | bytes 1966084
  58.9 0.7 copy-start.18

commit v16 on v15

--- a/solution.py
+++ b/solution.py
@@ -257,7 +257,76 @@
     )
 
 
+def plane_kernel(sizes, value_ref, extended, across, send_sems, recv_sems):
+    length_x, length_y = value_ref.shape[1], value_ref.shape[2]
+    here = [lax.axis_index(axis) for axis in AXES]
+
+    def device(offset):
+        return tuple(
+            lax.rem(here[slot] + offset[slot] + sizes[slot], sizes[slot]) for slot in range(3)
+        )
+
+    barrier = pltpu.get_barrier_semaphore()
+    for offset in ((1, 0, 0), (-1, 0, 0), (0, 1, 0), (0, -1, 0)):
+        pl.semaphore_signal(barrier, inc=1, device_id=device(offset), device_id_type=MESH)
+    extended[:, WIDTH : WIDTH + length_x] = value_ref[...]
+    pl.semaphore_wait(barrier, 4)
+    along_x = [
+        pltpu.make_async_remote_copy(
+            src_ref=value_ref.at[:, pl.ds(length_x - WIDTH, WIDTH)],
+            dst_ref=extended.at[:, pl.ds(0, WIDTH)],
+            send_sem=send_sems.at[0], recv_sem=recv_sems.at[0],
+            device_id=device((1, 0, 0)), device_id_type=MESH,
+        ),
+        pltpu.make_async_remote_copy(
+            src_ref=value_ref.at[:, pl.ds(0, WIDTH)],
+            dst_ref=extended.at[:, pl.ds(WIDTH + length_x, WIDTH)],
+            send_sem=send_sems.at[1], recv_sem=recv_sems.at[1],
+            device_id=device((-1, 0, 0)), device_id_type=MESH,
+        ),
+    ]
+    for copy in along_x:
+        copy.start()
+    for copy in along_x:
+        copy.wait()
+    along_y = [
+        pltpu.make_async_remote_copy(
+            src_ref=extended.at[:, :, pl.ds(length_y - WIDTH, WIDTH)],
+            dst_ref=across.at[0],
+            send_sem=send_sems.at[2], recv_sem=recv_sems.at[2],
+            device_id=device((0, 1, 0)), device_id_type=MESH,
+        ),
+        pltpu.make_async_remote_copy(
+            src_ref=extended.at[:, :, pl.ds(0, WIDTH)],
+            dst_ref=across.at[1],
+            send_sem=send_sems.at[3], recv_sem=recv_sems.at[3],
+            device_id=device((0, -1, 0)), device_id_type=MESH,
+        ),
+    ]
+    for copy in along_y:
+        copy.start()
+    for copy in along_y:
+        copy.wait()
+
+
 def exchange_plane(value, tag):
+    sizes = tuple(lax.axis_size(axis) for axis in AXES)
+    fields, length_x, length_y, depth = value.shape
+    extended, across = pl.pallas_call(
+        functools.partial(plane_kernel, sizes),
+        out_shape=[
+            jax.ShapeDtypeStruct((fields, length_x + 2 * WIDTH, length_y, depth), value.dtype),
+            jax.ShapeDtypeStruct((2, fields, length_x + 2 * WIDTH, WIDTH, depth), value.dtype),
+        ],
+        in_specs=[pl.BlockSpec(memory_space=pltpu.VMEM)],
+        out_specs=[pl.BlockSpec(memory_space=pltpu.VMEM), pl.BlockSpec(memory_space=pl.ANY)],
+        scratch_shapes=[pltpu.SemaphoreType.DMA((4,)), pltpu.SemaphoreType.DMA((4,))],
+        compiler_params=pltpu.CompilerParams(collective_id=tag, has_side_effects=True),
+    )(value)
+    return jnp.concatenate([across[0], extended, across[1]], axis=2)
+
+
+def exchange_plane_edges(value, tag):
     length_x, length_y = value.shape[1], value.shape[2]
     faces_y = jnp.stack(
         [

time: 75.8 us -> 83.9 us (1.11)
  Pallas kernels: 54.2 us -> 62.2 us
  other arithmetic: 6.43 us -> 5.42 us
  matrix products: 9.03 us -> 9.88 us
    pallas_call x0 -> x1, Pallas kernels: none -> 21.3 us  [exchange_plane(): pl.pallas_call(functools.partial(plane_kernel, sizes), out_shape=[jax.Sha...]
    pallas_call x4 -> x3, Pallas kernels: 54.2 us -> 40.9 us  [exchange(): pl.pallas_call(functools.partial(exchange_kernel, tuple(routes), sizes, l...]
    another operation x1 -> x0, other arithmetic: 0.99 us -> none  [exchange_plane(): jnp.stack([lax.slice_in_dim(value, length_y - WIDTH, length_y, axis=2), l...]
    dot_general x6, matrix products: 9.03 us -> 9.88 us  [sweep_lines(): jnp.einsum(line_forms[dim], matrix, padded, precision=lax.Precision.HIGHEST)]
    unnamed x40 -> x34, local copies, waits for them, and re-layouts: 3.29 us -> 3.25 us
where the time goes in v16:
time: 83.9 us; the launch traced here: 82.6 us
  Pallas kernels  62.2 us (74%)
  matrix products  9.88 us (12%)
  other arithmetic  5.42 us (6%)
  local copies, waits for them, and re-layouts  4.85 us (6%)
    pallas_call x3, Pallas kernels, exchange(): pl.pallas_call(functools.partial(exchange_kernel, tuple(routes), sizes, l...  40.9 us
    pallas_call x1, Pallas kernels, exchange_plane(): pl.pallas_call(functools.partial(plane_kernel, sizes), out_shape=[jax.Sha...  21.3 us
    dot_general x6, matrix products, sweep_lines(): jnp.einsum(line_forms[dim], matrix, padded, precision=lax.Precision.HIGHEST)  9.88 us
    unnamed x34, local copies, waits for them, and re-layouts  3.25 us

profile of v16, /device:TPU:1, one launch (start us, length us, event | category | flops | bytes accessed | tf_op | source)
XLA Modules:
  0.0 82.6 jit_solution(669432003142917343)
XLA Ops:
  0.0 16.8 %shard_map.91 = (f32[4,5,16,128]{3,2,1,0:T(8,128)}, f32[4,5,16,128]{3,2,1,0:T(8,128)}, f32[4,16,5,128]{3,2,1,0:T(8,128)}, f32[4,16,5,128]{3,2,1,0:T(8,128)}, f32...) custom-call(f32[5,16,16,128]{3,2,1,0:T(8,128)} %refs_0_.1, ...), custom_call_target="tpu_custom_call" | custom-call | tf_op jit(solution)/shard_map/pallas_call | solution.py:159
  16.8 1.2 %pad_maximum_fusion.2 = f32[4,26,16,128]{3,2,1,0:T(8,128)S(1)} fusion(f32[4,5,16,128]{3,2,1,0:T(8,128)} %get-tuple-element.21, f32[4,16,16,128]{3,2,1,0:T(8,128)} %get-tuple-element.19, f32[4,5,16,128]{3,2,1,0:T(8,128)} %get-tuple-element.20), kind=kLoop, calls=%fused_computation.29 | loop fusion | flops 425984 | bytes 1703936 | tf_op jit(solution)/shard_map/concatenate | solution.py:252
  18.0 0.0 copy-done.14
  18.0 0.0 copy-start.1
  18.0 0.0 copy-start.12
  18.0 0.0 copy-start.13
  18.1 1.0 %fusion.36 = f32[4,16,128,16]{2,3,1,0:T(8,128)S(1)} fusion(f32[16,26,1,1]{1,0,3,2:T(8,128)S(1)} %copy-done.14, f32[4,26,16,128]{3,2,1,0:T(8,128)S(1)} %pad_maximum_fusion.2), kind=kOutput, calls=%fused_computation.27 | convolution fusion | flops 40894464 | bytes 1377920 | tf_op jit(solution)/shard_map/al,flyz->fayz/dot_general | solution.py:447
  19.0 0.0 copy-start.2
  19.0 0.0 copy-start.7
  19.1 0.2 copy.32
  19.2 0.0 copy-start
  19.2 0.0 copy-start.3
  19.2 0.0 copy-start.6
  19.3 0.0 copy-done.1
  19.3 0.0 copy-done.12
  19.3 0.0 copy-done.13
  19.3 0.9 %convolution_bitcast_fusion = f32[4,16,16,128]{3,2,1,0:T(8,128)S(1)} fusion(f32[16,26,1,1]{1,0,3,2:T(8,128)S(1)} %copy-done.14, f32[4,16,5,128]{3,2,1,0:T(8,128)S(1)} %copy-done.13, f32[4,16,16,128]{3,2,1,0:T(8,128)S(1)} %copy-done.1, f32[4,16,5,128]{3,2,1,0:T(8,128)S(1)} %copy-done.12), kind=kOutput, calls=%fused_computation.20 | convolution fusion | flops 41320448 | bytes 1377920 | tf_op jit(solution)/shard_map/al,fxlz->fxaz/dot_general | solution.py:447
  20.2 0.0 copy-done.2
  20.2 0.1 copy-done.7
  20.3 0.4 copy-done
  20.7 0.0 copy-done.6
  20.7 0.2 bitcast_dynamic-update-slice_fusion.11
  20.9 0.1 bitcast_dynamic-update-slice_fusion.10
  21.1 0.1 bitcast_dynamic-update-slice_fusion.9
  21.2 0.2 bitcast_dynamic-update-slice_fusion.8
  21.4 0.1 bitcast_dynamic-update-slice_fusion.6
  21.5 0.1 bitcast_dynamic-update-slice_fusion.5
  21.6 0.1 bitcast_dynamic-update-slice_fusion.4
  21.9 0.1 bitcast_dynamic-update-slice_fusion
  22.0 0.1 slice_bitcast_fusion.16
  22.1 1.5 %multiply_add_fusion = (f32[5,16,16,128]{3,2,1,0:T(8,128)}, f32[5,16,16,128]{3,2,1,0:T(8,128)}, f32[5,16,16,128]{3,2,1,0:T(8,128)}) fusion(f32[5,16,16,128]{3,2,1,0:T(8,128)S(1)} %bitcast_dynamic-update-slice_fusion, f32[5,16,16,128]{3,2,1,0:T(8,128)S(1)} %bitcast_dynamic-update-slice_fusion.4, f32[5,16,16,128]{3,2,1,0:T(8,128)S(1)} %get-tuple-element.60, ...), kind=kLoop, calls=%fused_computation.30 | loop fusion | flops 2457600 | bytes 5111808 | tf_op jit(solution)/shard_map/add | solution.py:511
  23.6 15.4 %shard_map.92 = (f32[5,5,16,128]{3,2,1,0:T(8,128)}, f32[5,5,16,128]{3,2,1,0:T(8,128)}, f32[5,16,5,128]{3,2,1,0:T(8,128)}, f32[5,16,5,128]{3,2,1,0:T(8,128)}, f32[5,16,16,128]{3,2,1,0:T(8,128)}) custom-call(f32[5,16,16,128]{3,2,1,0:T(8,128)} %get-tuple-element.46.refs_0_, f32[5,16,16,128]{3,2,1,0:T(8,128)} %get-tuple-element.45.refs_1_, ...), custom_call_target="tpu_custom_call" | custom-call | tf_op jit(solution)/shard_map/pallas_call | solution.py:159
  39.0 1.1 %pad_maximum_fusion.1 = f32[5,26,16,128]{3,2,1,0:T(8,128)S(1)} fusion(f32[5,5,16,128]{3,2,1,0:T(8,128)} %get-tuple-element.27, f32[5,16,16,128]{3,2,1,0:T(8,128)S(1)} %copy-done.5, f32[5,5,16,128]{3,2,1,0:T(8,128)} %get-tuple-element.26), kind=kLoop, calls=%fused_computation.21 | loop fusion | flops 532480 | bytes 2129920 | tf_op jit(solution)/shard_map/concatenate | solution.py:229
  40.1 1.2 %fusion.11 = f32[5,16,128,16]{2,3,1,0:T(8,128)S(1)} fusion(f32[16,26,1,1]{1,0,3,2:T(8,128)S(1)} %copy-done.14, f32[5,26,16,128]{3,2,1,0:T(8,128)S(1)} %pad_maximum_fusion.1), kind=kOutput, calls=%fused_computation.12 | convolution fusion | flops 51118080 | bytes 1721984 | tf_op jit(solution)/shard_map/al,flyz->fayz/dot_general | solution.py:447
  41.4 0.0 copy-done.9
  41.4 0.1 copy-done.10
  41.5 0.1 copy-done.11
  41.6 2.2 %fusion.28.value_ref = f32[5,16,16,128]{3,2,1,0:T(8,128)} fusion(f32[5,16,16,128]{3,2,1,0:T(8,128)S(1)} %copy-done.2, f32[5,16,16,128]{3,2,1,0:T(8,128)S(1)} %copy-done.9, f32[16,26,1,1]{1,0,3,2:T(8,128)S(1)} %copy-done.14, f32[5,16,5,128]{3,2,1,0:T(8,128)S(1)} %copy-done.11, f32[5,16,16,128]{3,2,1,0:T(8,128)S(1)} %copy-done.4, ...), kind=kOutput, calls=%fused_computation.19 | convolution fusion | flops 52305920 | bytes 3819136 | tf_op jit(solution)/shard_map/al,fxlz->fxaz/dot_general | solution.py:447
  43.8 21.3 %shard_map.93 = (f32[5,26,16,128]{3,2,1,0:T(8,128)}, f32[2,5,26,5,128]{4,3,2,1,0:T(8,128)}) custom-call(f32[5,16,16,128]{3,2,1,0:T(8,128)} %fusion.28.value_ref), custom_call_target="tpu_custom_call" | custom-call | tf_op jit(solution)/shard_map/pallas_call | solution.py:315
  65.0 0.0 copy-start.8
  65.0 1.4 %slice_bitcast_fusion.1 = (f32[5,26,5,128]{3,2,1,0:T(8,128)S(1)}, f32[5,26,5,128]{3,2,1,0:T(8,128)S(1)}) fusion(f32[2,5,26,5,128]{4,3,2,1,0:T(8,128)} %get-tuple-element.31), kind=kLoop, calls=%fused_computation.34 | loop fusion | bytes 1331200 | tf_op jit(solution)/shard_map/squeeze | solution.py:326
  66.4 0.2 copy-done.8
  66.6 0.4 pad_maximum_fusion
  66.9 0.3 copy-done.15
  67.3 2.6 %fusion = f32[5,26,128,16]{2,3,1,0:T(8,128)S(1)} fusion(f32[16,26,1,1]{1,0,3,2:T(8,128)S(1)} %copy-done.15, f32[5,26,26,128]{3,2,1,0:T(8,128)S(1)} %pad_maximum_fusion), kind=kOutput, calls=%fused_computation.1 | convolution fusion | flops 83066880 | bytes 2797184 | tf_op jit(solution)/shard_map/al,flyz->fayz/dot_general | solution.py:447
  69.9 2.0 %fusion.13.refs_0_ = f32[5,16,16,128]{3,2,1,0:T(8,128)} fusion(f32[16,26,1,1]{1,0,3,2:T(8,128)S(1)} %copy-done.15, f32[5,26,128,16]{2,3,1,0:T(8,128)S(1)} %fusion), kind=kOutput, calls=%fused_computation.14 | convolution fusion | flops 51118080 | bytes 1721984 | tf_op jit(solution)/shard_map/al,fxlz->fxaz/dot_general | solution.py:447
  71.9 8.7 %shard_map.94 = f32[5,16,16,128]{3,2,1,0:T(8,128)} custom-call(f32[5,16,16,128]{3,2,1,0:T(8,128)} %fusion.13.refs_0_, f32[128,128]{1,0:T(8,128)} %constant.35.refs_1_, f32[128,8]{1,0:T(8,128)} %constant.37.refs_2_, f32[128,8]{1,0:T(8,128)} %constant.39.refs_3_), custom_call_target="tpu_custom_call" | custom-call | tf_op jit(solution)/shard_map/pallas_call | solution.py:159
  80.6 2.0 %copy.46 = f32[5,16,16,128]{3,2,1,0:T(8,128)} copy(f32[5,16,16,128]{3,2,1,0:T(8,128)} %shard_map.94) | data formatting | bytes 1310720
  (15 shorter events, 0.2 us)
Async XLA Ops:
  0.0 18.0 %copy-start.14 = (f32[16,26,1,1]{1,0,3,2:T(8,128)S(1)}, f32[16,26,1,1]{1,0,3,2:T(8,128)}, u32[]{:S(2)}) copy-start(f32[16,26,1,1]{1,0,3,2:T(8,128)} %constant.40) | copy-start | bytes 4996
  18.0 1.2 %copy-start.1 = (f32[4,16,16,128]{3,2,1,0:T(8,128)S(1)}, f32[4,16,16,128]{3,2,1,0:T(8,128)}, u32[]{:S(2)}) copy-start(f32[4,16,16,128]{3,2,1,0:T(8,128)} %get-tuple-element.19) | copy-start | bytes 1572868
  18.0 1.2 %copy-start.12 = (f32[4,16,5,128]{3,2,1,0:T(8,128)S(1)}, f32[4,16,5,128]{3,2,1,0:T(8,128)}, u32[]{:S(2)}) copy-start(f32[4,16,5,128]{3,2,1,0:T(8,128)} %get-tuple-element.22) | copy-start | bytes 491524
  18.0 1.2 %copy-start.13 = (f32[4,16,5,128]{3,2,1,0:T(8,128)S(1)}, f32[4,16,5,128]{3,2,1,0:T(8,128)}, u32[]{:S(2)}) copy-start(f32[4,16,5,128]{3,2,1,0:T(8,128)} %get-tuple-element.23) | copy-start | bytes 491524
  19.0 1.2 %copy-start.2 = (f32[5,16,16,128]{3,2,1,0:T(8,128)S(1)}, f32[5,16,16,128]{3,2,1,0:T(8,128)}, u32[]{:S(2)}) copy-start(f32[5,16,16,128]{3,2,1,0:T(8,128)} %refs_0_.1) | copy-start | bytes 1966084
  19.0 1.3 %copy-start.7 = (f32[4,16,16,128]{3,2,1,0:T(8,128)S(1)}, f32[4,16,16,128]{3,2,1,0:T(8,128)}, u32[]{:S(2)}) copy-start(f32[4,16,16,128]{3,2,1,0:T(8,128)} %get-tuple-element.24) | copy-start | bytes 1572868
  19.2 1.5 %copy-start = (f32[3,3,16,16,128]{4,3,2,1,0:T(8,128)S(1)}, f32[3,3,16,16,128]{4,3,2,1,0:T(8,128)}, u32[]{:S(2)}) copy-start(f32[3,3,16,16,128]{4,3,2,1,0:T(8,128)} %param.10) | copy-start | bytes 3538948
  19.2 1.5 %copy-start.3 = (f32[16,16,128]{2,1,0:T(8,128)S(1)}, f32[16,16,128]{2,1,0:T(8,128)}, u32[]{:S(2)}) copy-start(f32[16,16,128]{2,1,0:T(8,128)} %param.11) | copy-start | bytes 393220
  19.2 1.5 %copy-start.6 = (f32[16,16,128]{2,1,0:T(8,128)S(1)}, f32[16,16,128]{2,1,0:T(8,128)}, u32[]{:S(2)}) copy-start(f32[16,16,128]{2,1,0:T(8,128)} %get-tuple-element.25) | copy-start | bytes 393220
  23.6 15.4 %copy-start.5 = (f32[5,16,16,128]{3,2,1,0:T(8,128)S(1)}, f32[5,16,16,128]{3,2,1,0:T(8,128)}, u32[]{:S(2)}) copy-start(f32[5,16,16,128]{3,2,1,0:T(8,128)} %get-tuple-element.46.refs_0_) | copy-start | bytes 1966084
  40.1 1.3 %copy-start.4 = (f32[5,16,16,128]{3,2,1,0:T(8,128)S(1)}, f32[5,16,16,128]{3,2,1,0:T(8,128)}, u32[]{:S(2)}) copy-start(f32[5,16,16,128]{3,2,1,0:T(8,128)} %get-tuple-element.45.refs_1_) | copy-start | bytes 1966084
  40.1 1.3 %copy-start.9 = (f32[5,16,16,128]{3,2,1,0:T(8,128)S(1)}, f32[5,16,16,128]{3,2,1,0:T(8,128)}, u32[]{:S(2)}) copy-start(f32[5,16,16,128]{3,2,1,0:T(8,128)} %get-tuple-element.30) | copy-start | bytes 1966084
  40.1 1.3 %copy-start.10 = (f32[5,16,5,128]{3,2,1,0:T(8,128)S(1)}, f32[5,16,5,128]{3,2,1,0:T(8,128)}, u32[]{:S(2)}) copy-start(f32[5,16,5,128]{3,2,1,0:T(8,128)} %get-tuple-element.28) | copy-start | bytes 614404
  40.1 1.4 %copy-start.11 = (f32[5,16,5,128]{3,2,1,0:T(8,128)S(1)}, f32[5,16,5,128]{3,2,1,0:T(8,128)}, u32[]{:S(2)}) copy-start(f32[5,16,5,128]{3,2,1,0:T(8,128)} %get-tuple-element.29) | copy-start | bytes 614404
  65.0 1.6 %copy-start.8 = (f32[5,26,16,128]{3,2,1,0:T(8,128)S(1)}, f32[5,26,16,128]{3,2,1,0:T(8,128)}, u32[]{:S(2)}) copy-start(f32[5,26,16,128]{3,2,1,0:T(8,128)} %get-tuple-element.32) | copy-start | bytes 3194884
  66.6 0.7 copy-start.15

commit v17 on v15

--- a/solution.py
+++ b/solution.py
@@ -466,9 +466,9 @@
     divergence = divergence + sweep_lines(padded[1], derive[1], 2)
     divergence = divergence + padded[2]
     sectioned = conserved_solution - step_duration * jacobian * divergence
-    result = sweep_lines(exchange_plane(sectioned, 2), smooth[0], 1)
+    result = sweep_zeta(sectioned, smooth[2], 4)
+    result = sweep_lines(exchange_plane(result, 2), smooth[0], 1)
     result = sweep_lines(result, smooth[1], 2)
-    result = sweep_zeta(result, smooth[2], 4)
     return result
 
 

time: 75.8 us -> 76.3 us (level)
  Pallas kernels: 54.2 us -> 55.6 us
  local copies, waits for them, and re-layouts: 4.87 us -> 3.95 us
    unnamed x40 -> x37, local copies, waits for them, and re-layouts: 3.29 us -> 1.3 us
    pallas_call x4, Pallas kernels: 54.2 us -> 55.6 us  [exchange(): pl.pallas_call(functools.partial(exchange_kernel, tuple(routes), sizes, l...]
    another operation x1, local copies, waits for them, and re-layouts: 0.05 us -> 1.12 us  [exchange_plane(): jnp.stack([lax.slice_in_dim(value, length_y - WIDTH, length_y, axis=2), l...]
where the time goes in v17:
time: 76.3 us; the launch traced here: 76 us
  Pallas kernels  55.6 us (73%)
  matrix products  9.7 us (13%)
  other arithmetic  6.34 us (8%)
  local copies, waits for them, and re-layouts  3.95 us (5%)
    pallas_call x4, Pallas kernels, exchange(): pl.pallas_call(functools.partial(exchange_kernel, tuple(routes), sizes, l...  55.6 us
    dot_general x6, matrix products, sweep_lines(): jnp.einsum(line_forms[dim], matrix, padded, precision=lax.Precision.HIGHEST)  9.7 us

profile of v17, /device:TPU:1, one launch (start us, length us, event | category | flops | bytes accessed | tf_op | source)
XLA Modules:
  0.0 76.0 jit_solution(6952034875107251718)
XLA Ops:
  0.0 16.8 %shard_map.91 = (f32[4,5,16,128]{3,2,1,0:T(8,128)}, f32[4,5,16,128]{3,2,1,0:T(8,128)}, f32[4,16,5,128]{3,2,1,0:T(8,128)}, f32[4,16,5,128]{3,2,1,0:T(8,128)}, f32...) custom-call(f32[5,16,16,128]{3,2,1,0:T(8,128)} %refs_0_.1, ...), custom_call_target="tpu_custom_call" | custom-call | tf_op jit(solution)/shard_map/pallas_call | solution.py:159
  16.8 1.2 %pad_maximum_fusion.1 = f32[4,26,16,128]{3,2,1,0:T(8,128)S(1)} fusion(f32[4,5,16,128]{3,2,1,0:T(8,128)} %get-tuple-element.22, f32[4,16,16,128]{3,2,1,0:T(8,128)} %get-tuple-element.20, f32[4,5,16,128]{3,2,1,0:T(8,128)} %get-tuple-element.21), kind=kLoop, calls=%fused_computation.29 | loop fusion | flops 425984 | bytes 1703936 | tf_op jit(solution)/shard_map/concatenate | solution.py:252
  18.1 1.0 %fusion.36 = f32[4,16,128,16]{2,3,1,0:T(8,128)S(1)} fusion(f32[16,26,1,1]{1,0,3,2:T(8,128)S(1)} %copy-done.16, f32[4,26,16,128]{3,2,1,0:T(8,128)S(1)} %pad_maximum_fusion.1), kind=kOutput, calls=%fused_computation.27 | convolution fusion | flops 40894464 | bytes 1377920 | tf_op jit(solution)/shard_map/al,flyz->fayz/dot_general | solution.py:378
  19.0 0.0 copy-start.2
  19.0 0.0 copy-start
  19.1 0.0 copy-start.4
  19.1 0.0 copy-start.7
  19.1 0.0 copy-start.8
  19.1 0.2 copy.32
  19.3 0.9 %convolution_bitcast_fusion = f32[4,16,16,128]{3,2,1,0:T(8,128)S(1)} fusion(f32[16,26,1,1]{1,0,3,2:T(8,128)S(1)} %copy-done.16, f32[4,16,5,128]{3,2,1,0:T(8,128)S(1)} %copy-done.15, f32[4,16,16,128]{3,2,1,0:T(8,128)S(1)} %copy-done.1, f32[4,16,5,128]{3,2,1,0:T(8,128)S(1)} %copy-done.14), kind=kOutput, calls=%fused_computation.20 | convolution fusion | flops 41320448 | bytes 1377920 | tf_op jit(solution)/shard_map/al,fxlz->fxaz/dot_general | solution.py:378
  20.2 0.0 copy-done.2
  20.2 0.3 copy-done
  20.5 0.0 copy-done.4
  20.5 0.0 copy-done.7
  20.6 0.2 copy-done.8
  20.7 0.2 bitcast_dynamic-update-slice_fusion.11
  20.9 0.1 bitcast_dynamic-update-slice_fusion.10
  21.1 0.1 bitcast_dynamic-update-slice_fusion.9
  21.2 0.2 bitcast_dynamic-update-slice_fusion.8
  21.4 0.1 bitcast_dynamic-update-slice_fusion.6
  21.5 0.1 bitcast_dynamic-update-slice_fusion.5
  21.6 0.1 bitcast_dynamic-update-slice_fusion.4
  21.9 0.1 bitcast_dynamic-update-slice_fusion
  22.0 0.1 slice_bitcast_fusion.20
  22.1 1.5 %multiply_add_fusion = (f32[5,16,16,128]{3,2,1,0:T(8,128)}, f32[5,16,16,128]{3,2,1,0:T(8,128)}, f32[5,16,16,128]{3,2,1,0:T(8,128)}) fusion(f32[5,16,16,128]{3,2,1,0:T(8,128)S(1)} %bitcast_dynamic-update-slice_fusion, f32[5,16,16,128]{3,2,1,0:T(8,128)S(1)} %bitcast_dynamic-update-slice_fusion.4, f32[5,16,16,128]{3,2,1,0:T(8,128)S(1)} %get-tuple-element.64, ...), kind=kLoop, calls=%fused_computation.31 | loop fusion | flops 2457600 | bytes 5111808 | tf_op jit(solution)/shard_map/add | solution.py:442
  23.6 15.4 %shard_map.92 = (f32[5,5,16,128]{3,2,1,0:T(8,128)}, f32[5,5,16,128]{3,2,1,0:T(8,128)}, f32[5,16,5,128]{3,2,1,0:T(8,128)}, f32[5,16,5,128]{3,2,1,0:T(8,128)}, f32[5,16,16,128]{3,2,1,0:T(8,128)}) custom-call(f32[5,16,16,128]{3,2,1,0:T(8,128)} %get-tuple-element.48.refs_0_, f32[5,16,16,128]{3,2,1,0:T(8,128)} %get-tuple-element.47.refs_1_, ...), custom_call_target="tpu_custom_call" | custom-call | tf_op jit(solution)/shard_map/pallas_call | solution.py:159
  39.0 1.1 %pad_maximum_fusion = f32[5,26,16,128]{3,2,1,0:T(8,128)S(1)} fusion(f32[5,5,16,128]{3,2,1,0:T(8,128)} %get-tuple-element.28, f32[5,16,16,128]{3,2,1,0:T(8,128)S(1)} %copy-done.6, f32[5,5,16,128]{3,2,1,0:T(8,128)} %get-tuple-element.27), kind=kLoop, calls=%fused_computation.21 | loop fusion | flops 532480 | bytes 2129920 | tf_op jit(solution)/shard_map/concatenate | solution.py:229
  40.1 0.0 copy-start.5
  40.1 0.0 copy-start.9
  40.1 0.0 copy-start.12
  40.1 0.0 copy-start.13
  40.1 1.2 %fusion.11 = f32[5,16,128,16]{2,3,1,0:T(8,128)S(1)} fusion(f32[16,26,1,1]{1,0,3,2:T(8,128)S(1)} %copy-done.16, f32[5,26,16,128]{3,2,1,0:T(8,128)S(1)} %pad_maximum_fusion), kind=kOutput, calls=%fused_computation.12 | convolution fusion | flops 51118080 | bytes 1721984 | tf_op jit(solution)/shard_map/al,flyz->fayz/dot_general | solution.py:378
  41.4 0.0 copy-done.5
  41.4 0.0 copy-done.9
  41.4 0.1 copy-done.12
  41.5 0.1 copy-done.13
  41.6 2.2 %fusion.28.refs_0_ = f32[5,16,16,128]{3,2,1,0:T(8,128)} fusion(f32[5,16,16,128]{3,2,1,0:T(8,128)S(1)} %copy-done.2, f32[5,16,16,128]{3,2,1,0:T(8,128)S(1)} %copy-done.9, f32[16,26,1,1]{1,0,3,2:T(8,128)S(1)} %copy-done.16, f32[5,16,5,128]{3,2,1,0:T(8,128)S(1)} %copy-done.13, f32[5,16,16,128]{3,2,1,0:T(8,128)S(1)} %copy-done.5, ...), kind=kOutput, calls=%fused_computation.19 | convolution fusion | flops 52305920 | bytes 3819136 | tf_op jit(solution)/shard_map/al,fxlz->fxaz/dot_general | solution.py:378
  43.8 8.9 %shard_map.93.refs_0_ = f32[5,16,16,128]{3,2,1,0:T(8,128)} custom-call(f32[5,16,16,128]{3,2,1,0:T(8,128)} %fusion.28.refs_0_, f32[128,128]{1,0:T(8,128)} %constant.35.refs_1_, f32[128,8]{1,0:T(8,128)} %constant.37.refs_2_, f32[128,8]{1,0:T(8,128)} %constant.39.refs_3_), custom_call_target="tpu_custom_call" | custom-call | tf_op jit(solution)/shard_map/pallas_call | solution.py:159
  52.7 1.1 %slice_bitcast_fusion.3 = (f32[1,5,16,5,128]{4,3,2,1,0:T(8,128)S(1)}, f32[1,5,16,5,128]{4,3,2,1,0:T(8,128)S(1)}) fusion(f32[5,16,16,128]{3,2,1,0:T(8,128)} %shard_map.93.refs_0_), kind=kLoop, calls=%fused_computation.38 | loop fusion | bytes 819200 | tf_op jit(solution)/shard_map/stack | solution.py:262
  53.8 0.9 %pad_maximum_fusion.2.refs_1_ = f32[2,5,16,5,128]{4,3,2,1,0:T(8,128)} fusion(f32[1,5,16,5,128]{4,3,2,1,0:T(8,128)S(1)} %get-tuple-element.63, f32[1,5,16,5,128]{4,3,2,1,0:T(8,128)S(1)} %get-tuple-element.62), kind=kLoop, calls=%fused_computation.30 | loop fusion | flops 102400 | bytes 819200 | tf_op jit(solution)/shard_map/stack | solution.py:262
  54.7 14.6 %shard_map.94 = (f32[2,5,5,16,128]{4,3,2,1,0:T(8,128)}, f32[2,5,16,5,128]{4,3,2,1,0:T(8,128)}, f32[2,2,5,5,5,128]{5,4,3,2,1,0:T(8,128)}) custom-call(f32[5,16,16,128]{3,2,1,0:T(8,128)} %shard_map.93.refs_0_, f32[2,5,16,5,128]{4,3,2,1,0:T(8,128)} %pad_maximum_fusion.2.refs_1_), custom_call_target="tpu_custom_call" | custom-call | tf_op jit(solution)/shard_map/pallas_call | solution.py:159
  69.3 1.2 %slice_bitcast_fusion.1 = (f32[5,16,5,128]{3,2,1,0:T(8,128)S(1)}, f32[5,16,5,128]{3,2,1,0:T(8,128)S(1)}) fusion(f32[2,5,16,5,128]{4,3,2,1,0:T(8,128)} %get-tuple-element.34), kind=kLoop, calls=%fused_computation.36 | loop fusion | bytes 819200 | tf_op jit(solution)/shard_map/squeeze | solution.py:289
  70.6 0.0 copy-done.10
  70.6 0.2 copy-done.3
  70.8 0.4 maximum_maximum_fusion
  71.2 0.3 copy-done.17
  71.5 2.4 %fusion = f32[5,26,128,16]{2,3,1,0:T(8,128)S(1)} fusion(f32[16,26,1,1]{1,0,3,2:T(8,128)S(1)} %copy-done.17, f32[5,26,26,128]{3,2,1,0:T(8,128)S(1)} %maximum_maximum_fusion), kind=kOutput, calls=%fused_computation.1 | convolution fusion | flops 83066880 | bytes 2797184 | tf_op jit(solution)/shard_map/al,flyz->fayz/dot_general | solution.py:378
  73.9 2.0 %fusion.13 = f32[5,16,16,128]{3,2,1,0:T(8,128)} fusion(f32[16,26,1,1]{1,0,3,2:T(8,128)S(1)} %copy-done.17, f32[5,26,128,16]{2,3,1,0:T(8,128)S(1)} %fusion), kind=kOutput, calls=%fused_computation.14 | convolution fusion | flops 51118080 | bytes 1721984 | tf_op jit(solution)/shard_map/al,fxlz->fxaz/dot_general | solution.py:378
  (22 shorter events, 0.2 us)
Async XLA Ops:
  0.0 18.0 %copy-start.16 = (f32[16,26,1,1]{1,0,3,2:T(8,128)S(1)}, f32[16,26,1,1]{1,0,3,2:T(8,128)}, u32[]{:S(2)}) copy-start(f32[16,26,1,1]{1,0,3,2:T(8,128)} %constant.40) | copy-start | bytes 4996
  18.0 1.2 %copy-start.1 = (f32[4,16,16,128]{3,2,1,0:T(8,128)S(1)}, f32[4,16,16,128]{3,2,1,0:T(8,128)}, u32[]{:S(2)}) copy-start(f32[4,16,16,128]{3,2,1,0:T(8,128)} %get-tuple-element.20) | copy-start | bytes 1572868
  18.0 1.2 %copy-start.14 = (f32[4,16,5,128]{3,2,1,0:T(8,128)S(1)}, f32[4,16,5,128]{3,2,1,0:T(8,128)}, u32[]{:S(2)}) copy-start(f32[4,16,5,128]{3,2,1,0:T(8,128)} %get-tuple-element.23) | copy-start | bytes 491524
  18.0 1.2 %copy-start.15 = (f32[4,16,5,128]{3,2,1,0:T(8,128)S(1)}, f32[4,16,5,128]{3,2,1,0:T(8,128)}, u32[]{:S(2)}) copy-start(f32[4,16,5,128]{3,2,1,0:T(8,128)} %get-tuple-element.24) | copy-start | bytes 491524
  19.0 1.2 %copy-start.2 = (f32[5,16,16,128]{3,2,1,0:T(8,128)S(1)}, f32[5,16,16,128]{3,2,1,0:T(8,128)}, u32[]{:S(2)}) copy-start(f32[5,16,16,128]{3,2,1,0:T(8,128)} %refs_0_.1) | copy-start | bytes 1966084
  19.0 1.5 %copy-start = (f32[3,3,16,16,128]{4,3,2,1,0:T(8,128)S(1)}, f32[3,3,16,16,128]{4,3,2,1,0:T(8,128)}, u32[]{:S(2)}) copy-start(f32[3,3,16,16,128]{4,3,2,1,0:T(8,128)} %param.10) | copy-start | bytes 3538948
  19.1 1.5 %copy-start.4 = (f32[16,16,128]{2,1,0:T(8,128)S(1)}, f32[16,16,128]{2,1,0:T(8,128)}, u32[]{:S(2)}) copy-start(f32[16,16,128]{2,1,0:T(8,128)} %param.11) | copy-start | bytes 393220
  19.1 1.5 %copy-start.7 = (f32[16,16,128]{2,1,0:T(8,128)S(1)}, f32[16,16,128]{2,1,0:T(8,128)}, u32[]{:S(2)}) copy-start(f32[16,16,128]{2,1,0:T(8,128)} %get-tuple-element.26) | copy-start | bytes 393220
  19.1 1.7 %copy-start.8 = (f32[4,16,16,128]{3,2,1,0:T(8,128)S(1)}, f32[4,16,16,128]{3,2,1,0:T(8,128)}, u32[]{:S(2)}) copy-start(f32[4,16,16,128]{3,2,1,0:T(8,128)} %get-tuple-element.25) | copy-start | bytes 1572868
  23.6 15.4 %copy-start.6 = (f32[5,16,16,128]{3,2,1,0:T(8,128)S(1)}, f32[5,16,16,128]{3,2,1,0:T(8,128)}, u32[]{:S(2)}) copy-start(f32[5,16,16,128]{3,2,1,0:T(8,128)} %get-tuple-element.48.refs_0_) | copy-start | bytes 1966084
  40.1 1.3 %copy-start.5 = (f32[5,16,16,128]{3,2,1,0:T(8,128)S(1)}, f32[5,16,16,128]{3,2,1,0:T(8,128)}, u32[]{:S(2)}) copy-start(f32[5,16,16,128]{3,2,1,0:T(8,128)} %get-tuple-element.47.refs_1_) | copy-start | bytes 1966084
  40.1 1.3 %copy-start.9 = (f32[5,16,16,128]{3,2,1,0:T(8,128)S(1)}, f32[5,16,16,128]{3,2,1,0:T(8,128)}, u32[]{:S(2)}) copy-start(f32[5,16,16,128]{3,2,1,0:T(8,128)} %get-tuple-element.31) | copy-start | bytes 1966084
  40.1 1.3 %copy-start.12 = (f32[5,16,5,128]{3,2,1,0:T(8,128)S(1)}, f32[5,16,5,128]{3,2,1,0:T(8,128)}, u32[]{:S(2)}) copy-start(f32[5,16,5,128]{3,2,1,0:T(8,128)} %get-tuple-element.29) | copy-start | bytes 614404
  40.1 1.4 %copy-start.13 = (f32[5,16,5,128]{3,2,1,0:T(8,128)S(1)}, f32[5,16,5,128]{3,2,1,0:T(8,128)}, u32[]{:S(2)}) copy-start(f32[5,16,5,128]{3,2,1,0:T(8,128)} %get-tuple-element.30) | copy-start | bytes 614404
  69.3 1.3 %copy-start.11 = (f32[2,2,5,5,5,128]{5,4,3,2,1,0:T(8,128)S(1)}, f32[2,2,5,5,5,128]{5,4,3,2,1,0:T(8,128)}, u32[]{:S(2)}) copy-start(f32[2,2,5,5,5,128]{5,4,3,2,1,0:T(8,128)} %get-tuple-element.32) | copy-start | bytes 768004
  69.3 1.3 %copy-start.10 = (f32[2,5,5,16,128]{4,3,2,1,0:T(8,128)S(1)}, f32[2,5,5,16,128]{4,3,2,1,0:T(8,128)}, u32[]{:S(2)}) copy-start(f32[2,5,5,16,128]{4,3,2,1,0:T(8,128)} %get-tuple-element.33) | copy-start | bytes 1228804
  69.3 1.5 %copy-start.3 = (f32[5,16,16,128]{3,2,1,0:T(8,128)S(1)}, f32[5,16,16,128]{3,2,1,0:T(8,128)}, u32[]{:S(2)}) copy-start(f32[5,16,16,128]{3,2,1,0:T(8,128)} %shard_map.93.refs_0_) | copy-start | bytes 1966084
  70.8 0.7 copy-start.17

commit v18 on v15

--- a/solution.py
+++ b/solution.py
@@ -108,14 +108,14 @@
     for copy in copies:
         copy.start()
     if zeta:
-        total = jnp.dot(middle_ref[...], turned[...], precision=lax.Precision.HIGHEST,
+        total = jnp.dot(middle_ref[...], turned[...], precision=lax.Precision.HIGH,
                         preferred_element_type=jnp.float32)
     for copy in copies:
         copy.wait()
     if zeta:
-        total = total + jnp.dot(lower_ref[...], before[...], precision=lax.Precision.HIGHEST,
+        total = total + jnp.dot(lower_ref[...], before[...], precision=lax.Precision.HIGH,
                                 preferred_element_type=jnp.float32)
-        total = total + jnp.dot(upper_ref[...], after[...], precision=lax.Precision.HIGHEST,
+        total = total + jnp.dot(upper_ref[...], after[...], precision=lax.Precision.HIGH,
                                 preferred_element_type=jnp.float32)
         out_ref[...] = total.T.reshape(fields, length_x, length_y, depth)
 

time: 75.8 us -> 73.7 us (0.972)
  Pallas kernels: 54.2 us -> 52.1 us
    pallas_call x4, Pallas kernels: 54.2 us -> 52.1 us  [exchange(): pl.pallas_call(functools.partial(exchange_kernel, tuple(routes), sizes, l...]
where the time goes in v18:
time: 73.7 us; the launch traced here: 72.8 us
  Pallas kernels  52.1 us (71%)
  matrix products  9.03 us (12%)
  other arithmetic  6.43 us (9%)
  local copies, waits for them, and re-layouts  4.87 us (7%)
    pallas_call x4, Pallas kernels, exchange(): pl.pallas_call(functools.partial(exchange_kernel, tuple(routes), sizes, l...  52.1 us
    dot_general x6, matrix products, sweep_lines(): jnp.einsum(line_forms[dim], matrix, padded, precision=lax.Precision.HIGHEST)  9.03 us
    unnamed x40, local copies, waits for them, and re-layouts  3.29 us
    add x1, other arithmetic, fluxes(): metrics[direction, 0] * totals[0] + metrics[direction, 1] * totals[1]  1.48 us

profile of v18, /device:TPU:1, one launch (start us, length us, event | category | flops | bytes accessed | tf_op | source)
XLA Modules:
  0.0 72.8 jit_solution(13511020680125071834)
XLA Ops:
  0.0 16.1 %shard_map.91 = (f32[4,5,16,128]{3,2,1,0:T(8,128)}, f32[4,5,16,128]{3,2,1,0:T(8,128)}, f32[4,16,5,128]{3,2,1,0:T(8,128)}, f32[4,16,5,128]{3,2,1,0:T(8,128)}, f32...) custom-call(f32[5,16,16,128]{3,2,1,0:T(8,128)} %refs_0_.1, ...), custom_call_target="tpu_custom_call" | custom-call | tf_op jit(solution)/shard_map/pallas_call | solution.py:159
  16.1 1.2 %pad_maximum_fusion.1 = f32[4,26,16,128]{3,2,1,0:T(8,128)S(1)} fusion(f32[4,5,16,128]{3,2,1,0:T(8,128)} %get-tuple-element.22, f32[4,16,16,128]{3,2,1,0:T(8,128)} %get-tuple-element.20, f32[4,5,16,128]{3,2,1,0:T(8,128)} %get-tuple-element.21), kind=kLoop, calls=%fused_computation.29 | loop fusion | flops 425984 | bytes 1703936 | tf_op jit(solution)/shard_map/concatenate | solution.py:252
  17.4 0.0 copy-done.17
  17.4 0.0 copy-start.1
  17.4 0.0 copy-start.15
  17.4 1.0 %fusion.36 = f32[4,16,128,16]{2,3,1,0:T(8,128)S(1)} fusion(f32[16,26,1,1]{1,0,3,2:T(8,128)S(1)} %copy-done.17, f32[4,26,16,128]{3,2,1,0:T(8,128)S(1)} %pad_maximum_fusion.1), kind=kOutput, calls=%fused_computation.27 | convolution fusion | flops 40894464 | bytes 1377920 | tf_op jit(solution)/shard_map/al,flyz->fayz/dot_general | solution.py:378
  18.4 0.0 copy-start.2
  18.4 0.0 copy-start
  18.4 0.0 copy-start.5
  18.5 0.2 copy.32
  18.6 0.0 copy-done.1
  18.6 0.0 copy-done.15
  18.6 0.0 copy-done.16
  18.7 0.9 %convolution_bitcast_fusion = f32[4,16,16,128]{3,2,1,0:T(8,128)S(1)} fusion(f32[16,26,1,1]{1,0,3,2:T(8,128)S(1)} %copy-done.17, f32[4,16,5,128]{3,2,1,0:T(8,128)S(1)} %copy-done.16, f32[4,16,16,128]{3,2,1,0:T(8,128)S(1)} %copy-done.1, f32[4,16,5,128]{3,2,1,0:T(8,128)S(1)} %copy-done.15), kind=kOutput, calls=%fused_computation.20 | convolution fusion | flops 41320448 | bytes 1377920 | tf_op jit(solution)/shard_map/al,fxlz->fxaz/dot_general | solution.py:378
  19.6 0.3 copy-done
  19.9 0.0 copy-done.8
  19.9 0.2 copy-done.9
  20.1 0.2 bitcast_dynamic-update-slice_fusion.11
  20.3 0.1 bitcast_dynamic-update-slice_fusion.10
  20.4 0.1 bitcast_dynamic-update-slice_fusion.9
  20.6 0.2 bitcast_dynamic-update-slice_fusion.8
  20.8 0.1 bitcast_dynamic-update-slice_fusion.6
  20.9 0.1 bitcast_dynamic-update-slice_fusion.5
  21.0 0.1 bitcast_dynamic-update-slice_fusion.4
  21.2 0.1 bitcast_dynamic-update-slice_fusion
  21.4 0.1 slice_bitcast_fusion.20
  21.5 1.5 %multiply_add_fusion = (f32[5,16,16,128]{3,2,1,0:T(8,128)}, f32[5,16,16,128]{3,2,1,0:T(8,128)}, f32[5,16,16,128]{3,2,1,0:T(8,128)}) fusion(f32[5,16,16,128]{3,2,1,0:T(8,128)S(1)} %bitcast_dynamic-update-slice_fusion, f32[5,16,16,128]{3,2,1,0:T(8,128)S(1)} %bitcast_dynamic-update-slice_fusion.4, f32[5,16,16,128]{3,2,1,0:T(8,128)S(1)} %get-tuple-element.64, ...), kind=kLoop, calls=%fused_computation.31 | loop fusion | flops 2457600 | bytes 5111808 | tf_op jit(solution)/shard_map/add | solution.py:442
  23.0 14.6 %shard_map.92 = (f32[5,5,16,128]{3,2,1,0:T(8,128)}, f32[5,5,16,128]{3,2,1,0:T(8,128)}, f32[5,16,5,128]{3,2,1,0:T(8,128)}, f32[5,16,5,128]{3,2,1,0:T(8,128)}, f32[5,16,16,128]{3,2,1,0:T(8,128)}) custom-call(f32[5,16,16,128]{3,2,1,0:T(8,128)} %get-tuple-element.48.refs_0_, f32[5,16,16,128]{3,2,1,0:T(8,128)} %get-tuple-element.47.refs_1_, ...), custom_call_target="tpu_custom_call" | custom-call | tf_op jit(solution)/shard_map/pallas_call | solution.py:159
  37.6 0.0 copy-done.7
  37.6 1.1 %pad_maximum_fusion = f32[5,26,16,128]{3,2,1,0:T(8,128)S(1)} fusion(f32[5,5,16,128]{3,2,1,0:T(8,128)} %get-tuple-element.28, f32[5,16,16,128]{3,2,1,0:T(8,128)S(1)} %copy-done.7, f32[5,5,16,128]{3,2,1,0:T(8,128)} %get-tuple-element.27), kind=kLoop, calls=%fused_computation.21 | loop fusion | flops 532480 | bytes 2129920 | tf_op jit(solution)/shard_map/concatenate | solution.py:229
  38.7 1.2 %fusion.11 = f32[5,16,128,16]{2,3,1,0:T(8,128)S(1)} fusion(f32[16,26,1,1]{1,0,3,2:T(8,128)S(1)} %copy-done.17, f32[5,26,16,128]{3,2,1,0:T(8,128)S(1)} %pad_maximum_fusion), kind=kOutput, calls=%fused_computation.12 | convolution fusion | flops 51118080 | bytes 1721984 | tf_op jit(solution)/shard_map/al,flyz->fayz/dot_general | solution.py:378
  40.0 0.0 copy-done.10
  40.0 0.1 copy-done.13
  40.1 0.1 copy-done.14
  40.2 1.3 %fusion.28.refs_0_ = f32[5,16,16,128]{3,2,1,0:T(8,128)S(1)} fusion(f32[5,16,16,128]{3,2,1,0:T(8,128)S(1)} %copy-done.2, f32[5,16,16,128]{3,2,1,0:T(8,128)S(1)} %copy-done.10, f32[16,26,1,1]{1,0,3,2:T(8,128)S(1)} %copy-done.17, f32[5,16,5,128]{3,2,1,0:T(8,128)S(1)} %copy-done.14, f32[5,16,16,128]{3,2,1,0:T(8,128)S(1)} %copy-done.6, ...), kind=kOutput, calls=%fused_computation.19 | convolution fusion | flops 52305920 | bytes 3819136 | tf_op jit(solution)/shard_map/al,fxlz->fxaz/dot_general | solution.py:378
  41.5 0.0 copy-start.3
  41.6 1.0 %pad_maximum_fusion.2.refs_1_ = f32[2,5,16,5,128]{4,3,2,1,0:T(8,128)} fusion(f32[1,5,16,5,128]{4,3,2,1,0:T(8,128)S(1)} %get-tuple-element.63, f32[1,5,16,5,128]{4,3,2,1,0:T(8,128)S(1)} %get-tuple-element.62), kind=kLoop, calls=%fused_computation.30 | loop fusion | flops 102400 | bytes 819200 | tf_op jit(solution)/shard_map/stack | solution.py:262
  42.6 13.4 %shard_map.93 = (f32[2,5,5,16,128]{4,3,2,1,0:T(8,128)}, f32[2,5,16,5,128]{4,3,2,1,0:T(8,128)}, f32[2,2,5,5,5,128]{5,4,3,2,1,0:T(8,128)}) custom-call(f32[5,16,16,128]{3,2,1,0:T(8,128)} %copy-done.3, f32[2,5,16,5,128]{4,3,2,1,0:T(8,128)} %pad_maximum_fusion.2.refs_1_), custom_call_target="tpu_custom_call" | custom-call | tf_op jit(solution)/shard_map/pallas_call | solution.py:159
  56.0 0.0 copy-start.4
  56.0 1.2 %slice_bitcast_fusion.3 = (f32[5,16,5,128]{3,2,1,0:T(8,128)S(1)}, f32[5,16,5,128]{3,2,1,0:T(8,128)S(1)}) fusion(f32[2,5,16,5,128]{4,3,2,1,0:T(8,128)} %get-tuple-element.34), kind=kLoop, calls=%fused_computation.38 | loop fusion | bytes 819200 | tf_op jit(solution)/shard_map/squeeze | solution.py:289
  57.3 0.0 copy-done.11
  57.3 0.2 copy-done.4
  57.5 0.4 maximum_maximum_fusion
  57.9 0.3 copy-done.18
  58.2 2.6 %fusion = f32[5,26,128,16]{2,3,1,0:T(8,128)S(1)} fusion(f32[16,26,1,1]{1,0,3,2:T(8,128)S(1)} %copy-done.18, f32[5,26,26,128]{3,2,1,0:T(8,128)S(1)} %maximum_maximum_fusion), kind=kOutput, calls=%fused_computation.1 | convolution fusion | flops 83066880 | bytes 2797184 | tf_op jit(solution)/shard_map/al,flyz->fayz/dot_general | solution.py:378
  60.8 2.0 %fusion.13.refs_0_ = f32[5,16,16,128]{3,2,1,0:T(8,128)} fusion(f32[16,26,1,1]{1,0,3,2:T(8,128)S(1)} %copy-done.18, f32[5,26,128,16]{2,3,1,0:T(8,128)S(1)} %fusion), kind=kOutput, calls=%fused_computation.14 | convolution fusion | flops 51118080 | bytes 1721984 | tf_op jit(solution)/shard_map/al,fxlz->fxaz/dot_general | solution.py:378
  62.9 8.0 %shard_map.94 = f32[5,16,16,128]{3,2,1,0:T(8,128)} custom-call(f32[5,16,16,128]{3,2,1,0:T(8,128)} %fusion.13.refs_0_, f32[128,128]{1,0:T(8,128)} %constant.35.refs_1_, f32[128,8]{1,0:T(8,128)} %constant.37.refs_2_, f32[128,8]{1,0:T(8,128)} %constant.39.refs_3_), custom_call_target="tpu_custom_call" | custom-call | tf_op jit(solution)/shard_map/pallas_call | solution.py:159
  70.8 2.0 %copy.46 = f32[5,16,16,128]{3,2,1,0:T(8,128)} copy(f32[5,16,16,128]{3,2,1,0:T(8,128)} %shard_map.94) | data formatting | bytes 1310720
  (25 shorter events, 0.3 us)
Async XLA Ops:
  0.0 17.4 %copy-start.17 = (f32[16,26,1,1]{1,0,3,2:T(8,128)S(1)}, f32[16,26,1,1]{1,0,3,2:T(8,128)}, u32[]{:S(2)}) copy-start(f32[16,26,1,1]{1,0,3,2:T(8,128)} %constant.40) | copy-start | bytes 4996
  17.4 1.2 %copy-start.1 = (f32[4,16,16,128]{3,2,1,0:T(8,128)S(1)}, f32[4,16,16,128]{3,2,1,0:T(8,128)}, u32[]{:S(2)}) copy-start(f32[4,16,16,128]{3,2,1,0:T(8,128)} %get-tuple-element.20) | copy-start | bytes 1572868
  17.4 1.2 %copy-start.15 = (f32[4,16,5,128]{3,2,1,0:T(8,128)S(1)}, f32[4,16,5,128]{3,2,1,0:T(8,128)}, u32[]{:S(2)}) copy-start(f32[4,16,5,128]{3,2,1,0:T(8,128)} %get-tuple-element.23) | copy-start | bytes 491524
  17.4 1.2 %copy-start.16 = (f32[4,16,5,128]{3,2,1,0:T(8,128)S(1)}, f32[4,16,5,128]{3,2,1,0:T(8,128)}, u32[]{:S(2)}) copy-start(f32[4,16,5,128]{3,2,1,0:T(8,128)} %get-tuple-element.24) | copy-start | bytes 491524
  18.4 1.2 %copy-start.2 = (f32[5,16,16,128]{3,2,1,0:T(8,128)S(1)}, f32[5,16,16,128]{3,2,1,0:T(8,128)}, u32[]{:S(2)}) copy-start(f32[5,16,16,128]{3,2,1,0:T(8,128)} %refs_0_.1) | copy-start | bytes 1966084
  18.4 1.5 %copy-start = (f32[3,3,16,16,128]{4,3,2,1,0:T(8,128)S(1)}, f32[3,3,16,16,128]{4,3,2,1,0:T(8,128)}, u32[]{:S(2)}) copy-start(f32[3,3,16,16,128]{4,3,2,1,0:T(8,128)} %param.10) | copy-start | bytes 3538948
  18.4 1.5 %copy-start.5 = (f32[16,16,128]{2,1,0:T(8,128)S(1)}, f32[16,16,128]{2,1,0:T(8,128)}, u32[]{:S(2)}) copy-start(f32[16,16,128]{2,1,0:T(8,128)} %param.11) | copy-start | bytes 393220
  18.4 1.5 %copy-start.8 = (f32[16,16,128]{2,1,0:T(8,128)S(1)}, f32[16,16,128]{2,1,0:T(8,128)}, u32[]{:S(2)}) copy-start(f32[16,16,128]{2,1,0:T(8,128)} %get-tuple-element.26) | copy-start | bytes 393220
  18.4 1.7 %copy-start.9 = (f32[4,16,16,128]{3,2,1,0:T(8,128)S(1)}, f32[4,16,16,128]{3,2,1,0:T(8,128)}, u32[]{:S(2)}) copy-start(f32[4,16,16,128]{3,2,1,0:T(8,128)} %get-tuple-element.25) | copy-start | bytes 1572868
  23.0 14.6 %copy-start.7 = (f32[5,16,16,128]{3,2,1,0:T(8,128)S(1)}, f32[5,16,16,128]{3,2,1,0:T(8,128)}, u32[]{:S(2)}) copy-start(f32[5,16,16,128]{3,2,1,0:T(8,128)} %get-tuple-element.48.refs_0_) | copy-start | bytes 1966084
  38.7 1.3 %copy-start.6 = (f32[5,16,16,128]{3,2,1,0:T(8,128)S(1)}, f32[5,16,16,128]{3,2,1,0:T(8,128)}, u32[]{:S(2)}) copy-start(f32[5,16,16,128]{3,2,1,0:T(8,128)} %get-tuple-element.47.refs_1_) | copy-start | bytes 1966084
  38.7 1.3 %copy-start.10 = (f32[5,16,16,128]{3,2,1,0:T(8,128)S(1)}, f32[5,16,16,128]{3,2,1,0:T(8,128)}, u32[]{:S(2)}) copy-start(f32[5,16,16,128]{3,2,1,0:T(8,128)} %get-tuple-element.31) | copy-start | bytes 1966084
  38.7 1.3 %copy-start.13 = (f32[5,16,5,128]{3,2,1,0:T(8,128)S(1)}, f32[5,16,5,128]{3,2,1,0:T(8,128)}, u32[]{:S(2)}) copy-start(f32[5,16,5,128]{3,2,1,0:T(8,128)} %get-tuple-element.29) | copy-start | bytes 614404
  38.7 1.4 %copy-start.14 = (f32[5,16,5,128]{3,2,1,0:T(8,128)S(1)}, f32[5,16,5,128]{3,2,1,0:T(8,128)}, u32[]{:S(2)}) copy-start(f32[5,16,5,128]{3,2,1,0:T(8,128)} %get-tuple-element.30) | copy-start | bytes 614404
  41.5 1.1 %copy-start.3 = (f32[5,16,16,128]{3,2,1,0:T(8,128)}, f32[5,16,16,128]{3,2,1,0:T(8,128)S(1)}, u32[]{:S(2)}) copy-start(f32[5,16,16,128]{3,2,1,0:T(8,128)S(1)} %fusion.28.refs_0_) | copy-start | bytes 1966084
  56.0 1.3 %copy-start.12 = (f32[2,2,5,5,5,128]{5,4,3,2,1,0:T(8,128)S(1)}, f32[2,2,5,5,5,128]{5,4,3,2,1,0:T(8,128)}, u32[]{:S(2)}) copy-start(f32[2,2,5,5,5,128]{5,4,3,2,1,0:T(8,128)} %get-tuple-element.32) | copy-start | bytes 768004
  56.0 1.3 %copy-start.11 = (f32[2,5,5,16,128]{4,3,2,1,0:T(8,128)S(1)}, f32[2,5,5,16,128]{4,3,2,1,0:T(8,128)}, u32[]{:S(2)}) copy-start(f32[2,5,5,16,128]{4,3,2,1,0:T(8,128)} %get-tuple-element.33) | copy-start | bytes 1228804
  56.0 1.5 %copy-start.4 = (f32[5,16,16,128]{3,2,1,0:T(8,128)S(1)}, f32[5,16,16,128]{3,2,1,0:T(8,128)}, u32[]{:S(2)}) copy-start(f32[5,16,16,128]{3,2,1,0:T(8,128)} %copy-done.3) | copy-start | bytes 1966084
  57.5 0.7 copy-start.18

commit v19 on v18

--- a/solution.py
+++ b/solution.py
@@ -26,7 +26,7 @@
     return speed, pressure, pressure / density
 
 
-def exchange_kernel(routes, sizes, count, zeta, prepare, *refs):
+def exchange_kernel(routes, sizes, count, zeta, prepare, precision, *refs):
     sources = list(refs[:count])
     refs = refs[count:]
     if prepare:
@@ -108,19 +108,20 @@
     for copy in copies:
         copy.start()
     if zeta:
-        total = jnp.dot(middle_ref[...], turned[...], precision=lax.Precision.HIGH,
+        total = jnp.dot(middle_ref[...], turned[...], precision=precision,
                         preferred_element_type=jnp.float32)
     for copy in copies:
         copy.wait()
     if zeta:
-        total = total + jnp.dot(lower_ref[...], before[...], precision=lax.Precision.HIGH,
+        total = total + jnp.dot(lower_ref[...], before[...], precision=precision,
                                 preferred_element_type=jnp.float32)
-        total = total + jnp.dot(upper_ref[...], after[...], precision=lax.Precision.HIGH,
+        total = total + jnp.dot(upper_ref[...], after[...], precision=precision,
                                 preferred_element_type=jnp.float32)
         out_ref[...] = total.T.reshape(fields, length_x, length_y, depth)
 
 
-def exchange(arrays, routes, out_shapes, tag, zeta=None, prepare=None):
+def exchange(arrays, routes, out_shapes, tag, zeta=None, prepare=None,
+             precision=lax.Precision.HIGH):
     sizes = tuple(lax.axis_size(axis) for axis in AXES)
     operands = [array for array, _ in arrays]
     in_specs = [pl.BlockSpec(memory_space=space) for _, space in arrays]
@@ -159,7 +160,7 @@
     return pl.pallas_call(
         functools.partial(
             exchange_kernel, tuple(routes), sizes, len(arrays) + (prepare is not None),
-            zeta is not None, prepare is not None,
+            zeta is not None, prepare is not None, precision,
         ),
         out_shape=out_shapes,
         in_specs=in_specs,
@@ -293,7 +294,7 @@
 
 
 def sweep_zeta(value, matrix, tag):
-    return exchange([], [], [], tag, (value, matrix))[-1]
+    return exchange([], [], [], tag, (value, matrix), precision=lax.Precision.HIGHEST)[-1]
 
 
 def with_halo(value, sides, width):

time: 73.7 us -> 74.4 us (level)
  Pallas kernels: 52.1 us -> 52.9 us
    pallas_call x4, Pallas kernels: 52.1 us -> 52.9 us  [exchange(): pl.pallas_call(functools.partial(exchange_kernel, tuple(routes), sizes, l...]
where the time goes in v19:
time: 74.4 us; the launch traced here: 73.6 us
  Pallas kernels  52.9 us (71%)
  matrix products  9.03 us (12%)
  other arithmetic  6.43 us (9%)
  local copies, waits for them, and re-layouts  4.87 us (7%)
    pallas_call x4, Pallas kernels, exchange(): pl.pallas_call(functools.partial(exchange_kernel, tuple(routes), sizes, l...  52.9 us
    dot_general x6, matrix products, sweep_lines(): jnp.einsum(line_forms[dim], matrix, padded, precision=lax.Precision.HIGHEST)  9.03 us
    unnamed x40, local copies, waits for them, and re-layouts  3.29 us

profile of v19, /device:TPU:1, one launch (start us, length us, event | category | flops | bytes accessed | tf_op | source)
XLA Modules:
  0.0 73.6 jit_solution(2690669116214132810)
XLA Ops:
  0.0 16.1 %shard_map.91 = (f32[4,5,16,128]{3,2,1,0:T(8,128)}, f32[4,5,16,128]{3,2,1,0:T(8,128)}, f32[4,16,5,128]{3,2,1,0:T(8,128)}, f32[4,16,5,128]{3,2,1,0:T(8,128)}, f32...) custom-call(f32[5,16,16,128]{3,2,1,0:T(8,128)} %refs_0_.1, ...), custom_call_target="tpu_custom_call" | custom-call | tf_op jit(solution)/shard_map/pallas_call | solution.py:160
  16.1 1.2 %pad_maximum_fusion.1 = f32[4,26,16,128]{3,2,1,0:T(8,128)S(1)} fusion(f32[4,5,16,128]{3,2,1,0:T(8,128)} %get-tuple-element.22, f32[4,16,16,128]{3,2,1,0:T(8,128)} %get-tuple-element.20, f32[4,5,16,128]{3,2,1,0:T(8,128)} %get-tuple-element.21), kind=kLoop, calls=%fused_computation.29 | loop fusion | flops 425984 | bytes 1703936 | tf_op jit(solution)/shard_map/concatenate | solution.py:253
  17.4 0.0 copy-done.17
  17.4 0.0 copy-start.1
  17.4 0.0 copy-start.15
  17.4 1.0 %fusion.36 = f32[4,16,128,16]{2,3,1,0:T(8,128)S(1)} fusion(f32[16,26,1,1]{1,0,3,2:T(8,128)S(1)} %copy-done.17, f32[4,26,16,128]{3,2,1,0:T(8,128)S(1)} %pad_maximum_fusion.1), kind=kOutput, calls=%fused_computation.27 | convolution fusion | flops 40894464 | bytes 1377920 | tf_op jit(solution)/shard_map/al,flyz->fayz/dot_general | solution.py:379
  18.4 0.0 copy-start.2
  18.4 0.0 copy-start
  18.4 0.0 copy-start.5
  18.5 0.2 copy.32
  18.6 0.0 copy-done.1
  18.6 0.0 copy-done.15
  18.6 0.0 copy-done.16
  18.7 0.9 %convolution_bitcast_fusion = f32[4,16,16,128]{3,2,1,0:T(8,128)S(1)} fusion(f32[16,26,1,1]{1,0,3,2:T(8,128)S(1)} %copy-done.17, f32[4,16,5,128]{3,2,1,0:T(8,128)S(1)} %copy-done.16, f32[4,16,16,128]{3,2,1,0:T(8,128)S(1)} %copy-done.1, f32[4,16,5,128]{3,2,1,0:T(8,128)S(1)} %copy-done.15), kind=kOutput, calls=%fused_computation.20 | convolution fusion | flops 41320448 | bytes 1377920 | tf_op jit(solution)/shard_map/al,fxlz->fxaz/dot_general | solution.py:379
  19.6 0.3 copy-done
  19.9 0.0 copy-done.8
  19.9 0.2 copy-done.9
  20.1 0.2 bitcast_dynamic-update-slice_fusion.11
  20.3 0.1 bitcast_dynamic-update-slice_fusion.10
  20.4 0.1 bitcast_dynamic-update-slice_fusion.9
  20.6 0.2 bitcast_dynamic-update-slice_fusion.8
  20.8 0.1 bitcast_dynamic-update-slice_fusion.6
  20.9 0.1 bitcast_dynamic-update-slice_fusion.5
  21.0 0.1 bitcast_dynamic-update-slice_fusion.4
  21.2 0.1 bitcast_dynamic-update-slice_fusion
  21.4 0.1 slice_bitcast_fusion.20
  21.5 1.5 %multiply_add_fusion = (f32[5,16,16,128]{3,2,1,0:T(8,128)}, f32[5,16,16,128]{3,2,1,0:T(8,128)}, f32[5,16,16,128]{3,2,1,0:T(8,128)}) fusion(f32[5,16,16,128]{3,2,1,0:T(8,128)S(1)} %bitcast_dynamic-update-slice_fusion, f32[5,16,16,128]{3,2,1,0:T(8,128)S(1)} %bitcast_dynamic-update-slice_fusion.4, f32[5,16,16,128]{3,2,1,0:T(8,128)S(1)} %get-tuple-element.64, ...), kind=kLoop, calls=%fused_computation.31 | loop fusion | flops 2457600 | bytes 5111808 | tf_op jit(solution)/shard_map/add | solution.py:443
  23.0 14.6 %shard_map.92 = (f32[5,5,16,128]{3,2,1,0:T(8,128)}, f32[5,5,16,128]{3,2,1,0:T(8,128)}, f32[5,16,5,128]{3,2,1,0:T(8,128)}, f32[5,16,5,128]{3,2,1,0:T(8,128)}, f32[5,16,16,128]{3,2,1,0:T(8,128)}) custom-call(f32[5,16,16,128]{3,2,1,0:T(8,128)} %get-tuple-element.48.refs_0_, f32[5,16,16,128]{3,2,1,0:T(8,128)} %get-tuple-element.47.refs_1_, ...), custom_call_target="tpu_custom_call" | custom-call | tf_op jit(solution)/shard_map/pallas_call | solution.py:160
  37.6 0.0 copy-done.7
  37.6 1.1 %pad_maximum_fusion = f32[5,26,16,128]{3,2,1,0:T(8,128)S(1)} fusion(f32[5,5,16,128]{3,2,1,0:T(8,128)} %get-tuple-element.28, f32[5,16,16,128]{3,2,1,0:T(8,128)S(1)} %copy-done.7, f32[5,5,16,128]{3,2,1,0:T(8,128)} %get-tuple-element.27), kind=kLoop, calls=%fused_computation.21 | loop fusion | flops 532480 | bytes 2129920 | tf_op jit(solution)/shard_map/concatenate | solution.py:230
  38.7 1.2 %fusion.11 = f32[5,16,128,16]{2,3,1,0:T(8,128)S(1)} fusion(f32[16,26,1,1]{1,0,3,2:T(8,128)S(1)} %copy-done.17, f32[5,26,16,128]{3,2,1,0:T(8,128)S(1)} %pad_maximum_fusion), kind=kOutput, calls=%fused_computation.12 | convolution fusion | flops 51118080 | bytes 1721984 | tf_op jit(solution)/shard_map/al,flyz->fayz/dot_general | solution.py:379
  40.0 0.0 copy-done.10
  40.0 0.1 copy-done.13
  40.1 0.1 copy-done.14
  40.2 1.3 %fusion.28.refs_0_ = f32[5,16,16,128]{3,2,1,0:T(8,128)S(1)} fusion(f32[5,16,16,128]{3,2,1,0:T(8,128)S(1)} %copy-done.2, f32[5,16,16,128]{3,2,1,0:T(8,128)S(1)} %copy-done.10, f32[16,26,1,1]{1,0,3,2:T(8,128)S(1)} %copy-done.17, f32[5,16,5,128]{3,2,1,0:T(8,128)S(1)} %copy-done.14, f32[5,16,16,128]{3,2,1,0:T(8,128)S(1)} %copy-done.6, ...), kind=kOutput, calls=%fused_computation.19 | convolution fusion | flops 52305920 | bytes 3819136 | tf_op jit(solution)/shard_map/al,fxlz->fxaz/dot_general | solution.py:379
  41.5 0.0 copy-start.3
  41.6 1.0 %pad_maximum_fusion.2.refs_1_ = f32[2,5,16,5,128]{4,3,2,1,0:T(8,128)} fusion(f32[1,5,16,5,128]{4,3,2,1,0:T(8,128)S(1)} %get-tuple-element.63, f32[1,5,16,5,128]{4,3,2,1,0:T(8,128)S(1)} %get-tuple-element.62), kind=kLoop, calls=%fused_computation.30 | loop fusion | flops 102400 | bytes 819200 | tf_op jit(solution)/shard_map/stack | solution.py:263
  42.6 13.4 %shard_map.93 = (f32[2,5,5,16,128]{4,3,2,1,0:T(8,128)}, f32[2,5,16,5,128]{4,3,2,1,0:T(8,128)}, f32[2,2,5,5,5,128]{5,4,3,2,1,0:T(8,128)}) custom-call(f32[5,16,16,128]{3,2,1,0:T(8,128)} %copy-done.3, f32[2,5,16,5,128]{4,3,2,1,0:T(8,128)} %pad_maximum_fusion.2.refs_1_), custom_call_target="tpu_custom_call" | custom-call | tf_op jit(solution)/shard_map/pallas_call | solution.py:160
  56.0 0.0 copy-start.4
  56.0 1.2 %slice_bitcast_fusion.3 = (f32[5,16,5,128]{3,2,1,0:T(8,128)S(1)}, f32[5,16,5,128]{3,2,1,0:T(8,128)S(1)}) fusion(f32[2,5,16,5,128]{4,3,2,1,0:T(8,128)} %get-tuple-element.34), kind=kLoop, calls=%fused_computation.38 | loop fusion | bytes 819200 | tf_op jit(solution)/shard_map/squeeze | solution.py:290
  57.3 0.0 copy-done.11
  57.3 0.2 copy-done.4
  57.5 0.4 maximum_maximum_fusion
  57.9 0.3 copy-done.18
  58.2 2.6 %fusion = f32[5,26,128,16]{2,3,1,0:T(8,128)S(1)} fusion(f32[16,26,1,1]{1,0,3,2:T(8,128)S(1)} %copy-done.18, f32[5,26,26,128]{3,2,1,0:T(8,128)S(1)} %maximum_maximum_fusion), kind=kOutput, calls=%fused_computation.1 | convolution fusion | flops 83066880 | bytes 2797184 | tf_op jit(solution)/shard_map/al,flyz->fayz/dot_general | solution.py:379
  60.8 2.0 %fusion.13.refs_0_ = f32[5,16,16,128]{3,2,1,0:T(8,128)} fusion(f32[16,26,1,1]{1,0,3,2:T(8,128)S(1)} %copy-done.18, f32[5,26,128,16]{2,3,1,0:T(8,128)S(1)} %fusion), kind=kOutput, calls=%fused_computation.14 | convolution fusion | flops 51118080 | bytes 1721984 | tf_op jit(solution)/shard_map/al,fxlz->fxaz/dot_general | solution.py:379
  62.9 8.7 %shard_map.94 = f32[5,16,16,128]{3,2,1,0:T(8,128)} custom-call(f32[5,16,16,128]{3,2,1,0:T(8,128)} %fusion.13.refs_0_, f32[128,128]{1,0:T(8,128)} %constant.35.refs_1_, f32[128,8]{1,0:T(8,128)} %constant.37.refs_2_, f32[128,8]{1,0:T(8,128)} %constant.39.refs_3_), custom_call_target="tpu_custom_call" | custom-call | tf_op jit(solution)/shard_map/pallas_call | solution.py:160
  71.6 2.0 %copy.46 = f32[5,16,16,128]{3,2,1,0:T(8,128)} copy(f32[5,16,16,128]{3,2,1,0:T(8,128)} %shard_map.94) | data formatting | bytes 1310720
  (25 shorter events, 0.3 us)
Async XLA Ops:
  0.0 17.4 %copy-start.17 = (f32[16,26,1,1]{1,0,3,2:T(8,128)S(1)}, f32[16,26,1,1]{1,0,3,2:T(8,128)}, u32[]{:S(2)}) copy-start(f32[16,26,1,1]{1,0,3,2:T(8,128)} %constant.40) | copy-start | bytes 4996
  17.4 1.2 %copy-start.1 = (f32[4,16,16,128]{3,2,1,0:T(8,128)S(1)}, f32[4,16,16,128]{3,2,1,0:T(8,128)}, u32[]{:S(2)}) copy-start(f32[4,16,16,128]{3,2,1,0:T(8,128)} %get-tuple-element.20) | copy-start | bytes 1572868
  17.4 1.2 %copy-start.15 = (f32[4,16,5,128]{3,2,1,0:T(8,128)S(1)}, f32[4,16,5,128]{3,2,1,0:T(8,128)}, u32[]{:S(2)}) copy-start(f32[4,16,5,128]{3,2,1,0:T(8,128)} %get-tuple-element.23) | copy-start | bytes 491524
  17.4 1.2 %copy-start.16 = (f32[4,16,5,128]{3,2,1,0:T(8,128)S(1)}, f32[4,16,5,128]{3,2,1,0:T(8,128)}, u32[]{:S(2)}) copy-start(f32[4,16,5,128]{3,2,1,0:T(8,128)} %get-tuple-element.24) | copy-start | bytes 491524
  18.4 1.2 %copy-start.2 = (f32[5,16,16,128]{3,2,1,0:T(8,128)S(1)}, f32[5,16,16,128]{3,2,1,0:T(8,128)}, u32[]{:S(2)}) copy-start(f32[5,16,16,128]{3,2,1,0:T(8,128)} %refs_0_.1) | copy-start | bytes 1966084
  18.4 1.5 %copy-start = (f32[3,3,16,16,128]{4,3,2,1,0:T(8,128)S(1)}, f32[3,3,16,16,128]{4,3,2,1,0:T(8,128)}, u32[]{:S(2)}) copy-start(f32[3,3,16,16,128]{4,3,2,1,0:T(8,128)} %param.10) | copy-start | bytes 3538948
  18.4 1.5 %copy-start.5 = (f32[16,16,128]{2,1,0:T(8,128)S(1)}, f32[16,16,128]{2,1,0:T(8,128)}, u32[]{:S(2)}) copy-start(f32[16,16,128]{2,1,0:T(8,128)} %param.11) | copy-start | bytes 393220
  18.4 1.5 %copy-start.8 = (f32[16,16,128]{2,1,0:T(8,128)S(1)}, f32[16,16,128]{2,1,0:T(8,128)}, u32[]{:S(2)}) copy-start(f32[16,16,128]{2,1,0:T(8,128)} %get-tuple-element.26) | copy-start | bytes 393220
  18.4 1.7 %copy-start.9 = (f32[4,16,16,128]{3,2,1,0:T(8,128)S(1)}, f32[4,16,16,128]{3,2,1,0:T(8,128)}, u32[]{:S(2)}) copy-start(f32[4,16,16,128]{3,2,1,0:T(8,128)} %get-tuple-element.25) | copy-start | bytes 1572868
  23.0 14.6 %copy-start.7 = (f32[5,16,16,128]{3,2,1,0:T(8,128)S(1)}, f32[5,16,16,128]{3,2,1,0:T(8,128)}, u32[]{:S(2)}) copy-start(f32[5,16,16,128]{3,2,1,0:T(8,128)} %get-tuple-element.48.refs_0_) | copy-start | bytes 1966084
  38.7 1.3 %copy-start.6 = (f32[5,16,16,128]{3,2,1,0:T(8,128)S(1)}, f32[5,16,16,128]{3,2,1,0:T(8,128)}, u32[]{:S(2)}) copy-start(f32[5,16,16,128]{3,2,1,0:T(8,128)} %get-tuple-element.47.refs_1_) | copy-start | bytes 1966084
  38.7 1.3 %copy-start.10 = (f32[5,16,16,128]{3,2,1,0:T(8,128)S(1)}, f32[5,16,16,128]{3,2,1,0:T(8,128)}, u32[]{:S(2)}) copy-start(f32[5,16,16,128]{3,2,1,0:T(8,128)} %get-tuple-element.31) | copy-start | bytes 1966084
  38.7 1.3 %copy-start.13 = (f32[5,16,5,128]{3,2,1,0:T(8,128)S(1)}, f32[5,16,5,128]{3,2,1,0:T(8,128)}, u32[]{:S(2)}) copy-start(f32[5,16,5,128]{3,2,1,0:T(8,128)} %get-tuple-element.29) | copy-start | bytes 614404
  38.7 1.4 %copy-start.14 = (f32[5,16,5,128]{3,2,1,0:T(8,128)S(1)}, f32[5,16,5,128]{3,2,1,0:T(8,128)}, u32[]{:S(2)}) copy-start(f32[5,16,5,128]{3,2,1,0:T(8,128)} %get-tuple-element.30) | copy-start | bytes 614404
  41.5 1.1 %copy-start.3 = (f32[5,16,16,128]{3,2,1,0:T(8,128)}, f32[5,16,16,128]{3,2,1,0:T(8,128)S(1)}, u32[]{:S(2)}) copy-start(f32[5,16,16,128]{3,2,1,0:T(8,128)S(1)} %fusion.28.refs_0_) | copy-start | bytes 1966084
  56.0 1.3 %copy-start.12 = (f32[2,2,5,5,5,128]{5,4,3,2,1,0:T(8,128)S(1)}, f32[2,2,5,5,5,128]{5,4,3,2,1,0:T(8,128)}, u32[]{:S(2)}) copy-start(f32[2,2,5,5,5,128]{5,4,3,2,1,0:T(8,128)} %get-tuple-element.32) | copy-start | bytes 768004
  56.0 1.3 %copy-start.11 = (f32[2,5,5,16,128]{4,3,2,1,0:T(8,128)S(1)}, f32[2,5,5,16,128]{4,3,2,1,0:T(8,128)}, u32[]{:S(2)}) copy-start(f32[2,5,5,16,128]{4,3,2,1,0:T(8,128)} %get-tuple-element.33) | copy-start | bytes 1228804
  56.0 1.5 %copy-start.4 = (f32[5,16,16,128]{3,2,1,0:T(8,128)S(1)}, f32[5,16,16,128]{3,2,1,0:T(8,128)}, u32[]{:S(2)}) copy-start(f32[5,16,16,128]{3,2,1,0:T(8,128)} %copy-done.3) | copy-start | bytes 1966084
  57.5 0.7 copy-start.18

commit v20 on v19

--- a/solution.py
+++ b/solution.py
@@ -375,8 +375,8 @@
     return banded_solve(system, source)[WIDTH : WIDTH + length]
 
 
-def sweep_lines(padded, matrix, dim):
-    return jnp.einsum(line_forms[dim], matrix, padded, precision=lax.Precision.HIGHEST)
+def sweep_lines(padded, matrix, dim, precision=lax.Precision.HIGHEST):
+    return jnp.einsum(line_forms[dim], matrix, padded, precision=precision)
 
 
 def faces_xi(values):
@@ -452,7 +452,8 @@
     derive = [jnp.asarray(derivative_table(length), dtype=jnp.float32) for length in lengths]
     smooth = [jnp.asarray(filter_table(length), dtype=jnp.float32) for length in lengths]
     padded = exchange_primitive(conserved_solution, derive[2], 0)
-    slopes = [sweep_lines(padded[k], derive[k], k + 1) for k in range(2)] + [padded[2]]
+    slopes = [sweep_lines(padded[k], derive[k], k + 1, lax.Precision.HIGH) for k in range(2)]
+    slopes.append(padded[2])
     fluid_speed_vector, thermodynamic_stress_scalar = padded[3][0:3], padded[4]
     contra = fluxes(
         conserved_solution,
@@ -463,8 +464,8 @@
         jacobian,
     )
     padded = exchange_faces([(contra[0], "xi", 1), (contra[1], "eta", 2)], 1, (contra[2], derive[2]))
-    divergence = sweep_lines(padded[0], derive[0], 1)
-    divergence = divergence + sweep_lines(padded[1], derive[1], 2)
+    divergence = sweep_lines(padded[0], derive[0], 1, lax.Precision.HIGH)
+    divergence = divergence + sweep_lines(padded[1], derive[1], 2, lax.Precision.HIGH)
     divergence = divergence + padded[2]
     sectioned = conserved_solution - step_duration * jacobian * divergence
     result = sweep_lines(exchange_plane(sectioned, 2), smooth[0], 1)

time: 74.4 us -> 73.5 us (0.988)
  matrix products: 9.03 us -> 7.24 us
  local copies, waits for them, and re-layouts: 4.87 us -> 5.76 us
    dot_general x6, matrix products: 9.03 us -> 7.24 us  [sweep_lines(): return jnp.einsum(line_forms[dim], matrix, padded, precision=precision)]
    unnamed x40, local copies, waits for them, and re-layouts: 3.29 us -> 4.19 us
where the time goes in v20:
time: 73.5 us; the launch traced here: 72.6 us
  Pallas kernels  52.9 us (72%)
  matrix products  7.24 us (10%)
  other arithmetic  6.43 us (9%)
  local copies, waits for them, and re-layouts  5.76 us (8%)
    pallas_call x4, Pallas kernels, exchange(): pl.pallas_call(functools.partial(exchange_kernel, tuple(routes), sizes, l...  52.9 us
    dot_general x6, matrix products, sweep_lines(): return jnp.einsum(line_forms[dim], matrix, padded, precision=precision)  7.24 us
    unnamed x40, local copies, waits for them, and re-layouts  4.19 us
    add x1, other arithmetic, fluxes(): metrics[direction, 0] * totals[0] + metrics[direction, 1] * totals[1]  1.48 us

profile of v20, /device:TPU:1, one launch (start us, length us, event | category | flops | bytes accessed | tf_op | source)
XLA Modules:
  0.0 72.6 jit_solution(16825644188070952856)
XLA Ops:
  0.0 16.1 %shard_map.91 = (f32[4,5,16,128]{3,2,1,0:T(8,128)}, f32[4,5,16,128]{3,2,1,0:T(8,128)}, f32[4,16,5,128]{3,2,1,0:T(8,128)}, f32[4,16,5,128]{3,2,1,0:T(8,128)}, f32...) custom-call(f32[5,16,16,128]{3,2,1,0:T(8,128)} %refs_0_.1, ...), custom_call_target="tpu_custom_call" | custom-call | tf_op jit(solution)/shard_map/pallas_call | solution.py:160
  16.1 1.2 %pad_maximum_fusion.1 = f32[4,26,16,128]{3,2,1,0:T(8,128)S(1)} fusion(f32[4,5,16,128]{3,2,1,0:T(8,128)} %get-tuple-element.22, f32[4,16,16,128]{3,2,1,0:T(8,128)} %get-tuple-element.20, f32[4,5,16,128]{3,2,1,0:T(8,128)} %get-tuple-element.21), kind=kLoop, calls=%fused_computation.29 | loop fusion | flops 425984 | bytes 1703936 | tf_op jit(solution)/shard_map/concatenate | solution.py:253
  17.4 0.0 copy-done.17
  17.4 0.0 copy-start.1
  17.4 0.6 fusion.36
  18.1 0.0 copy-start.2
  18.1 0.0 copy-start
  18.1 0.0 copy-start.5
  18.1 0.2 copy.32
  18.3 0.1 copy-done.1
  18.4 0.1 copy-done.15
  18.5 0.1 copy-done.16
  18.6 0.5 convolution_bitcast_fusion
  19.1 0.1 copy-done.2
  19.2 0.4 copy-done
  19.6 0.0 copy-done.8
  19.6 0.2 copy-done.9
  19.8 0.2 bitcast_dynamic-update-slice_fusion.11
  20.0 0.1 bitcast_dynamic-update-slice_fusion.10
  20.1 0.1 bitcast_dynamic-update-slice_fusion.9
  20.3 0.2 bitcast_dynamic-update-slice_fusion.8
  20.5 0.1 bitcast_dynamic-update-slice_fusion.6
  20.6 0.1 bitcast_dynamic-update-slice_fusion.5
  20.7 0.1 bitcast_dynamic-update-slice_fusion.4
  20.9 0.1 bitcast_dynamic-update-slice_fusion
  21.1 0.1 slice_bitcast_fusion.20
  21.2 1.5 %multiply_add_fusion = (f32[5,16,16,128]{3,2,1,0:T(8,128)}, f32[5,16,16,128]{3,2,1,0:T(8,128)}, f32[5,16,16,128]{3,2,1,0:T(8,128)}) fusion(f32[5,16,16,128]{3,2,1,0:T(8,128)S(1)} %bitcast_dynamic-update-slice_fusion, f32[5,16,16,128]{3,2,1,0:T(8,128)S(1)} %bitcast_dynamic-update-slice_fusion.4, f32[5,16,16,128]{3,2,1,0:T(8,128)S(1)} %get-tuple-element.64, ...), kind=kLoop, calls=%fused_computation.31 | loop fusion | flops 2457600 | bytes 5111808 | tf_op jit(solution)/shard_map/add | solution.py:443
  22.7 14.6 %shard_map.92 = (f32[5,5,16,128]{3,2,1,0:T(8,128)}, f32[5,5,16,128]{3,2,1,0:T(8,128)}, f32[5,16,5,128]{3,2,1,0:T(8,128)}, f32[5,16,5,128]{3,2,1,0:T(8,128)}, f32[5,16,16,128]{3,2,1,0:T(8,128)}) custom-call(f32[5,16,16,128]{3,2,1,0:T(8,128)} %get-tuple-element.48.refs_0_, f32[5,16,16,128]{3,2,1,0:T(8,128)} %get-tuple-element.47.refs_1_, ...), custom_call_target="tpu_custom_call" | custom-call | tf_op jit(solution)/shard_map/pallas_call | solution.py:160
  37.3 1.1 %pad_maximum_fusion = f32[5,26,16,128]{3,2,1,0:T(8,128)S(1)} fusion(f32[5,5,16,128]{3,2,1,0:T(8,128)} %get-tuple-element.28, f32[5,16,16,128]{3,2,1,0:T(8,128)S(1)} %copy-done.7, f32[5,5,16,128]{3,2,1,0:T(8,128)} %get-tuple-element.27), kind=kLoop, calls=%fused_computation.21 | loop fusion | flops 532480 | bytes 2129920 | tf_op jit(solution)/shard_map/concatenate | solution.py:230
  38.5 0.8 %fusion.11 = f32[5,16,128,16]{2,3,1,0:T(8,128)S(1)} fusion(f32[16,26,1,1]{1,0,3,2:T(8,128)S(1)} %copy-done.17, f32[5,26,16,128]{3,2,1,0:T(8,128)S(1)} %pad_maximum_fusion), kind=kOutput, calls=%fused_computation.12 | convolution fusion | flops 25559040 | bytes 1721984 | tf_op jit(solution)/shard_map/al,flyz->fayz/dot_general | solution.py:379
  39.2 0.3 copy-done.6
  39.5 0.2 copy-done.10
  39.7 0.1 copy-done.13
  39.8 0.1 copy-done.14
  39.9 0.9 %fusion.28.refs_0_ = f32[5,16,16,128]{3,2,1,0:T(8,128)S(1)} fusion(f32[5,16,16,128]{3,2,1,0:T(8,128)S(1)} %copy-done.2, f32[5,16,16,128]{3,2,1,0:T(8,128)S(1)} %copy-done.10, f32[16,26,1,1]{1,0,3,2:T(8,128)S(1)} %copy-done.17, f32[5,16,5,128]{3,2,1,0:T(8,128)S(1)} %copy-done.14, f32[5,16,16,128]{3,2,1,0:T(8,128)S(1)} %copy-done.6, ...), kind=kOutput, calls=%fused_computation.19 | convolution fusion | flops 26746880 | bytes 3819136 | tf_op jit(solution)/shard_map/al,fxlz->fxaz/dot_general | solution.py:379
  40.8 0.0 copy-start.3
  40.8 1.0 %pad_maximum_fusion.2.refs_1_ = f32[2,5,16,5,128]{4,3,2,1,0:T(8,128)} fusion(f32[1,5,16,5,128]{4,3,2,1,0:T(8,128)S(1)} %get-tuple-element.63, f32[1,5,16,5,128]{4,3,2,1,0:T(8,128)S(1)} %get-tuple-element.62), kind=kLoop, calls=%fused_computation.30 | loop fusion | flops 102400 | bytes 819200 | tf_op jit(solution)/shard_map/stack | solution.py:263
  41.8 13.4 %shard_map.93 = (f32[2,5,5,16,128]{4,3,2,1,0:T(8,128)}, f32[2,5,16,5,128]{4,3,2,1,0:T(8,128)}, f32[2,2,5,5,5,128]{5,4,3,2,1,0:T(8,128)}) custom-call(f32[5,16,16,128]{3,2,1,0:T(8,128)} %copy-done.3, f32[2,5,16,5,128]{4,3,2,1,0:T(8,128)} %pad_maximum_fusion.2.refs_1_), custom_call_target="tpu_custom_call" | custom-call | tf_op jit(solution)/shard_map/pallas_call | solution.py:160
  55.3 0.0 copy-start.4
  55.3 1.2 %slice_bitcast_fusion.3 = (f32[5,16,5,128]{3,2,1,0:T(8,128)S(1)}, f32[5,16,5,128]{3,2,1,0:T(8,128)S(1)}) fusion(f32[2,5,16,5,128]{4,3,2,1,0:T(8,128)} %get-tuple-element.34), kind=kLoop, calls=%fused_computation.38 | loop fusion | bytes 819200 | tf_op jit(solution)/shard_map/squeeze | solution.py:290
  56.5 0.0 copy-done.11
  56.6 0.2 copy-done.4
  56.8 0.4 maximum_maximum_fusion
  57.2 0.3 copy-done.18
  57.5 2.4 %fusion = f32[5,26,128,16]{2,3,1,0:T(8,128)S(1)} fusion(f32[16,26,1,1]{1,0,3,2:T(8,128)S(1)} %copy-done.18, f32[5,26,26,128]{3,2,1,0:T(8,128)S(1)} %maximum_maximum_fusion), kind=kOutput, calls=%fused_computation.1 | convolution fusion | flops 83066880 | bytes 2797184 | tf_op jit(solution)/shard_map/al,flyz->fayz/dot_general | solution.py:379
  59.9 2.0 %fusion.13.refs_0_ = f32[5,16,16,128]{3,2,1,0:T(8,128)} fusion(f32[16,26,1,1]{1,0,3,2:T(8,128)S(1)} %copy-done.18, f32[5,26,128,16]{2,3,1,0:T(8,128)S(1)} %fusion), kind=kOutput, calls=%fused_computation.14 | convolution fusion | flops 51118080 | bytes 1721984 | tf_op jit(solution)/shard_map/al,fxlz->fxaz/dot_general | solution.py:379
  61.9 8.7 %shard_map.94 = f32[5,16,16,128]{3,2,1,0:T(8,128)} custom-call(f32[5,16,16,128]{3,2,1,0:T(8,128)} %fusion.13.refs_0_, f32[128,128]{1,0:T(8,128)} %constant.35.refs_1_, f32[128,8]{1,0:T(8,128)} %constant.37.refs_2_, f32[128,8]{1,0:T(8,128)} %constant.39.refs_3_), custom_call_target="tpu_custom_call" | custom-call | tf_op jit(solution)/shard_map/pallas_call | solution.py:160
  70.7 2.0 %copy.46 = f32[5,16,16,128]{3,2,1,0:T(8,128)} copy(f32[5,16,16,128]{3,2,1,0:T(8,128)} %shard_map.94) | data formatting | bytes 1310720
  (25 shorter events, 0.3 us)
Async XLA Ops:
  0.0 17.4 %copy-start.17 = (f32[16,26,1,1]{1,0,3,2:T(8,128)S(1)}, f32[16,26,1,1]{1,0,3,2:T(8,128)}, u32[]{:S(2)}) copy-start(f32[16,26,1,1]{1,0,3,2:T(8,128)} %constant.40) | copy-start | bytes 4996
  17.4 1.0 %copy-start.1 = (f32[4,16,16,128]{3,2,1,0:T(8,128)S(1)}, f32[4,16,16,128]{3,2,1,0:T(8,128)}, u32[]{:S(2)}) copy-start(f32[4,16,16,128]{3,2,1,0:T(8,128)} %get-tuple-element.20) | copy-start | bytes 1572868
  17.4 1.1 %copy-start.15 = (f32[4,16,5,128]{3,2,1,0:T(8,128)S(1)}, f32[4,16,5,128]{3,2,1,0:T(8,128)}, u32[]{:S(2)}) copy-start(f32[4,16,5,128]{3,2,1,0:T(8,128)} %get-tuple-element.23) | copy-start | bytes 491524
  17.4 1.2 %copy-start.16 = (f32[4,16,5,128]{3,2,1,0:T(8,128)S(1)}, f32[4,16,5,128]{3,2,1,0:T(8,128)}, u32[]{:S(2)}) copy-start(f32[4,16,5,128]{3,2,1,0:T(8,128)} %get-tuple-element.24) | copy-start | bytes 491524
  18.1 1.2 %copy-start.2 = (f32[5,16,16,128]{3,2,1,0:T(8,128)S(1)}, f32[5,16,16,128]{3,2,1,0:T(8,128)}, u32[]{:S(2)}) copy-start(f32[5,16,16,128]{3,2,1,0:T(8,128)} %refs_0_.1) | copy-start | bytes 1966084
  18.1 1.5 %copy-start = (f32[3,3,16,16,128]{4,3,2,1,0:T(8,128)S(1)}, f32[3,3,16,16,128]{4,3,2,1,0:T(8,128)}, u32[]{:S(2)}) copy-start(f32[3,3,16,16,128]{4,3,2,1,0:T(8,128)} %param.10) | copy-start | bytes 3538948
  18.1 1.5 %copy-start.5 = (f32[16,16,128]{2,1,0:T(8,128)S(1)}, f32[16,16,128]{2,1,0:T(8,128)}, u32[]{:S(2)}) copy-start(f32[16,16,128]{2,1,0:T(8,128)} %param.11) | copy-start | bytes 393220
  18.1 1.5 %copy-start.8 = (f32[16,16,128]{2,1,0:T(8,128)S(1)}, f32[16,16,128]{2,1,0:T(8,128)}, u32[]{:S(2)}) copy-start(f32[16,16,128]{2,1,0:T(8,128)} %get-tuple-element.26) | copy-start | bytes 393220
  18.1 1.7 %copy-start.9 = (f32[4,16,16,128]{3,2,1,0:T(8,128)S(1)}, f32[4,16,16,128]{3,2,1,0:T(8,128)}, u32[]{:S(2)}) copy-start(f32[4,16,16,128]{3,2,1,0:T(8,128)} %get-tuple-element.25) | copy-start | bytes 1572868
  22.7 14.6 %copy-start.7 = (f32[5,16,16,128]{3,2,1,0:T(8,128)S(1)}, f32[5,16,16,128]{3,2,1,0:T(8,128)}, u32[]{:S(2)}) copy-start(f32[5,16,16,128]{3,2,1,0:T(8,128)} %get-tuple-element.48.refs_0_) | copy-start | bytes 1966084
  38.4 1.1 %copy-start.6 = (f32[5,16,16,128]{3,2,1,0:T(8,128)S(1)}, f32[5,16,16,128]{3,2,1,0:T(8,128)}, u32[]{:S(2)}) copy-start(f32[5,16,16,128]{3,2,1,0:T(8,128)} %get-tuple-element.47.refs_1_) | copy-start | bytes 1966084
  38.4 1.3 %copy-start.10 = (f32[5,16,16,128]{3,2,1,0:T(8,128)S(1)}, f32[5,16,16,128]{3,2,1,0:T(8,128)}, u32[]{:S(2)}) copy-start(f32[5,16,16,128]{3,2,1,0:T(8,128)} %get-tuple-element.31) | copy-start | bytes 1966084
  38.4 1.3 %copy-start.13 = (f32[5,16,5,128]{3,2,1,0:T(8,128)S(1)}, f32[5,16,5,128]{3,2,1,0:T(8,128)}, u32[]{:S(2)}) copy-start(f32[5,16,5,128]{3,2,1,0:T(8,128)} %get-tuple-element.29) | copy-start | bytes 614404
  38.4 1.4 %copy-start.14 = (f32[5,16,5,128]{3,2,1,0:T(8,128)S(1)}, f32[5,16,5,128]{3,2,1,0:T(8,128)}, u32[]{:S(2)}) copy-start(f32[5,16,5,128]{3,2,1,0:T(8,128)} %get-tuple-element.30) | copy-start | bytes 614404
  40.8 1.1 %copy-start.3 = (f32[5,16,16,128]{3,2,1,0:T(8,128)}, f32[5,16,16,128]{3,2,1,0:T(8,128)S(1)}, u32[]{:S(2)}) copy-start(f32[5,16,16,128]{3,2,1,0:T(8,128)S(1)} %fusion.28.refs_0_) | copy-start | bytes 1966084
  55.2 1.3 %copy-start.12 = (f32[2,2,5,5,5,128]{5,4,3,2,1,0:T(8,128)S(1)}, f32[2,2,5,5,5,128]{5,4,3,2,1,0:T(8,128)}, u32[]{:S(2)}) copy-start(f32[2,2,5,5,5,128]{5,4,3,2,1,0:T(8,128)} %get-tuple-element.32) | copy-start | bytes 768004
  55.3 1.3 %copy-start.11 = (f32[2,5,5,16,128]{4,3,2,1,0:T(8,128)S(1)}, f32[2,5,5,16,128]{4,3,2,1,0:T(8,128)}, u32[]{:S(2)}) copy-start(f32[2,5,5,16,128]{4,3,2,1,0:T(8,128)} %get-tuple-element.33) | copy-start | bytes 1228804
  55.3 1.5 %copy-start.4 = (f32[5,16,16,128]{3,2,1,0:T(8,128)S(1)}, f32[5,16,16,128]{3,2,1,0:T(8,128)}, u32[]{:S(2)}) copy-start(f32[5,16,16,128]{3,2,1,0:T(8,128)} %copy-done.3) | copy-start | bytes 1966084
  56.8 0.7 copy-start.18

commit v21 on v20

--- a/solution.py
+++ b/solution.py
@@ -269,26 +269,28 @@
     last_x, first_x = slice(length_x - WIDTH, length_x), slice(0, WIDTH)
     every = slice(None)
     routes = [
-        ((1, 0, 0), 0, (every, last_x), 0, 0),
-        ((-1, 0, 0), 0, (every, first_x), 0, 1),
-        ((0, 1, 0), 1, 0, 1, 0),
-        ((0, -1, 0), 1, 1, 1, 1),
-        ((1, 1, 0), 1, (0, every, last_x), 2, (0, 0)),
-        ((-1, 1, 0), 1, (0, every, first_x), 2, (0, 1)),
-        ((1, -1, 0), 1, (1, every, last_x), 2, (1, 0)),
-        ((-1, -1, 0), 1, (1, every, first_x), 2, (1, 1)),
+        ((1, 0, 0), 0, (every, last_x), 0, every),
+        ((-1, 0, 0), 0, (every, first_x), 1, every),
+        ((0, 1, 0), 1, 0, 2, every),
+        ((0, -1, 0), 1, 1, 3, every),
+        ((1, 1, 0), 1, (0, every, last_x), 4, every),
+        ((-1, 1, 0), 1, (0, every, first_x), 5, every),
+        ((1, -1, 0), 1, (1, every, last_x), 6, every),
+        ((-1, -1, 0), 1, (1, every, first_x), 7, every),
     ]
     fields, depth = value.shape[0], value.shape[3]
-    out_shapes = [
-        jax.ShapeDtypeStruct((2, fields, WIDTH, length_y, depth), value.dtype),
-        jax.ShapeDtypeStruct((2, fields, length_x, WIDTH, depth), value.dtype),
-        jax.ShapeDtypeStruct((2, 2, fields, WIDTH, WIDTH, depth), value.dtype),
-    ]
-    along_x, along_y, edges = exchange([(value, pl.ANY), (faces_y, pl.ANY)], routes, out_shapes, tag)
+    out_shapes = (
+        [jax.ShapeDtypeStruct((fields, WIDTH, length_y, depth), value.dtype)] * 2
+        + [jax.ShapeDtypeStruct((fields, length_x, WIDTH, depth), value.dtype)] * 2
+        + [jax.ShapeDtypeStruct((fields, WIDTH, WIDTH, depth), value.dtype)] * 4
+    )
+    x_before, x_after, y_before, y_after, both_before, x_after_y_before, x_before_y_after, both_after = (
+        exchange([(value, pl.ANY), (faces_y, pl.ANY)], routes, out_shapes, tag)
+    )
     sections = [
-        jnp.concatenate([edges[0, 0], along_x[0], edges[1, 0]], axis=2),
-        jnp.concatenate([along_y[0], value, along_y[1]], axis=2),
-        jnp.concatenate([edges[0, 1], along_x[1], edges[1, 1]], axis=2),
+        jnp.concatenate([both_before, x_before, x_before_y_after], axis=2),
+        jnp.concatenate([y_before, value, y_after], axis=2),
+        jnp.concatenate([x_after_y_before, x_after, both_after], axis=2),
     ]
     return jnp.concatenate(sections, axis=1)
 

time: 73.5 us -> 73.3 us (level)
  local copies, waits for them, and re-layouts: 5.76 us -> 3.95 us
  other arithmetic: 6.43 us -> 8.02 us
    concatenate x1, other arithmetic: 0.36 us -> 1.95 us  [exchange_plane(): return jnp.concatenate(sections, axis=1)]
    squeeze x3 -> x0, local copies, waits for them, and re-layouts: 1.28 us -> none  [the longest x1 1.22 us: exchange_plane(): along_y[0]]
    unnamed x40 -> x34, local copies, waits for them, and re-layouts: 4.19 us -> 3.66 us
where the time goes in v21:
time: 73.3 us; the launch traced here: 72.5 us
  Pallas kernels  52.9 us (72%)
  other arithmetic  8.02 us (11%)
  matrix products  7.24 us (10%)
  local copies, waits for them, and re-layouts  3.95 us (5%)
    pallas_call x4, Pallas kernels, exchange(): pl.pallas_call(functools.partial(exchange_kernel, tuple(routes), sizes, l...  52.9 us
    dot_general x6, matrix products, sweep_lines(): return jnp.einsum(line_forms[dim], matrix, padded, precision=precision)  7.24 us
    unnamed x34, local copies, waits for them, and re-layouts  3.66 us
    concatenate x1, other arithmetic, exchange_plane(): return jnp.concatenate(sections, axis=1)  1.95 us
    add x1, other arithmetic, fluxes(): metrics[direction, 0] * totals[0] + metrics[direction, 1] * totals[1]  1.47 us

profile of v21, /device:TPU:1, one launch (start us, length us, event | category | flops | bytes accessed | tf_op | source)
XLA Modules:
  0.0 72.5 jit_solution(6319561875349752644)
XLA Ops:
  0.0 16.1 %shard_map.91 = (f32[4,5,16,128]{3,2,1,0:T(8,128)}, f32[4,5,16,128]{3,2,1,0:T(8,128)}, f32[4,16,5,128]{3,2,1,0:T(8,128)}, f32[4,16,5,128]{3,2,1,0:T(8,128)}, f32...) custom-call(f32[5,16,16,128]{3,2,1,0:T(8,128)} %refs_0_.1, ...), custom_call_target="tpu_custom_call" | custom-call | tf_op jit(solution)/shard_map/pallas_call | solution.py:160
  16.2 1.2 %pad_maximum_fusion.1 = f32[4,26,16,128]{3,2,1,0:T(8,128)S(1)} fusion(f32[4,5,16,128]{3,2,1,0:T(8,128)} %get-tuple-element.27, f32[4,16,16,128]{3,2,1,0:T(8,128)} %get-tuple-element.25, f32[4,5,16,128]{3,2,1,0:T(8,128)} %get-tuple-element.26), kind=kLoop, calls=%fused_computation.29 | loop fusion | flops 425984 | bytes 1703936 | tf_op jit(solution)/shard_map/concatenate | solution.py:253
  17.4 0.0 copy-done.14
  17.4 0.0 copy-start.1
  17.4 0.0 copy-start.12
  17.4 0.0 copy-start.13
  17.4 0.6 fusion.36
  18.1 0.0 copy-start.2
  18.1 0.0 copy-start
  18.1 0.0 copy-start.4
  18.1 0.0 copy-start.7
  18.1 0.0 copy-start.8
  18.1 0.2 copy.32
  18.3 0.1 copy-done.1
  18.5 0.1 copy-done.12
  18.5 0.1 copy-done.13
  18.6 0.5 convolution_bitcast_fusion
  19.1 0.1 copy-done.2
  19.3 0.4 copy-done
  19.6 0.0 copy-done.7
  19.7 0.2 copy-done.8
  19.8 0.2 bitcast_dynamic-update-slice_fusion.11
  20.0 0.1 bitcast_dynamic-update-slice_fusion.10
  20.2 0.1 bitcast_dynamic-update-slice_fusion.9
  20.3 0.2 bitcast_dynamic-update-slice_fusion.8
  20.5 0.1 bitcast_dynamic-update-slice_fusion.6
  20.6 0.1 bitcast_dynamic-update-slice_fusion.5
  20.7 0.1 bitcast_dynamic-update-slice_fusion.4
  21.0 0.1 bitcast_dynamic-update-slice_fusion
  21.1 0.1 slice_bitcast_fusion.16
  21.2 1.5 %multiply_add_fusion = (f32[5,16,16,128]{3,2,1,0:T(8,128)}, f32[5,16,16,128]{3,2,1,0:T(8,128)}, f32[5,16,16,128]{3,2,1,0:T(8,128)}) fusion(f32[5,16,16,128]{3,2,1,0:T(8,128)S(1)} %bitcast_dynamic-update-slice_fusion, f32[5,16,16,128]{3,2,1,0:T(8,128)S(1)} %bitcast_dynamic-update-slice_fusion.4, f32[5,16,16,128]{3,2,1,0:T(8,128)S(1)} %get-tuple-element.72, ...), kind=kLoop, calls=%fused_computation.31 | loop fusion | flops 2457600 | bytes 5111808 | tf_op jit(solution)/shard_map/add | solution.py:445
  22.7 14.6 %shard_map.92 = (f32[5,5,16,128]{3,2,1,0:T(8,128)}, f32[5,5,16,128]{3,2,1,0:T(8,128)}, f32[5,16,5,128]{3,2,1,0:T(8,128)}, f32[5,16,5,128]{3,2,1,0:T(8,128)}, f32[5,16,16,128]{3,2,1,0:T(8,128)}) custom-call(f32[5,16,16,128]{3,2,1,0:T(8,128)} %get-tuple-element.58.refs_0_, f32[5,16,16,128]{3,2,1,0:T(8,128)} %get-tuple-element.57.refs_1_, ...), custom_call_target="tpu_custom_call" | custom-call | tf_op jit(solution)/shard_map/pallas_call | solution.py:160
  37.3 1.1 %pad_maximum_fusion = f32[5,26,16,128]{3,2,1,0:T(8,128)S(1)} fusion(f32[5,5,16,128]{3,2,1,0:T(8,128)} %get-tuple-element.33, f32[5,16,16,128]{3,2,1,0:T(8,128)S(1)} %copy-done.6, f32[5,5,16,128]{3,2,1,0:T(8,128)} %get-tuple-element.32), kind=kLoop, calls=%fused_computation.21 | loop fusion | flops 532480 | bytes 2129920 | tf_op jit(solution)/shard_map/concatenate | solution.py:230
  38.5 0.8 %fusion.11 = f32[5,16,128,16]{2,3,1,0:T(8,128)S(1)} fusion(f32[16,26,1,1]{1,0,3,2:T(8,128)S(1)} %copy-done.14, f32[5,26,16,128]{3,2,1,0:T(8,128)S(1)} %pad_maximum_fusion), kind=kOutput, calls=%fused_computation.12 | convolution fusion | flops 25559040 | bytes 1721984 | tf_op jit(solution)/shard_map/al,flyz->fayz/dot_general | solution.py:381
  39.3 0.3 copy-done.5
  39.5 0.2 copy-done.9
  39.7 0.1 copy-done.10
  39.8 0.1 copy-done.11
  39.9 0.9 %fusion.28.refs_0_ = f32[5,16,16,128]{3,2,1,0:T(8,128)S(1)} fusion(f32[5,16,16,128]{3,2,1,0:T(8,128)S(1)} %copy-done.2, f32[5,16,16,128]{3,2,1,0:T(8,128)S(1)} %copy-done.9, f32[16,26,1,1]{1,0,3,2:T(8,128)S(1)} %copy-done.14, f32[5,16,5,128]{3,2,1,0:T(8,128)S(1)} %copy-done.11, f32[5,16,16,128]{3,2,1,0:T(8,128)S(1)} %copy-done.5, ...), kind=kOutput, calls=%fused_computation.19 | convolution fusion | flops 26746880 | bytes 3819136 | tf_op jit(solution)/shard_map/al,fxlz->fxaz/dot_general | solution.py:381
  40.8 0.0 copy-start.3
  40.9 1.0 %pad_maximum_fusion.2.refs_1_ = f32[2,5,16,5,128]{4,3,2,1,0:T(8,128)} fusion(f32[1,5,16,5,128]{4,3,2,1,0:T(8,128)S(1)} %get-tuple-element.71, f32[1,5,16,5,128]{4,3,2,1,0:T(8,128)S(1)} %get-tuple-element.70), kind=kLoop, calls=%fused_computation.30 | loop fusion | flops 102400 | bytes 819200 | tf_op jit(solution)/shard_map/stack | solution.py:263
  41.9 13.4 %shard_map.93 = (f32[5,5,16,128]{3,2,1,0:T(8,128)}, f32[5,5,16,128]{3,2,1,0:T(8,128)}, f32[5,16,5,128]{3,2,1,0:T(8,128)}, f32[5,16,5,128]{3,2,1,0:T(8,128)}, f32...) custom-call(f32[5,16,16,128]{3,2,1,0:T(8,128)} %copy-done.3, ...), custom_call_target="tpu_custom_call" | custom-call | tf_op jit(solution)/shard_map/pallas_call | solution.py:160
  55.3 0.0 copy-start.15
  55.3 1.9 %maximum_maximum_fusion = f32[5,26,26,128]{3,2,1,0:T(8,128)S(1)} fusion(f32[5,5,5,128]{3,2,1,0:T(8,128)} %get-tuple-element.44, f32[5,5,16,128]{3,2,1,0:T(8,128)} %get-tuple-element.43, f32[5,5,5,128]{3,2,1,0:T(8,128)} %get-tuple-element.42, f32[5,16,5,128]{3,2,1,0:T(8,128)} %get-tuple-element.41, f32[5,16,16,128]{3,2,1,0:T(8,128)} %copy-done.3, ...), kind=kLoop, calls=%fused_computation | loop fusion | flops 3461120 | bytes 3461120 | tf_op jit(solution)/shard_map/concatenate | solution.py:295
  57.3 2.4 %fusion = f32[5,26,128,16]{2,3,1,0:T(8,128)S(1)} fusion(f32[16,26,1,1]{1,0,3,2:T(8,128)S(1)} %copy-done.15, f32[5,26,26,128]{3,2,1,0:T(8,128)S(1)} %maximum_maximum_fusion), kind=kOutput, calls=%fused_computation.1 | convolution fusion | flops 83066880 | bytes 2797184 | tf_op jit(solution)/shard_map/al,flyz->fayz/dot_general | solution.py:381
  59.7 2.0 %fusion.13.refs_0_ = f32[5,16,16,128]{3,2,1,0:T(8,128)} fusion(f32[16,26,1,1]{1,0,3,2:T(8,128)S(1)} %copy-done.15, f32[5,26,128,16]{2,3,1,0:T(8,128)S(1)} %fusion), kind=kOutput, calls=%fused_computation.14 | convolution fusion | flops 51118080 | bytes 1721984 | tf_op jit(solution)/shard_map/al,fxlz->fxaz/dot_general | solution.py:381
  61.7 8.7 %shard_map.94 = f32[5,16,16,128]{3,2,1,0:T(8,128)} custom-call(f32[5,16,16,128]{3,2,1,0:T(8,128)} %fusion.13.refs_0_, f32[128,128]{1,0:T(8,128)} %constant.35.refs_1_, f32[128,8]{1,0:T(8,128)} %constant.37.refs_2_, f32[128,8]{1,0:T(8,128)} %constant.39.refs_3_), custom_call_target="tpu_custom_call" | custom-call | tf_op jit(solution)/shard_map/pallas_call | solution.py:160
  70.5 2.0 %copy.46 = f32[5,16,16,128]{3,2,1,0:T(8,128)} copy(f32[5,16,16,128]{3,2,1,0:T(8,128)} %shard_map.94) | data formatting | bytes 1310720
  (16 shorter events, 0.2 us)
Async XLA Ops:
  0.0 17.4 %copy-start.14 = (f32[16,26,1,1]{1,0,3,2:T(8,128)S(1)}, f32[16,26,1,1]{1,0,3,2:T(8,128)}, u32[]{:S(2)}) copy-start(f32[16,26,1,1]{1,0,3,2:T(8,128)} %constant.40) | copy-start | bytes 4996
  17.4 1.0 %copy-start.1 = (f32[4,16,16,128]{3,2,1,0:T(8,128)S(1)}, f32[4,16,16,128]{3,2,1,0:T(8,128)}, u32[]{:S(2)}) copy-start(f32[4,16,16,128]{3,2,1,0:T(8,128)} %get-tuple-element.25) | copy-start | bytes 1572868
  17.4 1.1 %copy-start.12 = (f32[4,16,5,128]{3,2,1,0:T(8,128)S(1)}, f32[4,16,5,128]{3,2,1,0:T(8,128)}, u32[]{:S(2)}) copy-start(f32[4,16,5,128]{3,2,1,0:T(8,128)} %get-tuple-element.28) | copy-start | bytes 491524
  17.4 1.2 %copy-start.13 = (f32[4,16,5,128]{3,2,1,0:T(8,128)S(1)}, f32[4,16,5,128]{3,2,1,0:T(8,128)}, u32[]{:S(2)}) copy-start(f32[4,16,5,128]{3,2,1,0:T(8,128)} %get-tuple-element.29) | copy-start | bytes 491524
  18.1 1.2 %copy-start.2 = (f32[5,16,16,128]{3,2,1,0:T(8,128)S(1)}, f32[5,16,16,128]{3,2,1,0:T(8,128)}, u32[]{:S(2)}) copy-start(f32[5,16,16,128]{3,2,1,0:T(8,128)} %refs_0_.1) | copy-start | bytes 1966084
  18.1 1.5 %copy-start = (f32[3,3,16,16,128]{4,3,2,1,0:T(8,128)S(1)}, f32[3,3,16,16,128]{4,3,2,1,0:T(8,128)}, u32[]{:S(2)}) copy-start(f32[3,3,16,16,128]{4,3,2,1,0:T(8,128)} %param.10) | copy-start | bytes 3538948
  18.1 1.5 %copy-start.4 = (f32[16,16,128]{2,1,0:T(8,128)S(1)}, f32[16,16,128]{2,1,0:T(8,128)}, u32[]{:S(2)}) copy-start(f32[16,16,128]{2,1,0:T(8,128)} %param.11) | copy-start | bytes 393220
  18.1 1.5 %copy-start.7 = (f32[16,16,128]{2,1,0:T(8,128)S(1)}, f32[16,16,128]{2,1,0:T(8,128)}, u32[]{:S(2)}) copy-start(f32[16,16,128]{2,1,0:T(8,128)} %get-tuple-element.31) | copy-start | bytes 393220
  18.1 1.7 %copy-start.8 = (f32[4,16,16,128]{3,2,1,0:T(8,128)S(1)}, f32[4,16,16,128]{3,2,1,0:T(8,128)}, u32[]{:S(2)}) copy-start(f32[4,16,16,128]{3,2,1,0:T(8,128)} %get-tuple-element.30) | copy-start | bytes 1572868
  22.7 14.7 %copy-start.6 = (f32[5,16,16,128]{3,2,1,0:T(8,128)S(1)}, f32[5,16,16,128]{3,2,1,0:T(8,128)}, u32[]{:S(2)}) copy-start(f32[5,16,16,128]{3,2,1,0:T(8,128)} %get-tuple-element.58.refs_0_) | copy-start | bytes 1966084
  38.5 1.1 %copy-start.5 = (f32[5,16,16,128]{3,2,1,0:T(8,128)S(1)}, f32[5,16,16,128]{3,2,1,0:T(8,128)}, u32[]{:S(2)}) copy-start(f32[5,16,16,128]{3,2,1,0:T(8,128)} %get-tuple-element.57.refs_1_) | copy-start | bytes 1966084
  38.5 1.3 %copy-start.9 = (f32[5,16,16,128]{3,2,1,0:T(8,128)S(1)}, f32[5,16,16,128]{3,2,1,0:T(8,128)}, u32[]{:S(2)}) copy-start(f32[5,16,16,128]{3,2,1,0:T(8,128)} %get-tuple-element.36) | copy-start | bytes 1966084
  38.5 1.3 %copy-start.10 = (f32[5,16,5,128]{3,2,1,0:T(8,128)S(1)}, f32[5,16,5,128]{3,2,1,0:T(8,128)}, u32[]{:S(2)}) copy-start(f32[5,16,5,128]{3,2,1,0:T(8,128)} %get-tuple-element.34) | copy-start | bytes 614404
  38.5 1.4 %copy-start.11 = (f32[5,16,5,128]{3,2,1,0:T(8,128)S(1)}, f32[5,16,5,128]{3,2,1,0:T(8,128)}, u32[]{:S(2)}) copy-start(f32[5,16,5,128]{3,2,1,0:T(8,128)} %get-tuple-element.35) | copy-start | bytes 614404
  40.8 1.1 %copy-start.3 = (f32[5,16,16,128]{3,2,1,0:T(8,128)}, f32[5,16,16,128]{3,2,1,0:T(8,128)S(1)}, u32[]{:S(2)}) copy-start(f32[5,16,16,128]{3,2,1,0:T(8,128)S(1)} %fusion.28.refs_0_) | copy-start | bytes 1966084
  55.3 2.0 %copy-start.15 = (f32[16,26,1,1]{1,0,3,2:T(8,128)S(1)}, f32[16,26,1,1]{1,0,3,2:T(8,128)}, u32[]{:S(2)}) copy-start(f32[16,26,1,1]{1,0,3,2:T(8,128)} %constant.41) | copy-start | bytes 4996

commit v22 on v21

--- a/solution.py
+++ b/solution.py
@@ -208,7 +208,7 @@
             routes.append((offset_along(axis, 1), source, last, target, whole))
             routes.append((offset_along(axis, -1), source, first, target + 1, whole))
         else:
-            arrays.append((value, pl.ANY))
+            arrays.append((value, pltpu.VMEM))
             face = value.shape[:dim] + (WIDTH,) + value.shape[dim + 1 :]
             out_shapes += [jax.ShapeDtypeStruct(face, value.dtype)] * 2
             source, target = len(arrays) - 1, len(out_shapes) - 2
@@ -285,7 +285,7 @@
         + [jax.ShapeDtypeStruct((fields, WIDTH, WIDTH, depth), value.dtype)] * 4
     )
     x_before, x_after, y_before, y_after, both_before, x_after_y_before, x_before_y_after, both_after = (
-        exchange([(value, pl.ANY), (faces_y, pl.ANY)], routes, out_shapes, tag)
+        exchange([(value, pltpu.VMEM), (faces_y, pl.ANY)], routes, out_shapes, tag)
     )
     sections = [
         jnp.concatenate([both_before, x_before, x_before_y_after], axis=2),

time: 73.3 us -> 74.2 us (1.012)
  Pallas kernels: 52.9 us -> 53.8 us
    pallas_call x4, Pallas kernels: 52.9 us -> 53.8 us  [exchange(): pl.pallas_call(functools.partial(exchange_kernel, tuple(routes), sizes, l...]
where the time goes in v22:
time: 74.2 us; the launch traced here: 73.3 us
  Pallas kernels  53.8 us (73%)
  other arithmetic  8.02 us (11%)
  matrix products  7.24 us (10%)
  local copies, waits for them, and re-layouts  3.95 us (5%)
    pallas_call x4, Pallas kernels, exchange(): pl.pallas_call(functools.partial(exchange_kernel, tuple(routes), sizes, l...  53.8 us
    dot_general x6, matrix products, sweep_lines(): return jnp.einsum(line_forms[dim], matrix, padded, precision=precision)  7.24 us
    unnamed x34, local copies, waits for them, and re-layouts  3.66 us
    concatenate x1, other arithmetic, exchange_plane(): return jnp.concatenate(sections, axis=1)  1.95 us

profile of v22, /device:TPU:1, one launch (start us, length us, event | category | flops | bytes accessed | tf_op | source)
XLA Modules:
  0.0 73.3 jit_solution(13917601344613850105)
XLA Ops:
  0.0 16.1 %shard_map.91 = (f32[4,5,16,128]{3,2,1,0:T(8,128)}, f32[4,5,16,128]{3,2,1,0:T(8,128)}, f32[4,16,5,128]{3,2,1,0:T(8,128)}, f32[4,16,5,128]{3,2,1,0:T(8,128)}, f32...) custom-call(f32[5,16,16,128]{3,2,1,0:T(8,128)} %refs_0_.1, ...), custom_call_target="tpu_custom_call" | custom-call | tf_op jit(solution)/shard_map/pallas_call | solution.py:160
  16.2 1.2 %pad_maximum_fusion.1 = f32[4,26,16,128]{3,2,1,0:T(8,128)S(1)} fusion(f32[4,5,16,128]{3,2,1,0:T(8,128)} %get-tuple-element.27, f32[4,16,16,128]{3,2,1,0:T(8,128)} %get-tuple-element.25, f32[4,5,16,128]{3,2,1,0:T(8,128)} %get-tuple-element.26), kind=kLoop, calls=%fused_computation.29 | loop fusion | flops 425984 | bytes 1703936 | tf_op jit(solution)/shard_map/concatenate | solution.py:253
  17.4 0.0 copy-done.14
  17.4 0.0 copy-start.1
  17.4 0.0 copy-start.12
  17.4 0.0 copy-start.13
  17.4 0.6 fusion.36
  18.1 0.0 copy-start.2
  18.1 0.0 copy-start
  18.1 0.0 copy-start.4
  18.1 0.0 copy-start.7
  18.1 0.0 copy-start.8
  18.1 0.2 copy.32
  18.3 0.1 copy-done.1
  18.5 0.1 copy-done.12
  18.5 0.1 copy-done.13
  18.6 0.5 convolution_bitcast_fusion
  19.1 0.1 copy-done.2
  19.3 0.4 copy-done
  19.6 0.0 copy-done.7
  19.7 0.2 copy-done.8
  19.8 0.2 bitcast_dynamic-update-slice_fusion.11
  20.0 0.1 bitcast_dynamic-update-slice_fusion.10
  20.2 0.1 bitcast_dynamic-update-slice_fusion.9
  20.3 0.2 bitcast_dynamic-update-slice_fusion.8
  20.5 0.1 bitcast_dynamic-update-slice_fusion.6
  20.6 0.1 bitcast_dynamic-update-slice_fusion.5
  20.7 0.1 bitcast_dynamic-update-slice_fusion.4
  21.0 0.1 bitcast_dynamic-update-slice_fusion
  21.1 0.1 slice_bitcast_fusion.16
  21.2 1.5 %multiply_add_fusion = (f32[5,16,16,128]{3,2,1,0:T(8,128)}, f32[5,16,16,128]{3,2,1,0:T(8,128)}, f32[5,16,16,128]{3,2,1,0:T(8,128)}) fusion(f32[5,16,16,128]{3,2,1,0:T(8,128)S(1)} %bitcast_dynamic-update-slice_fusion, f32[5,16,16,128]{3,2,1,0:T(8,128)S(1)} %bitcast_dynamic-update-slice_fusion.4, f32[5,16,16,128]{3,2,1,0:T(8,128)S(1)} %get-tuple-element.72, ...), kind=kLoop, calls=%fused_computation.31 | loop fusion | flops 2457600 | bytes 5111808 | tf_op jit(solution)/shard_map/add | solution.py:445
  22.7 14.6 %shard_map.92 = (f32[5,5,16,128]{3,2,1,0:T(8,128)}, f32[5,5,16,128]{3,2,1,0:T(8,128)}, f32[5,16,5,128]{3,2,1,0:T(8,128)}, f32[5,16,5,128]{3,2,1,0:T(8,128)}, f32[5,16,16,128]{3,2,1,0:T(8,128)}) custom-call(f32[5,16,16,128]{3,2,1,0:T(8,128)} %get-tuple-element.58.refs_0_, f32[5,16,16,128]{3,2,1,0:T(8,128)} %get-tuple-element.57.refs_1_, ...), custom_call_target="tpu_custom_call" | custom-call | tf_op jit(solution)/shard_map/pallas_call | solution.py:160
  37.3 1.1 %pad_maximum_fusion = f32[5,26,16,128]{3,2,1,0:T(8,128)S(1)} fusion(f32[5,5,16,128]{3,2,1,0:T(8,128)} %get-tuple-element.33, f32[5,16,16,128]{3,2,1,0:T(8,128)S(1)} %copy-done.6, f32[5,5,16,128]{3,2,1,0:T(8,128)} %get-tuple-element.32), kind=kLoop, calls=%fused_computation.21 | loop fusion | flops 532480 | bytes 2129920 | tf_op jit(solution)/shard_map/concatenate | solution.py:230
  38.5 0.8 %fusion.11 = f32[5,16,128,16]{2,3,1,0:T(8,128)S(1)} fusion(f32[16,26,1,1]{1,0,3,2:T(8,128)S(1)} %copy-done.14, f32[5,26,16,128]{3,2,1,0:T(8,128)S(1)} %pad_maximum_fusion), kind=kOutput, calls=%fused_computation.12 | convolution fusion | flops 25559040 | bytes 1721984 | tf_op jit(solution)/shard_map/al,flyz->fayz/dot_general | solution.py:381
  39.3 0.3 copy-done.5
  39.5 0.2 copy-done.9
  39.7 0.1 copy-done.10
  39.8 0.1 copy-done.11
  39.9 0.9 %fusion.28.refs_0_ = f32[5,16,16,128]{3,2,1,0:T(8,128)S(1)} fusion(f32[5,16,16,128]{3,2,1,0:T(8,128)S(1)} %copy-done.2, f32[5,16,16,128]{3,2,1,0:T(8,128)S(1)} %copy-done.9, f32[16,26,1,1]{1,0,3,2:T(8,128)S(1)} %copy-done.14, f32[5,16,5,128]{3,2,1,0:T(8,128)S(1)} %copy-done.11, f32[5,16,16,128]{3,2,1,0:T(8,128)S(1)} %copy-done.5, ...), kind=kOutput, calls=%fused_computation.19 | convolution fusion | flops 26746880 | bytes 3819136 | tf_op jit(solution)/shard_map/al,fxlz->fxaz/dot_general | solution.py:381
  40.8 0.0 copy-start.3
  40.9 1.0 %pad_maximum_fusion.2.refs_1_ = f32[2,5,16,5,128]{4,3,2,1,0:T(8,128)} fusion(f32[1,5,16,5,128]{4,3,2,1,0:T(8,128)S(1)} %get-tuple-element.71, f32[1,5,16,5,128]{4,3,2,1,0:T(8,128)S(1)} %get-tuple-element.70), kind=kLoop, calls=%fused_computation.30 | loop fusion | flops 102400 | bytes 819200 | tf_op jit(solution)/shard_map/stack | solution.py:263
  41.9 14.3 %shard_map.93 = (f32[5,5,16,128]{3,2,1,0:T(8,128)}, f32[5,5,16,128]{3,2,1,0:T(8,128)}, f32[5,16,5,128]{3,2,1,0:T(8,128)}, f32[5,16,5,128]{3,2,1,0:T(8,128)}, f32...) custom-call(f32[5,16,16,128]{3,2,1,0:T(8,128)} %copy-done.3, ...), custom_call_target="tpu_custom_call" | custom-call | tf_op jit(solution)/shard_map/pallas_call | solution.py:160
  56.2 0.0 copy-start.15
  56.2 1.9 %maximum_maximum_fusion = f32[5,26,26,128]{3,2,1,0:T(8,128)S(1)} fusion(f32[5,5,5,128]{3,2,1,0:T(8,128)} %get-tuple-element.44, f32[5,5,16,128]{3,2,1,0:T(8,128)} %get-tuple-element.43, f32[5,5,5,128]{3,2,1,0:T(8,128)} %get-tuple-element.42, f32[5,16,5,128]{3,2,1,0:T(8,128)} %get-tuple-element.41, f32[5,16,16,128]{3,2,1,0:T(8,128)} %copy-done.3, ...), kind=kLoop, calls=%fused_computation | loop fusion | flops 3461120 | bytes 3461120 | tf_op jit(solution)/shard_map/concatenate | solution.py:295
  58.1 2.4 %fusion = f32[5,26,128,16]{2,3,1,0:T(8,128)S(1)} fusion(f32[16,26,1,1]{1,0,3,2:T(8,128)S(1)} %copy-done.15, f32[5,26,26,128]{3,2,1,0:T(8,128)S(1)} %maximum_maximum_fusion), kind=kOutput, calls=%fused_computation.1 | convolution fusion | flops 83066880 | bytes 2797184 | tf_op jit(solution)/shard_map/al,flyz->fayz/dot_general | solution.py:381
  60.6 2.0 %fusion.13.refs_0_ = f32[5,16,16,128]{3,2,1,0:T(8,128)} fusion(f32[16,26,1,1]{1,0,3,2:T(8,128)S(1)} %copy-done.15, f32[5,26,128,16]{2,3,1,0:T(8,128)S(1)} %fusion), kind=kOutput, calls=%fused_computation.14 | convolution fusion | flops 51118080 | bytes 1721984 | tf_op jit(solution)/shard_map/al,fxlz->fxaz/dot_general | solution.py:381
  62.6 8.7 %shard_map.94 = f32[5,16,16,128]{3,2,1,0:T(8,128)} custom-call(f32[5,16,16,128]{3,2,1,0:T(8,128)} %fusion.13.refs_0_, f32[128,128]{1,0:T(8,128)} %constant.35.refs_1_, f32[128,8]{1,0:T(8,128)} %constant.37.refs_2_, f32[128,8]{1,0:T(8,128)} %constant.39.refs_3_), custom_call_target="tpu_custom_call" | custom-call | tf_op jit(solution)/shard_map/pallas_call | solution.py:160
  71.3 2.0 %copy.46 = f32[5,16,16,128]{3,2,1,0:T(8,128)} copy(f32[5,16,16,128]{3,2,1,0:T(8,128)} %shard_map.94) | data formatting | bytes 1310720
  (16 shorter events, 0.2 us)
Async XLA Ops:
  0.0 17.4 %copy-start.14 = (f32[16,26,1,1]{1,0,3,2:T(8,128)S(1)}, f32[16,26,1,1]{1,0,3,2:T(8,128)}, u32[]{:S(2)}) copy-start(f32[16,26,1,1]{1,0,3,2:T(8,128)} %constant.40) | copy-start | bytes 4996
  17.4 1.0 %copy-start.1 = (f32[4,16,16,128]{3,2,1,0:T(8,128)S(1)}, f32[4,16,16,128]{3,2,1,0:T(8,128)}, u32[]{:S(2)}) copy-start(f32[4,16,16,128]{3,2,1,0:T(8,128)} %get-tuple-element.25) | copy-start | bytes 1572868
  17.4 1.1 %copy-start.12 = (f32[4,16,5,128]{3,2,1,0:T(8,128)S(1)}, f32[4,16,5,128]{3,2,1,0:T(8,128)}, u32[]{:S(2)}) copy-start(f32[4,16,5,128]{3,2,1,0:T(8,128)} %get-tuple-element.28) | copy-start | bytes 491524
  17.4 1.2 %copy-start.13 = (f32[4,16,5,128]{3,2,1,0:T(8,128)S(1)}, f32[4,16,5,128]{3,2,1,0:T(8,128)}, u32[]{:S(2)}) copy-start(f32[4,16,5,128]{3,2,1,0:T(8,128)} %get-tuple-element.29) | copy-start | bytes 491524
  18.1 1.2 %copy-start.2 = (f32[5,16,16,128]{3,2,1,0:T(8,128)S(1)}, f32[5,16,16,128]{3,2,1,0:T(8,128)}, u32[]{:S(2)}) copy-start(f32[5,16,16,128]{3,2,1,0:T(8,128)} %refs_0_.1) | copy-start | bytes 1966084
  18.1 1.5 %copy-start = (f32[3,3,16,16,128]{4,3,2,1,0:T(8,128)S(1)}, f32[3,3,16,16,128]{4,3,2,1,0:T(8,128)}, u32[]{:S(2)}) copy-start(f32[3,3,16,16,128]{4,3,2,1,0:T(8,128)} %param.10) | copy-start | bytes 3538948
  18.1 1.5 %copy-start.4 = (f32[16,16,128]{2,1,0:T(8,128)S(1)}, f32[16,16,128]{2,1,0:T(8,128)}, u32[]{:S(2)}) copy-start(f32[16,16,128]{2,1,0:T(8,128)} %param.11) | copy-start | bytes 393220
  18.1 1.5 %copy-start.7 = (f32[16,16,128]{2,1,0:T(8,128)S(1)}, f32[16,16,128]{2,1,0:T(8,128)}, u32[]{:S(2)}) copy-start(f32[16,16,128]{2,1,0:T(8,128)} %get-tuple-element.31) | copy-start | bytes 393220
  18.1 1.7 %copy-start.8 = (f32[4,16,16,128]{3,2,1,0:T(8,128)S(1)}, f32[4,16,16,128]{3,2,1,0:T(8,128)}, u32[]{:S(2)}) copy-start(f32[4,16,16,128]{3,2,1,0:T(8,128)} %get-tuple-element.30) | copy-start | bytes 1572868
  22.7 14.6 %copy-start.6 = (f32[5,16,16,128]{3,2,1,0:T(8,128)S(1)}, f32[5,16,16,128]{3,2,1,0:T(8,128)}, u32[]{:S(2)}) copy-start(f32[5,16,16,128]{3,2,1,0:T(8,128)} %get-tuple-element.58.refs_0_) | copy-start | bytes 1966084
  38.4 1.1 %copy-start.5 = (f32[5,16,16,128]{3,2,1,0:T(8,128)S(1)}, f32[5,16,16,128]{3,2,1,0:T(8,128)}, u32[]{:S(2)}) copy-start(f32[5,16,16,128]{3,2,1,0:T(8,128)} %get-tuple-element.57.refs_1_) | copy-start | bytes 1966084
  38.5 1.3 %copy-start.9 = (f32[5,16,16,128]{3,2,1,0:T(8,128)S(1)}, f32[5,16,16,128]{3,2,1,0:T(8,128)}, u32[]{:S(2)}) copy-start(f32[5,16,16,128]{3,2,1,0:T(8,128)} %get-tuple-element.36) | copy-start | bytes 1966084
  38.5 1.3 %copy-start.10 = (f32[5,16,5,128]{3,2,1,0:T(8,128)S(1)}, f32[5,16,5,128]{3,2,1,0:T(8,128)}, u32[]{:S(2)}) copy-start(f32[5,16,5,128]{3,2,1,0:T(8,128)} %get-tuple-element.34) | copy-start | bytes 614404
  38.5 1.4 %copy-start.11 = (f32[5,16,5,128]{3,2,1,0:T(8,128)S(1)}, f32[5,16,5,128]{3,2,1,0:T(8,128)}, u32[]{:S(2)}) copy-start(f32[5,16,5,128]{3,2,1,0:T(8,128)} %get-tuple-element.35) | copy-start | bytes 614404
  40.8 1.1 %copy-start.3 = (f32[5,16,16,128]{3,2,1,0:T(8,128)}, f32[5,16,16,128]{3,2,1,0:T(8,128)S(1)}, u32[]{:S(2)}) copy-start(f32[5,16,16,128]{3,2,1,0:T(8,128)S(1)} %fusion.28.refs_0_) | copy-start | bytes 1966084
  56.2 2.0 %copy-start.15 = (f32[16,26,1,1]{1,0,3,2:T(8,128)S(1)}, f32[16,26,1,1]{1,0,3,2:T(8,128)}, u32[]{:S(2)}) copy-start(f32[16,26,1,1]{1,0,3,2:T(8,128)} %constant.41) | copy-start | bytes 4996

commit v23 on v21

--- a/solution.py
+++ b/solution.py
@@ -26,7 +26,7 @@
     return speed, pressure, pressure / density
 
 
-def exchange_kernel(routes, sizes, count, zeta, prepare, precision, *refs):
+def exchange_kernel(routes, sizes, count, zeta, prepare, precision, moves, *refs):
     sources = list(refs[:count])
     refs = refs[count:]
     if prepare:
@@ -38,7 +38,7 @@
         middle_ref, lower_ref, upper_ref = refs[:3]
         refs = refs[3:]
     extra = (1 if zeta else 0) + (2 if prepare else 0)
-    targets = refs[: len(refs) - 2 - (3 if zeta else 0) - extra]
+    targets = refs[: len(refs) - 3 - (3 if zeta else 0) - extra]
     refs = refs[len(targets) :]
     if zeta:
         out_ref = refs[0]
@@ -52,7 +52,7 @@
     if zeta:
         turned, before, after = refs[:3]
         refs = refs[3:]
-    send_sems, recv_sems = refs
+    send_sems, recv_sems, move_sems = refs
     here = [lax.axis_index(axis) for axis in AXES]
 
     def device(offset):
@@ -78,6 +78,14 @@
         fields, length_x, length_y, depth = block_ref.shape
         rows = fields * length_x * length_y
         turned[...] = block_ref[...].reshape(rows, depth).T
+    local = []
+    for index, (source, source_at, target, target_at) in enumerate(moves):
+        local.append(
+            pltpu.make_async_copy(
+                sources[source].at[source_at], targets[target].at[target_at], move_sems.at[index]
+            )
+        )
+        local[-1].start()
     pl.semaphore_wait(barrier, len(partners))
     copies = []
     for index, (offset, source, source_at, target, target_at) in enumerate(routes):
@@ -110,7 +118,7 @@
     if zeta:
         total = jnp.dot(middle_ref[...], turned[...], precision=precision,
                         preferred_element_type=jnp.float32)
-    for copy in copies:
+    for copy in copies + local:
         copy.wait()
     if zeta:
         total = total + jnp.dot(lower_ref[...], before[...], precision=precision,
@@ -121,7 +129,7 @@
 
 
 def exchange(arrays, routes, out_shapes, tag, zeta=None, prepare=None,
-             precision=lax.Precision.HIGH):
+             precision=lax.Precision.HIGH, moves=()):
     sizes = tuple(lax.axis_size(axis) for axis in AXES)
     operands = [array for array, _ in arrays]
     in_specs = [pl.BlockSpec(memory_space=space) for _, space in arrays]
@@ -160,7 +168,7 @@
     return pl.pallas_call(
         functools.partial(
             exchange_kernel, tuple(routes), sizes, len(arrays) + (prepare is not None),
-            zeta is not None, prepare is not None, precision,
+            zeta is not None, prepare is not None, precision, tuple(moves),
         ),
         out_shape=out_shapes,
         in_specs=in_specs,
@@ -168,6 +176,7 @@
         scratch_shapes=scratch + [
             pltpu.SemaphoreType.DMA((copies,)),
             pltpu.SemaphoreType.DMA((copies,)),
+            pltpu.SemaphoreType.DMA((max(1, len(moves)),)),
         ],
         compiler_params=pltpu.CompilerParams(collective_id=tag, has_side_effects=True),
     )(*operands)
@@ -182,7 +191,7 @@
 
 
 def exchange_faces(items, tag, zeta=None):
-    arrays, routes, out_shapes = [], [], []
+    arrays, routes, out_shapes, moves = [], [], [], []
     for value, axis, dim in items:
         ndim, length = value.ndim, value.shape[dim]
         if dim == ndim - 1:
@@ -208,15 +217,17 @@
             routes.append((offset_along(axis, 1), source, last, target, whole))
             routes.append((offset_along(axis, -1), source, first, target + 1, whole))
         else:
-            arrays.append((value, pl.ANY))
-            face = value.shape[:dim] + (WIDTH,) + value.shape[dim + 1 :]
-            out_shapes += [jax.ShapeDtypeStruct(face, value.dtype)] * 2
-            source, target = len(arrays) - 1, len(out_shapes) - 2
-            whole = window(ndim, dim, None, None)
+            arrays += [(value, pl.ANY), (value, pltpu.VMEM)]
+            extended = value.shape[:dim] + (length + 2 * WIDTH,) + value.shape[dim + 1 :]
+            out_shapes.append(jax.ShapeDtypeStruct(extended, value.dtype))
+            source, target = len(arrays) - 2, len(out_shapes) - 1
             last, first = window(ndim, dim, length - WIDTH, length), window(ndim, dim, 0, WIDTH)
-            routes.append((offset_along(axis, 1), source, last, target, whole))
-            routes.append((offset_along(axis, -1), source, first, target + 1, whole))
-    received = exchange(arrays, routes, out_shapes, tag, zeta)
+            ahead = window(ndim, dim, length + WIDTH, length + 2 * WIDTH)
+            routes.append((offset_along(axis, 1), source, last, target, first))
+            routes.append((offset_along(axis, -1), source, first, target, ahead))
+            moves.append((source + 1, window(ndim, dim, None, None), target,
+                          window(ndim, dim, WIDTH, length + WIDTH)))
+    received = exchange(arrays, routes, out_shapes, tag, zeta, moves=moves)
     padded, place = [], 0
     for value, axis, dim in items:
         if dim == value.ndim - 1:
@@ -224,9 +235,13 @@
             both = jnp.moveaxis(both, 2, dim + 1)
             before, after = both[0], both[1]
             place += 1
-        else:
+        elif dim == value.ndim - 2:
             before, after = received[place], received[place + 1]
             place += 2
+        else:
+            padded.append(received[place])
+            place += 1
+            continue
         padded.append(jnp.concatenate([before, value, after], axis=dim))
     if zeta is not None:
         padded.append(received[-1])
@@ -238,19 +253,20 @@
     length_x, length_y = primitive.shape[1], primitive.shape[2]
     every = slice(None)
     routes = [
-        ((1, 0, 0), 0, (every, slice(length_x - WIDTH, length_x)), 0, every),
-        ((-1, 0, 0), 0, (every, slice(0, WIDTH)), 1, every),
-        ((0, 1, 0), 0, (every, every, slice(length_y - WIDTH, length_y)), 2, every),
-        ((0, -1, 0), 0, (every, every, slice(0, WIDTH)), 3, every),
+        ((1, 0, 0), 0, (every, slice(length_x - WIDTH, length_x)), 0, (every, slice(0, WIDTH))),
+        ((-1, 0, 0), 0, (every, slice(0, WIDTH)), 0, (every, slice(length_x + WIDTH, length_x + 2 * WIDTH))),
+        ((0, 1, 0), 0, (every, every, slice(length_y - WIDTH, length_y)), 1, every),
+        ((0, -1, 0), 0, (every, every, slice(0, WIDTH)), 2, every),
     ]
-    face_x = (primitive.shape[0], WIDTH) + primitive.shape[2:]
+    moves = [(0, every, 0, (every, slice(WIDTH, length_x + WIDTH)))]
+    extended_x = (primitive.shape[0], length_x + 2 * WIDTH) + primitive.shape[2:]
     face_y = primitive.shape[:2] + (WIDTH,) + primitive.shape[3:]
-    out_shapes = [jax.ShapeDtypeStruct(face, primitive.dtype) for face in (face_x, face_x, face_y, face_y)]
-    before_x, after_x, before_y, after_y, swept, primitive, pressure = exchange(
-        [], routes, out_shapes, tag, (primitive, matrix), conserved
+    out_shapes = [jax.ShapeDtypeStruct(face, primitive.dtype) for face in (extended_x, face_y, face_y)]
+    padded_x, before_y, after_y, swept, primitive, pressure = exchange(
+        [], routes, out_shapes, tag, (primitive, matrix), conserved, moves=moves
     )
     return (
-        jnp.concatenate([before_x, primitive, after_x], axis=1),
+        padded_x,
         jnp.concatenate([before_y, primitive, after_y], axis=2),
         swept,
         primitive,

time: 73.3 us -> 72.8 us (level)
  matrix products: 7.24 us -> 9.85 us
  other arithmetic: 8.02 us -> 5.66 us
  local copies, waits for them, and re-layouts: 3.95 us -> 3.11 us
    dot_general x6, matrix products: 7.24 us -> 9.85 us  [sweep_lines(): return jnp.einsum(line_forms[dim], matrix, padded, precision=precision)]
    concatenate x2 -> x0, other arithmetic: 2.35 us -> none  [the longest x1 1.24 us: exchange_primitive(): jnp.concatenate([before_x, primitive, after_x], axis=1)]
    unnamed x34 -> x30, local copies, waits for them, and re-layouts: 3.66 us -> 2.82 us
where the time goes in v23:
time: 72.8 us; the launch traced here: 72.1 us
  Pallas kernels  53.1 us (73%)
  matrix products  9.85 us (14%)
  other arithmetic  5.66 us (8%)
  local copies, waits for them, and re-layouts  3.11 us (4%)
    pallas_call x4, Pallas kernels, exchange(): pl.pallas_call(functools.partial(exchange_kernel, tuple(routes), sizes, l...  53.1 us
    dot_general x6, matrix products, sweep_lines(): return jnp.einsum(line_forms[dim], matrix, padded, precision=precision)  9.85 us
    unnamed x30, local copies, waits for them, and re-layouts  2.82 us
    concatenate x1, other arithmetic, exchange_plane(): return jnp.concatenate(sections, axis=1)  1.95 us

profile of v23, /device:TPU:1, one launch (start us, length us, event | category | flops | bytes accessed | tf_op | source)
XLA Modules:
  0.0 72.1 jit_solution(2184414130903003492)
XLA Ops:
  0.0 16.2 %shard_map.91 = (f32[4,26,16,128]{3,2,1,0:T(8,128)}, f32[4,16,5,128]{3,2,1,0:T(8,128)}, f32[4,16,5,128]{3,2,1,0:T(8,128)}, f32[4,16,16,128]{3,2,1,0:T(8,128)}, f...) custom-call(f32[5,16,16,128]{3,2,1,0:T(8,128)} %refs_0_.1, f32[128,128]{1,0:T(8,128)} %constant.30.refs_1_.refs_4_, ...), custom_call_target="tpu_custom_call" | custom-call | tf_op jit(solution)/shard_map/pallas_call | solution.py:168
  16.2 0.0 copy-start.8
  16.2 0.0 copy-start.7
  16.2 1.8 %convolution_bitcast_fusion = f32[4,16,16,128]{3,2,1,0:T(8,128)S(1)} fusion(f32[16,26,1,1]{1,0,3,2:T(8,128)} %constant.40, f32[4,16,5,128]{3,2,1,0:T(8,128)} %get-tuple-element.26, f32[4,16,16,128]{3,2,1,0:T(8,128)} %get-tuple-element.23, f32[4,16,5,128]{3,2,1,0:T(8,128)} %get-tuple-element.25), kind=kOutput, calls=%fused_computation.20 | convolution fusion | flops 20873216 | bytes 1377920 | tf_op jit(solution)/shard_map/al,fxlz->fxaz/dot_general | solution.py:397
  18.0 0.0 copy-done.12
  18.1 0.0 copy-done.8
  18.1 0.0 copy-start.1
  18.1 0.0 copy-start
  18.1 0.0 copy-start.2
  18.1 0.0 copy-start.4
  18.1 0.0 copy-start.6
  18.1 0.6 fusion.36
  18.8 0.2 copy.32
  18.9 0.2 copy-done.1
  19.2 0.0 copy-done.7
  19.2 0.4 copy-done
  19.5 0.1 copy-done.2
  19.7 0.0 copy-done.4
  19.7 0.0 copy-done.6
  19.7 0.2 bitcast_dynamic-update-slice_fusion.11
  19.9 0.1 bitcast_dynamic-update-slice_fusion.10
  20.0 0.1 bitcast_dynamic-update-slice_fusion.9
  20.2 0.2 bitcast_dynamic-update-slice_fusion.8
  20.4 0.1 bitcast_dynamic-update-slice_fusion.6
  20.5 0.1 bitcast_dynamic-update-slice_fusion.5
  20.6 0.1 bitcast_dynamic-update-slice_fusion.4
  20.8 0.1 bitcast_dynamic-update-slice_fusion
  21.0 0.1 slice_bitcast_fusion.16
  21.1 1.4 %multiply_add_fusion = (f32[5,16,16,128]{3,2,1,0:T(8,128)}, f32[5,16,16,128]{3,2,1,0:T(8,128)}, f32[5,16,16,128]{3,2,1,0:T(8,128)}) fusion(f32[5,16,16,128]{3,2,1,0:T(8,128)S(1)} %bitcast_dynamic-update-slice_fusion, f32[5,16,16,128]{3,2,1,0:T(8,128)S(1)} %bitcast_dynamic-update-slice_fusion.4, f32[5,16,16,128]{3,2,1,0:T(8,128)S(1)} %get-tuple-element.68, ...), kind=kLoop, calls=%fused_computation.29 | loop fusion | flops 2457600 | bytes 5111808 | tf_op jit(solution)/shard_map/add | solution.py:461
  22.5 14.8 %shard_map.92 = (f32[5,26,16,128]{3,2,1,0:T(8,128)}, f32[5,16,5,128]{3,2,1,0:T(8,128)}, f32[5,16,5,128]{3,2,1,0:T(8,128)}, f32[5,16,16,128]{3,2,1,0:T(8,128)}) custom-call(f32[5,16,16,128]{3,2,1,0:T(8,128)} %get-tuple-element.54.refs_0_.refs_1_, f32[5,16,16,128]{3,2,1,0:T(8,128)} %get-tuple-element.54.refs_0_.refs_1_, ...), custom_call_target="tpu_custom_call" | custom-call | tf_op jit(solution)/shard_map/pallas_call | solution.py:168
  37.3 0.0 copy-start.5
  37.3 0.0 copy-start.9
  37.3 0.0 copy-start.10
  37.3 2.1 %fusion.11 = f32[5,16,128,16]{2,3,1,0:T(8,128)S(1)} fusion(f32[16,26,1,1]{1,0,3,2:T(8,128)S(1)} %copy-done.12, f32[5,26,16,128]{3,2,1,0:T(8,128)} %get-tuple-element.29), kind=kOutput, calls=%fused_computation.12 | convolution fusion | flops 25559040 | bytes 1721984 | tf_op jit(solution)/shard_map/al,flyz->fayz/dot_general | solution.py:397
  39.5 0.0 copy-done.5
  39.5 0.0 copy-done.9
  39.5 0.0 copy-done.10
  39.5 0.0 copy-done.11
  39.5 0.8 %fusion.28.refs_0_ = f32[5,16,16,128]{3,2,1,0:T(8,128)S(1)} fusion(f32[5,16,16,128]{3,2,1,0:T(8,128)S(1)} %copy-done.1, f32[5,16,16,128]{3,2,1,0:T(8,128)S(1)} %copy-done.9, f32[16,26,1,1]{1,0,3,2:T(8,128)S(1)} %copy-done.12, f32[5,16,5,128]{3,2,1,0:T(8,128)S(1)} %copy-done.11, f32[5,16,16,128]{3,2,1,0:T(8,128)S(1)} %copy-done.5, ...), kind=kOutput, calls=%fused_computation.19 | convolution fusion | flops 26746880 | bytes 3819136 | tf_op jit(solution)/shard_map/al,fxlz->fxaz/dot_general | solution.py:397
  40.4 0.0 copy-start.3
  40.4 1.0 %pad_maximum_fusion.refs_1_ = f32[2,5,16,5,128]{4,3,2,1,0:T(8,128)} fusion(f32[1,5,16,5,128]{4,3,2,1,0:T(8,128)S(1)} %get-tuple-element.67, f32[1,5,16,5,128]{4,3,2,1,0:T(8,128)S(1)} %get-tuple-element.66), kind=kLoop, calls=%fused_computation.28 | loop fusion | flops 102400 | bytes 819200 | tf_op jit(solution)/shard_map/stack | solution.py:279
  41.4 13.4 %shard_map.93 = (f32[5,5,16,128]{3,2,1,0:T(8,128)}, f32[5,5,16,128]{3,2,1,0:T(8,128)}, f32[5,16,5,128]{3,2,1,0:T(8,128)}, f32[5,16,5,128]{3,2,1,0:T(8,128)}, f32...) custom-call(f32[5,16,16,128]{3,2,1,0:T(8,128)} %copy-done.3, ...), custom_call_target="tpu_custom_call" | custom-call | tf_op jit(solution)/shard_map/pallas_call | solution.py:168
  54.9 0.0 copy-start.13
  54.9 1.9 %maximum_maximum_fusion = f32[5,26,26,128]{3,2,1,0:T(8,128)S(1)} fusion(f32[5,5,5,128]{3,2,1,0:T(8,128)} %get-tuple-element.40, f32[5,5,16,128]{3,2,1,0:T(8,128)} %get-tuple-element.39, f32[5,5,5,128]{3,2,1,0:T(8,128)} %get-tuple-element.38, f32[5,16,5,128]{3,2,1,0:T(8,128)} %get-tuple-element.37, f32[5,16,16,128]{3,2,1,0:T(8,128)} %copy-done.3, ...), kind=kLoop, calls=%fused_computation | loop fusion | flops 3461120 | bytes 3461120 | tf_op jit(solution)/shard_map/concatenate | solution.py:311
  56.9 2.4 %fusion = f32[5,26,128,16]{2,3,1,0:T(8,128)S(1)} fusion(f32[16,26,1,1]{1,0,3,2:T(8,128)S(1)} %copy-done.13, f32[5,26,26,128]{3,2,1,0:T(8,128)S(1)} %maximum_maximum_fusion), kind=kOutput, calls=%fused_computation.1 | convolution fusion | flops 83066880 | bytes 2797184 | tf_op jit(solution)/shard_map/al,flyz->fayz/dot_general | solution.py:397
  59.3 2.0 %fusion.13.refs_0_ = f32[5,16,16,128]{3,2,1,0:T(8,128)} fusion(f32[16,26,1,1]{1,0,3,2:T(8,128)S(1)} %copy-done.13, f32[5,26,128,16]{2,3,1,0:T(8,128)S(1)} %fusion), kind=kOutput, calls=%fused_computation.14 | convolution fusion | flops 51118080 | bytes 1721984 | tf_op jit(solution)/shard_map/al,fxlz->fxaz/dot_general | solution.py:397
  61.3 8.8 %shard_map.94 = f32[5,16,16,128]{3,2,1,0:T(8,128)} custom-call(f32[5,16,16,128]{3,2,1,0:T(8,128)} %fusion.13.refs_0_, f32[128,128]{1,0:T(8,128)} %constant.35.refs_1_, f32[128,8]{1,0:T(8,128)} %constant.37.refs_2_, f32[128,8]{1,0:T(8,128)} %constant.39.refs_3_), custom_call_target="tpu_custom_call" | custom-call | tf_op jit(solution)/shard_map/pallas_call | solution.py:168
  70.1 2.0 %copy.46 = f32[5,16,16,128]{3,2,1,0:T(8,128)} copy(f32[5,16,16,128]{3,2,1,0:T(8,128)} %shard_map.94) | data formatting | bytes 1310720
  (10 shorter events, 0.2 us)
Async XLA Ops:
  0.0 18.0 %copy-start.12 = (f32[16,26,1,1]{1,0,3,2:T(8,128)S(1)}, f32[16,26,1,1]{1,0,3,2:T(8,128)}, u32[]{:S(2)}) copy-start(f32[16,26,1,1]{1,0,3,2:T(8,128)} %constant.40) | copy-start | bytes 4996
  16.2 1.9 %copy-start.8 = (f32[4,26,16,128]{3,2,1,0:T(8,128)S(1)}, f32[4,26,16,128]{3,2,1,0:T(8,128)}, u32[]{:S(2)}) copy-start(f32[4,26,16,128]{3,2,1,0:T(8,128)} %get-tuple-element.24) | copy-start | bytes 2555908
  16.2 3.0 %copy-start.7 = (f32[4,16,16,128]{3,2,1,0:T(8,128)S(1)}, f32[4,16,16,128]{3,2,1,0:T(8,128)}, u32[]{:S(2)}) copy-start(f32[4,16,16,128]{3,2,1,0:T(8,128)} %get-tuple-element.27) | copy-start | bytes 1572868
  18.1 1.1 %copy-start.1 = (f32[5,16,16,128]{3,2,1,0:T(8,128)S(1)}, f32[5,16,16,128]{3,2,1,0:T(8,128)}, u32[]{:S(2)}) copy-start(f32[5,16,16,128]{3,2,1,0:T(8,128)} %refs_0_.1) | copy-start | bytes 1966084
  18.1 1.5 %copy-start = (f32[3,3,16,16,128]{4,3,2,1,0:T(8,128)S(1)}, f32[3,3,16,16,128]{4,3,2,1,0:T(8,128)}, u32[]{:S(2)}) copy-start(f32[3,3,16,16,128]{4,3,2,1,0:T(8,128)} %param.10) | copy-start | bytes 3538948
  18.1 1.6 %copy-start.2 = (f32[4,16,16,128]{3,2,1,0:T(8,128)S(1)}, f32[4,16,16,128]{3,2,1,0:T(8,128)}, u32[]{:S(2)}) copy-start(f32[4,16,16,128]{3,2,1,0:T(8,128)} %get-tuple-element.23) | copy-start | bytes 1572868
  18.1 1.6 %copy-start.4 = (f32[16,16,128]{2,1,0:T(8,128)S(1)}, f32[16,16,128]{2,1,0:T(8,128)}, u32[]{:S(2)}) copy-start(f32[16,16,128]{2,1,0:T(8,128)} %param.11) | copy-start | bytes 393220
  18.1 1.6 %copy-start.6 = (f32[16,16,128]{2,1,0:T(8,128)S(1)}, f32[16,16,128]{2,1,0:T(8,128)}, u32[]{:S(2)}) copy-start(f32[16,16,128]{2,1,0:T(8,128)} %get-tuple-element.28) | copy-start | bytes 393220
  37.3 2.2 %copy-start.5 = (f32[5,16,16,128]{3,2,1,0:T(8,128)S(1)}, f32[5,16,16,128]{3,2,1,0:T(8,128)}, u32[]{:S(2)}) copy-start(f32[5,16,16,128]{3,2,1,0:T(8,128)} %get-tuple-element.53.refs_2_) | copy-start | bytes 1966084
  37.3 2.2 %copy-start.9 = (f32[5,16,16,128]{3,2,1,0:T(8,128)S(1)}, f32[5,16,16,128]{3,2,1,0:T(8,128)}, u32[]{:S(2)}) copy-start(f32[5,16,16,128]{3,2,1,0:T(8,128)} %get-tuple-element.32) | copy-start | bytes 1966084
  37.3 2.2 %copy-start.10 = (f32[5,16,5,128]{3,2,1,0:T(8,128)S(1)}, f32[5,16,5,128]{3,2,1,0:T(8,128)}, u32[]{:S(2)}) copy-start(f32[5,16,5,128]{3,2,1,0:T(8,128)} %get-tuple-element.30) | copy-start | bytes 614404
  37.3 2.2 %copy-start.11 = (f32[5,16,5,128]{3,2,1,0:T(8,128)S(1)}, f32[5,16,5,128]{3,2,1,0:T(8,128)}, u32[]{:S(2)}) copy-start(f32[5,16,5,128]{3,2,1,0:T(8,128)} %get-tuple-element.31) | copy-start | bytes 614404
  40.4 1.1 %copy-start.3 = (f32[5,16,16,128]{3,2,1,0:T(8,128)}, f32[5,16,16,128]{3,2,1,0:T(8,128)S(1)}, u32[]{:S(2)}) copy-start(f32[5,16,16,128]{3,2,1,0:T(8,128)S(1)} %fusion.28.refs_0_) | copy-start | bytes 1966084
  54.9 2.0 %copy-start.13 = (f32[16,26,1,1]{1,0,3,2:T(8,128)S(1)}, f32[16,26,1,1]{1,0,3,2:T(8,128)}, u32[]{:S(2)}) copy-start(f32[16,26,1,1]{1,0,3,2:T(8,128)} %constant.41) | copy-start | bytes 4996

commit v24 on v23

--- a/solution.py
+++ b/solution.py
@@ -129,11 +129,14 @@
 
 
 def exchange(arrays, routes, out_shapes, tag, zeta=None, prepare=None,
-             precision=lax.Precision.HIGH, moves=()):
+             precision=lax.Precision.HIGH, moves=(), near=()):
     sizes = tuple(lax.axis_size(axis) for axis in AXES)
     operands = [array for array, _ in arrays]
     in_specs = [pl.BlockSpec(memory_space=space) for _, space in arrays]
-    out_specs = [pl.BlockSpec(memory_space=pl.ANY)] * len(out_shapes)
+    out_specs = [
+        pl.BlockSpec(memory_space=pltpu.VMEM if index in near else pl.ANY)
+        for index in range(len(out_shapes))
+    ]
     out_shapes = list(out_shapes)
     scratch = []
     copies = len(routes)
@@ -227,7 +230,8 @@
             routes.append((offset_along(axis, -1), source, first, target, ahead))
             moves.append((source + 1, window(ndim, dim, None, None), target,
                           window(ndim, dim, WIDTH, length + WIDTH)))
-    received = exchange(arrays, routes, out_shapes, tag, zeta, moves=moves)
+    near = tuple(move[2] for move in moves)
+    received = exchange(arrays, routes, out_shapes, tag, zeta, moves=moves, near=near)
     padded, place = [], 0
     for value, axis, dim in items:
         if dim == value.ndim - 1:
@@ -263,7 +267,7 @@
     face_y = primitive.shape[:2] + (WIDTH,) + primitive.shape[3:]
     out_shapes = [jax.ShapeDtypeStruct(face, primitive.dtype) for face in (extended_x, face_y, face_y)]
     padded_x, before_y, after_y, swept, primitive, pressure = exchange(
-        [], routes, out_shapes, tag, (primitive, matrix), conserved, moves=moves
+        [], routes, out_shapes, tag, (primitive, matrix), conserved, moves=moves, near=(0,)
     )
     return (
         padded_x,

time: 72.8 us -> 73 us (level)
  no operation moved by 1% of the time
where the time goes in v24:
time: 73 us; the launch traced here: 72.2 us
  Pallas kernels  53.3 us (73%)
  matrix products  9.85 us (13%)
  other arithmetic  5.66 us (8%)
  local copies, waits for them, and re-layouts  3.11 us (4%)
    pallas_call x4, Pallas kernels, exchange(): pl.pallas_call(functools.partial(exchange_kernel, tuple(routes), sizes, l...  53.3 us
    dot_general x6, matrix products, sweep_lines(): return jnp.einsum(line_forms[dim], matrix, padded, precision=precision)  9.85 us
    unnamed x30, local copies, waits for them, and re-layouts  2.82 us
    concatenate x1, other arithmetic, exchange_plane(): return jnp.concatenate(sections, axis=1)  1.95 us

profile of v24, /device:TPU:1, one launch (start us, length us, event | category | flops | bytes accessed | tf_op | source)
XLA Modules:
  0.0 72.2 jit_solution(9448838614291774049)
XLA Ops:
  0.0 16.2 %shard_map.91 = (f32[4,26,16,128]{3,2,1,0:T(8,128)}, f32[4,16,5,128]{3,2,1,0:T(8,128)}, f32[4,16,5,128]{3,2,1,0:T(8,128)}, f32[4,16,16,128]{3,2,1,0:T(8,128)}, f...) custom-call(f32[5,16,16,128]{3,2,1,0:T(8,128)} %refs_0_.1, f32[128,128]{1,0:T(8,128)} %constant.30.refs_1_.refs_4_, ...), custom_call_target="tpu_custom_call" | custom-call | tf_op jit(solution)/shard_map/pallas_call | solution.py:171
  16.3 0.0 copy-start.8
  16.3 0.0 copy-start.7
  16.3 1.8 %convolution_bitcast_fusion = f32[4,16,16,128]{3,2,1,0:T(8,128)S(1)} fusion(f32[16,26,1,1]{1,0,3,2:T(8,128)} %constant.40, f32[4,16,5,128]{3,2,1,0:T(8,128)} %get-tuple-element.26, f32[4,16,16,128]{3,2,1,0:T(8,128)} %get-tuple-element.23, f32[4,16,5,128]{3,2,1,0:T(8,128)} %get-tuple-element.25), kind=kOutput, calls=%fused_computation.20 | convolution fusion | flops 20873216 | bytes 1377920 | tf_op jit(solution)/shard_map/al,fxlz->fxaz/dot_general | solution.py:401
  18.1 0.0 copy-done.12
  18.1 0.0 copy-done.8
  18.1 0.0 copy-start.1
  18.1 0.0 copy-start
  18.2 0.0 copy-start.2
  18.2 0.0 copy-start.4
  18.2 0.0 copy-start.6
  18.2 0.6 fusion.36
  18.8 0.2 copy.32
  19.0 0.2 copy-done.1
  19.2 0.0 copy-done.7
  19.2 0.4 copy-done
  19.6 0.1 copy-done.2
  19.7 0.0 copy-done.4
  19.7 0.0 copy-done.6
  19.8 0.2 bitcast_dynamic-update-slice_fusion.11
  20.0 0.1 bitcast_dynamic-update-slice_fusion.10
  20.1 0.1 bitcast_dynamic-update-slice_fusion.9
  20.3 0.2 bitcast_dynamic-update-slice_fusion.8
  20.5 0.1 bitcast_dynamic-update-slice_fusion.6
  20.5 0.1 bitcast_dynamic-update-slice_fusion.5
  20.7 0.1 bitcast_dynamic-update-slice_fusion.4
  20.9 0.1 bitcast_dynamic-update-slice_fusion
  21.1 0.1 slice_bitcast_fusion.16
  21.2 1.4 %multiply_add_fusion = (f32[5,16,16,128]{3,2,1,0:T(8,128)}, f32[5,16,16,128]{3,2,1,0:T(8,128)}, f32[5,16,16,128]{3,2,1,0:T(8,128)}) fusion(f32[5,16,16,128]{3,2,1,0:T(8,128)S(1)} %bitcast_dynamic-update-slice_fusion, f32[5,16,16,128]{3,2,1,0:T(8,128)S(1)} %bitcast_dynamic-update-slice_fusion.4, f32[5,16,16,128]{3,2,1,0:T(8,128)S(1)} %get-tuple-element.68, ...), kind=kLoop, calls=%fused_computation.29 | loop fusion | flops 2457600 | bytes 5111808 | tf_op jit(solution)/shard_map/add | solution.py:465
  22.6 14.9 %shard_map.92 = (f32[5,26,16,128]{3,2,1,0:T(8,128)}, f32[5,16,5,128]{3,2,1,0:T(8,128)}, f32[5,16,5,128]{3,2,1,0:T(8,128)}, f32[5,16,16,128]{3,2,1,0:T(8,128)}) custom-call(f32[5,16,16,128]{3,2,1,0:T(8,128)} %get-tuple-element.54.refs_0_.refs_1_, f32[5,16,16,128]{3,2,1,0:T(8,128)} %get-tuple-element.54.refs_0_.refs_1_, ...), custom_call_target="tpu_custom_call" | custom-call | tf_op jit(solution)/shard_map/pallas_call | solution.py:171
  37.5 0.0 copy-start.5
  37.5 0.0 copy-start.9
  37.5 0.0 copy-start.10
  37.5 0.0 copy-start.11
  37.5 2.1 %fusion.11 = f32[5,16,128,16]{2,3,1,0:T(8,128)S(1)} fusion(f32[16,26,1,1]{1,0,3,2:T(8,128)S(1)} %copy-done.12, f32[5,26,16,128]{3,2,1,0:T(8,128)} %get-tuple-element.29), kind=kOutput, calls=%fused_computation.12 | convolution fusion | flops 25559040 | bytes 1721984 | tf_op jit(solution)/shard_map/al,flyz->fayz/dot_general | solution.py:401
  39.7 0.0 copy-done.5
  39.7 0.0 copy-done.9
  39.7 0.0 copy-done.10
  39.7 0.8 %fusion.28.refs_0_ = f32[5,16,16,128]{3,2,1,0:T(8,128)S(1)} fusion(f32[5,16,16,128]{3,2,1,0:T(8,128)S(1)} %copy-done.1, f32[5,16,16,128]{3,2,1,0:T(8,128)S(1)} %copy-done.9, f32[16,26,1,1]{1,0,3,2:T(8,128)S(1)} %copy-done.12, f32[5,16,5,128]{3,2,1,0:T(8,128)S(1)} %copy-done.11, f32[5,16,16,128]{3,2,1,0:T(8,128)S(1)} %copy-done.5, ...), kind=kOutput, calls=%fused_computation.19 | convolution fusion | flops 26746880 | bytes 3819136 | tf_op jit(solution)/shard_map/al,fxlz->fxaz/dot_general | solution.py:401
  40.5 0.0 copy-start.3
  40.6 1.0 %pad_maximum_fusion.refs_1_ = f32[2,5,16,5,128]{4,3,2,1,0:T(8,128)} fusion(f32[1,5,16,5,128]{4,3,2,1,0:T(8,128)S(1)} %get-tuple-element.67, f32[1,5,16,5,128]{4,3,2,1,0:T(8,128)S(1)} %get-tuple-element.66), kind=kLoop, calls=%fused_computation.28 | loop fusion | flops 102400 | bytes 819200 | tf_op jit(solution)/shard_map/stack | solution.py:283
  41.6 13.4 %shard_map.93 = (f32[5,5,16,128]{3,2,1,0:T(8,128)}, f32[5,5,16,128]{3,2,1,0:T(8,128)}, f32[5,16,5,128]{3,2,1,0:T(8,128)}, f32[5,16,5,128]{3,2,1,0:T(8,128)}, f32...) custom-call(f32[5,16,16,128]{3,2,1,0:T(8,128)} %copy-done.3, ...), custom_call_target="tpu_custom_call" | custom-call | tf_op jit(solution)/shard_map/pallas_call | solution.py:171
  55.1 0.0 copy-start.13
  55.1 1.9 %maximum_maximum_fusion = f32[5,26,26,128]{3,2,1,0:T(8,128)S(1)} fusion(f32[5,5,5,128]{3,2,1,0:T(8,128)} %get-tuple-element.40, f32[5,5,16,128]{3,2,1,0:T(8,128)} %get-tuple-element.39, f32[5,5,5,128]{3,2,1,0:T(8,128)} %get-tuple-element.38, f32[5,16,5,128]{3,2,1,0:T(8,128)} %get-tuple-element.37, f32[5,16,16,128]{3,2,1,0:T(8,128)} %copy-done.3, ...), kind=kLoop, calls=%fused_computation | loop fusion | flops 3461120 | bytes 3461120 | tf_op jit(solution)/shard_map/concatenate | solution.py:315
  57.0 2.4 %fusion = f32[5,26,128,16]{2,3,1,0:T(8,128)S(1)} fusion(f32[16,26,1,1]{1,0,3,2:T(8,128)S(1)} %copy-done.13, f32[5,26,26,128]{3,2,1,0:T(8,128)S(1)} %maximum_maximum_fusion), kind=kOutput, calls=%fused_computation.1 | convolution fusion | flops 83066880 | bytes 2797184 | tf_op jit(solution)/shard_map/al,flyz->fayz/dot_general | solution.py:401
  59.5 2.0 %fusion.13.refs_0_ = f32[5,16,16,128]{3,2,1,0:T(8,128)} fusion(f32[16,26,1,1]{1,0,3,2:T(8,128)S(1)} %copy-done.13, f32[5,26,128,16]{2,3,1,0:T(8,128)S(1)} %fusion), kind=kOutput, calls=%fused_computation.14 | convolution fusion | flops 51118080 | bytes 1721984 | tf_op jit(solution)/shard_map/al,fxlz->fxaz/dot_general | solution.py:401
  61.5 8.8 %shard_map.94 = f32[5,16,16,128]{3,2,1,0:T(8,128)} custom-call(f32[5,16,16,128]{3,2,1,0:T(8,128)} %fusion.13.refs_0_, f32[128,128]{1,0:T(8,128)} %constant.35.refs_1_, f32[128,8]{1,0:T(8,128)} %constant.37.refs_2_, f32[128,8]{1,0:T(8,128)} %constant.39.refs_3_), custom_call_target="tpu_custom_call" | custom-call | tf_op jit(solution)/shard_map/pallas_call | solution.py:171
  70.3 2.0 %copy.46 = f32[5,16,16,128]{3,2,1,0:T(8,128)} copy(f32[5,16,16,128]{3,2,1,0:T(8,128)} %shard_map.94) | data formatting | bytes 1310720
  (10 shorter events, 0.2 us)
Async XLA Ops:
  0.0 18.1 %copy-start.12 = (f32[16,26,1,1]{1,0,3,2:T(8,128)S(1)}, f32[16,26,1,1]{1,0,3,2:T(8,128)}, u32[]{:S(2)}) copy-start(f32[16,26,1,1]{1,0,3,2:T(8,128)} %constant.40) | copy-start | bytes 4996
  16.3 1.9 %copy-start.8 = (f32[4,26,16,128]{3,2,1,0:T(8,128)S(1)}, f32[4,26,16,128]{3,2,1,0:T(8,128)}, u32[]{:S(2)}) copy-start(f32[4,26,16,128]{3,2,1,0:T(8,128)} %get-tuple-element.24) | copy-start | bytes 2555908
  16.3 3.0 %copy-start.7 = (f32[4,16,16,128]{3,2,1,0:T(8,128)S(1)}, f32[4,16,16,128]{3,2,1,0:T(8,128)}, u32[]{:S(2)}) copy-start(f32[4,16,16,128]{3,2,1,0:T(8,128)} %get-tuple-element.27) | copy-start | bytes 1572868
  18.1 1.1 %copy-start.1 = (f32[5,16,16,128]{3,2,1,0:T(8,128)S(1)}, f32[5,16,16,128]{3,2,1,0:T(8,128)}, u32[]{:S(2)}) copy-start(f32[5,16,16,128]{3,2,1,0:T(8,128)} %refs_0_.1) | copy-start | bytes 1966084
  18.1 1.5 %copy-start = (f32[3,3,16,16,128]{4,3,2,1,0:T(8,128)S(1)}, f32[3,3,16,16,128]{4,3,2,1,0:T(8,128)}, u32[]{:S(2)}) copy-start(f32[3,3,16,16,128]{4,3,2,1,0:T(8,128)} %param.10) | copy-start | bytes 3538948
  18.2 1.6 %copy-start.2 = (f32[4,16,16,128]{3,2,1,0:T(8,128)S(1)}, f32[4,16,16,128]{3,2,1,0:T(8,128)}, u32[]{:S(2)}) copy-start(f32[4,16,16,128]{3,2,1,0:T(8,128)} %get-tuple-element.23) | copy-start | bytes 1572868
  18.2 1.6 %copy-start.4 = (f32[16,16,128]{2,1,0:T(8,128)S(1)}, f32[16,16,128]{2,1,0:T(8,128)}, u32[]{:S(2)}) copy-start(f32[16,16,128]{2,1,0:T(8,128)} %param.11) | copy-start | bytes 393220
  18.2 1.6 %copy-start.6 = (f32[16,16,128]{2,1,0:T(8,128)S(1)}, f32[16,16,128]{2,1,0:T(8,128)}, u32[]{:S(2)}) copy-start(f32[16,16,128]{2,1,0:T(8,128)} %get-tuple-element.28) | copy-start | bytes 393220
  37.5 2.2 %copy-start.5 = (f32[5,16,16,128]{3,2,1,0:T(8,128)S(1)}, f32[5,16,16,128]{3,2,1,0:T(8,128)}, u32[]{:S(2)}) copy-start(f32[5,16,16,128]{3,2,1,0:T(8,128)} %get-tuple-element.53.refs_2_) | copy-start | bytes 1966084
  37.5 2.2 %copy-start.9 = (f32[5,16,16,128]{3,2,1,0:T(8,128)S(1)}, f32[5,16,16,128]{3,2,1,0:T(8,128)}, u32[]{:S(2)}) copy-start(f32[5,16,16,128]{3,2,1,0:T(8,128)} %get-tuple-element.32) | copy-start | bytes 1966084
  37.5 2.2 %copy-start.10 = (f32[5,16,5,128]{3,2,1,0:T(8,128)S(1)}, f32[5,16,5,128]{3,2,1,0:T(8,128)}, u32[]{:S(2)}) copy-start(f32[5,16,5,128]{3,2,1,0:T(8,128)} %get-tuple-element.30) | copy-start | bytes 614404
  37.5 2.2 %copy-start.11 = (f32[5,16,5,128]{3,2,1,0:T(8,128)S(1)}, f32[5,16,5,128]{3,2,1,0:T(8,128)}, u32[]{:S(2)}) copy-start(f32[5,16,5,128]{3,2,1,0:T(8,128)} %get-tuple-element.31) | copy-start | bytes 614404
  40.5 1.1 %copy-start.3 = (f32[5,16,16,128]{3,2,1,0:T(8,128)}, f32[5,16,16,128]{3,2,1,0:T(8,128)S(1)}, u32[]{:S(2)}) copy-start(f32[5,16,16,128]{3,2,1,0:T(8,128)S(1)} %fusion.28.refs_0_) | copy-start | bytes 1966084
  55.1 2.0 %copy-start.13 = (f32[16,26,1,1]{1,0,3,2:T(8,128)S(1)}, f32[16,26,1,1]{1,0,3,2:T(8,128)}, u32[]{:S(2)}) copy-start(f32[16,26,1,1]{1,0,3,2:T(8,128)} %constant.41) | copy-start | bytes 4996

commit v25 on v23

--- a/solution.py
+++ b/solution.py
@@ -78,6 +78,8 @@
         fields, length_x, length_y, depth = block_ref.shape
         rows = fields * length_x * length_y
         turned[...] = block_ref[...].reshape(rows, depth).T
+        total = jnp.dot(middle_ref[...], turned[...], precision=precision,
+                        preferred_element_type=jnp.float32)
     local = []
     for index, (source, source_at, target, target_at) in enumerate(moves):
         local.append(
@@ -115,9 +117,6 @@
             )
     for copy in copies:
         copy.start()
-    if zeta:
-        total = jnp.dot(middle_ref[...], turned[...], precision=precision,
-                        preferred_element_type=jnp.float32)
     for copy in copies + local:
         copy.wait()
     if zeta:

time: 72.8 us -> 72.8 us (level)
  no operation moved by 1% of the time
where the time goes in v25:
time: 72.8 us; the launch traced here: 72.1 us
  Pallas kernels  53.1 us (73%)
  matrix products  9.85 us (14%)
  other arithmetic  5.66 us (8%)
  local copies, waits for them, and re-layouts  3.11 us (4%)
    pallas_call x4, Pallas kernels, exchange(): pl.pallas_call(functools.partial(exchange_kernel, tuple(routes), sizes, l...  53.1 us
    dot_general x6, matrix products, sweep_lines(): return jnp.einsum(line_forms[dim], matrix, padded, precision=precision)  9.85 us
    unnamed x30, local copies, waits for them, and re-layouts  2.82 us
    concatenate x1, other arithmetic, exchange_plane(): return jnp.concatenate(sections, axis=1)  1.95 us

profile of v25, /device:TPU:1, one launch (start us, length us, event | category | flops | bytes accessed | tf_op | source)
XLA Modules:
  0.0 72.1 jit_solution(7050348185238762881)
XLA Ops:
  0.0 16.2 %shard_map.91 = (f32[4,26,16,128]{3,2,1,0:T(8,128)}, f32[4,16,5,128]{3,2,1,0:T(8,128)}, f32[4,16,5,128]{3,2,1,0:T(8,128)}, f32[4,16,16,128]{3,2,1,0:T(8,128)}, f...) custom-call(f32[5,16,16,128]{3,2,1,0:T(8,128)} %refs_0_.1, f32[128,128]{1,0:T(8,128)} %constant.30.refs_1_.refs_4_, ...), custom_call_target="tpu_custom_call" | custom-call | tf_op jit(solution)/shard_map/pallas_call | solution.py:167
  16.2 0.0 copy-start.8
  16.2 0.0 copy-start.7
  16.2 1.8 %convolution_bitcast_fusion = f32[4,16,16,128]{3,2,1,0:T(8,128)S(1)} fusion(f32[16,26,1,1]{1,0,3,2:T(8,128)} %constant.40, f32[4,16,5,128]{3,2,1,0:T(8,128)} %get-tuple-element.26, f32[4,16,16,128]{3,2,1,0:T(8,128)} %get-tuple-element.23, f32[4,16,5,128]{3,2,1,0:T(8,128)} %get-tuple-element.25), kind=kOutput, calls=%fused_computation.20 | convolution fusion | flops 20873216 | bytes 1377920 | tf_op jit(solution)/shard_map/al,fxlz->fxaz/dot_general | solution.py:396
  18.0 0.0 copy-done.12
  18.1 0.0 copy-done.8
  18.1 0.0 copy-start.1
  18.1 0.0 copy-start
  18.1 0.0 copy-start.2
  18.1 0.0 copy-start.4
  18.1 0.0 copy-start.6
  18.1 0.6 fusion.36
  18.8 0.2 copy.32
  18.9 0.2 copy-done.1
  19.2 0.0 copy-done.7
  19.2 0.4 copy-done
  19.5 0.1 copy-done.2
  19.7 0.0 copy-done.4
  19.7 0.0 copy-done.6
  19.7 0.2 bitcast_dynamic-update-slice_fusion.11
  19.9 0.1 bitcast_dynamic-update-slice_fusion.10
  20.0 0.1 bitcast_dynamic-update-slice_fusion.9
  20.2 0.2 bitcast_dynamic-update-slice_fusion.8
  20.4 0.1 bitcast_dynamic-update-slice_fusion.6
  20.5 0.1 bitcast_dynamic-update-slice_fusion.5
  20.6 0.1 bitcast_dynamic-update-slice_fusion.4
  20.8 0.1 bitcast_dynamic-update-slice_fusion
  21.0 0.1 slice_bitcast_fusion.16
  21.1 1.4 %multiply_add_fusion = (f32[5,16,16,128]{3,2,1,0:T(8,128)}, f32[5,16,16,128]{3,2,1,0:T(8,128)}, f32[5,16,16,128]{3,2,1,0:T(8,128)}) fusion(f32[5,16,16,128]{3,2,1,0:T(8,128)S(1)} %bitcast_dynamic-update-slice_fusion, f32[5,16,16,128]{3,2,1,0:T(8,128)S(1)} %bitcast_dynamic-update-slice_fusion.4, f32[5,16,16,128]{3,2,1,0:T(8,128)S(1)} %get-tuple-element.68, ...), kind=kLoop, calls=%fused_computation.29 | loop fusion | flops 2457600 | bytes 5111808 | tf_op jit(solution)/shard_map/add | solution.py:460
  22.5 14.8 %shard_map.92 = (f32[5,26,16,128]{3,2,1,0:T(8,128)}, f32[5,16,5,128]{3,2,1,0:T(8,128)}, f32[5,16,5,128]{3,2,1,0:T(8,128)}, f32[5,16,16,128]{3,2,1,0:T(8,128)}) custom-call(f32[5,16,16,128]{3,2,1,0:T(8,128)} %get-tuple-element.54.refs_0_.refs_1_, f32[5,16,16,128]{3,2,1,0:T(8,128)} %get-tuple-element.54.refs_0_.refs_1_, ...), custom_call_target="tpu_custom_call" | custom-call | tf_op jit(solution)/shard_map/pallas_call | solution.py:167
  37.3 0.0 copy-start.5
  37.3 0.0 copy-start.9
  37.3 0.0 copy-start.10
  37.3 2.1 %fusion.11 = f32[5,16,128,16]{2,3,1,0:T(8,128)S(1)} fusion(f32[16,26,1,1]{1,0,3,2:T(8,128)S(1)} %copy-done.12, f32[5,26,16,128]{3,2,1,0:T(8,128)} %get-tuple-element.29), kind=kOutput, calls=%fused_computation.12 | convolution fusion | flops 25559040 | bytes 1721984 | tf_op jit(solution)/shard_map/al,flyz->fayz/dot_general | solution.py:396
  39.5 0.0 copy-done.5
  39.5 0.0 copy-done.9
  39.5 0.0 copy-done.10
  39.5 0.0 copy-done.11
  39.5 0.8 %fusion.28.refs_0_ = f32[5,16,16,128]{3,2,1,0:T(8,128)S(1)} fusion(f32[5,16,16,128]{3,2,1,0:T(8,128)S(1)} %copy-done.1, f32[5,16,16,128]{3,2,1,0:T(8,128)S(1)} %copy-done.9, f32[16,26,1,1]{1,0,3,2:T(8,128)S(1)} %copy-done.12, f32[5,16,5,128]{3,2,1,0:T(8,128)S(1)} %copy-done.11, f32[5,16,16,128]{3,2,1,0:T(8,128)S(1)} %copy-done.5, ...), kind=kOutput, calls=%fused_computation.19 | convolution fusion | flops 26746880 | bytes 3819136 | tf_op jit(solution)/shard_map/al,fxlz->fxaz/dot_general | solution.py:396
  40.4 0.0 copy-start.3
  40.4 1.0 %pad_maximum_fusion.refs_1_ = f32[2,5,16,5,128]{4,3,2,1,0:T(8,128)} fusion(f32[1,5,16,5,128]{4,3,2,1,0:T(8,128)S(1)} %get-tuple-element.67, f32[1,5,16,5,128]{4,3,2,1,0:T(8,128)S(1)} %get-tuple-element.66), kind=kLoop, calls=%fused_computation.28 | loop fusion | flops 102400 | bytes 819200 | tf_op jit(solution)/shard_map/stack | solution.py:278
  41.4 13.4 %shard_map.93 = (f32[5,5,16,128]{3,2,1,0:T(8,128)}, f32[5,5,16,128]{3,2,1,0:T(8,128)}, f32[5,16,5,128]{3,2,1,0:T(8,128)}, f32[5,16,5,128]{3,2,1,0:T(8,128)}, f32...) custom-call(f32[5,16,16,128]{3,2,1,0:T(8,128)} %copy-done.3, ...), custom_call_target="tpu_custom_call" | custom-call | tf_op jit(solution)/shard_map/pallas_call | solution.py:167
  54.9 0.0 copy-start.13
  54.9 1.9 %maximum_maximum_fusion = f32[5,26,26,128]{3,2,1,0:T(8,128)S(1)} fusion(f32[5,5,5,128]{3,2,1,0:T(8,128)} %get-tuple-element.40, f32[5,5,16,128]{3,2,1,0:T(8,128)} %get-tuple-element.39, f32[5,5,5,128]{3,2,1,0:T(8,128)} %get-tuple-element.38, f32[5,16,5,128]{3,2,1,0:T(8,128)} %get-tuple-element.37, f32[5,16,16,128]{3,2,1,0:T(8,128)} %copy-done.3, ...), kind=kLoop, calls=%fused_computation | loop fusion | flops 3461120 | bytes 3461120 | tf_op jit(solution)/shard_map/concatenate | solution.py:310
  56.9 2.4 %fusion = f32[5,26,128,16]{2,3,1,0:T(8,128)S(1)} fusion(f32[16,26,1,1]{1,0,3,2:T(8,128)S(1)} %copy-done.13, f32[5,26,26,128]{3,2,1,0:T(8,128)S(1)} %maximum_maximum_fusion), kind=kOutput, calls=%fused_computation.1 | convolution fusion | flops 83066880 | bytes 2797184 | tf_op jit(solution)/shard_map/al,flyz->fayz/dot_general | solution.py:396
  59.3 2.0 %fusion.13.refs_0_ = f32[5,16,16,128]{3,2,1,0:T(8,128)} fusion(f32[16,26,1,1]{1,0,3,2:T(8,128)S(1)} %copy-done.13, f32[5,26,128,16]{2,3,1,0:T(8,128)S(1)} %fusion), kind=kOutput, calls=%fused_computation.14 | convolution fusion | flops 51118080 | bytes 1721984 | tf_op jit(solution)/shard_map/al,fxlz->fxaz/dot_general | solution.py:396
  61.3 8.8 %shard_map.94 = f32[5,16,16,128]{3,2,1,0:T(8,128)} custom-call(f32[5,16,16,128]{3,2,1,0:T(8,128)} %fusion.13.refs_0_, f32[128,128]{1,0:T(8,128)} %constant.35.refs_1_, f32[128,8]{1,0:T(8,128)} %constant.37.refs_2_, f32[128,8]{1,0:T(8,128)} %constant.39.refs_3_), custom_call_target="tpu_custom_call" | custom-call | tf_op jit(solution)/shard_map/pallas_call | solution.py:167
  70.1 2.0 %copy.46 = f32[5,16,16,128]{3,2,1,0:T(8,128)} copy(f32[5,16,16,128]{3,2,1,0:T(8,128)} %shard_map.94) | data formatting | bytes 1310720
  (10 shorter events, 0.2 us)
Async XLA Ops:
  0.0 18.0 %copy-start.12 = (f32[16,26,1,1]{1,0,3,2:T(8,128)S(1)}, f32[16,26,1,1]{1,0,3,2:T(8,128)}, u32[]{:S(2)}) copy-start(f32[16,26,1,1]{1,0,3,2:T(8,128)} %constant.40) | copy-start | bytes 4996
  16.2 1.9 %copy-start.8 = (f32[4,26,16,128]{3,2,1,0:T(8,128)S(1)}, f32[4,26,16,128]{3,2,1,0:T(8,128)}, u32[]{:S(2)}) copy-start(f32[4,26,16,128]{3,2,1,0:T(8,128)} %get-tuple-element.24) | copy-start | bytes 2555908
  16.2 3.0 %copy-start.7 = (f32[4,16,16,128]{3,2,1,0:T(8,128)S(1)}, f32[4,16,16,128]{3,2,1,0:T(8,128)}, u32[]{:S(2)}) copy-start(f32[4,16,16,128]{3,2,1,0:T(8,128)} %get-tuple-element.27) | copy-start | bytes 1572868
  18.1 1.1 %copy-start.1 = (f32[5,16,16,128]{3,2,1,0:T(8,128)S(1)}, f32[5,16,16,128]{3,2,1,0:T(8,128)}, u32[]{:S(2)}) copy-start(f32[5,16,16,128]{3,2,1,0:T(8,128)} %refs_0_.1) | copy-start | bytes 1966084
  18.1 1.5 %copy-start = (f32[3,3,16,16,128]{4,3,2,1,0:T(8,128)S(1)}, f32[3,3,16,16,128]{4,3,2,1,0:T(8,128)}, u32[]{:S(2)}) copy-start(f32[3,3,16,16,128]{4,3,2,1,0:T(8,128)} %param.10) | copy-start | bytes 3538948
  18.1 1.6 %copy-start.2 = (f32[4,16,16,128]{3,2,1,0:T(8,128)S(1)}, f32[4,16,16,128]{3,2,1,0:T(8,128)}, u32[]{:S(2)}) copy-start(f32[4,16,16,128]{3,2,1,0:T(8,128)} %get-tuple-element.23) | copy-start | bytes 1572868
  18.1 1.6 %copy-start.4 = (f32[16,16,128]{2,1,0:T(8,128)S(1)}, f32[16,16,128]{2,1,0:T(8,128)}, u32[]{:S(2)}) copy-start(f32[16,16,128]{2,1,0:T(8,128)} %param.11) | copy-start | bytes 393220
  18.1 1.6 %copy-start.6 = (f32[16,16,128]{2,1,0:T(8,128)S(1)}, f32[16,16,128]{2,1,0:T(8,128)}, u32[]{:S(2)}) copy-start(f32[16,16,128]{2,1,0:T(8,128)} %get-tuple-element.28) | copy-start | bytes 393220
  37.3 2.2 %copy-start.5 = (f32[5,16,16,128]{3,2,1,0:T(8,128)S(1)}, f32[5,16,16,128]{3,2,1,0:T(8,128)}, u32[]{:S(2)}) copy-start(f32[5,16,16,128]{3,2,1,0:T(8,128)} %get-tuple-element.53.refs_2_) | copy-start | bytes 1966084
  37.3 2.2 %copy-start.9 = (f32[5,16,16,128]{3,2,1,0:T(8,128)S(1)}, f32[5,16,16,128]{3,2,1,0:T(8,128)}, u32[]{:S(2)}) copy-start(f32[5,16,16,128]{3,2,1,0:T(8,128)} %get-tuple-element.32) | copy-start | bytes 1966084
  37.3 2.2 %copy-start.10 = (f32[5,16,5,128]{3,2,1,0:T(8,128)S(1)}, f32[5,16,5,128]{3,2,1,0:T(8,128)}, u32[]{:S(2)}) copy-start(f32[5,16,5,128]{3,2,1,0:T(8,128)} %get-tuple-element.30) | copy-start | bytes 614404
  37.3 2.2 %copy-start.11 = (f32[5,16,5,128]{3,2,1,0:T(8,128)S(1)}, f32[5,16,5,128]{3,2,1,0:T(8,128)}, u32[]{:S(2)}) copy-start(f32[5,16,5,128]{3,2,1,0:T(8,128)} %get-tuple-element.31) | copy-start | bytes 614404
  40.4 1.1 %copy-start.3 = (f32[5,16,16,128]{3,2,1,0:T(8,128)}, f32[5,16,16,128]{3,2,1,0:T(8,128)S(1)}, u32[]{:S(2)}) copy-start(f32[5,16,16,128]{3,2,1,0:T(8,128)S(1)} %fusion.28.refs_0_) | copy-start | bytes 1966084
  54.9 2.0 %copy-start.13 = (f32[16,26,1,1]{1,0,3,2:T(8,128)S(1)}, f32[16,26,1,1]{1,0,3,2:T(8,128)}, u32[]{:S(2)}) copy-start(f32[16,26,1,1]{1,0,3,2:T(8,128)} %constant.41) | copy-start | bytes 4996

commit v26 on v25

--- a/solution.py
+++ b/solution.py
@@ -310,6 +310,111 @@
     return jnp.concatenate(sections, axis=1)
 
 
+def filter_kernel(sizes, value_ref, middle_ref, lower_ref, upper_ref, smooth_ref, *refs):
+    faces = refs[:8]
+    turned, before, after, stacked, send_sems, recv_sems = refs[8:]
+    fields, length_x, length_y, depth = value_ref.shape
+    rows = fields * length_x * length_y
+    here = [lax.axis_index(axis) for axis in AXES]
+
+    def device(offset):
+        return tuple(
+            lax.rem(here[slot] + offset[slot] + sizes[slot], sizes[slot]) for slot in range(3)
+        )
+
+    plane = [(1, 0, 0), (-1, 0, 0), (0, 1, 0), (0, -1, 0), (1, 1, 0), (-1, 1, 0), (1, -1, 0), (-1, -1, 0)]
+    partners = plane + [(0, 0, 1), (0, 0, -1)]
+    barrier = pltpu.get_barrier_semaphore()
+    for offset in partners:
+        pl.semaphore_signal(barrier, inc=1, device_id=device(offset), device_id_type=MESH)
+    turned[...] = value_ref[...].reshape(rows, depth).T
+    total = jnp.dot(middle_ref[...], turned[...], precision=lax.Precision.HIGHEST,
+                    preferred_element_type=jnp.float32)
+    pl.semaphore_wait(barrier, len(partners))
+    along_z = [
+        pltpu.make_async_remote_copy(
+            src_ref=turned.at[pl.ds(depth - 8, 8)], dst_ref=before,
+            send_sem=send_sems.at[8], recv_sem=recv_sems.at[8],
+            device_id=device((0, 0, 1)), device_id_type=MESH,
+        ),
+        pltpu.make_async_remote_copy(
+            src_ref=turned.at[pl.ds(0, 8)], dst_ref=after,
+            send_sem=send_sems.at[9], recv_sem=recv_sems.at[9],
+            device_id=device((0, 0, -1)), device_id_type=MESH,
+        ),
+    ]
+    for copy in along_z:
+        copy.start()
+    for copy in along_z:
+        copy.wait()
+    total = total + jnp.dot(lower_ref[...], before[...], precision=lax.Precision.HIGHEST,
+                            preferred_element_type=jnp.float32)
+    total = total + jnp.dot(upper_ref[...], after[...], precision=lax.Precision.HIGHEST,
+                            preferred_element_type=jnp.float32)
+    smooth_ref[...] = total.T.reshape(fields, length_x, length_y, depth)
+    stacked[0] = smooth_ref[:, :, length_y - WIDTH :, :]
+    stacked[1] = smooth_ref[:, :, :WIDTH, :]
+    last_x, first_x = pl.ds(length_x - WIDTH, WIDTH), pl.ds(0, WIDTH)
+    every = slice(None)
+    sources = [
+        smooth_ref.at[every, last_x], smooth_ref.at[every, first_x],
+        stacked.at[0], stacked.at[1],
+        stacked.at[0, every, last_x], stacked.at[0, every, first_x],
+        stacked.at[1, every, last_x], stacked.at[1, every, first_x],
+    ]
+    copies = []
+    for index, offset in enumerate(plane):
+        copies.append(
+            pltpu.make_async_remote_copy(
+                src_ref=sources[index], dst_ref=faces[index],
+                send_sem=send_sems.at[index], recv_sem=recv_sems.at[index],
+                device_id=device(offset), device_id_type=MESH,
+            )
+        )
+        copies[-1].start()
+    for copy in copies:
+        copy.wait()
+
+
+def filter_all(value, smooth, tag):
+    sizes = tuple(lax.axis_size(axis) for axis in AXES)
+    fields, length_x, length_y, depth = value.shape
+    rows = fields * length_x * length_y
+    matrix = smooth[2]
+    padding = jnp.zeros((depth, 8 - WIDTH), matrix.dtype)
+    x_face = jax.ShapeDtypeStruct((fields, WIDTH, length_y, depth), value.dtype)
+    y_face = jax.ShapeDtypeStruct((fields, length_x, WIDTH, depth), value.dtype)
+    edge = jax.ShapeDtypeStruct((fields, WIDTH, WIDTH, depth), value.dtype)
+    outs = pl.pallas_call(
+        functools.partial(filter_kernel, sizes),
+        out_shape=[jax.ShapeDtypeStruct(value.shape, value.dtype)] + [x_face] * 2 + [y_face] * 2 + [edge] * 4,
+        in_specs=[pl.BlockSpec(memory_space=pltpu.VMEM)] * 4,
+        out_specs=[pl.BlockSpec(memory_space=pltpu.VMEM)] + [pl.BlockSpec(memory_space=pl.ANY)] * 8,
+        scratch_shapes=[
+            pltpu.VMEM((depth, rows), jnp.float32),
+            pltpu.VMEM((8, rows), jnp.float32),
+            pltpu.VMEM((8, rows), jnp.float32),
+            pltpu.VMEM((2, fields, length_x, WIDTH, depth), jnp.float32),
+            pltpu.SemaphoreType.DMA((10,)),
+            pltpu.SemaphoreType.DMA((10,)),
+        ],
+        compiler_params=pltpu.CompilerParams(collective_id=tag, has_side_effects=True),
+    )(
+        value,
+        matrix[:, WIDTH : WIDTH + depth],
+        jnp.concatenate([padding, matrix[:, :WIDTH]], axis=1),
+        jnp.concatenate([matrix[:, WIDTH + depth :], padding], axis=1),
+    )
+    smoothed, x_before, x_after, y_before, y_after, both_before, x_after_y_before, x_before_y_after, both_after = outs
+    sections = [
+        jnp.concatenate([both_before, x_before, x_before_y_after], axis=2),
+        jnp.concatenate([y_before, smoothed, y_after], axis=2),
+        jnp.concatenate([x_after_y_before, x_after, both_after], axis=2),
+    ]
+    result = sweep_lines(jnp.concatenate(sections, axis=1), smooth[0], 1)
+    return sweep_lines(result, smooth[1], 2)
+
+
 def sweep_zeta(value, matrix, tag):
     return exchange([], [], [], tag, (value, matrix), precision=lax.Precision.HIGHEST)[-1]
 
@@ -485,10 +590,7 @@
     divergence = divergence + sweep_lines(padded[1], derive[1], 2, lax.Precision.HIGH)
     divergence = divergence + padded[2]
     sectioned = conserved_solution - step_duration * jacobian * divergence
-    result = sweep_lines(exchange_plane(sectioned, 2), smooth[0], 1)
-    result = sweep_lines(result, smooth[1], 2)
-    result = sweep_zeta(result, smooth[2], 4)
-    return result
+    return filter_all(sectioned, smooth, 2)
 
 
 def solution(mesh):

time: 72.8 us -> 70.8 us (0.973)
  local copies, waits for them, and re-layouts: 3.11 us -> 1.07 us
  other arithmetic: 5.66 us -> 4.66 us
  matrix products: 9.85 us -> 10.7 us
    pallas_call x0 -> x1, Pallas kernels: none -> 22.9 us  [filter_all(): pl.pallas_call(functools.partial(filter_kernel, sizes), out_shape=[jax.Sh...]
    pallas_call x4 -> x2, Pallas kernels: 53.1 us -> 30.9 us  [exchange(): pl.pallas_call(functools.partial(exchange_kernel, tuple(routes), sizes, l...]
    unnamed x30 -> x27, local copies, waits for them, and re-layouts: 2.82 us -> 0.83 us
    another operation x1 -> x0, other arithmetic: 1.01 us -> none  [exchange_plane(): jnp.stack([lax.slice_in_dim(value, length_y - WIDTH, length_y, axis=2), l...]
    dot_general x6, matrix products: 9.85 us -> 10.7 us  [sweep_lines(): return jnp.einsum(line_forms[dim], matrix, padded, precision=precision)]
where the time goes in v26:
time: 70.8 us; the launch traced here: 70.5 us
  Pallas kernels  53.8 us (76%)
  matrix products  10.7 us (15%)
  other arithmetic  4.66 us (7%)
  local copies, waits for them, and re-layouts  1.07 us (2%)
    pallas_call x2, Pallas kernels, exchange(): pl.pallas_call(functools.partial(exchange_kernel, tuple(routes), sizes, l...  30.9 us
    pallas_call x1, Pallas kernels, filter_all(): pl.pallas_call(functools.partial(filter_kernel, sizes), out_shape=[jax.Sh...  22.9 us
    dot_general x6, matrix products, sweep_lines(): return jnp.einsum(line_forms[dim], matrix, padded, precision=precision)  10.7 us
    concatenate x1, other arithmetic, filter_all(): result = sweep_lines(jnp.concatenate(sections, axis=1), smooth[0], 1)  1.95 us
    add x1, other arithmetic, fluxes(): metrics[direction, 0] * totals[0] + metrics[direction, 1] * totals[1]  1.45 us

profile of v26, /device:TPU:1, one launch (start us, length us, event | category | flops | bytes accessed | tf_op | source)
XLA Modules:
  0.0 70.5 jit_solution(9225320474356879765)
XLA Ops:
  0.0 0.0 copy-start.11
  0.0 16.2 %shard_map.91 = (f32[4,26,16,128]{3,2,1,0:T(8,128)}, f32[4,16,5,128]{3,2,1,0:T(8,128)}, f32[4,16,5,128]{3,2,1,0:T(8,128)}, f32[4,16,16,128]{3,2,1,0:T(8,128)}, f...) custom-call(f32[5,16,16,128]{3,2,1,0:T(8,128)} %refs_0_.1, f32[128,128]{1,0:T(8,128)} %constant.30.refs_1_.refs_4_, ...), custom_call_target="tpu_custom_call" | custom-call | tf_op jit(solution)/shard_map/pallas_call | solution.py:167
  16.2 0.0 copy-start.7
  16.2 0.0 copy-start.6
  16.2 1.8 %convolution_bitcast_fusion = f32[4,16,16,128]{3,2,1,0:T(8,128)S(1)} fusion(f32[16,26,1,1]{1,0,3,2:T(8,128)} %constant.40, f32[4,16,5,128]{3,2,1,0:T(8,128)} %get-tuple-element.27, f32[4,16,16,128]{3,2,1,0:T(8,128)} %get-tuple-element.24, f32[4,16,5,128]{3,2,1,0:T(8,128)} %get-tuple-element.26), kind=kOutput, calls=%fused_computation.20 | convolution fusion | flops 20873216 | bytes 1377920 | tf_op jit(solution)/shard_map/al,fxlz->fxaz/dot_general | solution.py:501
  18.0 0.0 copy-done.11
  18.0 0.0 copy-done.7
  18.0 0.0 copy-start.1
  18.1 0.0 copy-start
  18.1 0.0 copy-start.2
  18.1 0.0 copy-start.3
  18.1 0.0 copy-start.5
  18.1 0.6 fusion.36
  18.7 0.2 copy.32
  18.9 0.2 copy-done.1
  19.2 0.0 copy-done.6
  19.2 0.4 copy-done
  19.5 0.1 copy-done.2
  19.6 0.0 copy-done.3
  19.7 0.0 copy-done.5
  19.7 0.2 bitcast_dynamic-update-slice_fusion.11
  19.9 0.1 bitcast_dynamic-update-slice_fusion.10
  20.0 0.1 bitcast_dynamic-update-slice_fusion.9
  20.2 0.2 bitcast_dynamic-update-slice_fusion.8
  20.4 0.1 bitcast_dynamic-update-slice_fusion.6
  20.5 0.1 bitcast_dynamic-update-slice_fusion.5
  20.6 0.1 bitcast_dynamic-update-slice_fusion.4
  20.8 0.1 bitcast_dynamic-update-slice_fusion
  21.0 0.1 slice_bitcast_fusion.14
  21.1 1.5 %multiply_add_fusion = (f32[5,16,16,128]{3,2,1,0:T(8,128)}, f32[5,16,16,128]{3,2,1,0:T(8,128)}, f32[5,16,16,128]{3,2,1,0:T(8,128)}) fusion(f32[5,16,16,128]{3,2,1,0:T(8,128)S(1)} %bitcast_dynamic-update-slice_fusion, f32[5,16,16,128]{3,2,1,0:T(8,128)S(1)} %bitcast_dynamic-update-slice_fusion.4, f32[5,16,16,128]{3,2,1,0:T(8,128)S(1)} %get-tuple-element.68, ...), kind=kLoop, calls=%fused_computation.28 | loop fusion | flops 2457600 | bytes 5111808 | tf_op jit(solution)/shard_map/add | solution.py:565
  22.5 14.8 %shard_map.92 = (f32[5,26,16,128]{3,2,1,0:T(8,128)}, f32[5,16,5,128]{3,2,1,0:T(8,128)}, f32[5,16,5,128]{3,2,1,0:T(8,128)}, f32[5,16,16,128]{3,2,1,0:T(8,128)}) custom-call(f32[5,16,16,128]{3,2,1,0:T(8,128)} %get-tuple-element.56.refs_0_.refs_1_, f32[5,16,16,128]{3,2,1,0:T(8,128)} %get-tuple-element.56.refs_0_.refs_1_, ...), custom_call_target="tpu_custom_call" | custom-call | tf_op jit(solution)/shard_map/pallas_call | solution.py:167
  37.3 0.0 copy-start.4
  37.3 0.0 copy-start.8
  37.3 0.0 copy-start.9
  37.3 0.0 copy-start.10
  37.3 2.1 %fusion.11 = f32[5,16,128,16]{2,3,1,0:T(8,128)S(1)} fusion(f32[16,26,1,1]{1,0,3,2:T(8,128)S(1)} %copy-done.11, f32[5,26,16,128]{3,2,1,0:T(8,128)} %get-tuple-element.30), kind=kOutput, calls=%fused_computation.12 | convolution fusion | flops 25559040 | bytes 1721984 | tf_op jit(solution)/shard_map/al,flyz->fayz/dot_general | solution.py:501
  39.5 0.0 copy-done.4
  39.5 0.0 copy-done.8
  39.5 0.0 copy-done.9
  39.5 0.0 copy-done.10
  39.5 1.7 %fusion.28.value_ref = f32[5,16,16,128]{3,2,1,0:T(8,128)} fusion(f32[5,16,16,128]{3,2,1,0:T(8,128)S(1)} %copy-done.1, f32[5,16,16,128]{3,2,1,0:T(8,128)S(1)} %copy-done.8, f32[16,26,1,1]{1,0,3,2:T(8,128)S(1)} %copy-done.11, f32[5,16,5,128]{3,2,1,0:T(8,128)S(1)} %copy-done.10, f32[5,16,16,128]{3,2,1,0:T(8,128)S(1)} %copy-done.4, ...), kind=kOutput, calls=%fused_computation.19 | convolution fusion | flops 26746880 | bytes 3819136 | tf_op jit(solution)/shard_map/al,fxlz->fxaz/dot_general | solution.py:501
  41.2 22.9 %shard_map.93 = (f32[5,16,16,128]{3,2,1,0:T(8,128)}, f32[5,5,16,128]{3,2,1,0:T(8,128)}, f32[5,5,16,128]{3,2,1,0:T(8,128)}, f32[5,16,5,128]{3,2,1,0:T(8,128)}, f3...) custom-call(f32[5,16,16,128]{3,2,1,0:T(8,128)} %fusion.28.value_ref,, ...), custom_call_target="tpu_custom_call" | custom-call | tf_op jit(solution)/shard_map/pallas_call | solution.py:388
  64.1 0.0 copy-start.12
  64.1 1.9 %maximum_maximum_fusion = f32[5,26,26,128]{3,2,1,0:T(8,128)S(1)} fusion(f32[5,5,5,128]{3,2,1,0:T(8,128)} %get-tuple-element.42, f32[5,5,16,128]{3,2,1,0:T(8,128)} %get-tuple-element.41, f32[5,5,5,128]{3,2,1,0:T(8,128)} %get-tuple-element.40, f32[5,16,5,128]{3,2,1,0:T(8,128)} %get-tuple-element.39, f32[5,16,16,128]{3,2,1,0:T(8,128)} %get-tuple-element.38, ...), kind=kLoop, calls=%fused_computation | loop fusion | flops 3461120 | bytes 3461120 | tf_op jit(solution)/shard_map/concatenate | solution.py:414
  66.1 0.0 copy-done.12
  66.1 2.4 %fusion = f32[5,26,128,16]{2,3,1,0:T(8,128)S(1)} fusion(f32[16,26,1,1]{1,0,3,2:T(8,128)S(1)} %copy-done.12, f32[5,26,26,128]{3,2,1,0:T(8,128)S(1)} %maximum_maximum_fusion), kind=kOutput, calls=%fused_computation.1 | convolution fusion | flops 83066880 | bytes 2797184 | tf_op jit(solution)/shard_map/al,flyz->fayz/dot_general | solution.py:501
  68.5 2.0 %fusion.13 = f32[5,16,16,128]{3,2,1,0:T(8,128)} fusion(f32[16,26,1,1]{1,0,3,2:T(8,128)S(1)} %copy-done.12, f32[5,26,128,16]{2,3,1,0:T(8,128)S(1)} %fusion), kind=kOutput, calls=%fused_computation.14 | convolution fusion | flops 51118080 | bytes 1721984 | tf_op jit(solution)/shard_map/al,fxlz->fxaz/dot_general | solution.py:501
  (5 shorter events, 0.1 us)
Async XLA Ops:
  0.0 18.0 %copy-start.11 = (f32[16,26,1,1]{1,0,3,2:T(8,128)S(1)}, f32[16,26,1,1]{1,0,3,2:T(8,128)}, u32[]{:S(2)}) copy-start(f32[16,26,1,1]{1,0,3,2:T(8,128)} %constant.40) | copy-start | bytes 4996
  16.2 1.9 %copy-start.7 = (f32[4,26,16,128]{3,2,1,0:T(8,128)S(1)}, f32[4,26,16,128]{3,2,1,0:T(8,128)}, u32[]{:S(2)}) copy-start(f32[4,26,16,128]{3,2,1,0:T(8,128)} %get-tuple-element.25) | copy-start | bytes 2555908
  16.2 3.0 %copy-start.6 = (f32[4,16,16,128]{3,2,1,0:T(8,128)S(1)}, f32[4,16,16,128]{3,2,1,0:T(8,128)}, u32[]{:S(2)}) copy-start(f32[4,16,16,128]{3,2,1,0:T(8,128)} %get-tuple-element.28) | copy-start | bytes 1572868
  18.0 1.1 %copy-start.1 = (f32[5,16,16,128]{3,2,1,0:T(8,128)S(1)}, f32[5,16,16,128]{3,2,1,0:T(8,128)}, u32[]{:S(2)}) copy-start(f32[5,16,16,128]{3,2,1,0:T(8,128)} %refs_0_.1) | copy-start | bytes 1966084
  18.1 1.5 %copy-start = (f32[3,3,16,16,128]{4,3,2,1,0:T(8,128)S(1)}, f32[3,3,16,16,128]{4,3,2,1,0:T(8,128)}, u32[]{:S(2)}) copy-start(f32[3,3,16,16,128]{4,3,2,1,0:T(8,128)} %param.10) | copy-start | bytes 3538948
  18.1 1.6 %copy-start.2 = (f32[4,16,16,128]{3,2,1,0:T(8,128)S(1)}, f32[4,16,16,128]{3,2,1,0:T(8,128)}, u32[]{:S(2)}) copy-start(f32[4,16,16,128]{3,2,1,0:T(8,128)} %get-tuple-element.24) | copy-start | bytes 1572868
  18.1 1.6 %copy-start.3 = (f32[16,16,128]{2,1,0:T(8,128)S(1)}, f32[16,16,128]{2,1,0:T(8,128)}, u32[]{:S(2)}) copy-start(f32[16,16,128]{2,1,0:T(8,128)} %param.11) | copy-start | bytes 393220
  18.1 1.6 %copy-start.5 = (f32[16,16,128]{2,1,0:T(8,128)S(1)}, f32[16,16,128]{2,1,0:T(8,128)}, u32[]{:S(2)}) copy-start(f32[16,16,128]{2,1,0:T(8,128)} %get-tuple-element.29) | copy-start | bytes 393220
  37.3 2.2 %copy-start.4 = (f32[5,16,16,128]{3,2,1,0:T(8,128)S(1)}, f32[5,16,16,128]{3,2,1,0:T(8,128)}, u32[]{:S(2)}) copy-start(f32[5,16,16,128]{3,2,1,0:T(8,128)} %get-tuple-element.55.refs_2_) | copy-start | bytes 1966084
  37.3 2.2 %copy-start.8 = (f32[5,16,16,128]{3,2,1,0:T(8,128)S(1)}, f32[5,16,16,128]{3,2,1,0:T(8,128)}, u32[]{:S(2)}) copy-start(f32[5,16,16,128]{3,2,1,0:T(8,128)} %get-tuple-element.33) | copy-start | bytes 1966084
  37.3 2.2 %copy-start.9 = (f32[5,16,5,128]{3,2,1,0:T(8,128)S(1)}, f32[5,16,5,128]{3,2,1,0:T(8,128)}, u32[]{:S(2)}) copy-start(f32[5,16,5,128]{3,2,1,0:T(8,128)} %get-tuple-element.31) | copy-start | bytes 614404
  37.3 2.2 %copy-start.10 = (f32[5,16,5,128]{3,2,1,0:T(8,128)S(1)}, f32[5,16,5,128]{3,2,1,0:T(8,128)}, u32[]{:S(2)}) copy-start(f32[5,16,5,128]{3,2,1,0:T(8,128)} %get-tuple-element.32) | copy-start | bytes 614404
  64.1 2.0 %copy-start.12 = (f32[16,26,1,1]{1,0,3,2:T(8,128)S(1)}, f32[16,26,1,1]{1,0,3,2:T(8,128)}, u32[]{:S(2)}) copy-start(f32[16,26,1,1]{1,0,3,2:T(8,128)} %constant.41) | copy-start | bytes 4996

commit v27 on v26

--- a/solution.py
+++ b/solution.py
@@ -78,8 +78,9 @@
         fields, length_x, length_y, depth = block_ref.shape
         rows = fields * length_x * length_y
         turned[...] = block_ref[...].reshape(rows, depth).T
-        total = jnp.dot(middle_ref[...], turned[...], precision=precision,
-                        preferred_element_type=jnp.float32)
+        if not prepare:
+            total = jnp.dot(middle_ref[...], turned[...], precision=precision,
+                            preferred_element_type=jnp.float32)
     local = []
     for index, (source, source_at, target, target_at) in enumerate(moves):
         local.append(
@@ -117,6 +118,9 @@
             )
     for copy in copies:
         copy.start()
+    if zeta and prepare:
+        total = jnp.dot(middle_ref[...], turned[...], precision=precision,
+                        preferred_element_type=jnp.float32)
     for copy in copies + local:
         copy.wait()
     if zeta:
@@ -352,8 +356,6 @@
     total = total + jnp.dot(upper_ref[...], after[...], precision=lax.Precision.HIGHEST,
                             preferred_element_type=jnp.float32)
     smooth_ref[...] = total.T.reshape(fields, length_x, length_y, depth)
-    stacked[0] = smooth_ref[:, :, length_y - WIDTH :, :]
-    stacked[1] = smooth_ref[:, :, :WIDTH, :]
     last_x, first_x = pl.ds(length_x - WIDTH, WIDTH), pl.ds(0, WIDTH)
     every = slice(None)
     sources = [
@@ -364,6 +366,9 @@
     ]
     copies = []
     for index, offset in enumerate(plane):
+        if index == 2:
+            stacked[0] = smooth_ref[:, :, length_y - WIDTH :, :]
+            stacked[1] = smooth_ref[:, :, :WIDTH, :]
         copies.append(
             pltpu.make_async_remote_copy(
                 src_ref=sources[index], dst_ref=faces[index],

time: 70.8 us -> 70.8 us (level)
  no operation moved by 1% of the time
where the time goes in v27:
time: 70.8 us; the launch traced here: 70.5 us
  Pallas kernels  53.8 us (76%)
  matrix products  10.7 us (15%)
  other arithmetic  4.66 us (7%)
  local copies, waits for them, and re-layouts  1.07 us (2%)
    pallas_call x2, Pallas kernels, exchange(): pl.pallas_call(functools.partial(exchange_kernel, tuple(routes), sizes, l...  30.9 us
    pallas_call x1, Pallas kernels, filter_all(): pl.pallas_call(functools.partial(filter_kernel, sizes), out_shape=[jax.Sh...  22.8 us
    dot_general x6, matrix products, sweep_lines(): return jnp.einsum(line_forms[dim], matrix, padded, precision=precision)  10.7 us
    concatenate x1, other arithmetic, filter_all(): result = sweep_lines(jnp.concatenate(sections, axis=1), smooth[0], 1)  1.95 us
    add x1, other arithmetic, fluxes(): metrics[direction, 0] * totals[0] + metrics[direction, 1] * totals[1]  1.45 us

profile of v27, /device:TPU:1, one launch (start us, length us, event | category | flops | bytes accessed | tf_op | source)
XLA Modules:
  0.0 70.5 jit_solution(14581001561934352327)
XLA Ops:
  0.0 0.0 copy-start.11
  0.0 16.2 %shard_map.91 = (f32[4,26,16,128]{3,2,1,0:T(8,128)}, f32[4,16,5,128]{3,2,1,0:T(8,128)}, f32[4,16,5,128]{3,2,1,0:T(8,128)}, f32[4,16,16,128]{3,2,1,0:T(8,128)}, f...) custom-call(f32[5,16,16,128]{3,2,1,0:T(8,128)} %refs_0_.1, f32[128,128]{1,0:T(8,128)} %constant.30.refs_1_.refs_4_, ...), custom_call_target="tpu_custom_call" | custom-call | tf_op jit(solution)/shard_map/pallas_call | solution.py:171
  16.2 0.0 copy-start.7
  16.2 0.0 copy-start.6
  16.2 1.8 %convolution_bitcast_fusion = f32[4,16,16,128]{3,2,1,0:T(8,128)S(1)} fusion(f32[16,26,1,1]{1,0,3,2:T(8,128)} %constant.40, f32[4,16,5,128]{3,2,1,0:T(8,128)} %get-tuple-element.27, f32[4,16,16,128]{3,2,1,0:T(8,128)} %get-tuple-element.24, f32[4,16,5,128]{3,2,1,0:T(8,128)} %get-tuple-element.26), kind=kOutput, calls=%fused_computation.20 | convolution fusion | flops 20873216 | bytes 1377920 | tf_op jit(solution)/shard_map/al,fxlz->fxaz/dot_general | solution.py:506
  18.0 0.0 copy-done.11
  18.0 0.0 copy-done.7
  18.0 0.0 copy-start.1
  18.1 0.0 copy-start
  18.1 0.0 copy-start.2
  18.1 0.0 copy-start.3
  18.1 0.0 copy-start.5
  18.1 0.6 fusion.36
  18.7 0.2 copy.32
  18.9 0.2 copy-done.1
  19.2 0.0 copy-done.6
  19.2 0.4 copy-done
  19.5 0.1 copy-done.2
  19.6 0.0 copy-done.3
  19.7 0.0 copy-done.5
  19.7 0.2 bitcast_dynamic-update-slice_fusion.11
  19.9 0.1 bitcast_dynamic-update-slice_fusion.10
  20.0 0.1 bitcast_dynamic-update-slice_fusion.9
  20.2 0.2 bitcast_dynamic-update-slice_fusion.8
  20.4 0.1 bitcast_dynamic-update-slice_fusion.6
  20.5 0.1 bitcast_dynamic-update-slice_fusion.5
  20.6 0.1 bitcast_dynamic-update-slice_fusion.4
  20.8 0.1 bitcast_dynamic-update-slice_fusion
  21.0 0.1 slice_bitcast_fusion.14
  21.1 1.5 %multiply_add_fusion = (f32[5,16,16,128]{3,2,1,0:T(8,128)}, f32[5,16,16,128]{3,2,1,0:T(8,128)}, f32[5,16,16,128]{3,2,1,0:T(8,128)}) fusion(f32[5,16,16,128]{3,2,1,0:T(8,128)S(1)} %bitcast_dynamic-update-slice_fusion, f32[5,16,16,128]{3,2,1,0:T(8,128)S(1)} %bitcast_dynamic-update-slice_fusion.4, f32[5,16,16,128]{3,2,1,0:T(8,128)S(1)} %get-tuple-element.68, ...), kind=kLoop, calls=%fused_computation.28 | loop fusion | flops 2457600 | bytes 5111808 | tf_op jit(solution)/shard_map/add | solution.py:570
  22.5 14.8 %shard_map.92 = (f32[5,26,16,128]{3,2,1,0:T(8,128)}, f32[5,16,5,128]{3,2,1,0:T(8,128)}, f32[5,16,5,128]{3,2,1,0:T(8,128)}, f32[5,16,16,128]{3,2,1,0:T(8,128)}) custom-call(f32[5,16,16,128]{3,2,1,0:T(8,128)} %get-tuple-element.56.refs_0_.refs_1_, f32[5,16,16,128]{3,2,1,0:T(8,128)} %get-tuple-element.56.refs_0_.refs_1_, ...), custom_call_target="tpu_custom_call" | custom-call | tf_op jit(solution)/shard_map/pallas_call | solution.py:171
  37.3 0.0 copy-start.4
  37.3 0.0 copy-start.8
  37.3 0.0 copy-start.9
  37.3 0.0 copy-start.10
  37.3 2.1 %fusion.11 = f32[5,16,128,16]{2,3,1,0:T(8,128)S(1)} fusion(f32[16,26,1,1]{1,0,3,2:T(8,128)S(1)} %copy-done.11, f32[5,26,16,128]{3,2,1,0:T(8,128)} %get-tuple-element.30), kind=kOutput, calls=%fused_computation.12 | convolution fusion | flops 25559040 | bytes 1721984 | tf_op jit(solution)/shard_map/al,flyz->fayz/dot_general | solution.py:506
  39.5 0.0 copy-done.4
  39.5 0.0 copy-done.8
  39.5 0.0 copy-done.9
  39.5 0.0 copy-done.10
  39.5 1.7 %fusion.28.value_ref = f32[5,16,16,128]{3,2,1,0:T(8,128)} fusion(f32[5,16,16,128]{3,2,1,0:T(8,128)S(1)} %copy-done.1, f32[5,16,16,128]{3,2,1,0:T(8,128)S(1)} %copy-done.8, f32[16,26,1,1]{1,0,3,2:T(8,128)S(1)} %copy-done.11, f32[5,16,5,128]{3,2,1,0:T(8,128)S(1)} %copy-done.10, f32[5,16,16,128]{3,2,1,0:T(8,128)S(1)} %copy-done.4, ...), kind=kOutput, calls=%fused_computation.19 | convolution fusion | flops 26746880 | bytes 3819136 | tf_op jit(solution)/shard_map/al,fxlz->fxaz/dot_general | solution.py:506
  41.2 22.8 %shard_map.93 = (f32[5,16,16,128]{3,2,1,0:T(8,128)}, f32[5,5,16,128]{3,2,1,0:T(8,128)}, f32[5,5,16,128]{3,2,1,0:T(8,128)}, f32[5,16,5,128]{3,2,1,0:T(8,128)}, f3...) custom-call(f32[5,16,16,128]{3,2,1,0:T(8,128)} %fusion.28.value_ref,, ...), custom_call_target="tpu_custom_call" | custom-call | tf_op jit(solution)/shard_map/pallas_call | solution.py:393
  64.0 0.0 copy-start.12
  64.1 1.9 %maximum_maximum_fusion = f32[5,26,26,128]{3,2,1,0:T(8,128)S(1)} fusion(f32[5,5,5,128]{3,2,1,0:T(8,128)} %get-tuple-element.42, f32[5,5,16,128]{3,2,1,0:T(8,128)} %get-tuple-element.41, f32[5,5,5,128]{3,2,1,0:T(8,128)} %get-tuple-element.40, f32[5,16,5,128]{3,2,1,0:T(8,128)} %get-tuple-element.39, f32[5,16,16,128]{3,2,1,0:T(8,128)} %get-tuple-element.38, ...), kind=kLoop, calls=%fused_computation | loop fusion | flops 3461120 | bytes 3461120 | tf_op jit(solution)/shard_map/concatenate | solution.py:419
  66.0 0.0 copy-done.12
  66.0 2.4 %fusion = f32[5,26,128,16]{2,3,1,0:T(8,128)S(1)} fusion(f32[16,26,1,1]{1,0,3,2:T(8,128)S(1)} %copy-done.12, f32[5,26,26,128]{3,2,1,0:T(8,128)S(1)} %maximum_maximum_fusion), kind=kOutput, calls=%fused_computation.1 | convolution fusion | flops 83066880 | bytes 2797184 | tf_op jit(solution)/shard_map/al,flyz->fayz/dot_general | solution.py:506
  68.4 2.0 %fusion.13 = f32[5,16,16,128]{3,2,1,0:T(8,128)} fusion(f32[16,26,1,1]{1,0,3,2:T(8,128)S(1)} %copy-done.12, f32[5,26,128,16]{2,3,1,0:T(8,128)S(1)} %fusion), kind=kOutput, calls=%fused_computation.14 | convolution fusion | flops 51118080 | bytes 1721984 | tf_op jit(solution)/shard_map/al,fxlz->fxaz/dot_general | solution.py:506
  (5 shorter events, 0.1 us)
Async XLA Ops:
  0.0 18.0 %copy-start.11 = (f32[16,26,1,1]{1,0,3,2:T(8,128)S(1)}, f32[16,26,1,1]{1,0,3,2:T(8,128)}, u32[]{:S(2)}) copy-start(f32[16,26,1,1]{1,0,3,2:T(8,128)} %constant.40) | copy-start | bytes 4996
  16.2 1.9 %copy-start.7 = (f32[4,26,16,128]{3,2,1,0:T(8,128)S(1)}, f32[4,26,16,128]{3,2,1,0:T(8,128)}, u32[]{:S(2)}) copy-start(f32[4,26,16,128]{3,2,1,0:T(8,128)} %get-tuple-element.25) | copy-start | bytes 2555908
  16.2 3.0 %copy-start.6 = (f32[4,16,16,128]{3,2,1,0:T(8,128)S(1)}, f32[4,16,16,128]{3,2,1,0:T(8,128)}, u32[]{:S(2)}) copy-start(f32[4,16,16,128]{3,2,1,0:T(8,128)} %get-tuple-element.28) | copy-start | bytes 1572868
  18.0 1.1 %copy-start.1 = (f32[5,16,16,128]{3,2,1,0:T(8,128)S(1)}, f32[5,16,16,128]{3,2,1,0:T(8,128)}, u32[]{:S(2)}) copy-start(f32[5,16,16,128]{3,2,1,0:T(8,128)} %refs_0_.1) | copy-start | bytes 1966084
  18.1 1.5 %copy-start = (f32[3,3,16,16,128]{4,3,2,1,0:T(8,128)S(1)}, f32[3,3,16,16,128]{4,3,2,1,0:T(8,128)}, u32[]{:S(2)}) copy-start(f32[3,3,16,16,128]{4,3,2,1,0:T(8,128)} %param.10) | copy-start | bytes 3538948
  18.1 1.6 %copy-start.2 = (f32[4,16,16,128]{3,2,1,0:T(8,128)S(1)}, f32[4,16,16,128]{3,2,1,0:T(8,128)}, u32[]{:S(2)}) copy-start(f32[4,16,16,128]{3,2,1,0:T(8,128)} %get-tuple-element.24) | copy-start | bytes 1572868
  18.1 1.6 %copy-start.3 = (f32[16,16,128]{2,1,0:T(8,128)S(1)}, f32[16,16,128]{2,1,0:T(8,128)}, u32[]{:S(2)}) copy-start(f32[16,16,128]{2,1,0:T(8,128)} %param.11) | copy-start | bytes 393220
  18.1 1.6 %copy-start.5 = (f32[16,16,128]{2,1,0:T(8,128)S(1)}, f32[16,16,128]{2,1,0:T(8,128)}, u32[]{:S(2)}) copy-start(f32[16,16,128]{2,1,0:T(8,128)} %get-tuple-element.29) | copy-start | bytes 393220
  37.3 2.2 %copy-start.4 = (f32[5,16,16,128]{3,2,1,0:T(8,128)S(1)}, f32[5,16,16,128]{3,2,1,0:T(8,128)}, u32[]{:S(2)}) copy-start(f32[5,16,16,128]{3,2,1,0:T(8,128)} %get-tuple-element.55.refs_2_) | copy-start | bytes 1966084
  37.3 2.2 %copy-start.8 = (f32[5,16,16,128]{3,2,1,0:T(8,128)S(1)}, f32[5,16,16,128]{3,2,1,0:T(8,128)}, u32[]{:S(2)}) copy-start(f32[5,16,16,128]{3,2,1,0:T(8,128)} %get-tuple-element.33) | copy-start | bytes 1966084
  37.3 2.2 %copy-start.9 = (f32[5,16,5,128]{3,2,1,0:T(8,128)S(1)}, f32[5,16,5,128]{3,2,1,0:T(8,128)}, u32[]{:S(2)}) copy-start(f32[5,16,5,128]{3,2,1,0:T(8,128)} %get-tuple-element.31) | copy-start | bytes 614404
  37.3 2.2 %copy-start.10 = (f32[5,16,5,128]{3,2,1,0:T(8,128)S(1)}, f32[5,16,5,128]{3,2,1,0:T(8,128)}, u32[]{:S(2)}) copy-start(f32[5,16,5,128]{3,2,1,0:T(8,128)} %get-tuple-element.32) | copy-start | bytes 614404
  64.0 2.0 %copy-start.12 = (f32[16,26,1,1]{1,0,3,2:T(8,128)S(1)}, f32[16,26,1,1]{1,0,3,2:T(8,128)}, u32[]{:S(2)}) copy-start(f32[16,26,1,1]{1,0,3,2:T(8,128)} %constant.41) | copy-start | bytes 4996

commit v28 on v27

--- a/solution.py
+++ b/solution.py
@@ -220,16 +220,14 @@
             routes.append((offset_along(axis, 1), source, last, target, whole))
             routes.append((offset_along(axis, -1), source, first, target + 1, whole))
         else:
-            arrays += [(value, pl.ANY), (value, pltpu.VMEM)]
-            extended = value.shape[:dim] + (length + 2 * WIDTH,) + value.shape[dim + 1 :]
-            out_shapes.append(jax.ShapeDtypeStruct(extended, value.dtype))
-            source, target = len(arrays) - 2, len(out_shapes) - 1
+            arrays.append((value, pl.ANY))
+            face = value.shape[:dim] + (WIDTH,) + value.shape[dim + 1 :]
+            out_shapes += [jax.ShapeDtypeStruct(face, value.dtype)] * 2
+            source, target = len(arrays) - 1, len(out_shapes) - 2
+            whole = window(ndim, dim, None, None)
             last, first = window(ndim, dim, length - WIDTH, length), window(ndim, dim, 0, WIDTH)
-            ahead = window(ndim, dim, length + WIDTH, length + 2 * WIDTH)
-            routes.append((offset_along(axis, 1), source, last, target, first))
-            routes.append((offset_along(axis, -1), source, first, target, ahead))
-            moves.append((source + 1, window(ndim, dim, None, None), target,
-                          window(ndim, dim, WIDTH, length + WIDTH)))
+            routes.append((offset_along(axis, 1), source, last, target, whole))
+            routes.append((offset_along(axis, -1), source, first, target + 1, whole))
     received = exchange(arrays, routes, out_shapes, tag, zeta, moves=moves)
     padded, place = [], 0
     for value, axis, dim in items:
@@ -238,13 +236,9 @@
             both = jnp.moveaxis(both, 2, dim + 1)
             before, after = both[0], both[1]
             place += 1
-        elif dim == value.ndim - 2:
+        else:
             before, after = received[place], received[place + 1]
             place += 2
-        else:
-            padded.append(received[place])
-            place += 1
-            continue
         padded.append(jnp.concatenate([before, value, after], axis=dim))
     if zeta is not None:
         padded.append(received[-1])

time: 70.8 us -> 71.1 us (level)
  matrix products: 10.7 us -> 9.38 us
  other arithmetic: 4.66 us -> 5.77 us
    dot_general x6, matrix products: 10.7 us -> 9.38 us  [sweep_lines(): return jnp.einsum(line_forms[dim], matrix, padded, precision=precision)]
    concatenate x0 -> x1, other arithmetic: none -> 1.11 us  [exchange_faces(): padded.append(jnp.concatenate([before, value, after], axis=dim))]
    unnamed x27 -> x29, local copies, waits for them, and re-layouts: 0.83 us -> 1.47 us
where the time goes in v28:
time: 71.1 us; the launch traced here: 70.8 us
  Pallas kernels  53.6 us (75%)
  matrix products  9.38 us (13%)
  other arithmetic  5.77 us (8%)
  local copies, waits for them, and re-layouts  1.71 us (2%)
    pallas_call x2, Pallas kernels, exchange(): pl.pallas_call(functools.partial(exchange_kernel, tuple(routes), sizes, l...  30.8 us
    pallas_call x1, Pallas kernels, filter_all(): pl.pallas_call(functools.partial(filter_kernel, sizes), out_shape=[jax.Sh...  22.8 us
    dot_general x6, matrix products, sweep_lines(): return jnp.einsum(line_forms[dim], matrix, padded, precision=precision)  9.38 us
    concatenate x1, other arithmetic, filter_all(): result = sweep_lines(jnp.concatenate(sections, axis=1), smooth[0], 1)  1.95 us
    unnamed x29, local copies, waits for them, and re-layouts  1.47 us
    add x1, other arithmetic, fluxes(): metrics[direction, 0] * totals[0] + metrics[direction, 1] * totals[1]  1.45 us

profile of v28, /device:TPU:1, one launch (start us, length us, event | category | flops | bytes accessed | tf_op | source)
XLA Modules:
  0.0 70.8 jit_solution(13516987228114083367)
XLA Ops:
  0.0 16.2 %shard_map.91 = (f32[4,26,16,128]{3,2,1,0:T(8,128)}, f32[4,16,5,128]{3,2,1,0:T(8,128)}, f32[4,16,5,128]{3,2,1,0:T(8,128)}, f32[4,16,16,128]{3,2,1,0:T(8,128)}, f...) custom-call(f32[5,16,16,128]{3,2,1,0:T(8,128)} %refs_0_.1, f32[128,128]{1,0:T(8,128)} %constant.30.refs_1_.refs_3_, ...), custom_call_target="tpu_custom_call" | custom-call | tf_op jit(solution)/shard_map/pallas_call | solution.py:171
  16.2 0.0 copy-start.8
  16.2 0.0 copy-start.7
  16.2 1.8 %convolution_bitcast_fusion = f32[4,16,16,128]{3,2,1,0:T(8,128)S(1)} fusion(f32[16,26,1,1]{1,0,3,2:T(8,128)} %constant.40, f32[4,16,5,128]{3,2,1,0:T(8,128)} %get-tuple-element.28, f32[4,16,16,128]{3,2,1,0:T(8,128)} %get-tuple-element.25, f32[4,16,5,128]{3,2,1,0:T(8,128)} %get-tuple-element.27), kind=kOutput, calls=%fused_computation.20 | convolution fusion | flops 20873216 | bytes 1377920 | tf_op jit(solution)/shard_map/al,fxlz->fxaz/dot_general | solution.py:500
  18.0 0.0 copy-done.12
  18.0 0.0 copy-done.8
  18.0 0.0 copy-start.1
  18.1 0.0 copy-start
  18.1 0.0 copy-start.2
  18.1 0.0 copy-start.3
  18.1 0.0 copy-start.6
  18.1 0.6 fusion.36
  18.7 0.2 copy.32
  18.9 0.2 copy-done.1
  19.1 0.0 copy-done.7
  19.2 0.4 copy-done
  19.5 0.1 copy-done.2
  19.6 0.0 copy-done.3
  19.7 0.0 copy-done.6
  19.7 0.2 bitcast_dynamic-update-slice_fusion.11
  19.9 0.1 bitcast_dynamic-update-slice_fusion.10
  20.0 0.1 bitcast_dynamic-update-slice_fusion.9
  20.2 0.2 bitcast_dynamic-update-slice_fusion.8
  20.4 0.1 bitcast_dynamic-update-slice_fusion.6
  20.5 0.1 bitcast_dynamic-update-slice_fusion.5
  20.6 0.1 bitcast_dynamic-update-slice_fusion.4
  20.8 0.1 bitcast_dynamic-update-slice_fusion
  21.0 0.1 slice_bitcast_fusion.14
  21.1 1.5 %multiply_add_fusion = (f32[5,16,16,128]{3,2,1,0:T(8,128)}, f32[5,16,16,128]{3,2,1,0:T(8,128)}, f32[5,16,16,128]{3,2,1,0:T(8,128)}) fusion(f32[5,16,16,128]{3,2,1,0:T(8,128)S(1)} %bitcast_dynamic-update-slice_fusion, f32[5,16,16,128]{3,2,1,0:T(8,128)S(1)} %bitcast_dynamic-update-slice_fusion.4, f32[5,16,16,128]{3,2,1,0:T(8,128)S(1)} %get-tuple-element.70, ...), kind=kLoop, calls=%fused_computation.29 | loop fusion | flops 2457600 | bytes 5111808 | tf_op jit(solution)/shard_map/add | solution.py:564
  22.5 14.6 %shard_map.92 = (f32[5,5,16,128]{3,2,1,0:T(8,128)}, f32[5,5,16,128]{3,2,1,0:T(8,128)}, f32[5,16,5,128]{3,2,1,0:T(8,128)}, f32[5,16,5,128]{3,2,1,0:T(8,128)}, f32[5,16,16,128]{3,2,1,0:T(8,128)}) custom-call(f32[5,16,16,128]{3,2,1,0:T(8,128)} %get-tuple-element.58.refs_0_, f32[5,16,16,128]{3,2,1,0:T(8,128)} %get-tuple-element.57.refs_1_, ...), custom_call_target="tpu_custom_call" | custom-call | tf_op jit(solution)/shard_map/pallas_call | solution.py:171
  37.2 0.0 copy-done.5
  37.2 1.1 %pad_maximum_fusion = f32[5,26,16,128]{3,2,1,0:T(8,128)S(1)} fusion(f32[5,5,16,128]{3,2,1,0:T(8,128)} %get-tuple-element.32, f32[5,16,16,128]{3,2,1,0:T(8,128)S(1)} %copy-done.5, f32[5,5,16,128]{3,2,1,0:T(8,128)} %get-tuple-element.31), kind=kLoop, calls=%fused_computation.21 | loop fusion | flops 532480 | bytes 2129920 | tf_op jit(solution)/shard_map/concatenate | solution.py:242
  38.3 0.0 copy-start.4
  38.3 0.0 copy-start.9
  38.3 0.0 copy-start.10
  38.3 0.0 copy-start.11
  38.3 0.8 %fusion.11 = f32[5,16,128,16]{2,3,1,0:T(8,128)S(1)} fusion(f32[16,26,1,1]{1,0,3,2:T(8,128)S(1)} %copy-done.12, f32[5,26,16,128]{3,2,1,0:T(8,128)S(1)} %pad_maximum_fusion), kind=kOutput, calls=%fused_computation.12 | convolution fusion | flops 25559040 | bytes 1721984 | tf_op jit(solution)/shard_map/al,flyz->fayz/dot_general | solution.py:500
  39.1 0.3 copy-done.4
  39.4 0.2 copy-done.9
  39.6 0.1 copy-done.10
  39.7 0.1 copy-done.11
  39.8 1.7 %fusion.28.value_ref = f32[5,16,16,128]{3,2,1,0:T(8,128)} fusion(f32[5,16,16,128]{3,2,1,0:T(8,128)S(1)} %copy-done.1, f32[5,16,16,128]{3,2,1,0:T(8,128)S(1)} %copy-done.9, f32[16,26,1,1]{1,0,3,2:T(8,128)S(1)} %copy-done.12, f32[5,16,5,128]{3,2,1,0:T(8,128)S(1)} %copy-done.11, f32[5,16,16,128]{3,2,1,0:T(8,128)S(1)} %copy-done.4, ...), kind=kOutput, calls=%fused_computation.19 | convolution fusion | flops 26746880 | bytes 3819136 | tf_op jit(solution)/shard_map/al,fxlz->fxaz/dot_general | solution.py:500
  41.5 22.8 %shard_map.93 = (f32[5,16,16,128]{3,2,1,0:T(8,128)}, f32[5,5,16,128]{3,2,1,0:T(8,128)}, f32[5,5,16,128]{3,2,1,0:T(8,128)}, f32[5,16,5,128]{3,2,1,0:T(8,128)}, f3...) custom-call(f32[5,16,16,128]{3,2,1,0:T(8,128)} %fusion.28.value_ref,, ...), custom_call_target="tpu_custom_call" | custom-call | tf_op jit(solution)/shard_map/pallas_call | solution.py:387
  64.3 0.0 copy-start.13
  64.4 1.9 %maximum_maximum_fusion = f32[5,26,26,128]{3,2,1,0:T(8,128)S(1)} fusion(f32[5,5,5,128]{3,2,1,0:T(8,128)} %get-tuple-element.44, f32[5,5,16,128]{3,2,1,0:T(8,128)} %get-tuple-element.43, f32[5,5,5,128]{3,2,1,0:T(8,128)} %get-tuple-element.42, f32[5,16,5,128]{3,2,1,0:T(8,128)} %get-tuple-element.41, f32[5,16,16,128]{3,2,1,0:T(8,128)} %get-tuple-element.40, ...), kind=kLoop, calls=%fused_computation | loop fusion | flops 3461120 | bytes 3461120 | tf_op jit(solution)/shard_map/concatenate | solution.py:413
  66.3 0.0 copy-done.13
  66.3 2.4 %fusion = f32[5,26,128,16]{2,3,1,0:T(8,128)S(1)} fusion(f32[16,26,1,1]{1,0,3,2:T(8,128)S(1)} %copy-done.13, f32[5,26,26,128]{3,2,1,0:T(8,128)S(1)} %maximum_maximum_fusion), kind=kOutput, calls=%fused_computation.1 | convolution fusion | flops 83066880 | bytes 2797184 | tf_op jit(solution)/shard_map/al,flyz->fayz/dot_general | solution.py:500
  68.7 2.0 %fusion.13 = f32[5,16,16,128]{3,2,1,0:T(8,128)} fusion(f32[16,26,1,1]{1,0,3,2:T(8,128)S(1)} %copy-done.13, f32[5,26,128,16]{2,3,1,0:T(8,128)S(1)} %fusion), kind=kOutput, calls=%fused_computation.14 | convolution fusion | flops 51118080 | bytes 1721984 | tf_op jit(solution)/shard_map/al,fxlz->fxaz/dot_general | solution.py:500
  (7 shorter events, 0.1 us)
Async XLA Ops:
  0.0 18.0 %copy-start.12 = (f32[16,26,1,1]{1,0,3,2:T(8,128)S(1)}, f32[16,26,1,1]{1,0,3,2:T(8,128)}, u32[]{:S(2)}) copy-start(f32[16,26,1,1]{1,0,3,2:T(8,128)} %constant.40) | copy-start | bytes 4996
  16.2 1.9 %copy-start.8 = (f32[4,26,16,128]{3,2,1,0:T(8,128)S(1)}, f32[4,26,16,128]{3,2,1,0:T(8,128)}, u32[]{:S(2)}) copy-start(f32[4,26,16,128]{3,2,1,0:T(8,128)} %get-tuple-element.26) | copy-start | bytes 2555908
  16.2 3.0 %copy-start.7 = (f32[4,16,16,128]{3,2,1,0:T(8,128)S(1)}, f32[4,16,16,128]{3,2,1,0:T(8,128)}, u32[]{:S(2)}) copy-start(f32[4,16,16,128]{3,2,1,0:T(8,128)} %get-tuple-element.29) | copy-start | bytes 1572868
  18.0 1.1 %copy-start.1 = (f32[5,16,16,128]{3,2,1,0:T(8,128)S(1)}, f32[5,16,16,128]{3,2,1,0:T(8,128)}, u32[]{:S(2)}) copy-start(f32[5,16,16,128]{3,2,1,0:T(8,128)} %refs_0_.1) | copy-start | bytes 1966084
  18.1 1.5 %copy-start = (f32[3,3,16,16,128]{4,3,2,1,0:T(8,128)S(1)}, f32[3,3,16,16,128]{4,3,2,1,0:T(8,128)}, u32[]{:S(2)}) copy-start(f32[3,3,16,16,128]{4,3,2,1,0:T(8,128)} %param.10) | copy-start | bytes 3538948
  18.1 1.6 %copy-start.2 = (f32[4,16,16,128]{3,2,1,0:T(8,128)S(1)}, f32[4,16,16,128]{3,2,1,0:T(8,128)}, u32[]{:S(2)}) copy-start(f32[4,16,16,128]{3,2,1,0:T(8,128)} %get-tuple-element.25) | copy-start | bytes 1572868
  18.1 1.6 %copy-start.3 = (f32[16,16,128]{2,1,0:T(8,128)S(1)}, f32[16,16,128]{2,1,0:T(8,128)}, u32[]{:S(2)}) copy-start(f32[16,16,128]{2,1,0:T(8,128)} %param.11) | copy-start | bytes 393220
  18.1 1.6 %copy-start.6 = (f32[16,16,128]{2,1,0:T(8,128)S(1)}, f32[16,16,128]{2,1,0:T(8,128)}, u32[]{:S(2)}) copy-start(f32[16,16,128]{2,1,0:T(8,128)} %get-tuple-element.30) | copy-start | bytes 393220
  22.5 14.7 %copy-start.5 = (f32[5,16,16,128]{3,2,1,0:T(8,128)S(1)}, f32[5,16,16,128]{3,2,1,0:T(8,128)}, u32[]{:S(2)}) copy-start(f32[5,16,16,128]{3,2,1,0:T(8,128)} %get-tuple-element.58.refs_0_) | copy-start | bytes 1966084
  38.3 1.1 %copy-start.4 = (f32[5,16,16,128]{3,2,1,0:T(8,128)S(1)}, f32[5,16,16,128]{3,2,1,0:T(8,128)}, u32[]{:S(2)}) copy-start(f32[5,16,16,128]{3,2,1,0:T(8,128)} %get-tuple-element.57.refs_1_) | copy-start | bytes 1966084
  38.3 1.3 %copy-start.9 = (f32[5,16,16,128]{3,2,1,0:T(8,128)S(1)}, f32[5,16,16,128]{3,2,1,0:T(8,128)}, u32[]{:S(2)}) copy-start(f32[5,16,16,128]{3,2,1,0:T(8,128)} %get-tuple-element.35) | copy-start | bytes 1966084
  38.3 1.3 %copy-start.10 = (f32[5,16,5,128]{3,2,1,0:T(8,128)S(1)}, f32[5,16,5,128]{3,2,1,0:T(8,128)}, u32[]{:S(2)}) copy-start(f32[5,16,5,128]{3,2,1,0:T(8,128)} %get-tuple-element.33) | copy-start | bytes 614404
  38.3 1.4 %copy-start.11 = (f32[5,16,5,128]{3,2,1,0:T(8,128)S(1)}, f32[5,16,5,128]{3,2,1,0:T(8,128)}, u32[]{:S(2)}) copy-start(f32[5,16,5,128]{3,2,1,0:T(8,128)} %get-tuple-element.34) | copy-start | bytes 614404
  64.3 2.0 %copy-start.13 = (f32[16,26,1,1]{1,0,3,2:T(8,128)S(1)}, f32[16,26,1,1]{1,0,3,2:T(8,128)}, u32[]{:S(2)}) copy-start(f32[16,26,1,1]{1,0,3,2:T(8,128)} %constant.41) | copy-start | bytes 4996

commit v29 on v27

--- a/solution.py
+++ b/solution.py
@@ -77,8 +77,8 @@
     if zeta:
         fields, length_x, length_y, depth = block_ref.shape
         rows = fields * length_x * length_y
-        turned[...] = block_ref[...].reshape(rows, depth).T
         if not prepare:
+            turned[...] = block_ref[...].reshape(rows, depth).T
             total = jnp.dot(middle_ref[...], turned[...], precision=precision,
                             preferred_element_type=jnp.float32)
     local = []
@@ -102,6 +102,9 @@
                 device_id_type=MESH,
             )
         )
+        copies[-1].start()
+    if zeta and prepare:
+        turned[...] = block_ref[...].reshape(rows, depth).T
     if zeta:
         for index, (rows_at, landing, offset) in enumerate(
             ((pl.ds(depth - 8, 8), before, (0, 0, 1)), (pl.ds(0, 8), after, (0, 0, -1)))
@@ -116,8 +119,7 @@
                     device_id_type=MESH,
                 )
             )
-    for copy in copies:
-        copy.start()
+            copies[-1].start()
     if zeta and prepare:
         total = jnp.dot(middle_ref[...], turned[...], precision=precision,
                         preferred_element_type=jnp.float32)

time: 70.8 us -> 70.8 us (level)
  no operation moved by 1% of the time
where the time goes in v29:
time: 70.8 us; the launch traced here: 70.5 us
  Pallas kernels  53.8 us (76%)
  matrix products  10.7 us (15%)
  other arithmetic  4.66 us (7%)
  local copies, waits for them, and re-layouts  1.07 us (2%)
    pallas_call x2, Pallas kernels, exchange(): pl.pallas_call(functools.partial(exchange_kernel, tuple(routes), sizes, l...  30.9 us
    pallas_call x1, Pallas kernels, filter_all(): pl.pallas_call(functools.partial(filter_kernel, sizes), out_shape=[jax.Sh...  22.8 us
    dot_general x6, matrix products, sweep_lines(): return jnp.einsum(line_forms[dim], matrix, padded, precision=precision)  10.7 us
    concatenate x1, other arithmetic, filter_all(): result = sweep_lines(jnp.concatenate(sections, axis=1), smooth[0], 1)  1.95 us
    add x1, other arithmetic, fluxes(): metrics[direction, 0] * totals[0] + metrics[direction, 1] * totals[1]  1.45 us

profile of v29, /device:TPU:1, one launch (start us, length us, event | category | flops | bytes accessed | tf_op | source)
XLA Modules:
  0.0 70.5 jit_solution(11933024606738829785)
XLA Ops:
  0.0 0.0 copy-start.11
  0.0 16.2 %shard_map.91 = (f32[4,26,16,128]{3,2,1,0:T(8,128)}, f32[4,16,5,128]{3,2,1,0:T(8,128)}, f32[4,16,5,128]{3,2,1,0:T(8,128)}, f32[4,16,16,128]{3,2,1,0:T(8,128)}, f...) custom-call(f32[5,16,16,128]{3,2,1,0:T(8,128)} %refs_0_.1, f32[128,128]{1,0:T(8,128)} %constant.30.refs_1_.refs_4_, ...), custom_call_target="tpu_custom_call" | custom-call | tf_op jit(solution)/shard_map/pallas_call | solution.py:173
  16.2 0.0 copy-start.7
  16.2 0.0 copy-start.6
  16.2 1.8 %convolution_bitcast_fusion = f32[4,16,16,128]{3,2,1,0:T(8,128)S(1)} fusion(f32[16,26,1,1]{1,0,3,2:T(8,128)} %constant.40, f32[4,16,5,128]{3,2,1,0:T(8,128)} %get-tuple-element.27, f32[4,16,16,128]{3,2,1,0:T(8,128)} %get-tuple-element.24, f32[4,16,5,128]{3,2,1,0:T(8,128)} %get-tuple-element.26), kind=kOutput, calls=%fused_computation.20 | convolution fusion | flops 20873216 | bytes 1377920 | tf_op jit(solution)/shard_map/al,fxlz->fxaz/dot_general | solution.py:508
  18.0 0.0 copy-done.11
  18.0 0.0 copy-done.7
  18.0 0.0 copy-start.1
  18.1 0.0 copy-start
  18.1 0.0 copy-start.2
  18.1 0.0 copy-start.3
  18.1 0.0 copy-start.5
  18.1 0.6 fusion.36
  18.7 0.2 copy.32
  18.9 0.2 copy-done.1
  19.2 0.0 copy-done.6
  19.2 0.4 copy-done
  19.5 0.1 copy-done.2
  19.6 0.0 copy-done.3
  19.7 0.0 copy-done.5
  19.7 0.2 bitcast_dynamic-update-slice_fusion.11
  19.9 0.1 bitcast_dynamic-update-slice_fusion.10
  20.0 0.1 bitcast_dynamic-update-slice_fusion.9
  20.2 0.2 bitcast_dynamic-update-slice_fusion.8
  20.4 0.1 bitcast_dynamic-update-slice_fusion.6
  20.5 0.1 bitcast_dynamic-update-slice_fusion.5
  20.6 0.1 bitcast_dynamic-update-slice_fusion.4
  20.8 0.1 bitcast_dynamic-update-slice_fusion
  21.0 0.1 slice_bitcast_fusion.14
  21.1 1.5 %multiply_add_fusion = (f32[5,16,16,128]{3,2,1,0:T(8,128)}, f32[5,16,16,128]{3,2,1,0:T(8,128)}, f32[5,16,16,128]{3,2,1,0:T(8,128)}) fusion(f32[5,16,16,128]{3,2,1,0:T(8,128)S(1)} %bitcast_dynamic-update-slice_fusion, f32[5,16,16,128]{3,2,1,0:T(8,128)S(1)} %bitcast_dynamic-update-slice_fusion.4, f32[5,16,16,128]{3,2,1,0:T(8,128)S(1)} %get-tuple-element.68, ...), kind=kLoop, calls=%fused_computation.28 | loop fusion | flops 2457600 | bytes 5111808 | tf_op jit(solution)/shard_map/add | solution.py:572
  22.5 14.8 %shard_map.92 = (f32[5,26,16,128]{3,2,1,0:T(8,128)}, f32[5,16,5,128]{3,2,1,0:T(8,128)}, f32[5,16,5,128]{3,2,1,0:T(8,128)}, f32[5,16,16,128]{3,2,1,0:T(8,128)}) custom-call(f32[5,16,16,128]{3,2,1,0:T(8,128)} %get-tuple-element.56.refs_0_.refs_1_, f32[5,16,16,128]{3,2,1,0:T(8,128)} %get-tuple-element.56.refs_0_.refs_1_, ...), custom_call_target="tpu_custom_call" | custom-call | tf_op jit(solution)/shard_map/pallas_call | solution.py:173
  37.3 0.0 copy-start.4
  37.3 0.0 copy-start.8
  37.3 0.0 copy-start.9
  37.3 0.0 copy-start.10
  37.3 2.1 %fusion.11 = f32[5,16,128,16]{2,3,1,0:T(8,128)S(1)} fusion(f32[16,26,1,1]{1,0,3,2:T(8,128)S(1)} %copy-done.11, f32[5,26,16,128]{3,2,1,0:T(8,128)} %get-tuple-element.30), kind=kOutput, calls=%fused_computation.12 | convolution fusion | flops 25559040 | bytes 1721984 | tf_op jit(solution)/shard_map/al,flyz->fayz/dot_general | solution.py:508
  39.5 0.0 copy-done.4
  39.5 0.0 copy-done.8
  39.5 0.0 copy-done.9
  39.5 0.0 copy-done.10
  39.5 1.7 %fusion.28.value_ref = f32[5,16,16,128]{3,2,1,0:T(8,128)} fusion(f32[5,16,16,128]{3,2,1,0:T(8,128)S(1)} %copy-done.1, f32[5,16,16,128]{3,2,1,0:T(8,128)S(1)} %copy-done.8, f32[16,26,1,1]{1,0,3,2:T(8,128)S(1)} %copy-done.11, f32[5,16,5,128]{3,2,1,0:T(8,128)S(1)} %copy-done.10, f32[5,16,16,128]{3,2,1,0:T(8,128)S(1)} %copy-done.4, ...), kind=kOutput, calls=%fused_computation.19 | convolution fusion | flops 26746880 | bytes 3819136 | tf_op jit(solution)/shard_map/al,fxlz->fxaz/dot_general | solution.py:508
  41.2 22.8 %shard_map.93 = (f32[5,16,16,128]{3,2,1,0:T(8,128)}, f32[5,5,16,128]{3,2,1,0:T(8,128)}, f32[5,5,16,128]{3,2,1,0:T(8,128)}, f32[5,16,5,128]{3,2,1,0:T(8,128)}, f3...) custom-call(f32[5,16,16,128]{3,2,1,0:T(8,128)} %fusion.28.value_ref,, ...), custom_call_target="tpu_custom_call" | custom-call | tf_op jit(solution)/shard_map/pallas_call | solution.py:395
  64.0 0.0 copy-start.12
  64.1 1.9 %maximum_maximum_fusion = f32[5,26,26,128]{3,2,1,0:T(8,128)S(1)} fusion(f32[5,5,5,128]{3,2,1,0:T(8,128)} %get-tuple-element.42, f32[5,5,16,128]{3,2,1,0:T(8,128)} %get-tuple-element.41, f32[5,5,5,128]{3,2,1,0:T(8,128)} %get-tuple-element.40, f32[5,16,5,128]{3,2,1,0:T(8,128)} %get-tuple-element.39, f32[5,16,16,128]{3,2,1,0:T(8,128)} %get-tuple-element.38, ...), kind=kLoop, calls=%fused_computation | loop fusion | flops 3461120 | bytes 3461120 | tf_op jit(solution)/shard_map/concatenate | solution.py:421
  66.0 0.0 copy-done.12
  66.0 2.4 %fusion = f32[5,26,128,16]{2,3,1,0:T(8,128)S(1)} fusion(f32[16,26,1,1]{1,0,3,2:T(8,128)S(1)} %copy-done.12, f32[5,26,26,128]{3,2,1,0:T(8,128)S(1)} %maximum_maximum_fusion), kind=kOutput, calls=%fused_computation.1 | convolution fusion | flops 83066880 | bytes 2797184 | tf_op jit(solution)/shard_map/al,flyz->fayz/dot_general | solution.py:508
  68.4 2.0 %fusion.13 = f32[5,16,16,128]{3,2,1,0:T(8,128)} fusion(f32[16,26,1,1]{1,0,3,2:T(8,128)S(1)} %copy-done.12, f32[5,26,128,16]{2,3,1,0:T(8,128)S(1)} %fusion), kind=kOutput, calls=%fused_computation.14 | convolution fusion | flops 51118080 | bytes 1721984 | tf_op jit(solution)/shard_map/al,fxlz->fxaz/dot_general | solution.py:508
  (5 shorter events, 0.1 us)
Async XLA Ops:
  0.0 18.0 %copy-start.11 = (f32[16,26,1,1]{1,0,3,2:T(8,128)S(1)}, f32[16,26,1,1]{1,0,3,2:T(8,128)}, u32[]{:S(2)}) copy-start(f32[16,26,1,1]{1,0,3,2:T(8,128)} %constant.40) | copy-start | bytes 4996
  16.2 1.9 %copy-start.7 = (f32[4,26,16,128]{3,2,1,0:T(8,128)S(1)}, f32[4,26,16,128]{3,2,1,0:T(8,128)}, u32[]{:S(2)}) copy-start(f32[4,26,16,128]{3,2,1,0:T(8,128)} %get-tuple-element.25) | copy-start | bytes 2555908
  16.2 3.0 %copy-start.6 = (f32[4,16,16,128]{3,2,1,0:T(8,128)S(1)}, f32[4,16,16,128]{3,2,1,0:T(8,128)}, u32[]{:S(2)}) copy-start(f32[4,16,16,128]{3,2,1,0:T(8,128)} %get-tuple-element.28) | copy-start | bytes 1572868
  18.0 1.1 %copy-start.1 = (f32[5,16,16,128]{3,2,1,0:T(8,128)S(1)}, f32[5,16,16,128]{3,2,1,0:T(8,128)}, u32[]{:S(2)}) copy-start(f32[5,16,16,128]{3,2,1,0:T(8,128)} %refs_0_.1) | copy-start | bytes 1966084
  18.1 1.5 %copy-start = (f32[3,3,16,16,128]{4,3,2,1,0:T(8,128)S(1)}, f32[3,3,16,16,128]{4,3,2,1,0:T(8,128)}, u32[]{:S(2)}) copy-start(f32[3,3,16,16,128]{4,3,2,1,0:T(8,128)} %param.10) | copy-start | bytes 3538948
  18.1 1.6 %copy-start.2 = (f32[4,16,16,128]{3,2,1,0:T(8,128)S(1)}, f32[4,16,16,128]{3,2,1,0:T(8,128)}, u32[]{:S(2)}) copy-start(f32[4,16,16,128]{3,2,1,0:T(8,128)} %get-tuple-element.24) | copy-start | bytes 1572868
  18.1 1.6 %copy-start.3 = (f32[16,16,128]{2,1,0:T(8,128)S(1)}, f32[16,16,128]{2,1,0:T(8,128)}, u32[]{:S(2)}) copy-start(f32[16,16,128]{2,1,0:T(8,128)} %param.11) | copy-start | bytes 393220
  18.1 1.6 %copy-start.5 = (f32[16,16,128]{2,1,0:T(8,128)S(1)}, f32[16,16,128]{2,1,0:T(8,128)}, u32[]{:S(2)}) copy-start(f32[16,16,128]{2,1,0:T(8,128)} %get-tuple-element.29) | copy-start | bytes 393220
  37.3 2.2 %copy-start.4 = (f32[5,16,16,128]{3,2,1,0:T(8,128)S(1)}, f32[5,16,16,128]{3,2,1,0:T(8,128)}, u32[]{:S(2)}) copy-start(f32[5,16,16,128]{3,2,1,0:T(8,128)} %get-tuple-element.55.refs_2_) | copy-start | bytes 1966084
  37.3 2.2 %copy-start.8 = (f32[5,16,16,128]{3,2,1,0:T(8,128)S(1)}, f32[5,16,16,128]{3,2,1,0:T(8,128)}, u32[]{:S(2)}) copy-start(f32[5,16,16,128]{3,2,1,0:T(8,128)} %get-tuple-element.33) | copy-start | bytes 1966084
  37.3 2.2 %copy-start.9 = (f32[5,16,5,128]{3,2,1,0:T(8,128)S(1)}, f32[5,16,5,128]{3,2,1,0:T(8,128)}, u32[]{:S(2)}) copy-start(f32[5,16,5,128]{3,2,1,0:T(8,128)} %get-tuple-element.31) | copy-start | bytes 614404
  37.3 2.2 %copy-start.10 = (f32[5,16,5,128]{3,2,1,0:T(8,128)S(1)}, f32[5,16,5,128]{3,2,1,0:T(8,128)}, u32[]{:S(2)}) copy-start(f32[5,16,5,128]{3,2,1,0:T(8,128)} %get-tuple-element.32) | copy-start | bytes 614404
  64.0 2.0 %copy-start.12 = (f32[16,26,1,1]{1,0,3,2:T(8,128)S(1)}, f32[16,26,1,1]{1,0,3,2:T(8,128)}, u32[]{:S(2)}) copy-start(f32[16,26,1,1]{1,0,3,2:T(8,128)} %constant.41) | copy-start | bytes 4996

commit v30 on v27

--- a/solution.py
+++ b/solution.py
@@ -416,7 +416,11 @@
         jnp.concatenate([y_before, smoothed, y_after], axis=2),
         jnp.concatenate([x_after_y_before, x_after, both_after], axis=2),
     ]
-    result = sweep_lines(jnp.concatenate(sections, axis=1), smooth[0], 1)
+    bounds = (0, WIDTH, WIDTH + length_x, length_x + 2 * WIDTH)
+    result = sum(
+        sweep_lines(section, smooth[0][:, bounds[index] : bounds[index + 1]], 1)
+        for index, section in enumerate(sections)
+    )
     return sweep_lines(result, smooth[1], 2)
 
 

time: 70.8 us -> 73.3 us (1.035)
  matrix products: 10.7 us -> 12.9 us
    dot_general x6 -> x8, matrix products: 10.7 us -> 12.9 us  [sweep_lines(): return jnp.einsum(line_forms[dim], matrix, padded, precision=precision)]
    concatenate x1 -> x2, other arithmetic: 1.95 us -> 1.61 us  [the longest x1 1.48 us: filter_all(): jnp.concatenate([y_before, smoothed, y_after], axis=2)]
where the time goes in v30:
time: 73.3 us; the launch traced here: 73 us
  Pallas kernels  53.7 us (73%)
  matrix products  12.9 us (18%)
  other arithmetic  4.32 us (6%)
  local copies, waits for them, and re-layouts  1.6 us (2%)
    pallas_call x2, Pallas kernels, exchange(): pl.pallas_call(functools.partial(exchange_kernel, tuple(routes), sizes, l...  30.9 us
    pallas_call x1, Pallas kernels, filter_all(): pl.pallas_call(functools.partial(filter_kernel, sizes), out_shape=[jax.Sh...  22.8 us
    dot_general x8, matrix products, sweep_lines(): return jnp.einsum(line_forms[dim], matrix, padded, precision=precision)  12.9 us
    concatenate x1, other arithmetic, filter_all(): jnp.concatenate([y_before, smoothed, y_after], axis=2)  1.48 us

profile of v30, /device:TPU:1, one launch (start us, length us, event | category | flops | bytes accessed | tf_op | source)
XLA Modules:
  0.0 73.0 jit_solution(2934804907462853657)
XLA Ops:
  0.0 16.1 %shard_map.91 = (f32[4,26,16,128]{3,2,1,0:T(8,128)}, f32[4,16,5,128]{3,2,1,0:T(8,128)}, f32[4,16,5,128]{3,2,1,0:T(8,128)}, f32[4,16,16,128]{3,2,1,0:T(8,128)}, f...) custom-call(f32[5,16,16,128]{3,2,1,0:T(8,128)} %refs_0_.1, f32[128,128]{1,0:T(8,128)} %constant.30.refs_1_.refs_4_, ...), custom_call_target="tpu_custom_call" | custom-call | tf_op jit(solution)/shard_map/pallas_call | solution.py:171
  16.2 1.8 %convolution_bitcast_fusion = f32[4,16,16,128]{3,2,1,0:T(8,128)S(1)} fusion(f32[16,26,1,1]{1,0,3,2:T(8,128)} %constant.43, f32[4,16,5,128]{3,2,1,0:T(8,128)} %get-tuple-element.27, f32[4,16,16,128]{3,2,1,0:T(8,128)} %get-tuple-element.24, f32[4,16,5,128]{3,2,1,0:T(8,128)} %get-tuple-element.26), kind=kOutput, calls=%fused_computation.20 | convolution fusion | flops 20873216 | bytes 1377920 | tf_op jit(solution)/shard_map/al,fxlz->fxaz/dot_general | solution.py:510
  18.0 0.0 copy-start.1
  18.0 0.0 copy-start
  18.1 0.0 copy-start.2
  18.1 0.0 copy-start.3
  18.1 0.6 fusion.36
  18.7 0.2 copy.55
  18.9 0.2 copy-done.1
  19.1 0.4 copy-done
  19.5 0.1 copy-done.2
  19.6 0.0 copy-done.3
  19.6 0.0 copy-done.5
  19.7 0.2 bitcast_dynamic-update-slice_fusion.11
  19.9 0.1 bitcast_dynamic-update-slice_fusion.10
  20.0 0.1 bitcast_dynamic-update-slice_fusion.9
  20.2 0.2 bitcast_dynamic-update-slice_fusion.8
  20.4 0.1 bitcast_dynamic-update-slice_fusion.6
  20.4 0.1 bitcast_dynamic-update-slice_fusion.5
  20.6 0.1 bitcast_dynamic-update-slice_fusion.4
  20.8 0.1 bitcast_dynamic-update-slice_fusion
  21.0 0.1 slice_bitcast_fusion.14
  21.1 1.5 %multiply_add_fusion = (f32[5,16,16,128]{3,2,1,0:T(8,128)}, f32[5,16,16,128]{3,2,1,0:T(8,128)}, f32[5,16,16,128]{3,2,1,0:T(8,128)}) fusion(f32[5,16,16,128]{3,2,1,0:T(8,128)S(1)} %bitcast_dynamic-update-slice_fusion, f32[5,16,16,128]{3,2,1,0:T(8,128)S(1)} %bitcast_dynamic-update-slice_fusion.4, f32[5,16,16,128]{3,2,1,0:T(8,128)S(1)} %get-tuple-element.68, ...), kind=kLoop, calls=%fused_computation.30 | loop fusion | flops 2457600 | bytes 5111808 | tf_op jit(solution)/shard_map/add | solution.py:574
  22.5 14.8 %shard_map.92 = (f32[5,26,16,128]{3,2,1,0:T(8,128)}, f32[5,16,5,128]{3,2,1,0:T(8,128)}, f32[5,16,5,128]{3,2,1,0:T(8,128)}, f32[5,16,16,128]{3,2,1,0:T(8,128)}) custom-call(f32[5,16,16,128]{3,2,1,0:T(8,128)} %get-tuple-element.56.refs_0_.refs_1_, f32[5,16,16,128]{3,2,1,0:T(8,128)} %get-tuple-element.56.refs_0_.refs_1_, ...), custom_call_target="tpu_custom_call" | custom-call | tf_op jit(solution)/shard_map/pallas_call | solution.py:171
  37.3 2.1 %fusion.9 = f32[5,16,128,16]{2,3,1,0:T(8,128)S(1)} fusion(f32[16,26,1,1]{1,0,3,2:T(8,128)S(1)} %copy-done.13, f32[5,26,16,128]{3,2,1,0:T(8,128)} %get-tuple-element.30), kind=kOutput, calls=%fused_computation.12 | convolution fusion | flops 25559040 | bytes 1721984 | tf_op jit(solution)/shard_map/al,flyz->fayz/dot_general | solution.py:510
  39.5 0.0 copy-done.4
  39.5 0.0 copy-done.8
  39.5 0.0 copy-done.9
  39.5 0.0 copy-done.10
  39.5 1.7 %fusion.26.value_ref = f32[5,16,16,128]{3,2,1,0:T(8,128)} fusion(f32[5,16,16,128]{3,2,1,0:T(8,128)S(1)} %copy-done.1, f32[5,16,16,128]{3,2,1,0:T(8,128)S(1)} %copy-done.8, f32[16,26,1,1]{1,0,3,2:T(8,128)S(1)} %copy-done.13, f32[5,16,5,128]{3,2,1,0:T(8,128)S(1)} %copy-done.10, f32[5,16,16,128]{3,2,1,0:T(8,128)S(1)} %copy-done.4, ...), kind=kOutput, calls=%fused_computation.19 | convolution fusion | flops 26746880 | bytes 3819136 | tf_op jit(solution)/shard_map/al,fxlz->fxaz/dot_general | solution.py:510
  41.2 22.8 %shard_map.93 = (f32[5,16,16,128]{3,2,1,0:T(8,128)}, f32[5,5,16,128]{3,2,1,0:T(8,128)}, f32[5,5,16,128]{3,2,1,0:T(8,128)}, f32[5,16,5,128]{3,2,1,0:T(8,128)}, f3...) custom-call(f32[5,16,16,128]{3,2,1,0:T(8,128)} %fusion.26.value_ref,, ...), custom_call_target="tpu_custom_call" | custom-call | tf_op jit(solution)/shard_map/pallas_call | solution.py:393
  64.0 0.0 copy-start.21
  64.0 1.5 %pad_maximum_fusion = f32[5,16,26,128]{3,2,1,0:T(8,128)S(1)} fusion(f32[5,16,5,128]{3,2,1,0:T(8,128)} %get-tuple-element.39, f32[5,16,16,128]{3,2,1,0:T(8,128)} %get-tuple-element.38, f32[5,16,5,128]{3,2,1,0:T(8,128)} %get-tuple-element.37), kind=kLoop, calls=%fused_computation.6 | loop fusion | flops 532480 | bytes 2129920 | tf_op jit(solution)/shard_map/concatenate | solution.py:416
  65.5 0.0 copy-done.21
  65.5 0.0 copy-start.11
  65.5 0.0 copy-start.12
  65.5 0.0 copy-start.14
  65.6 0.0 copy-start.15
  65.6 0.0 copy-start.16
  65.6 1.6 %fusion.29 = f32[5,26,128,16]{2,3,1,0:T(8,128)S(1)} fusion(f32[16,16,1,1]{1,0,3,2:T(8,128)S(1)} %copy-done.21, f32[5,16,26,128]{3,2,1,0:T(8,128)S(1)} %pad_maximum_fusion), kind=kOutput, calls=%fused_computation.21 | convolution fusion | flops 51118080 | bytes 2130944 | tf_op jit(solution)/shard_map/al,flyz->fayz/dot_general | solution.py:510
  67.2 0.0 copy-start.20
  67.3 0.1 pad_maximum_fusion.1
  67.4 0.0 copy-start.19
  67.4 0.5 copy-done.20
  67.9 1.3 %fusion.38 = f32[5,26,128,16]{2,3,1,0:T(8,128)S(1)} fusion(f32[16,5,1,1]{1,0,3,2:T(8,128)S(1)} %copy-done.20, f32[5,5,26,128]{3,2,1,0:T(8,128)S(1)} %get-tuple-element.72), kind=kOutput, calls=%fused_computation.33 | convolution fusion | flops 15974400 | bytes 1398080 | tf_op jit(solution)/shard_map/al,flyz->fayz/dot_general | solution.py:510
  69.2 0.0 copy-start.18
  69.2 1.1 %fusion.40 = f32[5,26,128,16]{2,3,1,0:T(8,128)S(1)} fusion(f32[16,5,1,1]{1,0,3,2:T(8,128)S(1)} %copy-done.19, f32[5,5,26,128]{3,2,1,0:T(8,128)S(1)} %get-tuple-element.71), kind=kOutput, calls=%fused_computation.35 | convolution fusion | flops 15974400 | bytes 1398080 | tf_op jit(solution)/shard_map/al,flyz->fayz/dot_general | solution.py:510
  70.3 2.7 %fusion.11 = f32[5,16,16,128]{3,2,1,0:T(8,128)} fusion(f32[16,26,1,1]{1,0,3,2:T(8,128)S(1)} %copy-done.18, f32[5,26,128,16]{2,3,1,0:T(8,128)S(1)} %fusion.38, f32[5,26,128,16]{2,3,1,0:T(8,128)S(1)} %fusion.29, f32[5,26,128,16]{2,3,1,0:T(8,128)S(1)} %fusion.40), kind=kOutput, calls=%fused_computation.14 | convolution fusion | flops 51650560 | bytes 3851904 | tf_op jit(solution)/shard_map/al,fxlz->fxaz/dot_general | solution.py:510
  (25 shorter events, 0.2 us)
Async XLA Ops:
  0.0 18.0 %copy-start.13 = (f32[16,26,1,1]{1,0,3,2:T(8,128)S(1)}, f32[16,26,1,1]{1,0,3,2:T(8,128)}, u32[]{:S(2)}) copy-start(f32[16,26,1,1]{1,0,3,2:T(8,128)} %constant.43) | copy-start | bytes 4996
  16.2 1.9 %copy-start.7 = (f32[4,26,16,128]{3,2,1,0:T(8,128)S(1)}, f32[4,26,16,128]{3,2,1,0:T(8,128)}, u32[]{:S(2)}) copy-start(f32[4,26,16,128]{3,2,1,0:T(8,128)} %get-tuple-element.25) | copy-start | bytes 2555908
  16.2 3.0 %copy-start.6 = (f32[4,16,16,128]{3,2,1,0:T(8,128)S(1)}, f32[4,16,16,128]{3,2,1,0:T(8,128)}, u32[]{:S(2)}) copy-start(f32[4,16,16,128]{3,2,1,0:T(8,128)} %get-tuple-element.28) | copy-start | bytes 1572868
  18.0 1.1 %copy-start.1 = (f32[5,16,16,128]{3,2,1,0:T(8,128)S(1)}, f32[5,16,16,128]{3,2,1,0:T(8,128)}, u32[]{:S(2)}) copy-start(f32[5,16,16,128]{3,2,1,0:T(8,128)} %refs_0_.1) | copy-start | bytes 1966084
  18.0 1.5 %copy-start = (f32[3,3,16,16,128]{4,3,2,1,0:T(8,128)S(1)}, f32[3,3,16,16,128]{4,3,2,1,0:T(8,128)}, u32[]{:S(2)}) copy-start(f32[3,3,16,16,128]{4,3,2,1,0:T(8,128)} %param.10) | copy-start | bytes 3538948
  18.1 1.6 %copy-start.2 = (f32[4,16,16,128]{3,2,1,0:T(8,128)S(1)}, f32[4,16,16,128]{3,2,1,0:T(8,128)}, u32[]{:S(2)}) copy-start(f32[4,16,16,128]{3,2,1,0:T(8,128)} %get-tuple-element.24) | copy-start | bytes 1572868
  18.1 1.6 %copy-start.3 = (f32[16,16,128]{2,1,0:T(8,128)S(1)}, f32[16,16,128]{2,1,0:T(8,128)}, u32[]{:S(2)}) copy-start(f32[16,16,128]{2,1,0:T(8,128)} %param.11) | copy-start | bytes 393220
  18.1 1.6 %copy-start.5 = (f32[16,16,128]{2,1,0:T(8,128)S(1)}, f32[16,16,128]{2,1,0:T(8,128)}, u32[]{:S(2)}) copy-start(f32[16,16,128]{2,1,0:T(8,128)} %get-tuple-element.29) | copy-start | bytes 393220
  37.3 2.2 %copy-start.4 = (f32[5,16,16,128]{3,2,1,0:T(8,128)S(1)}, f32[5,16,16,128]{3,2,1,0:T(8,128)}, u32[]{:S(2)}) copy-start(f32[5,16,16,128]{3,2,1,0:T(8,128)} %get-tuple-element.55.refs_2_) | copy-start | bytes 1966084
  37.3 2.2 %copy-start.8 = (f32[5,16,16,128]{3,2,1,0:T(8,128)S(1)}, f32[5,16,16,128]{3,2,1,0:T(8,128)}, u32[]{:S(2)}) copy-start(f32[5,16,16,128]{3,2,1,0:T(8,128)} %get-tuple-element.33) | copy-start | bytes 1966084
  37.3 2.2 %copy-start.9 = (f32[5,16,5,128]{3,2,1,0:T(8,128)S(1)}, f32[5,16,5,128]{3,2,1,0:T(8,128)}, u32[]{:S(2)}) copy-start(f32[5,16,5,128]{3,2,1,0:T(8,128)} %get-tuple-element.31) | copy-start | bytes 614404
  37.3 2.2 %copy-start.10 = (f32[5,16,5,128]{3,2,1,0:T(8,128)S(1)}, f32[5,16,5,128]{3,2,1,0:T(8,128)}, u32[]{:S(2)}) copy-start(f32[5,16,5,128]{3,2,1,0:T(8,128)} %get-tuple-element.32) | copy-start | bytes 614404
  64.0 1.5 %copy-start.21 = (f32[16,16,1,1]{1,0,3,2:T(8,128)S(1)}, f32[16,16,1,1]{1,0,3,2:T(8,128)}, u32[]{:S(2)}) copy-start(f32[16,16,1,1]{1,0,3,2:T(8,128)} %constant.45) | copy-start | bytes 3076
  65.5 1.7 %copy-start.11 = (f32[5,5,16,128]{3,2,1,0:T(8,128)S(1)}, f32[5,5,16,128]{3,2,1,0:T(8,128)}, u32[]{:S(2)}) copy-start(f32[5,5,16,128]{3,2,1,0:T(8,128)} %get-tuple-element.35) | copy-start | bytes 614404
  65.5 1.7 %copy-start.12 = (f32[5,5,16,128]{3,2,1,0:T(8,128)S(1)}, f32[5,5,16,128]{3,2,1,0:T(8,128)}, u32[]{:S(2)}) copy-start(f32[5,5,16,128]{3,2,1,0:T(8,128)} %get-tuple-element.41) | copy-start | bytes 614404
  65.5 1.7 %copy-start.14 = (f32[5,5,5,128]{3,2,1,0:T(8,128)S(1)}, f32[5,5,5,128]{3,2,1,0:T(8,128)}, u32[]{:S(2)}) copy-start(f32[5,5,5,128]{3,2,1,0:T(8,128)} %get-tuple-element.34) | copy-start | bytes 192004
  65.6 1.7 %copy-start.15 = (f32[5,5,5,128]{3,2,1,0:T(8,128)S(1)}, f32[5,5,5,128]{3,2,1,0:T(8,128)}, u32[]{:S(2)}) copy-start(f32[5,5,5,128]{3,2,1,0:T(8,128)} %get-tuple-element.40) | copy-start | bytes 192004
  65.6 1.7 %copy-start.16 = (f32[5,5,5,128]{3,2,1,0:T(8,128)S(1)}, f32[5,5,5,128]{3,2,1,0:T(8,128)}, u32[]{:S(2)}) copy-start(f32[5,5,5,128]{3,2,1,0:T(8,128)} %get-tuple-element.36) | copy-start | bytes 192004
  65.6 1.7 %copy-start.17 = (f32[5,5,5,128]{3,2,1,0:T(8,128)S(1)}, f32[5,5,5,128]{3,2,1,0:T(8,128)}, u32[]{:S(2)}) copy-start(f32[5,5,5,128]{3,2,1,0:T(8,128)} %get-tuple-element.42) | copy-start | bytes 192004
  67.2 0.7 copy-start.20
  67.4 1.8 %copy-start.19 = (f32[16,5,1,1]{1,0,3,2:T(8,128)S(1)}, f32[16,5,1,1]{1,0,3,2:T(8,128)}, u32[]{:S(2)}) copy-start(f32[16,5,1,1]{1,0,3,2:T(8,128)} %constant.44) | copy-start | bytes 964
  69.2 1.1 %copy-start.18 = (f32[16,26,1,1]{1,0,3,2:T(8,128)S(1)}, f32[16,26,1,1]{1,0,3,2:T(8,128)}, u32[]{:S(2)}) copy-start(f32[16,26,1,1]{1,0,3,2:T(8,128)} %constant.47) | copy-start | bytes 4996

commit v31 on v27

--- a/solution.py
+++ b/solution.py
@@ -394,7 +394,7 @@
         functools.partial(filter_kernel, sizes),
         out_shape=[jax.ShapeDtypeStruct(value.shape, value.dtype)] + [x_face] * 2 + [y_face] * 2 + [edge] * 4,
         in_specs=[pl.BlockSpec(memory_space=pltpu.VMEM)] * 4,
-        out_specs=[pl.BlockSpec(memory_space=pltpu.VMEM)] + [pl.BlockSpec(memory_space=pl.ANY)] * 8,
+        out_specs=[pl.BlockSpec(memory_space=pltpu.VMEM)] * 9,
         scratch_shapes=[
             pltpu.VMEM((depth, rows), jnp.float32),
             pltpu.VMEM((8, rows), jnp.float32),

time: 70.8 us -> 71.2 us (level)
  no operation moved by 1% of the time
where the time goes in v31:
time: 71.2 us; the launch traced here: 70.9 us
  Pallas kernels  54.2 us (76%)
  matrix products  10.7 us (15%)
  other arithmetic  4.66 us (7%)
  local copies, waits for them, and re-layouts  1.07 us (2%)
    pallas_call x2, Pallas kernels, exchange(): pl.pallas_call(functools.partial(exchange_kernel, tuple(routes), sizes, l...  30.9 us
    pallas_call x1, Pallas kernels, filter_all(): pl.pallas_call(functools.partial(filter_kernel, sizes), out_shape=[jax.Sh...  23.2 us
    dot_general x6, matrix products, sweep_lines(): return jnp.einsum(line_forms[dim], matrix, padded, precision=precision)  10.7 us
    concatenate x1, other arithmetic, filter_all(): result = sweep_lines(jnp.concatenate(sections, axis=1), smooth[0], 1)  1.95 us
    add x1, other arithmetic, fluxes(): metrics[direction, 0] * totals[0] + metrics[direction, 1] * totals[1]  1.45 us

profile of v31, /device:TPU:1, one launch (start us, length us, event | category | flops | bytes accessed | tf_op | source)
XLA Modules:
  0.0 70.9 jit_solution(10938474857707547057)
XLA Ops:
  0.0 0.0 copy-start.11
  0.0 16.2 %shard_map.91 = (f32[4,26,16,128]{3,2,1,0:T(8,128)}, f32[4,16,5,128]{3,2,1,0:T(8,128)}, f32[4,16,5,128]{3,2,1,0:T(8,128)}, f32[4,16,16,128]{3,2,1,0:T(8,128)}, f...) custom-call(f32[5,16,16,128]{3,2,1,0:T(8,128)} %refs_0_.1, f32[128,128]{1,0:T(8,128)} %constant.30.refs_1_.refs_4_, ...), custom_call_target="tpu_custom_call" | custom-call | tf_op jit(solution)/shard_map/pallas_call | solution.py:171
  16.2 0.0 copy-start.7
  16.2 0.0 copy-start.6
  16.2 1.8 %convolution_bitcast_fusion = f32[4,16,16,128]{3,2,1,0:T(8,128)S(1)} fusion(f32[16,26,1,1]{1,0,3,2:T(8,128)} %constant.40, f32[4,16,5,128]{3,2,1,0:T(8,128)} %get-tuple-element.27, f32[4,16,16,128]{3,2,1,0:T(8,128)} %get-tuple-element.24, f32[4,16,5,128]{3,2,1,0:T(8,128)} %get-tuple-element.26), kind=kOutput, calls=%fused_computation.20 | convolution fusion | flops 20873216 | bytes 1377920 | tf_op jit(solution)/shard_map/al,fxlz->fxaz/dot_general | solution.py:506
  18.0 0.0 copy-done.11
  18.0 0.0 copy-done.7
  18.0 0.0 copy-start.1
  18.1 0.0 copy-start
  18.1 0.0 copy-start.2
  18.1 0.0 copy-start.3
  18.1 0.0 copy-start.5
  18.1 0.6 fusion.36
  18.7 0.2 copy.32
  18.9 0.2 copy-done.1
  19.2 0.0 copy-done.6
  19.2 0.4 copy-done
  19.5 0.1 copy-done.2
  19.6 0.0 copy-done.3
  19.7 0.0 copy-done.5
  19.7 0.2 bitcast_dynamic-update-slice_fusion.11
  19.9 0.1 bitcast_dynamic-update-slice_fusion.10
  20.0 0.1 bitcast_dynamic-update-slice_fusion.9
  20.2 0.2 bitcast_dynamic-update-slice_fusion.8
  20.4 0.1 bitcast_dynamic-update-slice_fusion.6
  20.5 0.1 bitcast_dynamic-update-slice_fusion.5
  20.6 0.1 bitcast_dynamic-update-slice_fusion.4
  20.8 0.1 bitcast_dynamic-update-slice_fusion
  21.0 0.1 slice_bitcast_fusion.14
  21.1 1.5 %multiply_add_fusion = (f32[5,16,16,128]{3,2,1,0:T(8,128)}, f32[5,16,16,128]{3,2,1,0:T(8,128)}, f32[5,16,16,128]{3,2,1,0:T(8,128)}) fusion(f32[5,16,16,128]{3,2,1,0:T(8,128)S(1)} %bitcast_dynamic-update-slice_fusion, f32[5,16,16,128]{3,2,1,0:T(8,128)S(1)} %bitcast_dynamic-update-slice_fusion.4, f32[5,16,16,128]{3,2,1,0:T(8,128)S(1)} %get-tuple-element.68, ...), kind=kLoop, calls=%fused_computation.28 | loop fusion | flops 2457600 | bytes 5111808 | tf_op jit(solution)/shard_map/add | solution.py:570
  22.5 14.8 %shard_map.92 = (f32[5,26,16,128]{3,2,1,0:T(8,128)}, f32[5,16,5,128]{3,2,1,0:T(8,128)}, f32[5,16,5,128]{3,2,1,0:T(8,128)}, f32[5,16,16,128]{3,2,1,0:T(8,128)}) custom-call(f32[5,16,16,128]{3,2,1,0:T(8,128)} %get-tuple-element.56.refs_0_.refs_1_, f32[5,16,16,128]{3,2,1,0:T(8,128)} %get-tuple-element.56.refs_0_.refs_1_, ...), custom_call_target="tpu_custom_call" | custom-call | tf_op jit(solution)/shard_map/pallas_call | solution.py:171
  37.3 0.0 copy-start.4
  37.3 0.0 copy-start.8
  37.3 0.0 copy-start.9
  37.3 0.0 copy-start.10
  37.3 2.1 %fusion.11 = f32[5,16,128,16]{2,3,1,0:T(8,128)S(1)} fusion(f32[16,26,1,1]{1,0,3,2:T(8,128)S(1)} %copy-done.11, f32[5,26,16,128]{3,2,1,0:T(8,128)} %get-tuple-element.30), kind=kOutput, calls=%fused_computation.12 | convolution fusion | flops 25559040 | bytes 1721984 | tf_op jit(solution)/shard_map/al,flyz->fayz/dot_general | solution.py:506
  39.5 0.0 copy-done.4
  39.5 0.0 copy-done.8
  39.5 0.0 copy-done.9
  39.5 0.0 copy-done.10
  39.5 1.7 %fusion.28.value_ref = f32[5,16,16,128]{3,2,1,0:T(8,128)} fusion(f32[5,16,16,128]{3,2,1,0:T(8,128)S(1)} %copy-done.1, f32[5,16,16,128]{3,2,1,0:T(8,128)S(1)} %copy-done.8, f32[16,26,1,1]{1,0,3,2:T(8,128)S(1)} %copy-done.11, f32[5,16,5,128]{3,2,1,0:T(8,128)S(1)} %copy-done.10, f32[5,16,16,128]{3,2,1,0:T(8,128)S(1)} %copy-done.4, ...), kind=kOutput, calls=%fused_computation.19 | convolution fusion | flops 26746880 | bytes 3819136 | tf_op jit(solution)/shard_map/al,fxlz->fxaz/dot_general | solution.py:506
  41.2 23.2 %shard_map.93 = (f32[5,16,16,128]{3,2,1,0:T(8,128)}, f32[5,5,16,128]{3,2,1,0:T(8,128)}, f32[5,5,16,128]{3,2,1,0:T(8,128)}, f32[5,16,5,128]{3,2,1,0:T(8,128)}, f3...) custom-call(f32[5,16,16,128]{3,2,1,0:T(8,128)} %fusion.28.value_ref,, ...), custom_call_target="tpu_custom_call" | custom-call | tf_op jit(solution)/shard_map/pallas_call | solution.py:393
  64.4 0.0 copy-start.12
  64.4 1.9 %maximum_maximum_fusion = f32[5,26,26,128]{3,2,1,0:T(8,128)S(1)} fusion(f32[5,5,5,128]{3,2,1,0:T(8,128)} %get-tuple-element.42, f32[5,5,16,128]{3,2,1,0:T(8,128)} %get-tuple-element.41, f32[5,5,5,128]{3,2,1,0:T(8,128)} %get-tuple-element.40, f32[5,16,5,128]{3,2,1,0:T(8,128)} %get-tuple-element.39, f32[5,16,16,128]{3,2,1,0:T(8,128)} %get-tuple-element.38, ...), kind=kLoop, calls=%fused_computation | loop fusion | flops 3461120 | bytes 3461120 | tf_op jit(solution)/shard_map/concatenate | solution.py:419
  66.4 0.0 copy-done.12
  66.4 2.4 %fusion = f32[5,26,128,16]{2,3,1,0:T(8,128)S(1)} fusion(f32[16,26,1,1]{1,0,3,2:T(8,128)S(1)} %copy-done.12, f32[5,26,26,128]{3,2,1,0:T(8,128)S(1)} %maximum_maximum_fusion), kind=kOutput, calls=%fused_computation.1 | convolution fusion | flops 83066880 | bytes 2797184 | tf_op jit(solution)/shard_map/al,flyz->fayz/dot_general | solution.py:506
  68.8 2.0 %fusion.13 = f32[5,16,16,128]{3,2,1,0:T(8,128)} fusion(f32[16,26,1,1]{1,0,3,2:T(8,128)S(1)} %copy-done.12, f32[5,26,128,16]{2,3,1,0:T(8,128)S(1)} %fusion), kind=kOutput, calls=%fused_computation.14 | convolution fusion | flops 51118080 | bytes 1721984 | tf_op jit(solution)/shard_map/al,fxlz->fxaz/dot_general | solution.py:506
  (5 shorter events, 0.1 us)
Async XLA Ops:
  0.0 18.0 %copy-start.11 = (f32[16,26,1,1]{1,0,3,2:T(8,128)S(1)}, f32[16,26,1,1]{1,0,3,2:T(8,128)}, u32[]{:S(2)}) copy-start(f32[16,26,1,1]{1,0,3,2:T(8,128)} %constant.40) | copy-start | bytes 4996
  16.2 1.9 %copy-start.7 = (f32[4,26,16,128]{3,2,1,0:T(8,128)S(1)}, f32[4,26,16,128]{3,2,1,0:T(8,128)}, u32[]{:S(2)}) copy-start(f32[4,26,16,128]{3,2,1,0:T(8,128)} %get-tuple-element.25) | copy-start | bytes 2555908
  16.2 3.0 %copy-start.6 = (f32[4,16,16,128]{3,2,1,0:T(8,128)S(1)}, f32[4,16,16,128]{3,2,1,0:T(8,128)}, u32[]{:S(2)}) copy-start(f32[4,16,16,128]{3,2,1,0:T(8,128)} %get-tuple-element.28) | copy-start | bytes 1572868
  18.0 1.1 %copy-start.1 = (f32[5,16,16,128]{3,2,1,0:T(8,128)S(1)}, f32[5,16,16,128]{3,2,1,0:T(8,128)}, u32[]{:S(2)}) copy-start(f32[5,16,16,128]{3,2,1,0:T(8,128)} %refs_0_.1) | copy-start | bytes 1966084
  18.1 1.5 %copy-start = (f32[3,3,16,16,128]{4,3,2,1,0:T(8,128)S(1)}, f32[3,3,16,16,128]{4,3,2,1,0:T(8,128)}, u32[]{:S(2)}) copy-start(f32[3,3,16,16,128]{4,3,2,1,0:T(8,128)} %param.10) | copy-start | bytes 3538948
  18.1 1.6 %copy-start.2 = (f32[4,16,16,128]{3,2,1,0:T(8,128)S(1)}, f32[4,16,16,128]{3,2,1,0:T(8,128)}, u32[]{:S(2)}) copy-start(f32[4,16,16,128]{3,2,1,0:T(8,128)} %get-tuple-element.24) | copy-start | bytes 1572868
  18.1 1.6 %copy-start.3 = (f32[16,16,128]{2,1,0:T(8,128)S(1)}, f32[16,16,128]{2,1,0:T(8,128)}, u32[]{:S(2)}) copy-start(f32[16,16,128]{2,1,0:T(8,128)} %param.11) | copy-start | bytes 393220
  18.1 1.6 %copy-start.5 = (f32[16,16,128]{2,1,0:T(8,128)S(1)}, f32[16,16,128]{2,1,0:T(8,128)}, u32[]{:S(2)}) copy-start(f32[16,16,128]{2,1,0:T(8,128)} %get-tuple-element.29) | copy-start | bytes 393220
  37.3 2.2 %copy-start.4 = (f32[5,16,16,128]{3,2,1,0:T(8,128)S(1)}, f32[5,16,16,128]{3,2,1,0:T(8,128)}, u32[]{:S(2)}) copy-start(f32[5,16,16,128]{3,2,1,0:T(8,128)} %get-tuple-element.55.refs_2_) | copy-start | bytes 1966084
  37.3 2.2 %copy-start.8 = (f32[5,16,16,128]{3,2,1,0:T(8,128)S(1)}, f32[5,16,16,128]{3,2,1,0:T(8,128)}, u32[]{:S(2)}) copy-start(f32[5,16,16,128]{3,2,1,0:T(8,128)} %get-tuple-element.33) | copy-start | bytes 1966084
  37.3 2.2 %copy-start.9 = (f32[5,16,5,128]{3,2,1,0:T(8,128)S(1)}, f32[5,16,5,128]{3,2,1,0:T(8,128)}, u32[]{:S(2)}) copy-start(f32[5,16,5,128]{3,2,1,0:T(8,128)} %get-tuple-element.31) | copy-start | bytes 614404
  37.3 2.2 %copy-start.10 = (f32[5,16,5,128]{3,2,1,0:T(8,128)S(1)}, f32[5,16,5,128]{3,2,1,0:T(8,128)}, u32[]{:S(2)}) copy-start(f32[5,16,5,128]{3,2,1,0:T(8,128)} %get-tuple-element.32) | copy-start | bytes 614404
  64.4 2.0 %copy-start.12 = (f32[16,26,1,1]{1,0,3,2:T(8,128)S(1)}, f32[16,26,1,1]{1,0,3,2:T(8,128)}, u32[]{:S(2)}) copy-start(f32[16,26,1,1]{1,0,3,2:T(8,128)} %constant.41) | copy-start | bytes 4996

commit v32 on v27

--- a/solution.py
+++ b/solution.py
@@ -416,8 +416,8 @@
         jnp.concatenate([y_before, smoothed, y_after], axis=2),
         jnp.concatenate([x_after_y_before, x_after, both_after], axis=2),
     ]
-    result = sweep_lines(jnp.concatenate(sections, axis=1), smooth[0], 1)
-    return sweep_lines(result, smooth[1], 2)
+    result = sweep_lines(jnp.concatenate(sections, axis=1), smooth[1], 2)
+    return sweep_lines(result, smooth[0], 1)
 
 
 def sweep_zeta(value, matrix, tag):

time: 70.8 us -> 69.9 us (0.987)
  other arithmetic: 4.66 us -> 2.71 us
  local copies, waits for them, and re-layouts: 1.07 us -> 2.11 us
    concatenate x1 -> x0, other arithmetic: 1.95 us -> none  [filter_all(): result = sweep_lines(jnp.concatenate(sections, axis=1), smooth[0], 1)]
    transpose x0 -> x1, local copies, waits for them, and re-layouts: none -> 1.04 us  [sweep_lines(): return jnp.einsum(line_forms[dim], matrix, padded, precision=precision)]
where the time goes in v32:
time: 69.9 us; the launch traced here: 69.6 us
  Pallas kernels  53.8 us (77%)
  matrix products  10.7 us (15%)
  other arithmetic  2.71 us (4%)
  local copies, waits for them, and re-layouts  2.11 us (3%)
    pallas_call x2, Pallas kernels, exchange(): pl.pallas_call(functools.partial(exchange_kernel, tuple(routes), sizes, l...  30.9 us
    pallas_call x1, Pallas kernels, filter_all(): pl.pallas_call(functools.partial(filter_kernel, sizes), out_shape=[jax.Sh...  22.8 us
    dot_general x6, matrix products, sweep_lines(): return jnp.einsum(line_forms[dim], matrix, padded, precision=precision)  10.7 us
    add x1, other arithmetic, fluxes(): metrics[direction, 0] * totals[0] + metrics[direction, 1] * totals[1]  1.45 us

profile of v32, /device:TPU:1, one launch (start us, length us, event | category | flops | bytes accessed | tf_op | source)
XLA Modules:
  0.0 69.6 jit_solution(16121901950678751074)
XLA Ops:
  0.0 0.0 copy-start.11
  0.0 16.2 %shard_map.91 = (f32[4,26,16,128]{3,2,1,0:T(8,128)}, f32[4,16,5,128]{3,2,1,0:T(8,128)}, f32[4,16,5,128]{3,2,1,0:T(8,128)}, f32[4,16,16,128]{3,2,1,0:T(8,128)}, f...) custom-call(f32[5,16,16,128]{3,2,1,0:T(8,128)} %refs_0_.1, f32[128,128]{1,0:T(8,128)} %constant.30.refs_1_.refs_4_, ...), custom_call_target="tpu_custom_call" | custom-call | tf_op jit(solution)/shard_map/pallas_call | solution.py:171
  16.2 0.0 copy-start.7
  16.2 0.0 copy-start.6
  16.2 1.8 %convolution_bitcast_fusion = f32[4,16,16,128]{3,2,1,0:T(8,128)S(1)} fusion(f32[16,26,1,1]{1,0,3,2:T(8,128)} %constant.40, f32[4,16,5,128]{3,2,1,0:T(8,128)} %get-tuple-element.27, f32[4,16,16,128]{3,2,1,0:T(8,128)} %get-tuple-element.24, f32[4,16,5,128]{3,2,1,0:T(8,128)} %get-tuple-element.26), kind=kOutput, calls=%fused_computation.35 | convolution fusion | flops 20873216 | bytes 1377920 | tf_op jit(solution)/shard_map/al,fxlz->fxaz/dot_general | solution.py:506
  18.0 0.0 copy-done.11
  18.0 0.0 copy-done.7
  18.0 0.0 copy-start.1
  18.1 0.0 copy-start
  18.1 0.0 copy-start.2
  18.1 0.0 copy-start.3
  18.1 0.0 copy-start.5
  18.1 0.6 fusion.52
  18.7 0.2 copy.30
  18.9 0.2 copy-done.1
  19.2 0.0 copy-done.6
  19.2 0.4 copy-done
  19.5 0.1 copy-done.2
  19.6 0.0 copy-done.3
  19.7 0.0 copy-done.5
  19.7 0.2 bitcast_dynamic-update-slice_fusion.11
  19.9 0.1 bitcast_dynamic-update-slice_fusion.10
  20.0 0.1 bitcast_dynamic-update-slice_fusion.9
  20.2 0.2 bitcast_dynamic-update-slice_fusion.8
  20.4 0.1 bitcast_dynamic-update-slice_fusion.6
  20.5 0.1 bitcast_dynamic-update-slice_fusion.5
  20.6 0.1 bitcast_dynamic-update-slice_fusion.4
  20.8 0.1 bitcast_dynamic-update-slice_fusion
  21.0 0.1 slice_bitcast_fusion.14
  21.1 1.5 %multiply_add_fusion = (f32[5,16,16,128]{3,2,1,0:T(8,128)}, f32[5,16,16,128]{3,2,1,0:T(8,128)}, f32[5,16,16,128]{3,2,1,0:T(8,128)}) fusion(f32[5,16,16,128]{3,2,1,0:T(8,128)S(1)} %bitcast_dynamic-update-slice_fusion, f32[5,16,16,128]{3,2,1,0:T(8,128)S(1)} %bitcast_dynamic-update-slice_fusion.4, f32[5,16,16,128]{3,2,1,0:T(8,128)S(1)} %get-tuple-element.68, ...), kind=kLoop, calls=%fused_computation.43 | loop fusion | flops 2457600 | bytes 5111808 | tf_op jit(solution)/shard_map/add | solution.py:570
  22.5 14.8 %shard_map.92 = (f32[5,26,16,128]{3,2,1,0:T(8,128)}, f32[5,16,5,128]{3,2,1,0:T(8,128)}, f32[5,16,5,128]{3,2,1,0:T(8,128)}, f32[5,16,16,128]{3,2,1,0:T(8,128)}) custom-call(f32[5,16,16,128]{3,2,1,0:T(8,128)} %get-tuple-element.56.refs_0_.refs_1_, f32[5,16,16,128]{3,2,1,0:T(8,128)} %get-tuple-element.56.refs_0_.refs_1_, ...), custom_call_target="tpu_custom_call" | custom-call | tf_op jit(solution)/shard_map/pallas_call | solution.py:171
  37.3 0.0 copy-start.4
  37.3 0.0 copy-start.8
  37.3 0.0 copy-start.9
  37.3 0.0 copy-start.10
  37.3 2.1 %fusion.27 = f32[5,16,128,16]{2,3,1,0:T(8,128)S(1)} fusion(f32[16,26,1,1]{1,0,3,2:T(8,128)S(1)} %copy-done.11, f32[5,26,16,128]{3,2,1,0:T(8,128)} %get-tuple-element.30), kind=kOutput, calls=%fused_computation.27 | convolution fusion | flops 25559040 | bytes 1721984 | tf_op jit(solution)/shard_map/al,flyz->fayz/dot_general | solution.py:506
  39.5 0.0 copy-done.4
  39.5 0.0 copy-done.8
  39.5 0.0 copy-done.9
  39.5 0.0 copy-done.10
  39.5 0.0 copy-start.12
  39.6 1.7 %fusion.44.value_ref = f32[5,16,16,128]{3,2,1,0:T(8,128)} fusion(f32[5,16,16,128]{3,2,1,0:T(8,128)S(1)} %copy-done.1, f32[5,16,16,128]{3,2,1,0:T(8,128)S(1)} %copy-done.8, f32[16,26,1,1]{1,0,3,2:T(8,128)S(1)} %copy-done.11, f32[5,16,5,128]{3,2,1,0:T(8,128)S(1)} %copy-done.10, f32[5,16,16,128]{3,2,1,0:T(8,128)S(1)} %copy-done.4, ...), kind=kOutput, calls=%fused_computation.34 | convolution fusion | flops 26746880 | bytes 3819136 | tf_op jit(solution)/shard_map/al,fxlz->fxaz/dot_general | solution.py:506
  41.2 22.8 %shard_map.93 = (f32[5,16,16,128]{3,2,1,0:T(8,128)}, f32[5,5,16,128]{3,2,1,0:T(8,128)}, f32[5,5,16,128]{3,2,1,0:T(8,128)}, f32[5,16,5,128]{3,2,1,0:T(8,128)}, f3...) custom-call(f32[5,16,16,128]{3,2,1,0:T(8,128)} %fusion.44.value_ref,, ...), custom_call_target="tpu_custom_call" | custom-call | tf_op jit(solution)/shard_map/pallas_call | solution.py:393
  64.0 0.0 copy-done.12
  64.1 3.3 %fusion = f32[5,26,128,16]{2,3,1,0:T(8,128)S(1)} fusion(f32[16,26,1,1]{1,0,3,2:T(8,128)S(1)} %copy-done.12, f32[5,5,5,128]{3,2,1,0:T(8,128)} %get-tuple-element.42, f32[5,5,16,128]{3,2,1,0:T(8,128)} %get-tuple-element.41, f32[5,5,5,128]{3,2,1,0:T(8,128)} %get-tuple-element.40, f32[5,16,5,128]{3,2,1,0:T(8,128)} %get-tuple-element.39, ...), kind=kOutput, calls=%fused_computation | convolution fusion | flops 86528000 | bytes 2797184 | tf_op jit(solution)/shard_map/al,fxlz->fxaz/dot_general | solution.py:506
  67.4 1.2 %fusion.29 = f32[5,16,16,128]{3,1,2,0:T(8,128)S(1)} fusion(f32[16,26,1,1]{1,0,3,2:T(8,128)S(1)} %copy-done.12, f32[5,26,128,16]{2,3,1,0:T(8,128)S(1)} %fusion), kind=kOutput, calls=%fused_computation.29 | convolution fusion | flops 51118080 | bytes 1721984 | tf_op jit(solution)/shard_map/al,flyz->fayz/dot_general | solution.py:506
  68.6 1.0 %copy.14 = f32[5,16,16,128]{3,2,1,0:T(8,128)} copy(f32[5,16,16,128]{3,1,2,0:T(8,128)S(1)} %fusion.29) | data formatting | bytes 1310720 | tf_op jit(solution)/shard_map/al,flyz->fayz/transpose | solution.py:506
  (5 shorter events, 0.1 us)
Async XLA Ops:
  0.0 18.0 %copy-start.11 = (f32[16,26,1,1]{1,0,3,2:T(8,128)S(1)}, f32[16,26,1,1]{1,0,3,2:T(8,128)}, u32[]{:S(2)}) copy-start(f32[16,26,1,1]{1,0,3,2:T(8,128)} %constant.40) | copy-start | bytes 4996
  16.2 1.9 %copy-start.7 = (f32[4,26,16,128]{3,2,1,0:T(8,128)S(1)}, f32[4,26,16,128]{3,2,1,0:T(8,128)}, u32[]{:S(2)}) copy-start(f32[4,26,16,128]{3,2,1,0:T(8,128)} %get-tuple-element.25) | copy-start | bytes 2555908
  16.2 3.0 %copy-start.6 = (f32[4,16,16,128]{3,2,1,0:T(8,128)S(1)}, f32[4,16,16,128]{3,2,1,0:T(8,128)}, u32[]{:S(2)}) copy-start(f32[4,16,16,128]{3,2,1,0:T(8,128)} %get-tuple-element.28) | copy-start | bytes 1572868
  18.0 1.1 %copy-start.1 = (f32[5,16,16,128]{3,2,1,0:T(8,128)S(1)}, f32[5,16,16,128]{3,2,1,0:T(8,128)}, u32[]{:S(2)}) copy-start(f32[5,16,16,128]{3,2,1,0:T(8,128)} %refs_0_.1) | copy-start | bytes 1966084
  18.1 1.5 %copy-start = (f32[3,3,16,16,128]{4,3,2,1,0:T(8,128)S(1)}, f32[3,3,16,16,128]{4,3,2,1,0:T(8,128)}, u32[]{:S(2)}) copy-start(f32[3,3,16,16,128]{4,3,2,1,0:T(8,128)} %param.10) | copy-start | bytes 3538948
  18.1 1.6 %copy-start.2 = (f32[4,16,16,128]{3,2,1,0:T(8,128)S(1)}, f32[4,16,16,128]{3,2,1,0:T(8,128)}, u32[]{:S(2)}) copy-start(f32[4,16,16,128]{3,2,1,0:T(8,128)} %get-tuple-element.24) | copy-start | bytes 1572868
  18.1 1.6 %copy-start.3 = (f32[16,16,128]{2,1,0:T(8,128)S(1)}, f32[16,16,128]{2,1,0:T(8,128)}, u32[]{:S(2)}) copy-start(f32[16,16,128]{2,1,0:T(8,128)} %param.11) | copy-start | bytes 393220
  18.1 1.6 %copy-start.5 = (f32[16,16,128]{2,1,0:T(8,128)S(1)}, f32[16,16,128]{2,1,0:T(8,128)}, u32[]{:S(2)}) copy-start(f32[16,16,128]{2,1,0:T(8,128)} %get-tuple-element.29) | copy-start | bytes 393220
  37.3 2.2 %copy-start.4 = (f32[5,16,16,128]{3,2,1,0:T(8,128)S(1)}, f32[5,16,16,128]{3,2,1,0:T(8,128)}, u32[]{:S(2)}) copy-start(f32[5,16,16,128]{3,2,1,0:T(8,128)} %get-tuple-element.55.refs_2_) | copy-start | bytes 1966084
  37.3 2.2 %copy-start.8 = (f32[5,16,16,128]{3,2,1,0:T(8,128)S(1)}, f32[5,16,16,128]{3,2,1,0:T(8,128)}, u32[]{:S(2)}) copy-start(f32[5,16,16,128]{3,2,1,0:T(8,128)} %get-tuple-element.33) | copy-start | bytes 1966084
  37.3 2.2 %copy-start.9 = (f32[5,16,5,128]{3,2,1,0:T(8,128)S(1)}, f32[5,16,5,128]{3,2,1,0:T(8,128)}, u32[]{:S(2)}) copy-start(f32[5,16,5,128]{3,2,1,0:T(8,128)} %get-tuple-element.31) | copy-start | bytes 614404
  37.3 2.2 %copy-start.10 = (f32[5,16,5,128]{3,2,1,0:T(8,128)S(1)}, f32[5,16,5,128]{3,2,1,0:T(8,128)}, u32[]{:S(2)}) copy-start(f32[5,16,5,128]{3,2,1,0:T(8,128)} %get-tuple-element.32) | copy-start | bytes 614404
  39.5 24.5 %copy-start.12 = (f32[16,26,1,1]{1,0,3,2:T(8,128)S(1)}, f32[16,26,1,1]{1,0,3,2:T(8,128)}, u32[]{:S(2)}) copy-start(f32[16,26,1,1]{1,0,3,2:T(8,128)} %constant.41) | copy-start | bytes 4996

commit v33 on v32

--- a/solution.py
+++ b/solution.py
@@ -412,11 +412,11 @@
     )
     smoothed, x_before, x_after, y_before, y_after, both_before, x_after_y_before, x_before_y_after, both_after = outs
     sections = [
-        jnp.concatenate([both_before, x_before, x_before_y_after], axis=2),
-        jnp.concatenate([y_before, smoothed, y_after], axis=2),
-        jnp.concatenate([x_after_y_before, x_after, both_after], axis=2),
-    ]
-    result = sweep_lines(jnp.concatenate(sections, axis=1), smooth[1], 2)
+        jnp.concatenate([both_before, y_before, x_after_y_before], axis=1),
+        jnp.concatenate([x_before, smoothed, x_after], axis=1),
+        jnp.concatenate([x_before_y_after, y_after, both_after], axis=1),
+    ]
+    result = sweep_lines(jnp.concatenate(sections, axis=2), smooth[1], 2)
     return sweep_lines(result, smooth[0], 1)
 
 

time: 69.9 us -> 69.9 us (level)
  no operation moved by 1% of the time
where the time goes in v33:
time: 69.9 us; the launch traced here: 69.6 us
  Pallas kernels  53.8 us (77%)
  matrix products  10.7 us (15%)
  other arithmetic  2.71 us (4%)
  local copies, waits for them, and re-layouts  2.11 us (3%)
    pallas_call x2, Pallas kernels, exchange(): pl.pallas_call(functools.partial(exchange_kernel, tuple(routes), sizes, l...  30.9 us
    pallas_call x1, Pallas kernels, filter_all(): pl.pallas_call(functools.partial(filter_kernel, sizes), out_shape=[jax.Sh...  22.8 us
    dot_general x6, matrix products, sweep_lines(): return jnp.einsum(line_forms[dim], matrix, padded, precision=precision)  10.7 us
    add x1, other arithmetic, fluxes(): metrics[direction, 0] * totals[0] + metrics[direction, 1] * totals[1]  1.45 us

profile of v33, /device:TPU:1, one launch (start us, length us, event | category | flops | bytes accessed | tf_op | source)
XLA Modules:
  0.0 69.6 jit_solution(12483349336509318256)
XLA Ops:
  0.0 0.0 copy-start.11
  0.0 16.2 %shard_map.91 = (f32[4,26,16,128]{3,2,1,0:T(8,128)}, f32[4,16,5,128]{3,2,1,0:T(8,128)}, f32[4,16,5,128]{3,2,1,0:T(8,128)}, f32[4,16,16,128]{3,2,1,0:T(8,128)}, f...) custom-call(f32[5,16,16,128]{3,2,1,0:T(8,128)} %refs_0_.1, f32[128,128]{1,0:T(8,128)} %constant.30.refs_1_.refs_4_, ...), custom_call_target="tpu_custom_call" | custom-call | tf_op jit(solution)/shard_map/pallas_call | solution.py:171
  16.2 0.0 copy-start.7
  16.2 0.0 copy-start.6
  16.2 1.8 %convolution_bitcast_fusion = f32[4,16,16,128]{3,2,1,0:T(8,128)S(1)} fusion(f32[16,26,1,1]{1,0,3,2:T(8,128)} %constant.40, f32[4,16,5,128]{3,2,1,0:T(8,128)} %get-tuple-element.27, f32[4,16,16,128]{3,2,1,0:T(8,128)} %get-tuple-element.24, f32[4,16,5,128]{3,2,1,0:T(8,128)} %get-tuple-element.26), kind=kOutput, calls=%fused_computation.35 | convolution fusion | flops 20873216 | bytes 1377920 | tf_op jit(solution)/shard_map/al,fxlz->fxaz/dot_general | solution.py:506
  18.0 0.0 copy-done.11
  18.0 0.0 copy-done.7
  18.0 0.0 copy-start.1
  18.1 0.0 copy-start
  18.1 0.0 copy-start.2
  18.1 0.0 copy-start.3
  18.1 0.0 copy-start.5
  18.1 0.6 fusion.52
  18.7 0.2 copy.30
  18.9 0.2 copy-done.1
  19.2 0.0 copy-done.6
  19.2 0.4 copy-done
  19.5 0.1 copy-done.2
  19.6 0.0 copy-done.3
  19.7 0.0 copy-done.5
  19.7 0.2 bitcast_dynamic-update-slice_fusion.11
  19.9 0.1 bitcast_dynamic-update-slice_fusion.10
  20.0 0.1 bitcast_dynamic-update-slice_fusion.9
  20.2 0.2 bitcast_dynamic-update-slice_fusion.8
  20.4 0.1 bitcast_dynamic-update-slice_fusion.6
  20.5 0.1 bitcast_dynamic-update-slice_fusion.5
  20.6 0.1 bitcast_dynamic-update-slice_fusion.4
  20.8 0.1 bitcast_dynamic-update-slice_fusion
  21.0 0.1 slice_bitcast_fusion.14
  21.1 1.5 %multiply_add_fusion = (f32[5,16,16,128]{3,2,1,0:T(8,128)}, f32[5,16,16,128]{3,2,1,0:T(8,128)}, f32[5,16,16,128]{3,2,1,0:T(8,128)}) fusion(f32[5,16,16,128]{3,2,1,0:T(8,128)S(1)} %bitcast_dynamic-update-slice_fusion, f32[5,16,16,128]{3,2,1,0:T(8,128)S(1)} %bitcast_dynamic-update-slice_fusion.4, f32[5,16,16,128]{3,2,1,0:T(8,128)S(1)} %get-tuple-element.68, ...), kind=kLoop, calls=%fused_computation.43 | loop fusion | flops 2457600 | bytes 5111808 | tf_op jit(solution)/shard_map/add | solution.py:570
  22.5 14.8 %shard_map.92 = (f32[5,26,16,128]{3,2,1,0:T(8,128)}, f32[5,16,5,128]{3,2,1,0:T(8,128)}, f32[5,16,5,128]{3,2,1,0:T(8,128)}, f32[5,16,16,128]{3,2,1,0:T(8,128)}) custom-call(f32[5,16,16,128]{3,2,1,0:T(8,128)} %get-tuple-element.56.refs_0_.refs_1_, f32[5,16,16,128]{3,2,1,0:T(8,128)} %get-tuple-element.56.refs_0_.refs_1_, ...), custom_call_target="tpu_custom_call" | custom-call | tf_op jit(solution)/shard_map/pallas_call | solution.py:171
  37.3 0.0 copy-start.4
  37.3 0.0 copy-start.8
  37.3 0.0 copy-start.9
  37.3 0.0 copy-start.10
  37.3 2.1 %fusion.27 = f32[5,16,128,16]{2,3,1,0:T(8,128)S(1)} fusion(f32[16,26,1,1]{1,0,3,2:T(8,128)S(1)} %copy-done.11, f32[5,26,16,128]{3,2,1,0:T(8,128)} %get-tuple-element.30), kind=kOutput, calls=%fused_computation.27 | convolution fusion | flops 25559040 | bytes 1721984 | tf_op jit(solution)/shard_map/al,flyz->fayz/dot_general | solution.py:506
  39.5 0.0 copy-done.4
  39.5 0.0 copy-done.8
  39.5 0.0 copy-done.9
  39.5 0.0 copy-done.10
  39.5 0.0 copy-start.12
  39.6 1.7 %fusion.44.value_ref = f32[5,16,16,128]{3,2,1,0:T(8,128)} fusion(f32[5,16,16,128]{3,2,1,0:T(8,128)S(1)} %copy-done.1, f32[5,16,16,128]{3,2,1,0:T(8,128)S(1)} %copy-done.8, f32[16,26,1,1]{1,0,3,2:T(8,128)S(1)} %copy-done.11, f32[5,16,5,128]{3,2,1,0:T(8,128)S(1)} %copy-done.10, f32[5,16,16,128]{3,2,1,0:T(8,128)S(1)} %copy-done.4, ...), kind=kOutput, calls=%fused_computation.34 | convolution fusion | flops 26746880 | bytes 3819136 | tf_op jit(solution)/shard_map/al,fxlz->fxaz/dot_general | solution.py:506
  41.2 22.8 %shard_map.93 = (f32[5,16,16,128]{3,2,1,0:T(8,128)}, f32[5,5,16,128]{3,2,1,0:T(8,128)}, f32[5,5,16,128]{3,2,1,0:T(8,128)}, f32[5,16,5,128]{3,2,1,0:T(8,128)}, f3...) custom-call(f32[5,16,16,128]{3,2,1,0:T(8,128)} %fusion.44.value_ref,, ...), custom_call_target="tpu_custom_call" | custom-call | tf_op jit(solution)/shard_map/pallas_call | solution.py:393
  64.0 0.0 copy-done.12
  64.1 3.3 %fusion = f32[5,26,128,16]{2,3,1,0:T(8,128)S(1)} fusion(f32[16,26,1,1]{1,0,3,2:T(8,128)S(1)} %copy-done.12, f32[5,5,5,128]{3,2,1,0:T(8,128)} %get-tuple-element.42, f32[5,16,5,128]{3,2,1,0:T(8,128)} %get-tuple-element.41, f32[5,5,5,128]{3,2,1,0:T(8,128)} %get-tuple-element.40, f32[5,5,16,128]{3,2,1,0:T(8,128)} %get-tuple-element.39, ...), kind=kOutput, calls=%fused_computation | convolution fusion | flops 86528000 | bytes 2797184 | tf_op jit(solution)/shard_map/al,fxlz->fxaz/dot_general | solution.py:506
  67.3 1.2 %fusion.29 = f32[5,16,16,128]{3,1,2,0:T(8,128)S(1)} fusion(f32[16,26,1,1]{1,0,3,2:T(8,128)S(1)} %copy-done.12, f32[5,26,128,16]{2,3,1,0:T(8,128)S(1)} %fusion), kind=kOutput, calls=%fused_computation.29 | convolution fusion | flops 51118080 | bytes 1721984 | tf_op jit(solution)/shard_map/al,flyz->fayz/dot_general | solution.py:506
  68.5 1.0 %copy.14 = f32[5,16,16,128]{3,2,1,0:T(8,128)} copy(f32[5,16,16,128]{3,1,2,0:T(8,128)S(1)} %fusion.29) | data formatting | bytes 1310720 | tf_op jit(solution)/shard_map/al,flyz->fayz/transpose | solution.py:506
  (5 shorter events, 0.1 us)
Async XLA Ops:
  0.0 18.0 %copy-start.11 = (f32[16,26,1,1]{1,0,3,2:T(8,128)S(1)}, f32[16,26,1,1]{1,0,3,2:T(8,128)}, u32[]{:S(2)}) copy-start(f32[16,26,1,1]{1,0,3,2:T(8,128)} %constant.40) | copy-start | bytes 4996
  16.2 1.9 %copy-start.7 = (f32[4,26,16,128]{3,2,1,0:T(8,128)S(1)}, f32[4,26,16,128]{3,2,1,0:T(8,128)}, u32[]{:S(2)}) copy-start(f32[4,26,16,128]{3,2,1,0:T(8,128)} %get-tuple-element.25) | copy-start | bytes 2555908
  16.2 3.0 %copy-start.6 = (f32[4,16,16,128]{3,2,1,0:T(8,128)S(1)}, f32[4,16,16,128]{3,2,1,0:T(8,128)}, u32[]{:S(2)}) copy-start(f32[4,16,16,128]{3,2,1,0:T(8,128)} %get-tuple-element.28) | copy-start | bytes 1572868
  18.0 1.1 %copy-start.1 = (f32[5,16,16,128]{3,2,1,0:T(8,128)S(1)}, f32[5,16,16,128]{3,2,1,0:T(8,128)}, u32[]{:S(2)}) copy-start(f32[5,16,16,128]{3,2,1,0:T(8,128)} %refs_0_.1) | copy-start | bytes 1966084
  18.1 1.5 %copy-start = (f32[3,3,16,16,128]{4,3,2,1,0:T(8,128)S(1)}, f32[3,3,16,16,128]{4,3,2,1,0:T(8,128)}, u32[]{:S(2)}) copy-start(f32[3,3,16,16,128]{4,3,2,1,0:T(8,128)} %param.10) | copy-start | bytes 3538948
  18.1 1.6 %copy-start.2 = (f32[4,16,16,128]{3,2,1,0:T(8,128)S(1)}, f32[4,16,16,128]{3,2,1,0:T(8,128)}, u32[]{:S(2)}) copy-start(f32[4,16,16,128]{3,2,1,0:T(8,128)} %get-tuple-element.24) | copy-start | bytes 1572868
  18.1 1.6 %copy-start.3 = (f32[16,16,128]{2,1,0:T(8,128)S(1)}, f32[16,16,128]{2,1,0:T(8,128)}, u32[]{:S(2)}) copy-start(f32[16,16,128]{2,1,0:T(8,128)} %param.11) | copy-start | bytes 393220
  18.1 1.6 %copy-start.5 = (f32[16,16,128]{2,1,0:T(8,128)S(1)}, f32[16,16,128]{2,1,0:T(8,128)}, u32[]{:S(2)}) copy-start(f32[16,16,128]{2,1,0:T(8,128)} %get-tuple-element.29) | copy-start | bytes 393220
  37.3 2.2 %copy-start.4 = (f32[5,16,16,128]{3,2,1,0:T(8,128)S(1)}, f32[5,16,16,128]{3,2,1,0:T(8,128)}, u32[]{:S(2)}) copy-start(f32[5,16,16,128]{3,2,1,0:T(8,128)} %get-tuple-element.55.refs_2_) | copy-start | bytes 1966084
  37.3 2.2 %copy-start.8 = (f32[5,16,16,128]{3,2,1,0:T(8,128)S(1)}, f32[5,16,16,128]{3,2,1,0:T(8,128)}, u32[]{:S(2)}) copy-start(f32[5,16,16,128]{3,2,1,0:T(8,128)} %get-tuple-element.33) | copy-start | bytes 1966084
  37.3 2.2 %copy-start.9 = (f32[5,16,5,128]{3,2,1,0:T(8,128)S(1)}, f32[5,16,5,128]{3,2,1,0:T(8,128)}, u32[]{:S(2)}) copy-start(f32[5,16,5,128]{3,2,1,0:T(8,128)} %get-tuple-element.31) | copy-start | bytes 614404
  37.3 2.2 %copy-start.10 = (f32[5,16,5,128]{3,2,1,0:T(8,128)S(1)}, f32[5,16,5,128]{3,2,1,0:T(8,128)}, u32[]{:S(2)}) copy-start(f32[5,16,5,128]{3,2,1,0:T(8,128)} %get-tuple-element.32) | copy-start | bytes 614404
  39.5 24.5 %copy-start.12 = (f32[16,26,1,1]{1,0,3,2:T(8,128)S(1)}, f32[16,26,1,1]{1,0,3,2:T(8,128)}, u32[]{:S(2)}) copy-start(f32[16,26,1,1]{1,0,3,2:T(8,128)} %constant.41) | copy-start | bytes 4996
